TPU v7x, 32 devices: a whole 2x2x4 slice. The times are simulated.
32 devices in a mesh: fsdp: 8 (over z, y), tp: 4 (over x, core).
Axes of the slice: x: 2, y: 2, z: 4, core: 2. Of those that a mesh axis runs over, the one named last changes fastest.
Arguments:
- tokens: bfloat16 [2, 2048, 1024], P(None, 'fsdp'), may hold values from -6 to 6
- cotangent: bfloat16 [2, 2048, 1024], P(None, 'fsdp'), may hold values from -6 to 6
- perm: int32 [2, 2048], replicated, may hold values from 0 to 2047, as said below
- lengths: int32 [2, 8], replicated, may hold values from 1 to 1024, 2048 in all within a row
- w_qkv: bfloat16 [1024, 3, 1024], P('fsdp', None, 'tp'), may hold values from -0.1875 to 0.1875
- w_attn_out: bfloat16 [1024, 1024], P('fsdp', 'tp'), may hold values from -6 to 6
- w_in: bfloat16 [1024, 2, 2624], P('fsdp', None, 'tp'), may hold values from -0.1875 to 0.1875
- w_down: bfloat16 [1024, 2624], P('fsdp', 'tp'), may hold values from -0.125 to 0.125
- gain_one: bfloat16 [1024], P('fsdp'), may hold values from 0.099609375 to 1.8984375
- gain_two: bfloat16 [1024], P('fsdp'), may hold values from 0.099609375 to 1.8984375
Outputs:
- output: bfloat16 [2, 2048, 1024], P(None, 'fsdp')
- input_grad: bfloat16 [2, 2048, 1024], P(None, 'fsdp')
- grad_qkv: float32 [1024, 3, 1024], P('fsdp', None, 'tp')
- grad_attn_out: float32 [1024, 1024], P('fsdp', 'tp')
- grad_in: float32 [1024, 2, 2624], P('fsdp', None, 'tp')
- grad_down: float32 [1024, 2624], P('fsdp', 'tp')
- grad_gain_one: float32 [1024], P('fsdp')
- grad_gain_two: float32 [1024], P('fsdp')
Inputs may be any that keep to these rules, and one draw needn't show every extreme that they name: perm[m, d * 256 + j] is the initial token of micro-batch m taken at slot j of fsdp index d; each row is a permutation, and fsdp index d takes exactly 32 tokens from each index's block of 256 initial tokens. lengths[m] sum to 2048; the longest is exactly 1024.
All inputs are finite; a program needn't handle non-finite values.
Results may differ from a plain program's by a relative error of at most 0.025.
Values may be sent and summed in bfloat16 or wider, within the bound.
No kernel may reach another device: no remote copies, remote signals or barrier semaphores. Data moves between devices by JAX's collectives and lax.ppermute only.
A program may use at most 192 MiB of HBM per device.

v0:
```python
import jax
import jax.numpy as jnp
from jax import lax
from jax.sharding import PartitionSpec as P

D = 1024
HD = 64


EPS = 1e-05
THETA = 160000.0
key_block = 2048


def layer_norm(values, gain):
    center = values - jnp.mean(values, axis=-1, keepdims=True)
    spread = jnp.mean(center * center, axis=-1, keepdims=True)
    return center * lax.rsqrt(spread + EPS) * gain


def rope_tables(position, width):
    freqs = jnp.power(THETA, -jnp.arange(width // 2, dtype=jnp.float32) * 2.0 / width)
    angle = position.astype(jnp.float32)[:, None] * freqs[None, :]
    angle = jnp.concatenate([angle, angle], axis=-1)
    return (jnp.cos(angle), jnp.sin(angle))


def rotate(values, cosine, sine):
    half = values.shape[-1] // 2
    turned = jnp.concatenate([-values[..., half:], values[..., :half]], axis=-1)
    return values * cosine[:, None, :] + turned * sine[:, None, :]


def seq_info(anchor, seq_lens):
    ends = jnp.cumsum(seq_lens)
    starts = ends - seq_lens
    segment = jnp.sum((anchor[:, None] >= ends[None, :]).astype(jnp.int32), axis=1)
    onehot = segment[:, None] == jnp.arange(seq_lens.shape[0], dtype=jnp.int32)[None, :]
    position = anchor - jnp.sum(jnp.where(onehot, starts[None, :], 0), axis=1)
    return (segment, position)


def blockwise(running, pieces, offset, step_fn):
    piece_len = pieces[0].shape[0]
    if piece_len > key_block and piece_len % key_block == 0:
        block_count = piece_len // key_block
        stacked = tuple((one.reshape((block_count, key_block) + one.shape[1:]) for one in pieces))

        def inner(state_now, scan_item):
            block_index, piece_parts = scan_item
            return (step_fn(state_now, piece_parts, offset + block_index * key_block), None)

        running, _ = lax.scan(inner, running, (jnp.arange(block_count, dtype=jnp.int32), stacked))
        return running
    return step_fn(running, pieces, offset)


def on_device(
    tokens, cotangent, perm, lengths, w_qkv, w_attn_out, w_in, w_down, gain_one, gain_two
):
    groups = lax.axis_size("fsdp")
    my_index = lax.axis_index("fsdp")
    micro_count = tokens.shape[0]
    tok_rows = tokens.shape[1]
    total_rows = tok_rows * groups
    per_pair = tok_rows // groups
    head_cols = w_qkv.shape[2]
    head_count = head_cols // HD
    unit_cols = w_in.shape[2]
    score_scale = HD ** (-0.5)
    rows_idx = jnp.arange(tok_rows, dtype=jnp.int32)
    f32 = jnp.float32
    bf16 = jnp.bfloat16
    dims_rows = (((0,), (0,)), ((), ()))
    dims_cols = (((1,), (1,)), ((), ()))
    acc_qkv = jnp.zeros((D, 3, head_cols), f32)
    acc_out = jnp.zeros((D, head_cols), f32)
    acc_in = jnp.zeros((D, 2, unit_cols), f32)
    acc_down = jnp.zeros((D, unit_cols), f32)
    acc_gain_one = jnp.zeros((D,), f32)
    acc_gain_two = jnp.zeros((D,), f32)
    outputs = []
    input_grads = []
    for micro_idx in range(micro_count):
        perm_row = perm[micro_idx]
        seq_lens = lengths[micro_idx]
        inverse = (
            jnp.zeros((total_rows,), jnp.int32)
            .at[perm_row]
            .set(jnp.arange(total_rows, dtype=jnp.int32))
        )
        placed = lax.dynamic_slice_in_dim(inverse, my_index * tok_rows, tok_rows)
        send_order = jnp.argsort(placed)
        outgoing = tokens[micro_idx][send_order].reshape(groups, per_pair, D)
        arrived = lax.all_to_all(outgoing, "fsdp", split_axis=0, concat_axis=0, tiled=True).reshape(
            tok_rows, D
        )
        my_tokens = lax.dynamic_slice_in_dim(perm_row, my_index * tok_rows, tok_rows)
        source = my_tokens // tok_rows
        recv_order = jnp.argsort(source * tok_rows + rows_idx)
        recv_slot = jnp.zeros((tok_rows,), jnp.int32).at[recv_order].set(rows_idx)
        dealt = arrived[recv_slot]
        fetched = (
            lax.all_gather(gain_one, "fsdp", axis=0, tiled=True),
            lax.all_gather(gain_two, "fsdp", axis=0, tiled=True),
            lax.all_gather(w_qkv, "fsdp", axis=0, tiled=True),
            lax.all_gather(w_attn_out, "fsdp", axis=0, tiled=True),
            lax.all_gather(w_in, "fsdp", axis=0, tiled=True),
            lax.all_gather(w_down, "fsdp", axis=0, tiled=True),
        )
        gain_first = fetched[0].astype(f32)
        gain_second = fetched[1].astype(f32)
        query_seg, query_pos = seq_info(my_tokens, seq_lens)
        cosine, sine = rope_tables(query_pos, HD)
        x_float = dealt.astype(f32)
        normed_low = layer_norm(x_float, gain_first).astype(bf16)
        raw_proj = jnp.einsum("td,dcf->tcf", normed_low, fetched[2], preferred_element_type=f32)
        raw_heads = raw_proj.reshape(tok_rows, 3, head_count, HD)
        query_low = rotate(raw_heads[:, 0], cosine, sine).astype(bf16)
        key_low = rotate(raw_heads[:, 1], cosine, sine).astype(bf16)
        value_low = raw_heads[:, 2].astype(bf16)

        def forward_step(running, piece_parts, offset):
            run_peak, run_total, run_acc = running
            key_part, value_part = piece_parts
            key_seg, _ = seq_info(
                lax.dynamic_slice_in_dim(perm_row, offset, key_part.shape[0]), seq_lens
            )
            scores = (
                jnp.einsum("qhe,khe->hqk", query_low, key_part, preferred_element_type=f32)
                * score_scale
            )
            same_seq = (query_seg[:, None] == key_seg[None, :])[None]
            block_top = jnp.max(jnp.where(same_seq, scores, -1e30), axis=-1)
            new_peak = jnp.maximum(run_peak, block_top)
            weights = jnp.where(same_seq, jnp.exp(scores - new_peak[..., None]), 0.0)
            fade_factor = jnp.exp(run_peak - new_peak)
            run_acc = run_acc * jnp.transpose(fade_factor)[:, :, None] + jnp.einsum(
                "hqk,khe->qhe", weights.astype(bf16), value_part, preferred_element_type=f32
            )
            run_total = run_total * fade_factor + jnp.sum(weights, axis=-1)
            return (new_peak, run_total, run_acc)

        start_state = (
            jnp.full((head_count, tok_rows), -1e30, f32),
            jnp.zeros((head_count, tok_rows), f32),
            jnp.zeros((tok_rows, head_count, HD), f32),
        )
        run_peak, run_total, run_acc = blockwise(
            start_state,
            (
                lax.all_gather(key_low, "fsdp", axis=0, tiled=True),
                lax.all_gather(value_low, "fsdp", axis=0, tiled=True),
            ),
            jnp.int32(0),
            forward_step,
        )
        log_total = run_peak + jnp.log(run_total)
        mixed_heads = run_acc / jnp.transpose(run_total)[:, :, None]
        mixed_low = mixed_heads.reshape(tok_rows, head_cols).astype(bf16)
        attn_part = lax.dot_general(mixed_low, fetched[3], dims_cols, preferred_element_type=f32)
        branch = lax.psum(attn_part.astype(jnp.bfloat16), "tp").astype(jnp.float32)
        hidden = x_float + branch
        normed_two = layer_norm(hidden, gain_second).astype(bf16)
        ffn_proj = jnp.einsum("td,dcf->tcf", normed_two, fetched[4], preferred_element_type=f32)
        act_low = (jax.nn.gelu(ffn_proj[:, 0], approximate=False) * ffn_proj[:, 1]).astype(bf16)
        ffn_part = lax.dot_general(act_low, fetched[5], dims_cols, preferred_element_type=f32)
        branch_two = lax.psum(ffn_part.astype(jnp.bfloat16), "tp").astype(jnp.float32)
        outputs.append((hidden + branch_two).astype(bf16))
        again = (
            lax.all_gather(gain_one, "fsdp", axis=0, tiled=True),
            lax.all_gather(gain_two, "fsdp", axis=0, tiled=True),
            lax.all_gather(w_qkv, "fsdp", axis=0, tiled=True),
            lax.all_gather(w_attn_out, "fsdp", axis=0, tiled=True),
            lax.all_gather(w_in, "fsdp", axis=0, tiled=True),
            lax.all_gather(w_down, "fsdp", axis=0, tiled=True),
        )
        gain_first = again[0].astype(f32)
        gain_second = again[1].astype(f32)
        grad_low = cotangent[micro_idx]
        grad_float = grad_low.astype(f32)
        acc_down = acc_down + lax.dot_general(
            grad_low, act_low, dims_rows, preferred_element_type=f32
        )
        d_act = jnp.dot(grad_low, again[5], preferred_element_type=f32)
        _, gelu_pull = jax.vjp(
            lambda inputs, gates: jax.nn.gelu(inputs, approximate=False) * gates,
            ffn_proj[:, 0],
            ffn_proj[:, 1],
        )
        d_inputs, d_gates = gelu_pull(d_act)
        d_proj = jnp.stack([d_inputs, d_gates], axis=1).astype(bf16)
        acc_in = acc_in + jnp.einsum("td,tcf->dcf", normed_two, d_proj, preferred_element_type=f32)
        norm_part = jnp.einsum("tcf,dcf->td", d_proj, again[4], preferred_element_type=f32)
        d_norm_two = lax.psum(norm_part.astype(jnp.bfloat16), "tp").astype(jnp.float32)
        _, second_pull = jax.vjp(layer_norm, hidden, gain_second)
        d_hid_norm, d_gain_two = second_pull(d_norm_two)
        acc_gain_two = acc_gain_two + d_gain_two
        d_hidden = grad_float + d_hid_norm
        hidden_low = d_hidden.astype(bf16)
        acc_out = acc_out + lax.dot_general(
            hidden_low, mixed_low, dims_rows, preferred_element_type=f32
        )
        d_mixed = jnp.dot(hidden_low, again[3], preferred_element_type=f32).astype(bf16)
        d_mixed = d_mixed.reshape(tok_rows, head_count, HD)
        delta_rows = jnp.sum(d_mixed.astype(f32) * mixed_heads, axis=-1)
        delta_heads = jnp.transpose(delta_rows)

        def query_step(grad_query, piece_parts, offset):
            key_part, value_part = piece_parts
            key_seg, _ = seq_info(
                lax.dynamic_slice_in_dim(perm_row, offset, key_part.shape[0]), seq_lens
            )
            scores = (
                jnp.einsum("qhe,khe->hqk", query_low, key_part, preferred_element_type=f32)
                * score_scale
            )
            same_seq = (query_seg[:, None] == key_seg[None, :])[None]
            weights = jnp.where(same_seq, jnp.exp(scores - log_total[..., None]), 0.0)
            d_weights = jnp.einsum("qhe,khe->hqk", d_mixed, value_part, preferred_element_type=f32)
            d_scores = (weights * (d_weights - delta_heads[..., None])).astype(bf16)
            return grad_query + score_scale * jnp.einsum(
                "hqk,khe->qhe", d_scores, key_part, preferred_element_type=f32
            )

        query_start = jnp.zeros((tok_rows, head_count, HD), f32)
        grad_query = blockwise(
            query_start,
            (
                lax.all_gather(key_low, "fsdp", axis=0, tiled=True),
                lax.all_gather(value_low, "fsdp", axis=0, tiled=True),
            ),
            jnp.int32(0),
            query_step,
        )
        stat_total, stat_delta = (
            lax.all_gather(jnp.transpose(log_total), "fsdp", axis=0, tiled=True),
            lax.all_gather(delta_rows, "fsdp", axis=0, tiled=True),
        )

        def key_step(running, piece_parts, offset):
            grad_key, grad_value = running
            query_part, dmix_part = piece_parts
            piece_len = query_part.shape[0]
            piece_seg, _ = seq_info(lax.dynamic_slice_in_dim(perm_row, offset, piece_len), seq_lens)
            total_part = jnp.transpose(lax.dynamic_slice_in_dim(stat_total, offset, piece_len))
            delta_part = jnp.transpose(lax.dynamic_slice_in_dim(stat_delta, offset, piece_len))
            scores = (
                jnp.einsum("qhe,khe->hqk", query_part, key_low, preferred_element_type=f32)
                * score_scale
            )
            same_seq = (piece_seg[:, None] == query_seg[None, :])[None]
            weights = jnp.where(same_seq, jnp.exp(scores - total_part[..., None]), 0.0)
            d_weights = jnp.einsum("qhe,khe->hqk", dmix_part, value_low, preferred_element_type=f32)
            d_scores = (weights * (d_weights - delta_part[..., None])).astype(bf16)
            grad_key = grad_key + score_scale * jnp.einsum(
                "hqk,qhe->khe", d_scores, query_part, preferred_element_type=f32
            )
            grad_value = grad_value + jnp.einsum(
                "hqk,qhe->khe", weights.astype(bf16), dmix_part, preferred_element_type=f32
            )
            return (grad_key, grad_value)

        grad_key, grad_value = blockwise(
            (
                jnp.zeros((tok_rows, head_count, HD), f32),
                jnp.zeros((tok_rows, head_count, HD), f32),
            ),
            (
                lax.all_gather(query_low, "fsdp", axis=0, tiled=True),
                lax.all_gather(d_mixed, "fsdp", axis=0, tiled=True),
            ),
            jnp.int32(0),
            key_step,
        )
        _, rope_pull = jax.vjp(lambda heads_in: rotate(heads_in, cosine, sine), raw_heads[:, 0])
        d_raw_query = rope_pull(grad_query)[0]
        d_raw_key = rope_pull(grad_key)[0]
        d_raw = (
            jnp.stack([d_raw_query, d_raw_key, grad_value], axis=1)
            .reshape(tok_rows, 3, head_cols)
            .astype(bf16)
        )
        acc_qkv = acc_qkv + jnp.einsum("td,tcf->dcf", normed_low, d_raw, preferred_element_type=f32)
        first_part = jnp.einsum("tcf,dcf->td", d_raw, again[2], preferred_element_type=f32)
        d_norm_one = lax.psum(first_part.astype(jnp.bfloat16), "tp").astype(jnp.float32)
        _, first_pull = jax.vjp(layer_norm, x_float, gain_first)
        d_x_norm, d_gain_one = first_pull(d_norm_one)
        acc_gain_one = acc_gain_one + d_gain_one
        d_input = (d_hidden + d_x_norm).astype(bf16)
        back_rows = d_input[recv_order].reshape(groups, per_pair, D)
        returned = lax.all_to_all(
            back_rows, "fsdp", split_axis=0, concat_axis=0, tiled=True
        ).reshape(tok_rows, D)
        send_slot = jnp.zeros((tok_rows,), jnp.int32).at[send_order].set(rows_idx)
        input_grads.append(returned[send_slot])
    summed = (
        lax.psum_scatter(acc_qkv, "fsdp", scatter_dimension=0, tiled=True),
        lax.psum_scatter(acc_out, "fsdp", scatter_dimension=0, tiled=True),
        lax.psum_scatter(acc_in, "fsdp", scatter_dimension=0, tiled=True),
        lax.psum_scatter(acc_down, "fsdp", scatter_dimension=0, tiled=True),
        lax.psum_scatter(acc_gain_one, "fsdp", scatter_dimension=0, tiled=True),
        lax.psum_scatter(acc_gain_two, "fsdp", scatter_dimension=0, tiled=True),
    )
    return (
        jnp.stack(outputs),
        jnp.stack(input_grads),
        summed[0],
        summed[1],
        summed[2],
        summed[3],
        summed[4],
        summed[5],
    )


def solution(mesh):
    placed = (
        P(None, "fsdp", None),
        P(None, "fsdp", None),
        P(),
        P(),
        P("fsdp", None, "tp"),
        P("fsdp", "tp"),
        P("fsdp", None, "tp"),
        P("fsdp", "tp"),
        P("fsdp"),
        P("fsdp"),
    )
    return jax.shard_map(
        on_device,
        mesh=mesh,
        in_specs=placed,
        out_specs=(
            P(None, "fsdp", None),
            P(None, "fsdp", None),
            P("fsdp", None, "tp"),
            P("fsdp", "tp"),
            P("fsdp", None, "tp"),
            P("fsdp", "tp"),
            P("fsdp"),
            P("fsdp"),
        ),
        check_vma=False,
    )
```

profile of v0, /device:TPU:0, one launch (start us, length us, event | category | flops | bytes accessed | tf_op | source)
XLA Modules:
  0.0 1068.1 jit_solution(1980122411433525915)
XLA Ops:
  59.7 22.5 %all-gather.2 = bf16[8,1,128]{2,1,0:T(2,128)(2,1)S(1)} all-gather(bf16[1,1,128]{2,1,0:T(2,128)(2,1)S(1)} %bitcast.517), channel_id=1, replica_groups=mesh['fsdp'=8,'tp'=4] {'fsdp'}, dimensions={0}, use_global_device_ids=true | all-gather | bytes 2304 | tf_op jit(solution)/shard_map/all_gather | solution.py:104
  100.1 32.4 %all_gather.80 = bf16[1024,256]{1,0:T(8,128)(2,1)S(1)} all-gather(bf16[128,256]{1,0:T(8,128)(2,1)} %param.15), channel_id=1, replica_groups=mesh['fsdp'=8,'tp'=4] {'fsdp'}, dimensions={0}, use_global_device_ids=true | all-gather | bytes 589824 | tf_op jit(solution)/shard_map/all_gather | solution.py:107
  140.7 33.4 %all-gather.18.cloned.1.call-done = bf16[2048,4,64]{0,2,1:T(8,128)(2,1)} async-done(((bf16[256,4,64]{0,2,1:T(8,128)(2,1)}), bf16[2048,4,64]{0,2,1:T(8,128)(2,1)}) %all-gather.18.cloned.1.call-update) | async-done | bytes 1048592 | tf_op jit(solution)/shard_map/all_gather | solution.py:152
  183.7 31.4 %all-gather.36.cloned.1.call-done = bf16[2048,1,4,64]{0,3,2,1:T(8,128)(2,1)} async-done(((bf16[256,1,4,64]{0,3,2,1:T(8,128)(2,1)}), bf16[2048,1,4,64]{0,3,2,1:T(8,128)(2,1)}) %all-gather.36.cloned.1.call-update) | async-done | bytes 1048592 | tf_op jit(solution)/shard_map/all_gather | solution.py:153
  221.9 34.1 %all-gather.34.cloned.1.call-done = bf16[2048,1,4,64]{0,3,2,1:T(8,128)(2,1)} async-done(((bf16[256,1,4,64]{0,3,2,1:T(8,128)(2,1)}), bf16[2048,1,4,64]{0,3,2,1:T(8,128)(2,1)}) %all-gather.34.cloned.1.call-update) | async-done | bytes 1048592 | tf_op jit(solution)/shard_map/all_gather | solution.py:153
  264.9 18.8 %all-gather.3 = bf16[8,1,128]{2,1,0:T(2,128)(2,1)S(1)} all-gather(bf16[1,1,128]{2,1,0:T(2,128)(2,1)S(1)} %bitcast.518), channel_id=1, replica_groups=mesh['fsdp'=8,'tp'=4] {'fsdp'}, dimensions={0}, use_global_device_ids=true | all-gather | bytes 2304 | tf_op jit(solution)/shard_map/all_gather | solution.py:105
  284.3 15.2 %all-gather.22.cloned.1.call-done = bf16[1024,656]{0,1:T(8,128)(2,1)} async-done(((bf16[128,656]{0,1:T(8,128)(2,1)}), bf16[1024,656]{0,1:T(8,128)(2,1)}) %all-gather.22.cloned.1.call-update) | async-done | bytes 1343504 | tf_op jit(solution)/shard_map/all_gather | solution.py:109
  304.1 33.2 %all-reduce.22.cloned.1.call-done = (bf16[256,1024]{1,0:T(8,128)(2,1)}, bf16[256,1024]{1,0:T(8,128)(2,1)}) async-done(((bf16[256,1024]{1,0:T(8,128)(2,1)}, bf16[256,1024]{1,0:T(8,128)(2,1)}), (bf16[256,1024]{1,0:T(8,128)(2,1)}, bf16[256,1024]{1,0:T(8,128)(2,1)})) %all-reduce.22.cloned.1.call-update) | async-done | bytes 1048592 | tf_op jit(solution)/shard_map/psum | solution.py:162
  342.6 55.0 %all-gather.20.cloned.1.call-done = bf16[1024,2,656]{0,2,1:T(8,128)(2,1)} async-done(((bf16[128,2,656]{0,2,1:T(8,128)(2,1)}), bf16[1024,2,656]{0,2,1:T(8,128)(2,1)}) %all-gather.20.cloned.1.call-update) | async-done | bytes 2686992 | tf_op jit(solution)/shard_map/all_gather | solution.py:108
  419.4 31.9 %all_gather.91 = f32[2048,4]{0,1:T(4,128)} all-gather(f32[256,4]{0,1:T(4,128)} %get-tuple-element.97), channel_id=1, replica_groups=mesh['fsdp'=8,'tp'=4] {'fsdp'}, dimensions={0}, use_global_device_ids=true | all-gather | bytes 36864 | tf_op jit(solution)/shard_map/all_gather | solution.py:237
  461.0 32.1 %all_gather.87 = f32[2048,4]{0,1:T(4,128)} all-gather(f32[256,4]{0,1:T(4,128)S(1)} %copy-done.86), channel_id=1, replica_groups=mesh['fsdp'=8,'tp'=4] {'fsdp'}, dimensions={0}, use_global_device_ids=true | all-gather | bytes 36864 | tf_op jit(solution)/shard_map/all_gather | solution.py:237
  499.0 30.7 %all-gather.26.cloned.1.call-done = bf16[2048,4,64]{0,2,1:T(8,128)(2,1)} async-done(((bf16[256,4,64]{0,2,1:T(8,128)(2,1)}), bf16[2048,4,64]{0,2,1:T(8,128)(2,1)}) %all-gather.26.cloned.1.call-update) | async-done | bytes 1048592 | tf_op jit(solution)/shard_map/all_gather | solution.py:270
  538.6 30.6 %all_gather.93 = f32[2048,4]{0,1:T(4,128)S(1)} all-gather(f32[256,4]{0,1:T(4,128)S(1)} %copy-done.83), channel_id=1, replica_groups=mesh['fsdp'=8,'tp'=4] {'fsdp'}, dimensions={0}, use_global_device_ids=true | all-gather | bytes 36864 | tf_op jit(solution)/shard_map/all_gather | solution.py:238
  570.2 31.3 %all_gather.89 = f32[2048,4]{0,1:T(4,128)} all-gather(f32[256,4]{0,1:T(4,128)S(1)} %get-tuple-element.126), channel_id=1, replica_groups=mesh['fsdp'=8,'tp'=4] {'fsdp'}, dimensions={0}, use_global_device_ids=true | all-gather | bytes 36864 | tf_op jit(solution)/shard_map/all_gather | solution.py:238
  601.8 8.4 fusion.42
  615.9 8.7 broadcast_multiply_fusion.1
  628.4 12.0 %all-gather.28.cloned.1.call-done = bf16[2048,4,64]{0,2,1:T(8,128)(2,1)} async-done(((bf16[256,4,64]{0,2,1:T(8,128)(2,1)}), bf16[2048,4,64]{0,2,1:T(8,128)(2,1)}) %all-gather.28.cloned.1.call-update) | async-done | bytes 1048592 | tf_op jit(solution)/shard_map/all_gather | solution.py:271
  654.2 8.7 broadcast_multiply_fusion.3
  697.1 27.8 %all-reduce.18.cloned.1.call-done = (bf16[256,1024]{1,0:T(8,128)(2,1)}, bf16[256,1024]{1,0:T(8,128)(2,1)}, bf16[256,1024]{1,0:T(8,128)(2,1)}, bf16[256,1024]{1,0:T(8,128)(2,1)}) async-done(((bf16[256,1024]{1,0:T(8,128)(2,1)}, bf16[256,1024]{1,0:T(8,128)(2,1)}, bf16[256,1024]{1,0:T(8,128)(2,1)}, bf16[256,1024]{1,0:T(8,128)(2,1)}), (bf16[256,1024]{1,0:T(8,128)(2,1)}, bf16[256,1024]{1,0:T(8,128)(2,1)}, ...) | async-done | bytes 2097168 | tf_op jit(solution)/shard_map/psum | solution.py:168
  744.2 17.8 %all-to-all-done.3 = bf16[8,32,1024]{2,1,0:T(8,128)(2,1)S(1)} async-done(((bf16[8,32,1024]{2,1,0:T(8,128)(2,1)}), bf16[8,32,1024]{2,1,0:T(8,128)(2,1)S(1)}, u32[]{:S(2)}, u32[]{:S(2)}) %all-to-all-start.3) | async-done | bytes 524320 | tf_op jit(solution)/shard_map/all_to_all | solution.py:292
  770.3 22.3 %all-reduce.10 = (f32[1024]{0:T(1024)S(1)}, f32[1024]{0:T(1024)S(1)}) all-reduce(f32[1024]{0:T(1024)S(1)} %add.299, f32[1024]{0:T(1024)S(1)} %add.300), channel_id=8, replica_groups=mesh['fsdp'=8,'tp'=4] {'fsdp'}, use_global_device_ids=true, to_apply=%region_54.55.clone | all-reduce | flops 2048 | bytes 16384
  798.3 75.9 %reduce-scatter.11.cloned.1.call-done = f32[128,656]{0,1:T(8,128)} async-done(((f32[1024,656]{0,1:T(8,128)}), f32[128,656]{0,1:T(8,128)}) %reduce-scatter.11.cloned.1.call-update) | async-done | bytes 335888 | tf_op jit(solution)/shard_map/reduce_scatter | solution.py:301
  874.2 78.2 %reduce-scatter.5.cloned.1.call-done = f32[128,3,256]{2,0,1:T(8,128)} async-done(((f32[1024,3,256]{2,0,1:T(8,128)}), f32[128,3,256]{2,0,1:T(8,128)}) %reduce-scatter.5.cloned.1.call-update) | async-done | bytes 393232 | tf_op jit(solution)/shard_map/reduce_scatter | solution.py:298
  952.4 108.7 %reduce-scatter.9.cloned.1.call-done = f32[128,2,656]{0,2,1:T(8,128)} async-done(((f32[1024,2,656]{0,2,1:T(8,128)}), f32[128,2,656]{0,2,1:T(8,128)}) %reduce-scatter.9.cloned.1.call-update) | async-done | bytes 671760 | tf_op jit(solution)/shard_map/reduce_scatter | solution.py:300
  (459 shorter events, 250.0 us)
Async XLA Ops:
  7.2 81.1 %all-gather.16.cloned.1.call-start = ((), (), s32[]{:S(2)}) async-start(), calls=%async_computation.8 | async-start | bytes 1769472 | tf_op jit(solution)/shard_map/all_gather | solution.py:106
  24.4 29.2 %all-to-all-start.1 = ((bf16[8,32,1024]{2,1,0:T(8,128)(2,1)}), bf16[8,32,1024]{2,1,0:T(8,128)(2,1)S(1)}, u32[]{:S(2)}, u32[]{:S(2)}) async-start(bf16[8,32,1024]{2,1,0:T(8,128)(2,1)} %bitcast.32), calls=%async_computation.1 | async-start | bytes 1048576 | tf_op jit(solution)/shard_map/all_to_all | solution.py:95
  53.6 32.9 %all-to-all-start = ((bf16[8,32,1024]{2,1,0:T(8,128)(2,1)}), bf16[8,32,1024]{2,1,0:T(8,128)(2,1)S(1)}, u32[]{:S(2)}, u32[]{:S(2)}) async-start(bf16[8,32,1024]{2,1,0:T(8,128)(2,1)} %bitcast.3), calls=%async_computation | async-start | bytes 1048576 | tf_op jit(solution)/shard_map/all_to_all | solution.py:95
  59.6 74.7 %all-gather.24.cloned.1.call-start = ((), (), s32[]{:S(2)}) async-start(), calls=%async_computation.12 | async-start | bytes 1179648 | tf_op jit(solution)/shard_map/all_gather | solution.py:152
  91.4 82.7 %all-gather.18.cloned.1.call-start = ((), (), s32[]{:S(2)}) async-start(), calls=%async_computation.9 | async-start | bytes 1179648 | tf_op jit(solution)/shard_map/all_gather | solution.py:152
  95.9 119.2 %all-gather.36.cloned.1.call-start = ((), (), s32[]{:S(2)}) async-start(), calls=%async_computation.22 | async-start | bytes 1179648 | tf_op jit(solution)/shard_map/all_gather | solution.py:153
  96.6 159.4 %all-gather.34.cloned.1.call-start = ((), (), s32[]{:S(2)}) async-start(), calls=%async_computation.21 | async-start | bytes 1179648 | tf_op jit(solution)/shard_map/all_gather | solution.py:153
  97.4 202.1 %all-gather.22.cloned.1.call-start = ((), (), s32[]{:S(2)}) async-start(), calls=%async_computation.11 | async-start | bytes 1511424 | tf_op jit(solution)/shard_map/all_gather | solution.py:109
  97.9 239.3 %all-reduce.22.cloned.1.call-start = ((), (), s32[]{:S(2)}) async-start(), calls=%async_computation.25 | async-start | bytes 2097152 | tf_op jit(solution)/shard_map/psum | solution.py:162
  132.5 326.8 %copy-start.5 = (bf16[1024,256]{1,0:T(8,128)(2,1)}, bf16[1024,256]{1,0:T(8,128)(2,1)S(1)}, u32[]{:S(2)}) copy-start(bf16[1024,256]{1,0:T(8,128)(2,1)S(1)} %all_gather.80) | copy-start | bytes 1572868
  134.3 121.7 %copy-start.22 = (pred[256,2048]{1,0:T(8,128)(4,1)}, pred[256,2048]{1,0:T(8,128)(4,1)S(1)}, u32[]{:S(2)}) copy-start(pred[256,2048]{1,0:T(8,128)(4,1)S(1)} %broadcast_compare_fusion.3) | copy-start | bytes 1572868
  264.1 133.5 %all-gather.20.cloned.1.call-start = ((), (), s32[]{:S(2)}) async-start(), calls=%async_computation.10 | async-start | bytes 3022848 | tf_op jit(solution)/shard_map/all_gather | solution.py:108
  264.9 186.5 %all-reduce.20.cloned.1.call-start = ((), (), s32[]{:S(2)}) async-start(), calls=%async_computation.24 | async-start | bytes 2097152 | tf_op jit(solution)/shard_map/psum | solution.py:195
  412.4 80.7 %all-gather.30.cloned.1.call-start = ((), (), s32[]{:S(2)}) async-start(), calls=%async_computation.15 | async-start | bytes 1179648 | tf_op jit(solution)/shard_map/all_gather | solution.py:270
  413.0 116.7 %all-gather.26.cloned.1.call-start = ((), (), s32[]{:S(2)}) async-start(), calls=%async_computation.13 | async-start | bytes 1179648 | tf_op jit(solution)/shard_map/all_gather | solution.py:270
  416.8 185.0 %all-gather.32.cloned.1.call-start = ((), (), s32[]{:S(2)}) async-start(), calls=%async_computation.16 | async-start | bytes 1179648 | tf_op jit(solution)/shard_map/all_gather | solution.py:271
  460.9 179.5 %all-gather.28.cloned.1.call-start = ((), (), s32[]{:S(2)}) async-start(), calls=%async_computation.14 | async-start | bytes 1179648 | tf_op jit(solution)/shard_map/all_gather | solution.py:271
  601.5 123.4 %all-reduce.18.cloned.1.call-start = ((), (), s32[]{:S(2)}) async-start(), calls=%async_computation.23 | async-start | bytes 4194304 | tf_op jit(solution)/shard_map/psum | solution.py:168
  673.9 124.4 %reduce-scatter.7.cloned.1.call-start = ((), (), s32[]{:S(2)}) async-start(), calls=%async_computation.18 | async-start | bytes 1179648 | tf_op jit(solution)/shard_map/reduce_scatter | solution.py:299
  677.8 196.4 %reduce-scatter.11.cloned.1.call-start = ((), (), s32[]{:S(2)}) async-start(), calls=%async_computation.20 | async-start | bytes 3022848 | tf_op jit(solution)/shard_map/reduce_scatter | solution.py:301
  684.9 267.4 %reduce-scatter.5.cloned.1.call-start = ((), (), s32[]{:S(2)}) async-start(), calls=%async_computation.17 | async-start | bytes 3538944 | tf_op jit(solution)/shard_map/reduce_scatter | solution.py:298
  690.4 370.7 %reduce-scatter.9.cloned.1.call-start = ((), (), s32[]{:S(2)}) async-start(), calls=%async_computation.19 | async-start | bytes 6045696 | tf_op jit(solution)/shard_map/reduce_scatter | solution.py:300
  736.7 25.3 %all-to-all-start.3 = ((bf16[8,32,1024]{2,1,0:T(8,128)(2,1)}), bf16[8,32,1024]{2,1,0:T(8,128)(2,1)S(1)}, u32[]{:S(2)}, u32[]{:S(2)}) async-start(bf16[8,32,1024]{2,1,0:T(8,128)(2,1)} %bitcast.89), calls=%async_computation.3 | async-start | bytes 1048576 | tf_op jit(solution)/shard_map/all_to_all | solution.py:292
  762.0 34.0 %all-to-all-start.2 = ((bf16[8,32,1024]{2,1,0:T(8,128)(2,1)}), bf16[8,32,1024]{2,1,0:T(8,128)(2,1)S(1)}, u32[]{:S(2)}, u32[]{:S(2)}) async-start(bf16[8,32,1024]{2,1,0:T(8,128)(2,1)} %bitcast.70), calls=%async_computation.2 | async-start | bytes 1048576 | tf_op jit(solution)/shard_map/all_to_all | solution.py:292
  (114 other events, 2787.5 us)
Sparse Core Ops, SparseCore 0:
  10.7 51.3 all-gather.15
  91.5 41.9 all-gather.23
  136.2 37.9 all-gather.17
  176.6 38.4 all-gather.35
  217.6 38.4 all-gather.33
  257.9 41.4 all-gather.21
  302.5 34.7 all-reduce.21
  339.5 58.0 all-gather.19
  412.5 34.1 all-reduce.19
  448.7 40.0 all-gather.29
  490.8 38.8 all-gather.25
  531.6 38.5 all-gather.31
  601.6 38.7 all-gather.27
  674.1 50.8 all-reduce.17
  729.1 68.7 reduce-scatter.6
  801.8 72.3 reduce-scatter.10
  878.7 73.6 reduce-scatter.4
  956.8 104.1 reduce-scatter.8
where the time goes:
time: 1080 us; the launch traced here: 1070 us
  waiting for transfers between devices  555 us (51%)
  blocking collectives  222 us (21%)
  matrix products  130 us (12%)
  other arithmetic  71.9 us (7%)
  local copies, waits for them, and re-layouts  48.3 us (4%)
  starting transfers between devices  24 us (2%)
  between operations  17 us (2%)
    reduce_scatter x1, waiting for transfers between devices, on_device(): lax.psum_scatter(acc_in, 'fsdp', scatter_dimension=0, tiled=True)  109 us
    reduce_scatter x1, waiting for transfers between devices, on_device(): lax.psum_scatter(acc_qkv, 'fsdp', scatter_dimension=0, tiled=True)  78.2 us
    reduce_scatter x1, waiting for transfers between devices, on_device(): lax.psum_scatter(acc_down, 'fsdp', scatter_dimension=0, tiled=True)  75.9 us
    all_gather x2, waiting for transfers between devices, on_device(): lax.all_gather(value_low, 'fsdp', axis=0, tiled=True)  65.5 us
    all_gather x2, blocking collectives, on_device(): lax.all_gather(jnp.transpose(log_total), 'fsdp', axis=0, tiled=True)  64 us
    all_gather x2, blocking collectives, on_device(): lax.all_gather(delta_rows, 'fsdp', axis=0, tiled=True)  61.9 us
    all_gather x1, waiting for transfers between devices, on_device(): lax.all_gather(w_in, 'fsdp', axis=0, tiled=True)  55 us
    all_gather x2, waiting for transfers between devices, on_device(): lax.all_gather(key_low, 'fsdp', axis=0, tiled=True)  33.5 us
  transfers between devices with their start and end apart: 22, of which 13 were waited for; matrix products, arithmetic and copies ran while one was open for 18% of the time, Pallas kernels for 0%

commit v1 on v0

--- a/solution.py
+++ b/solution.py
@@ -1,6 +1,8 @@
 import jax
 import jax.numpy as jnp
 from jax import lax
+from jax.experimental import pallas as pl
+from jax.experimental.pallas import tpu as pltpu
 from jax.sharding import PartitionSpec as P
 
 D = 1024
@@ -31,8 +33,13 @@
     return values * cosine[:, None, :] + turned * sine[:, None, :]
 
 
+def running_ends(seq_lens):
+    order = jnp.arange(seq_lens.shape[0], dtype=jnp.int32)
+    return jnp.sum(jnp.where(order[None, :] <= order[:, None], seq_lens[None, :], 0), axis=1)
+
+
 def seq_info(anchor, seq_lens):
-    ends = jnp.cumsum(seq_lens)
+    ends = running_ends(seq_lens)
     starts = ends - seq_lens
     segment = jnp.sum((anchor[:, None] >= ends[None, :]).astype(jnp.int32), axis=1)
     onehot = segment[:, None] == jnp.arange(seq_lens.shape[0], dtype=jnp.int32)[None, :]
@@ -55,7 +62,7 @@
     return step_fn(running, pieces, offset)
 
 
-def on_device(
+def general_layer(
     tokens, cotangent, perm, lengths, w_qkv, w_attn_out, w_in, w_down, gain_one, gain_two
 ):
     groups = lax.axis_size("fsdp")
@@ -314,6 +321,442 @@
     )
 
 
+BLOCK = 256
+FAR = -1e30
+ORDER = (0, 2, 4, 6, 1, 3, 5, 7)
+NT = (((1,), (1,)), ((), ()))
+TN = (((0,), (0,)), ((), ()))
+NN = (((1,), (0,)), ((), ()))
+
+
+def mm(left, right, dims):
+    return lax.dot_general(left, right, dims, preferred_element_type=jnp.float32)
+
+
+def hop(value, step):
+    return lax.ppermute(value, "fsdp", [(i, i ^ step) for i in range(8)])
+
+
+def twin(value):
+    return lax.ppermute(value, "tp", [(i, i ^ 1) for i in range(4)])
+
+
+def across(value):
+    return lax.ppermute(value, "tp", [(i, i ^ 2) for i in range(4)])
+
+
+def gather_shards(shard):
+    same = [shard] + [hop(shard, step) for step in ORDER[1:4]]
+    return same + [hop(one, 1) for one in same]
+
+
+def scatter_sum(total):
+    cols = total.shape[1] // 8
+    low = total.astype(jnp.bfloat16)
+    near = total[:, : 4 * cols] + hop(low[:, 4 * cols :], 1).astype(jnp.float32)
+    result = near[:, :cols]
+    for place in range(1, 4):
+        piece = near[:, place * cols : (place + 1) * cols].astype(jnp.bfloat16)
+        result = result + hop(piece, ORDER[place]).astype(jnp.float32)
+    return result
+
+
+def key_range(lens_ref, low, high):
+    first = jnp.int32(0)
+    last = jnp.int32(0)
+    total = jnp.int32(0)
+    for index in range(lens_ref.shape[0]):
+        start = total
+        total = total + lens_ref[index]
+        first = jnp.where((start <= low) & (low < total), start, first)
+        last = jnp.where((start <= high) & (high < total), total, last)
+    return first, last
+
+
+def query_bounds(lens_ref, base, width):
+    place = base + lax.broadcasted_iota(jnp.int32, (1, width), 1)
+    first = jnp.zeros((1, width), jnp.int32)
+    last = jnp.zeros((1, width), jnp.int32)
+    total = jnp.int32(0)
+    for index in range(lens_ref.shape[0]):
+        start = total
+        total = total + lens_ref[index]
+        inside = (place >= start) & (place < total)
+        first = jnp.where(inside, start, first)
+        last = jnp.where(inside, total, last)
+    return first, last
+
+
+def attend_kernel(lens_ref, qkv_ref, mixed_ref, exact_ref, log_ref, key_ref):
+    count = qkv_ref.shape[0]
+
+    def turn(index, carry):
+        block = qkv_ref[index, HD : 2 * HD, :].astype(jnp.float32)
+        key_ref[index] = jnp.transpose(block).astype(jnp.bfloat16)
+        return carry
+
+    lax.fori_loop(0, count, turn, 0)
+
+    def one_query(index, carry):
+        base = index * BLOCK
+        first, last = key_range(lens_ref, base, base + BLOCK - 1)
+        low, high = query_bounds(lens_ref, base, BLOCK)
+        query = qkv_ref[index, :HD, :] * jnp.bfloat16(HD**-0.5)
+
+        def one_key(at, state):
+            peak, total, acc = state
+            scores = mm(key_ref[at], query, NN)
+            place = at * BLOCK + lax.broadcasted_iota(jnp.int32, (BLOCK, BLOCK), 0)
+            scores = jnp.where((place >= low) & (place < high), scores, FAR)
+            top = jnp.maximum(peak, jnp.max(scores, axis=0, keepdims=True))
+            weights = jnp.exp(scores - top)
+            fade = jnp.exp(peak - top)
+            total = total * fade + jnp.sum(weights, axis=0, keepdims=True)
+            acc = acc * fade + mm(qkv_ref[at, 2 * HD :, :], weights.astype(jnp.bfloat16), NN)
+            return top, total, acc
+
+        peak, total, acc = lax.fori_loop(
+            first // BLOCK,
+            (last + BLOCK - 1) // BLOCK,
+            one_key,
+            (
+                jnp.full((1, BLOCK), FAR, jnp.float32),
+                jnp.zeros((1, BLOCK), jnp.float32),
+                jnp.zeros((HD, BLOCK), jnp.float32),
+            ),
+        )
+        result = acc / total
+        mixed_ref[index] = result.astype(jnp.bfloat16)
+        exact_ref[index] = result
+        log_ref[index] = peak + jnp.log(total)
+        return carry
+
+    lax.fori_loop(0, count, one_query, 0)
+
+
+def attend(lens, qkv):
+    count = qkv.shape[0]
+    return pl.pallas_call(
+        attend_kernel,
+        in_specs=[
+            pl.BlockSpec(memory_space=pltpu.SMEM),
+            pl.BlockSpec(memory_space=pltpu.VMEM),
+        ],
+        out_specs=[pl.BlockSpec(memory_space=pltpu.VMEM)] * 3,
+        out_shape=[
+            jax.ShapeDtypeStruct((count, HD, BLOCK), jnp.bfloat16),
+            jax.ShapeDtypeStruct((count, HD, BLOCK), jnp.float32),
+            jax.ShapeDtypeStruct((count, 1, BLOCK), jnp.float32),
+        ],
+        scratch_shapes=[pltpu.VMEM((count, BLOCK, HD), jnp.bfloat16)],
+        compiler_params=pltpu.CompilerParams(vmem_limit_bytes=40 * 1024 * 1024),
+        name="attend",
+    )(lens, qkv)
+
+
+def attend_back_kernel(
+    lens_ref, qkv_ref, exact_ref, log_ref, grad_ref, table_ref, raw_ref,
+    key_ref, value_ref, dkey_ref, dvalue_ref,
+):
+    count = qkv_ref.shape[0]
+    half = HD // 2
+
+    def turn(index, carry):
+        block = qkv_ref[index, HD : 2 * HD, :].astype(jnp.float32)
+        key_ref[index] = jnp.transpose(block).astype(jnp.bfloat16)
+        block = qkv_ref[index, 2 * HD :, :].astype(jnp.float32)
+        value_ref[index] = jnp.transpose(block).astype(jnp.bfloat16)
+        dkey_ref[index] = jnp.zeros((HD, BLOCK), jnp.float32)
+        dvalue_ref[index] = jnp.zeros((HD, BLOCK), jnp.float32)
+        return carry
+
+    lax.fori_loop(0, count, turn, 0)
+
+    def unturn(index, grad):
+        cosine = table_ref[index, :half, :]
+        sine = table_ref[index, half:, :]
+        upper, lower = grad[:half], grad[half:]
+        return upper * cosine + lower * sine, lower * cosine - upper * sine
+
+    def one_query(index, carry):
+        base = index * BLOCK
+        first, last = key_range(lens_ref, base, base + BLOCK - 1)
+        low, high = query_bounds(lens_ref, base, BLOCK)
+        query = qkv_ref[index, :HD, :] * jnp.bfloat16(HD**-0.5)
+        grad = grad_ref[index]
+        logs = log_ref[index]
+        delta = jnp.sum(grad.astype(jnp.float32) * exact_ref[index], axis=0, keepdims=True)
+
+        def one_key(at, dquery):
+            scores = mm(key_ref[at], query, NN)
+            place = at * BLOCK + lax.broadcasted_iota(jnp.int32, (BLOCK, BLOCK), 0)
+            weights = jnp.where((place >= low) & (place < high), jnp.exp(scores - logs), 0.0)
+            dweights = mm(value_ref[at], grad, NN)
+            dscores = (weights * (dweights - delta)).astype(jnp.bfloat16)
+            dkey_ref[at] += mm(query, dscores, NT)
+            dvalue_ref[at] += mm(grad, weights.astype(jnp.bfloat16), NT)
+            return dquery + mm(qkv_ref[at, HD : 2 * HD, :], dscores, NN)
+
+        dquery = lax.fori_loop(
+            first // BLOCK,
+            (last + BLOCK - 1) // BLOCK,
+            one_key,
+            jnp.zeros((HD, BLOCK), jnp.float32),
+        )
+        upper, lower = unturn(index, dquery * (HD**-0.5))
+        raw_ref[index, :half, :] = upper.astype(jnp.bfloat16)
+        raw_ref[index, half:HD, :] = lower.astype(jnp.bfloat16)
+        return carry
+
+    lax.fori_loop(0, count, one_query, 0)
+
+    def finish(index, carry):
+        upper, lower = unturn(index, dkey_ref[index])
+        raw_ref[index, HD : HD + half, :] = upper.astype(jnp.bfloat16)
+        raw_ref[index, HD + half : 2 * HD, :] = lower.astype(jnp.bfloat16)
+        raw_ref[index, 2 * HD :, :] = dvalue_ref[index].astype(jnp.bfloat16)
+        return carry
+
+    lax.fori_loop(0, count, finish, 0)
+
+
+def attend_back(lens, qkv, exact, logs, grad, table):
+    count = qkv.shape[0]
+    return pl.pallas_call(
+        attend_back_kernel,
+        in_specs=[pl.BlockSpec(memory_space=pltpu.SMEM)] + [pl.BlockSpec(memory_space=pltpu.VMEM)] * 5,
+        out_specs=pl.BlockSpec(memory_space=pltpu.VMEM),
+        out_shape=jax.ShapeDtypeStruct((count, 3 * HD, BLOCK), jnp.bfloat16),
+        scratch_shapes=[
+            pltpu.VMEM((count, BLOCK, HD), jnp.bfloat16),
+            pltpu.VMEM((count, BLOCK, HD), jnp.bfloat16),
+            pltpu.VMEM((count, HD, BLOCK), jnp.float32),
+            pltpu.VMEM((count, HD, BLOCK), jnp.float32),
+        ],
+        compiler_params=pltpu.CompilerParams(vmem_limit_bytes=40 * 1024 * 1024),
+        name="attend_back",
+    )(lens, qkv, exact, logs, grad, table)
+
+
+def positions(anchor, seq_lens):
+    ends = running_ends(seq_lens)
+    starts = ends - seq_lens
+    inside = (anchor[:, None] >= starts[None, :]) & (anchor[:, None] < ends[None, :])
+    return anchor - jnp.sum(jnp.where(inside, starts[None, :], 0), axis=1)
+
+
+def turn_tables(place):
+    freqs = jnp.power(THETA, -jnp.arange(HD // 2, dtype=jnp.float32) * 2.0 / HD)
+    angle = freqs[:, None] * place.astype(jnp.float32)[None, :]
+    return jnp.concatenate([jnp.cos(angle), jnp.sin(angle)], axis=0)
+
+
+def statistics(values):
+    center = values - jnp.mean(values, axis=-1, keepdims=True)
+    spread = lax.rsqrt(jnp.mean(center * center, axis=-1, keepdims=True) + EPS)
+    return center * spread, spread
+
+
+def norm_back(xhat, spread, gain, grad):
+    scaled = grad * gain
+    inner = scaled - jnp.mean(scaled, axis=-1, keepdims=True)
+    inner = inner - xhat * jnp.mean(scaled * xhat, axis=-1, keepdims=True)
+    return inner * spread, jnp.sum(grad * xhat, axis=0)
+
+
+def paired_layer(
+    tokens, cotangent, perm, lengths, w_qkv, w_attn_out, w_in, w_down, gain_one, gain_two
+):
+    f32, bf16 = jnp.float32, jnp.bfloat16
+    mine = lax.axis_index("fsdp")
+    part = lax.axis_index("tp")
+    core, side = part % 2, part // 2
+    rows = tokens.shape[1]
+    width = w_qkv.shape[0]
+    head_cols = w_qkv.shape[2]
+    heads = head_cols // HD
+    units = w_in.shape[2]
+    per_pair = rows // 8
+    order = jnp.bitwise_xor(jnp.array(ORDER, jnp.int32), mine)
+    back = jnp.bitwise_xor(jnp.arange(8, dtype=jnp.int32), mine)
+    back = (back % 2) * 4 + back // 2
+
+    def reorder(value, index):
+        axis = value.ndim - 1
+        pieces = [lax.dynamic_slice_in_dim(value, index[at] * width, width, axis) for at in range(8)]
+        return jnp.concatenate(pieces, axis=axis)
+
+    def pick(value, index):
+        return lax.dynamic_index_in_dim(value, index, 0, keepdims=False)
+
+    def tp_sum(value):
+        got = twin(pick(value, 1 - core).astype(bf16))
+        half = (pick(value, core) + got.astype(f32)).astype(bf16)
+        return half.astype(f32) + across(half).astype(f32)
+
+    def both(value):
+        other = twin(value)
+        return jnp.stack([jnp.where(core == 0, value, other), jnp.where(core == 0, other, value)])
+
+    turned = jnp.transpose(w_qkv.reshape(width, 3, heads, HD), (2, 1, 3, 0)).reshape(3 * head_cols, width)
+    gains = jnp.zeros((16, width), bf16).at[0].set(gain_one).at[1].set(gain_two)
+    first_pack = gather_shards(jnp.concatenate([turned, gains], axis=0))
+    first_all = jnp.concatenate(first_pack, axis=1)
+    qkv_w = first_all[: 3 * head_cols]
+    gain_first = first_all[3 * head_cols].astype(f32)
+    gain_second = first_all[3 * head_cols + 1].astype(f32)
+
+    x_rel = reorder(tokens, order).astype(f32)
+    xhat_one, spread_one = statistics(x_rel)
+    n_one = (xhat_one * gain_first).astype(bf16)
+    raw = mm(qkv_w, n_one.reshape(2 * rows, 8 * width), NT)
+    raw = raw.reshape(heads, 3, HD, 2, rows)
+    anchor = mine * rows + jnp.arange(rows, dtype=jnp.int32)
+    own_table = jnp.stack([turn_tables(positions(anchor, lengths[m])) for m in range(2)], axis=1)
+    cosine, sine = own_table[: HD // 2], own_table[HD // 2 :]
+
+    def spin(value):
+        upper, lower = value[:, : HD // 2], value[:, HD // 2 :]
+        return jnp.concatenate([upper * cosine - lower * sine, lower * cosine + upper * sine], axis=1)
+
+    turned_qkv = jnp.stack([spin(raw[:, 0]), spin(raw[:, 1]), raw[:, 2]], axis=1).astype(bf16)
+    outgoing = jnp.transpose(turned_qkv, (3, 0, 1, 2, 4)).reshape(8, 3 * HD, rows)
+    qkv = lax.all_to_all(outgoing, "fsdp", 0, 0, tiled=True)
+    my_lens = lengths[mine // heads]
+    mixed_out, exact, logs = attend(my_lens, qkv)
+    mixed = lax.all_to_all(mixed_out, "fsdp", 0, 0, tiled=True).reshape(2, head_cols, rows)
+
+    second = jnp.concatenate(
+        [
+            jnp.transpose(w_attn_out),
+            jnp.transpose(w_in.reshape(width, 2 * units)),
+            jnp.transpose(w_down),
+        ],
+        axis=0,
+    )
+    second_all = jnp.concatenate(gather_shards(second), axis=1)
+    out_w = second_all[:head_cols]
+    in_w = second_all[head_cols : head_cols + 2 * units]
+    down_w = second_all[head_cols + 2 * units :]
+
+    slots = perm.reshape(2, 8, rows)
+    from_me = (slots // rows == mine).astype(f32)
+    slot_no = jnp.arange(rows, dtype=jnp.int32)
+    before = (slot_no[:, None] < slot_no[None, :]).astype(f32)
+    rank_me = jnp.einsum("mds,st->mdt", from_me, before).astype(jnp.int32)
+    ranks = jnp.arange(per_pair, dtype=jnp.int32)
+    chosen = (from_me[..., None] > 0) & (rank_me[..., None] == ranks)
+    local = jnp.sum(jnp.where(chosen, (slots % rows)[..., None], 0), axis=2)
+    my_slots = lax.dynamic_index_in_dim(slots, mine, 1, keepdims=False)
+    target = my_slots // rows
+    same = (target[:, :, None] == target[:, None, :]) & (slot_no[:, None] < slot_no[None, :])[None]
+    rank_own = jnp.sum(same.astype(jnp.int32), axis=1)
+    place_own = target * per_pair + rank_own
+
+    quarter = per_pair // 4
+    wanted = jnp.arange(8, dtype=jnp.int32)[:, None] * per_pair + part * quarter
+    wanted = (wanted + jnp.arange(quarter, dtype=jnp.int32)[None, :]).reshape(-1)
+    packer = (place_own[:, None, :] == wanted[None, :, None]).astype(bf16)
+    packed = jnp.einsum("mps,msd->mpd", packer, cotangent, preferred_element_type=f32).astype(bf16)
+    packed = jnp.transpose(packed.reshape(2, 8, quarter, 8 * width), (1, 0, 2, 3))
+    arrived = lax.all_to_all(packed, "fsdp", 0, 0, tiled=True)
+    near = twin(arrived)
+    pair = jnp.stack([jnp.where(core == 0, arrived, near), jnp.where(core == 0, near, arrived)])
+    far = across(pair)
+    four = jnp.concatenate([jnp.where(side == 0, pair, far), jnp.where(side == 0, far, pair)])
+    four = jnp.transpose(four, (2, 1, 0, 3, 4)).reshape(2, rows, 8 * width)
+    spread_rows = (local.reshape(2, 1, rows) == slot_no[None, :, None]).astype(bf16)
+    four = four.astype(bf16)
+    grad_nat = jnp.einsum("mps,msd->mpd", spread_rows, four, preferred_element_type=f32).astype(bf16)
+    grad = reorder(grad_nat, order)
+
+    out_part = jnp.stack([mm(mixed[m], out_w, TN) for m in range(2)])
+    hidden = pick(x_rel, core) + tp_sum(out_part)
+    xhat_two, spread_two = statistics(hidden)
+    n_two = both((xhat_two * gain_second).astype(bf16)).reshape(2 * rows, 8 * width)
+
+    grad_flat = grad.reshape(2 * rows, 8 * width)
+    projected = mm(n_two, in_w, NT)
+    inp, gate = projected[:, :units], projected[:, units:]
+    d_act = mm(grad_flat, down_w, NT)
+    cdf = 0.5 * (1.0 + lax.erf(inp * (0.5**0.5)))
+    density = jnp.exp(-0.5 * inp * inp) * ((0.5 / jnp.pi) ** 0.5)
+    gelu = inp * cdf
+    act = (gelu * gate).astype(bf16)
+    d_inp = d_act * gate * (cdf + inp * density)
+    d_proj = jnp.concatenate([d_inp, d_act * gelu], axis=1).astype(bf16)
+    d_two_part = mm(d_proj, in_w, NN).reshape(2, rows, 8 * width)
+    d_two = tp_sum(d_two_part)
+    d_norm, d_gain_two = norm_back(xhat_two, spread_two, gain_second, d_two)
+    d_hidden = pick(grad, core).astype(f32) + d_norm
+    low_hidden = both(d_hidden.astype(bf16))
+
+    down_part = mm(act, down_w, NN).reshape(2, rows, 8 * width)
+    result = (hidden + tp_sum(down_part)).astype(bf16)
+    grad_in = mm(d_proj, n_two, TN)
+    grad_down = mm(act, grad_flat, TN)
+
+    result = reorder(result, back)
+    local_own = pick(local, core)
+    halfway = per_pair // 2
+    mine_half = lax.dynamic_slice_in_dim(local_own, side * halfway, halfway, 1).reshape(-1)
+    packer = (mine_half[:, None] == slot_no[None, :]).astype(bf16)
+    packed = mm(packer, result, NN).astype(bf16).reshape(8, halfway, 8 * width)
+    arrived = lax.all_to_all(packed, "fsdp", 0, 0, tiled=True)
+    far = across(arrived)
+    full = jnp.concatenate(
+        [jnp.where(side == 0, arrived, far), jnp.where(side == 0, far, arrived)], axis=1
+    ).reshape(rows, 8 * width)
+    full = both(full)
+    unpack = (place_own[:, :, None] == slot_no[None, None, :]).astype(bf16)
+    output = jnp.einsum("msp,mpd->msd", unpack, full, preferred_element_type=f32).astype(bf16)
+
+    d_mixed = mm(out_w, low_hidden.reshape(2 * rows, 8 * width), NT).astype(bf16)
+    d_mixed = jnp.transpose(d_mixed.reshape(heads, HD, 2, rows), (2, 0, 1, 3)).reshape(8, HD, rows)
+    grad_mixed = lax.all_to_all(d_mixed, "fsdp", 0, 0, tiled=True)
+    grad_out = mm(mixed[0], low_hidden[0], NN) + mm(mixed[1], low_hidden[1], NN)
+    second_grad = scatter_sum(jnp.concatenate([grad_out, grad_in, grad_down], axis=0))
+    all_anchor = jnp.arange(8 * rows, dtype=jnp.int32)
+    table = turn_tables(positions(all_anchor, my_lens))
+    table = jnp.transpose(table.reshape(HD, 8, rows), (1, 0, 2))
+    d_raw_out = attend_back(my_lens, qkv, exact, logs, grad_mixed, table)
+    d_raw = lax.all_to_all(d_raw_out, "fsdp", 0, 0, tiled=True).reshape(2, 3 * head_cols, rows)
+    d_one_part = jnp.stack([mm(d_raw[m], qkv_w, TN) for m in range(2)])
+    d_one = tp_sum(d_one_part)
+    grad_qkv = mm(d_raw[0], n_one[0], NN) + mm(d_raw[1], n_one[1], NN)
+    d_x, d_gain_one = norm_back(
+        pick(xhat_one, core), pick(spread_one, core), gain_first, d_one
+    )
+    input_grad = both(reorder((d_hidden + d_x).astype(bf16), back))
+
+    gain_grads = jnp.stack([d_gain_one, d_gain_two])
+    high = gain_grads.astype(bf16).astype(f32)
+    rest = jnp.zeros((12, 8 * width), f32)
+    first_grad = scatter_sum(jnp.concatenate([grad_qkv, high, gain_grads - high, rest], axis=0))
+    gain_rows = first_grad[3 * head_cols : 3 * head_cols + 2] + first_grad[3 * head_cols + 2 : 3 * head_cols + 4]
+    gain_rows = gain_rows + twin(gain_rows)
+    qkv_out = first_grad[: 3 * head_cols].reshape(heads, 3, HD, width)
+    return (
+        output,
+        input_grad,
+        jnp.transpose(qkv_out, (3, 1, 0, 2)).reshape(width, 3, head_cols),
+        jnp.transpose(second_grad[:head_cols]),
+        jnp.transpose(second_grad[head_cols : head_cols + 2 * units]).reshape(width, 2, units),
+        jnp.transpose(second_grad[head_cols + 2 * units :]),
+        gain_rows[0],
+        gain_rows[1],
+    )
+
+
+def on_device(*operands):
+    micro_count, tok_rows = operands[0].shape[0], operands[0].shape[1]
+    groups, parts = lax.axis_size("fsdp"), lax.axis_size("tp")
+    heads = operands[4].shape[2] // HD
+    if groups == 8 and parts == 4 and micro_count == 2 and micro_count * heads == groups and tok_rows % 256 == 0:
+        return paired_layer(*operands)
+    return general_layer(*operands)
+
+
 def solution(mesh):
     placed = (
         P(None, "fsdp", None),

time: 1080 us -> 429 us (0.40)
  waiting for transfers between devices: 555 us -> 200 us
  blocking collectives: 222 us -> 0 us
  matrix products: 130 us -> 29.5 us
  starting transfers between devices: 24 us -> 78.7 us
  other arithmetic: 71.9 us -> 37.6 us
  Pallas kernels: 0 us -> 25.9 us
    reduce_scatter x4 -> x0, waiting for transfers between devices: 263 us -> none  [the longest x1 109 us: on_device(): lax.psum_scatter(acc_in, 'fsdp', scatter_dimension=0, tiled=True)]
    all_gather x11 -> x0, waiting for transfers between devices: 212 us -> none  [the longest x2 65.5 us: on_device(): lax.all_gather(value_low, 'fsdp', axis=0, tiled=True)]
    all_gather x7 -> x0, blocking collectives: 200 us -> none  [the longest x2 64 us: on_device(): lax.all_gather(jnp.transpose(log_total), 'fsdp', axis=0, tiled=True)]
    ppermute x0 -> x38, waiting for transfers between devices: none -> 165 us  [the longest x22 127 us: hop(): return lax.ppermute(value, 'fsdp', [(i, i ^ step) for i in range(8)])]
    dot_general x36 -> x21, matrix products: 130 us -> 29.5 us  [the longest x17 27.1 us: mm(): lax.dot_general(left, right, dims, preferred_element_type=jnp.float32)]
    psum x3 -> x0, waiting for transfers between devices: 61 us -> none  [the longest x1 33.2 us: on_device(): branch = lax.psum(attn_part.astype(jnp.bfloat16), 'tp').astype(jnp.float32)]
    ppermute x0 -> x38, starting transfers between devices: none -> 45.5 us  [the longest x22 37.2 us: hop(): return lax.ppermute(value, 'fsdp', [(i, i ^ step) for i in range(8)])]
    pallas_call x0 -> x2, Pallas kernels: none -> 25.9 us  [the longest x1 13.2 us: attend_back(): pl.pallas_call(attend_back_kernel, in_specs=[pl.BlockSpec(memory_space=pl...]
  transfers between devices with their start and end apart: 22 -> 44, of which waited for: 13 -> 22; matrix products, arithmetic and copies ran while one was open for 18% -> 21% of each run, Pallas kernels for 0% -> 6%
where the time goes in v1:
time: 429 us; the launch traced here: 426 us
  waiting for transfers between devices  200 us (47%)
  starting transfers between devices  78.7 us (18%)
  local copies, waits for them, and re-layouts  41.9 us (10%)
  other arithmetic  37.6 us (9%)
  matrix products  29.5 us (7%)
  Pallas kernels  25.9 us (6%)
  between operations  12.5 us (3%)
    ppermute x22, waiting for transfers between devices, hop(): return lax.ppermute(value, 'fsdp', [(i, i ^ step) for i in range(8)])  127 us
    ppermute x22, starting transfers between devices, hop(): return lax.ppermute(value, 'fsdp', [(i, i ^ step) for i in range(8)])  37.2 us
    ppermute x6, waiting for transfers between devices, across(): return lax.ppermute(value, 'tp', [(i, i ^ 2) for i in range(4)])  33.2 us
    all_to_all x1, waiting for transfers between devices, paired_layer(): lax.all_to_all(d_raw_out, 'fsdp', 0, 0, tiled=True)  32.2 us
    dot_general x17, matrix products, mm(): lax.dot_general(left, right, dims, preferred_element_type=jnp.float32)  27.1 us
    unnamed x108, local copies, waits for them, and re-layouts  23.2 us
    pallas_call x1, Pallas kernels, attend_back(): pl.pallas_call(attend_back_kernel, in_specs=[pl.BlockSpec(memory_space=pl...  13.2 us
    pallas_call x1, Pallas kernels, attend(): pl.pallas_call(attend_kernel, in_specs=[pl.BlockSpec(memory_space=pltpu.S...  12.8 us
  transfers between devices with their start and end apart: 44, of which 22 were waited for; matrix products, arithmetic and copies ran while one was open for 21% of the time, Pallas kernels for 6%

profile of v1, /device:TPU:0, one launch (start us, length us, event | category | flops | bytes accessed | tf_op | source)
XLA Modules:
  0.0 426.4 jit_solution(151225127865484260)
XLA Ops:
  37.2 12.4 %collective-permute-done = bf16[784,128]{1,0:T(8,128)(2,1)} collective-permute-done((bf16[784,128]{1,0:T(8,128)(2,1)}, bf16[784,128]{1,0:T(8,128)(2,1)}, u32[]{:S(2)}, u32[]{:S(2)}) %collective-permute-start) | collective-permute-done | bytes 200736 | tf_op jit(solution)/shard_map/ppermute | solution.py:337
  55.0 21.3 %collective-permute-done.1 = bf16[784,128]{1,0:T(8,128)(2,1)} collective-permute-done((bf16[784,128]{1,0:T(8,128)(2,1)}, bf16[784,128]{1,0:T(8,128)(2,1)}, u32[]{:S(2)}, u32[]{:S(2)}) %collective-permute-start.1) | collective-permute-done | bytes 200736 | tf_op jit(solution)/shard_map/ppermute | solution.py:337
  104.5 5.2 %all-to-all-start = ((bf16[8,192,256]{2,1,0:T(8,128)(2,1)}), bf16[8,192,256]{2,1,0:T(8,128)(2,1)S(1)}, u32[]{:S(2)}, u32[]{:S(2)}) async-start(bf16[8,192,256]{2,1,0:T(8,128)(2,1)} %bitcast.36), calls=%async_computation | async-start | bytes 1572864 | tf_op jit(solution)/shard_map/all_to_all | solution.py:624
  123.0 9.0 %collective-permute-done.11 = bf16[2224,128]{1,0:T(8,128)(2,1)S(1)} collective-permute-done((bf16[2224,128]{1,0:T(8,128)(2,1)}, bf16[2224,128]{1,0:T(8,128)(2,1)S(1)}, u32[]{:S(2)}, u32[]{:S(2)}) %collective-permute-start.11) | collective-permute-done | bytes 569376 | tf_op jit(solution)/shard_map/ppermute | solution.py:337
  132.9 12.8 %attend.1 = (bf16[8,64,256]{2,1,0:T(8,128)(2,1)}, f32[8,64,256]{2,1,0:T(8,128)S(1)}, f32[8,1,256]{2,1,0:T(1,128)S(1)}) custom-call(s32[8]{0:T(128)S(1)} %get-tuple-element.164.lens_ref, bf16[8,192,256]{2,1,0:T(8,128)(2,1)S(1)} %all-to-all-done.qkv_ref), custom_call_target="tpu_custom_call" | custom-call | tf_op jit(solution)/shard_map/attend/pallas_call | solution.py:439
  145.7 7.2 %all-to-all-start.1 = ((bf16[8,64,256]{2,1,0:T(8,128)(2,1)}), bf16[8,64,256]{2,1,0:T(8,128)(2,1)S(1)}, u32[]{:S(2)}, u32[]{:S(2)}) async-start(bf16[8,64,256]{2,1,0:T(8,128)(2,1)} %get-tuple-element.35), calls=%async_computation.1 | async-start | bytes 524288 | tf_op jit(solution)/shard_map/all_to_all | solution.py:627
  168.6 11.8 %collective-permute-done.15 = bf16[256,1024]{1,0:T(8,128)(2,1)S(1)} collective-permute-done((bf16[256,1024]{1,0:T(8,128)(2,1)S(1)}, bf16[256,1024]{1,0:T(8,128)(2,1)S(1)}, u32[]{:S(2)}, u32[]{:S(2)}) %collective-permute-start.15) | collective-permute-done | bytes 524320 | tf_op jit(solution)/shard_map/ppermute | solution.py:345
  198.6 11.4 %collective-permute-done.24 = bf16[256,1024]{1,0:T(8,128)(2,1)S(1)} collective-permute-done((bf16[256,1024]{1,0:T(8,128)(2,1)S(1)}, bf16[256,1024]{1,0:T(8,128)(2,1)S(1)}, u32[]{:S(2)}, u32[]{:S(2)}) %collective-permute-start.24) | collective-permute-done | bytes 524320 | tf_op jit(solution)/shard_map/ppermute | solution.py:345
  210.6 9.9 %collective-permute-done.18 = bf16[256,1024]{1,0:T(8,128)(2,1)S(1)} collective-permute-done((bf16[256,1024]{1,0:T(8,128)(2,1)S(1)}, bf16[256,1024]{1,0:T(8,128)(2,1)S(1)}, u32[]{:S(2)}, u32[]{:S(2)}) %collective-permute-start.18) | collective-permute-done | bytes 524320 | tf_op jit(solution)/shard_map/ppermute | solution.py:345
  223.6 4.3 %all-to-all-start.2 = ((bf16[8,16,1024]{2,1,0:T(8,128)(2,1)}), bf16[8,16,1024]{2,1,0:T(8,128)(2,1)}, u32[]{:S(2)}, u32[]{:S(2)}) async-start(bf16[8,16,1024]{2,1,0:T(8,128)(2,1)} %bitcast.62), calls=%async_computation.2 | async-start | bytes 524288 | tf_op jit(solution)/shard_map/all_to_all | solution.py:705
  228.0 4.0 fusion.96
  232.0 4.0 fusion.44
  241.0 5.3 %all-to-all-start.4 = ((bf16[8,64,256]{2,1,0:T(8,128)(2,1)}), bf16[8,64,256]{2,1,0:T(8,128)(2,1)S(1)}, u32[]{:S(2)}, u32[]{:S(2)}) async-start(bf16[8,64,256]{2,1,0:T(8,128)(2,1)} %bitcast.81), calls=%async_computation.4 | async-start | bytes 524288 | tf_op jit(solution)/shard_map/all_to_all | solution.py:716
  247.9 8.7 %pad_maximum_fusion = f32[2224,1024]{1,0:T(8,128)} fusion(f32[656,1024]{1,0:T(8,128)} %fusion.96, f32[1312,1024]{1,0:T(8,128)} %fusion.44, f32[256,1024]{1,0:T(8,128)S(1)} %convolution_add_fusion.1), kind=kLoop, calls=%fused_computation | loop fusion | flops 4554752 | bytes 18219008 | tf_op jit(solution)/shard_map/concatenate | solution.py:718
  256.7 4.0 slice.425
  262.7 13.2 %attend_back.1 = bf16[8,192,256]{2,1,0:T(8,128)(2,1)} custom-call(s32[8]{0:T(128)S(1)} %get-tuple-element.164.lens_ref, bf16[8,192,256]{2,1,0:T(8,128)(2,1)S(1)} %all-to-all-done.qkv_ref, f32[8,64,256]{2,1,0:T(8,128)S(1)} %get-tuple-element.36.exact_ref, f32[8,1,256]{2,1,0:T(1,128)S(1)} %get-tuple-element.37.log_ref, ...), custom_call_target="tpu_custom_call" | custom-call | tf_op jit(solution)/shard_map/attend_back/pallas_call | solution.py:525
  275.8 7.7 %all-to-all-start.5 = ((bf16[8,192,256]{2,1,0:T(8,128)(2,1)}), bf16[8,192,256]{2,1,0:T(8,128)(2,1)S(1)}, u32[]{:S(2)}, u32[]{:S(2)}) async-start(bf16[8,192,256]{2,1,0:T(8,128)(2,1)} %attend_back.1), calls=%async_computation.5 | async-start | bytes 1572864 | tf_op jit(solution)/shard_map/all_to_all | solution.py:723
  288.3 32.2 %all-to-all-done.5 = bf16[8,192,256]{2,1,0:T(8,128)(2,1)S(1)} async-done(((bf16[8,192,256]{2,1,0:T(8,128)(2,1)}), bf16[8,192,256]{2,1,0:T(8,128)(2,1)S(1)}, u32[]{:S(2)}, u32[]{:S(2)}) %all-to-all-start.5) | async-done | bytes 786464 | tf_op jit(solution)/shard_map/all_to_all | solution.py:723
  323.6 4.0 fusion.85
  335.5 10.2 %collective-permute-done.36 = bf16[2224,128]{1,0:T(8,128)(2,1)S(1)} collective-permute-done((bf16[2224,128]{1,0:T(8,128)(2,1)S(1)}, bf16[2224,128]{1,0:T(8,128)(2,1)S(1)}, u32[]{:S(2)}, u32[]{:S(2)}) %collective-permute-start.36) | collective-permute-done | bytes 569376 | tf_op jit(solution)/shard_map/ppermute | solution.py:337
  345.7 34.4 %collective-permute-done.35 = bf16[2224,128]{1,0:T(8,128)(2,1)S(1)} collective-permute-done((bf16[2224,128]{1,0:T(8,128)(2,1)S(1)}, bf16[2224,128]{1,0:T(8,128)(2,1)S(1)}, u32[]{:S(2)}, u32[]{:S(2)}) %collective-permute-start.35) | collective-permute-done | bytes 569376 | tf_op jit(solution)/shard_map/ppermute | solution.py:337
  390.2 15.9 %collective-permute-done.29 = bf16[784,512]{1,0:T(8,128)(2,1)S(1)} collective-permute-done((bf16[784,512]{1,0:T(8,128)(2,1)S(1)}, bf16[784,512]{1,0:T(8,128)(2,1)S(1)}, u32[]{:S(2)}, u32[]{:S(2)}) %collective-permute-start.29) | collective-permute-done | bytes 802848 | tf_op jit(solution)/shard_map/ppermute | solution.py:337
  411.1 5.3 %collective-permute-done.32 = bf16[784,128]{1,0:T(8,128)(2,1)S(1)} collective-permute-done((bf16[784,128]{1,0:T(8,128)(2,1)S(1)}, bf16[784,128]{1,0:T(8,128)(2,1)S(1)}, u32[]{:S(2)}, u32[]{:S(2)}) %collective-permute-start.32) | collective-permute-done | bytes 200736 | tf_op jit(solution)/shard_map/ppermute | solution.py:337
  416.4 7.2 %collective-permute-done.31 = bf16[784,128]{1,0:T(8,128)(2,1)S(1)} collective-permute-done((bf16[784,128]{1,0:T(8,128)(2,1)S(1)}, bf16[784,128]{1,0:T(8,128)(2,1)S(1)}, u32[]{:S(2)}, u32[]{:S(2)}) %collective-permute-start.31) | collective-permute-done | bytes 200736 | tf_op jit(solution)/shard_map/ppermute | solution.py:337
  (322 shorter events, 152.5 us)
Async XLA Ops:
  4.0 105.7 %collective-permute-start.7 = (bf16[2224,128]{1,0:T(8,128)(2,1)}, bf16[2224,128]{1,0:T(8,128)(2,1)}, u32[]{:S(2)}, u32[]{:S(2)}) collective-permute-start(bf16[2224,128]{1,0:T(8,128)(2,1)} %get-tuple-element.138), channel_id=1, source_target_pairs={{0,8},{4,12},{8,0},{12,4},{16,24},{20,28},{24,16},{28,20},{1,9},{5... | collective-permute-start | bytes 1708040 | tf_op jit(solution)/shard_map/ppermute | solution.py:337
  7.0 104.8 %collective-permute-start.8 = (bf16[2224,128]{1,0:T(8,128)(2,1)}, bf16[2224,128]{1,0:T(8,128)(2,1)}, u32[]{:S(2)}, u32[]{:S(2)}) collective-permute-start(bf16[2224,128]{1,0:T(8,128)(2,1)} %get-tuple-element.138), channel_id=1, source_target_pairs={{0,16},{4,20},{8,24},{12,28},{16,0},{20,4},{24,8},{28,12},{1,17},{... | collective-permute-start | bytes 1708040 | tf_op jit(solution)/shard_map/ppermute | solution.py:337
  9.6 104.3 %collective-permute-start.9 = (bf16[2224,128]{1,0:T(8,128)(2,1)}, bf16[2224,128]{1,0:T(8,128)(2,1)}, u32[]{:S(2)}, u32[]{:S(2)}) collective-permute-start(bf16[2224,128]{1,0:T(8,128)(2,1)} %get-tuple-element.138), channel_id=1, source_target_pairs={{0,24},{4,28},{8,16},{12,20},{16,8},{20,12},{24,0},{28,4},{1,25},{... | collective-permute-start | bytes 1708040 | tf_op jit(solution)/shard_map/ppermute | solution.py:337
  11.6 38.0 %collective-permute-start = (bf16[784,128]{1,0:T(8,128)(2,1)}, bf16[784,128]{1,0:T(8,128)(2,1)}, u32[]{:S(2)}, u32[]{:S(2)}) collective-permute-start(bf16[784,128]{1,0:T(8,128)(2,1)} %get-tuple-element.146), channel_id=1, source_target_pairs={{0,8},{4,12},{8,0},{12,4},{16,24},{20,28},{24,16},{28,20},{1,9},{5... | collective-permute-start | bytes 602120 | tf_op jit(solution)/shard_map/ppermute | solution.py:337
  12.5 63.9 %collective-permute-start.1 = (bf16[784,128]{1,0:T(8,128)(2,1)}, bf16[784,128]{1,0:T(8,128)(2,1)}, u32[]{:S(2)}, u32[]{:S(2)}) collective-permute-start(bf16[784,128]{1,0:T(8,128)(2,1)} %get-tuple-element.146), channel_id=1, source_target_pairs={{0,16},{4,20},{8,24},{12,28},{16,0},{20,4},{24,8},{28,12},{1,17},{... | collective-permute-start | bytes 602120 | tf_op jit(solution)/shard_map/ppermute | solution.py:337
  17.5 87.0 %all-to-all-start.3 = ((bf16[8,2,8,1024]{3,2,1,0:T(8,128)(2,1)}), bf16[8,2,8,1024]{3,2,1,0:T(8,128)(2,1)S(1)}, u32[]{:S(2)}, u32[]{:S(2)}) async-start(bf16[8,2,8,1024]{3,2,1,0:T(8,128)(2,1)} %bitcast.257), calls=%async_computation.3 | async-start | bytes 524288 | tf_op jit(solution)/shard_map/all_to_all | solution.py:662
  49.6 29.9 %collective-permute-start.2 = (bf16[784,128]{1,0:T(8,128)(2,1)}, bf16[784,128]{1,0:T(8,128)(2,1)S(1)}, u32[]{:S(2)}, u32[]{:S(2)}) collective-permute-start(bf16[784,128]{1,0:T(8,128)(2,1)} %get-tuple-element.146), channel_id=1, source_target_pairs={{0,24},{4,28},{8,16},{12,20},{16,8},{20,12},{24,0},{28,4},{1,25},{... | collective-permute-start | bytes 602120 | tf_op jit(solution)/shard_map/ppermute | solution.py:337
  93.0 26.7 %collective-permute-start.10 = (bf16[2224,128]{1,0:T(8,128)(2,1)}, bf16[2224,128]{1,0:T(8,128)(2,1)S(1)}, u32[]{:S(2)}, u32[]{:S(2)}) collective-permute-start(bf16[2224,128]{1,0:T(8,128)(2,1)} %get-tuple-element.138), channel_id=1, source_target_pairs={{0,4},{4,0},{8,12},{12,8},{16,20},{20,16},{24,28},{28,24},{1,5},{5... | collective-permute-start | bytes 1708040 | tf_op jit(solution)/shard_map/ppermute | solution.py:337
  104.5 28.4 %all-to-all-start = ((bf16[8,192,256]{2,1,0:T(8,128)(2,1)}), bf16[8,192,256]{2,1,0:T(8,128)(2,1)S(1)}, u32[]{:S(2)}, u32[]{:S(2)}) async-start(bf16[8,192,256]{2,1,0:T(8,128)(2,1)} %bitcast.36), calls=%async_computation | async-start | bytes 1572864 | tf_op jit(solution)/shard_map/all_to_all | solution.py:624
  109.7 22.3 %collective-permute-start.11 = (bf16[2224,128]{1,0:T(8,128)(2,1)}, bf16[2224,128]{1,0:T(8,128)(2,1)S(1)}, u32[]{:S(2)}, u32[]{:S(2)}) collective-permute-start(bf16[2224,128]{1,0:T(8,128)(2,1)} %collective-permute-done.7), channel_id=1, source_target_pairs={{0,4},{4,0},{8,12},{12,8},{16,20},{20,16},{24,28},{28,24},{1,5},{5... | collective-permute-start | bytes 1708040 | tf_op jit(solution)/shard_map/ppermute | solution.py:337
  111.8 41.1 %collective-permute-start.12 = (bf16[2224,128]{1,0:T(8,128)(2,1)}, bf16[2224,128]{1,0:T(8,128)(2,1)}, u32[]{:S(2)}, u32[]{:S(2)}) collective-permute-start(bf16[2224,128]{1,0:T(8,128)(2,1)} %collective-permute-done.8), channel_id=1, source_target_pairs={{0,4},{4,0},{8,12},{12,8},{16,20},{20,16},{24,28},{28,24},{1,5},{5... | collective-permute-start | bytes 1708040 | tf_op jit(solution)/shard_map/ppermute | solution.py:337
  113.9 42.5 %collective-permute-start.13 = (bf16[2224,128]{1,0:T(8,128)(2,1)}, bf16[2224,128]{1,0:T(8,128)(2,1)}, u32[]{:S(2)}, u32[]{:S(2)}) collective-permute-start(bf16[2224,128]{1,0:T(8,128)(2,1)} %collective-permute-done.9), channel_id=1, source_target_pairs={{0,4},{4,0},{8,12},{12,8},{16,20},{20,16},{24,28},{28,24},{1,5},{5... | collective-permute-start | bytes 1708040 | tf_op jit(solution)/shard_map/ppermute | solution.py:337
  121.5 42.6 %collective-permute-start.22 = (bf16[2,8,2,8,1024]{4,3,2,1,0:T(8,128)(2,1)}, bf16[2,8,2,8,1024]{4,3,2,1,0:T(8,128)(2,1)S(1)}, u32[]{:S(2)}, u32[]{:S(2)}) collective-permute-start(bf16[2,8,2,8,1024]{4,3,2,1,0:T(8,128)(2,1)} %pad_maximum_fusion.9), channel_id=1, source_target_pairs={{0,2},{1,3},{2,0},{3,1},{4,6},{5,7},{6,4},{7,5},{8,10},{9,11},{10,... | collective-permute-start | bytes 1572872 | tf_op jit(solution)/shard_map/ppermute | solution.py:345
  198.1 22.5 %collective-permute-start.18 = (bf16[256,1024]{1,0:T(8,128)(2,1)S(1)}, bf16[256,1024]{1,0:T(8,128)(2,1)S(1)}, u32[]{:S(2)}, u32[]{:S(2)}) collective-permute-start(bf16[256,1024]{1,0:T(8,128)(2,1)S(1)} %fusion.41), channel_id=1, source_target_pairs={{0,2},{1,3},{2,0},{3,1},{4,6},{5,7},{6,4},{7,5},{8,10},{9,11},{10,... | collective-permute-start | bytes 1572872 | tf_op jit(solution)/shard_map/ppermute | solution.py:345
  236.4 47.2 %collective-permute-start.19 = (bf16[8,16,1024]{2,1,0:T(8,128)(2,1)}, bf16[8,16,1024]{2,1,0:T(8,128)(2,1)}, u32[]{:S(2)}, u32[]{:S(2)}) collective-permute-start(bf16[8,16,1024]{2,1,0:T(8,128)(2,1)} %all-to-all-done.2), channel_id=1, source_target_pairs={{0,2},{1,3},{2,0},{3,1},{4,6},{5,7},{6,4},{7,5},{8,10},{9,11},{10,... | collective-permute-start | bytes 786440 | tf_op jit(solution)/shard_map/ppermute | solution.py:345
  241.0 21.7 %all-to-all-start.4 = ((bf16[8,64,256]{2,1,0:T(8,128)(2,1)}), bf16[8,64,256]{2,1,0:T(8,128)(2,1)S(1)}, u32[]{:S(2)}, u32[]{:S(2)}) async-start(bf16[8,64,256]{2,1,0:T(8,128)(2,1)} %bitcast.81), calls=%async_computation.4 | async-start | bytes 524288 | tf_op jit(solution)/shard_map/all_to_all | solution.py:716
  260.7 62.9 %collective-permute-start.33 = (bf16[2224,512]{1,0:T(8,128)(2,1)}, bf16[2224,512]{1,0:T(8,128)(2,1)}, u32[]{:S(2)}, u32[]{:S(2)}) collective-permute-start(bf16[2224,512]{1,0:T(8,128)(2,1)} %slice.425), channel_id=1, source_target_pairs={{0,4},{4,0},{8,12},{12,8},{16,20},{20,16},{24,28},{28,24},{1,5},{5... | collective-permute-start | bytes 6832136 | tf_op jit(solution)/shard_map/ppermute | solution.py:337
  275.8 44.6 %all-to-all-start.5 = ((bf16[8,192,256]{2,1,0:T(8,128)(2,1)}), bf16[8,192,256]{2,1,0:T(8,128)(2,1)S(1)}, u32[]{:S(2)}, u32[]{:S(2)}) async-start(bf16[8,192,256]{2,1,0:T(8,128)(2,1)} %attend_back.1), calls=%async_computation.5 | async-start | bytes 1572864 | tf_op jit(solution)/shard_map/all_to_all | solution.py:723
  327.9 17.8 %collective-permute-start.36 = (bf16[2224,128]{1,0:T(8,128)(2,1)S(1)}, bf16[2224,128]{1,0:T(8,128)(2,1)S(1)}, u32[]{:S(2)}, u32[]{:S(2)}) collective-permute-start(bf16[2224,128]{1,0:T(8,128)(2,1)S(1)} %get-tuple-element.110), channel_id=1, source_target_pairs={{0,24},{4,28},{8,16},{12,20},{16,8},{20,12},{24,0},{28,4},{1,25},{... | collective-permute-start | bytes 1708040 | tf_op jit(solution)/shard_map/ppermute | solution.py:337
  331.5 48.6 %collective-permute-start.35 = (bf16[2224,128]{1,0:T(8,128)(2,1)S(1)}, bf16[2224,128]{1,0:T(8,128)(2,1)S(1)}, u32[]{:S(2)}, u32[]{:S(2)}) collective-permute-start(bf16[2224,128]{1,0:T(8,128)(2,1)S(1)} %get-tuple-element.111), channel_id=1, source_target_pairs={{0,16},{4,20},{8,24},{12,28},{16,0},{20,4},{24,8},{28,12},{1,17},{... | collective-permute-start | bytes 1708040 | tf_op jit(solution)/shard_map/ppermute | solution.py:337
  331.5 48.6 %collective-permute-start.34 = (bf16[2224,128]{1,0:T(8,128)(2,1)S(1)}, bf16[2224,128]{1,0:T(8,128)(2,1)S(1)}, u32[]{:S(2)}, u32[]{:S(2)}) collective-permute-start(bf16[2224,128]{1,0:T(8,128)(2,1)S(1)} %get-tuple-element.109), channel_id=1, source_target_pairs={{0,8},{4,12},{8,0},{12,4},{16,24},{20,28},{24,16},{28,20},{1,9},{5... | collective-permute-start | bytes 1708040 | tf_op jit(solution)/shard_map/ppermute | solution.py:337
  334.9 49.2 %collective-permute-start.27 = (bf16[256,1024]{1,0:T(8,128)(2,1)S(1)}, bf16[256,1024]{1,0:T(8,128)(2,1)S(1)}, u32[]{:S(2)}, u32[]{:S(2)}) collective-permute-start(bf16[256,1024]{1,0:T(8,128)(2,1)S(1)} %fusion.22), channel_id=1, source_target_pairs={{0,2},{1,3},{2,0},{3,1},{4,6},{5,7},{6,4},{7,5},{8,10},{9,11},{10,... | collective-permute-start | bytes 1572872 | tf_op jit(solution)/shard_map/ppermute | solution.py:345
  386.9 19.2 %collective-permute-start.29 = (bf16[784,512]{1,0:T(8,128)(2,1)S(1)}, bf16[784,512]{1,0:T(8,128)(2,1)S(1)}, u32[]{:S(2)}, u32[]{:S(2)}) collective-permute-start(bf16[784,512]{1,0:T(8,128)(2,1)S(1)} %slice.426), channel_id=1, source_target_pairs={{0,4},{4,0},{8,12},{12,8},{16,20},{20,16},{24,28},{28,24},{1,5},{5... | collective-permute-start | bytes 2408456 | tf_op jit(solution)/shard_map/ppermute | solution.py:337
  390.2 20.9 %collective-permute-start.28 = (bf16[256,1024]{1,0:T(8,128)(2,1)S(1)}, bf16[256,1024]{1,0:T(8,128)(2,1)S(1)}, u32[]{:S(2)}, u32[]{:S(2)}) collective-permute-start(bf16[256,1024]{1,0:T(8,128)(2,1)S(1)} %constant_dynamic-update-slice_fusion.24), channel_id=1, source_target_pairs={{0,1},{1,0},{2,3},{3,2},{4,5},{5,4},{6,7},{7,6},{8,9},{9,8},{10,11... | collective-permute-start | bytes 1572872 | tf_op jit(solution)/shard_map/ppermute | solution.py:341
  (51 other events, 418.8 us)

commit v2 on v0

--- a/solution.py
+++ b/solution.py
@@ -1,6 +1,10 @@
+import math
+
 import jax
 import jax.numpy as jnp
 from jax import lax
+from jax.experimental import pallas as pl
+from jax.experimental.pallas import tpu as pltpu
 from jax.sharding import PartitionSpec as P
 
 D = 1024
@@ -31,8 +35,13 @@
     return values * cosine[:, None, :] + turned * sine[:, None, :]
 
 
+def running_ends(seq_lens):
+    order = jnp.arange(seq_lens.shape[0], dtype=jnp.int32)
+    return jnp.sum(jnp.where(order[None, :] <= order[:, None], seq_lens[None, :], 0), axis=1)
+
+
 def seq_info(anchor, seq_lens):
-    ends = jnp.cumsum(seq_lens)
+    ends = running_ends(seq_lens)
     starts = ends - seq_lens
     segment = jnp.sum((anchor[:, None] >= ends[None, :]).astype(jnp.int32), axis=1)
     onehot = segment[:, None] == jnp.arange(seq_lens.shape[0], dtype=jnp.int32)[None, :]
@@ -55,7 +64,7 @@
     return step_fn(running, pieces, offset)
 
 
-def on_device(
+def general_layer(
     tokens, cotangent, perm, lengths, w_qkv, w_attn_out, w_in, w_down, gain_one, gain_two
 ):
     groups = lax.axis_size("fsdp")
@@ -314,6 +323,744 @@
     )
 
 
+JOIN = 2
+FAR = -1e30
+ORDER = (0, 2, 4, 6, 1, 3, 5, 7)
+NT = (((1,), (1,)), ((), ()))
+TN = (((0,), (0,)), ((), ()))
+NN = (((1,), (0,)), ((), ()))
+ROOM = 10 * 1024 * 1024
+
+
+def partial(kernel, *given):
+    return lambda *refs: kernel(*given, *refs)
+
+
+def mm(left, right, dims):
+    return lax.dot_general(left, right, dims, preferred_element_type=jnp.float32)
+
+
+def hop(value, step):
+    return lax.ppermute(value, "fsdp", [(i, i ^ step) for i in range(8)])
+
+
+def twin(value):
+    return lax.ppermute(value, "tp", [(i, i ^ 1) for i in range(4)])
+
+
+def across(value):
+    return lax.ppermute(value, "tp", [(i, i ^ 2) for i in range(4)])
+
+
+def deal_out(value):
+    return lax.all_to_all(value, "fsdp", 0, 0, tiled=True)
+
+
+def after(value, *earlier):
+    return lax.optimization_barrier((value,) + earlier)[0]
+
+
+def sync(values):
+    return lax.optimization_barrier(values)
+
+
+def z_phase(shard):
+    return [shard] + [hop(shard, step) for step in ORDER[1:4]]
+
+
+def y_phase(shards):
+    return [hop(one, 1) for one in shards]
+
+
+def local_call(kernel, name, scalars, arrays, outs, scratch=(), shards=(), copies=8, far_in=(), far_out=()):
+    shapes = [(one.shape, one.dtype) for one in arrays]
+    staged = [shapes[at] for at in far_in] + [outs[at] for at in far_out]
+    sems = [pltpu.SemaphoreType.DMA((copies,))] if shards else []
+    room = ROOM + sum(math.prod(shape) * jnp.dtype(kind).itemsize for shape, kind in [*shapes, *outs, *scratch])
+    counts = (len(scalars), len(arrays), len(shards), len(outs), len(scratch) + len(sems))
+
+    def body(*refs):
+        groups = []
+        for count in counts:
+            groups.append(list(refs[:count]))
+            refs = refs[count:]
+        given, ins, pieces, results, extra = groups
+        if not staged:
+            return kernel(*given, *ins, *pieces, *results, *extra)
+        stage, sem = refs[:-1], refs[-1]
+        incoming, outgoing = [], []
+        for slot, at in enumerate(far_in):
+            incoming.append(pltpu.make_async_copy(ins[at], stage[slot], sem.at[slot]))
+            incoming[-1].start()
+            ins[at] = stage[slot]
+        for slot, at in enumerate(far_out, len(far_in)):
+            outgoing.append(pltpu.make_async_copy(stage[slot], results[at], sem.at[slot]))
+            results[at] = stage[slot]
+        for copy in incoming:
+            copy.wait()
+        kernel(*given, *ins, *pieces, *results, *extra)
+        for copy in outgoing:
+            copy.start()
+        for copy in outgoing:
+            copy.wait()
+
+    def space(at, far):
+        return pl.BlockSpec(memory_space=pltpu.HBM if at in far else pltpu.VMEM)
+
+    result = pl.pallas_call(
+        body,
+        in_specs=[pl.BlockSpec(memory_space=pltpu.SMEM)] * len(scalars)
+        + [space(at, far_in) for at in range(len(arrays))]
+        + [pl.BlockSpec(memory_space=pl.ANY)] * len(shards),
+        out_specs=[space(at, far_out) for at in range(len(outs))],
+        out_shape=[jax.ShapeDtypeStruct(shape, kind) for shape, kind in outs],
+        scratch_shapes=[pltpu.VMEM(shape, kind) for shape, kind in scratch]
+        + sems
+        + [pltpu.VMEM(shape, kind) for shape, kind in staged]
+        + ([pltpu.SemaphoreType.DMA((len(staged),))] if staged else []),
+        compiler_params=pltpu.CompilerParams(vmem_limit_bytes=room),
+        name=name,
+    )(*scalars, *arrays, *shards)
+    return result if len(outs) > 1 else result[0]
+
+
+def block_at(order_ref, place, width):
+    return pl.ds(pl.multiple_of(order_ref[place] * width, width), width)
+
+
+def shard_copies(shards, low, high, into_ref, sem_ref, base=0):
+    width = shards[0].shape[1]
+    copies = []
+    for place, shard in enumerate(shards):
+        span = pl.ds(place * width, width)
+        source = shard.at[pl.ds(low, high - low), :]
+        copies.append(pltpu.make_async_copy(source, into_ref.at[:, span], sem_ref.at[base + place]))
+        copies[-1].start()
+    return copies
+
+
+def gathered_copies(order_ref, source, low, high, into_ref, sem_ref):
+    width = source.shape[2]
+    copies = []
+    for place in range(8):
+        copies.append(
+            pltpu.make_async_copy(
+                source.at[order_ref[place], pl.ds(low, high - low), :],
+                into_ref.at[:, pl.ds(place * width, width)],
+                sem_ref.at[place],
+            )
+        )
+        copies[-1].start()
+    return copies
+
+
+def finish(copies):
+    for copy in copies:
+        copy.wait()
+
+
+def project_kernel(order_ref, x_ref, table_ref, *refs):
+    shards = refs[:8]
+    norm_ref, gains_ref, send_ref, w_ref, sem_ref = refs[8:]
+    width = shards[0].shape[1]
+    rows = x_ref.shape[1]
+    wide = w_ref.shape[0] - 16
+    heads = wide // (3 * HD)
+    half = HD // 2
+    finish(shard_copies(shards, 0, wide + 16, w_ref, sem_ref))
+    gains_ref[...] = w_ref[wide:, :].astype(jnp.float32)[:2]
+    for micro in range(2):
+        x = x_ref[micro].astype(jnp.float32)
+        mean = jnp.mean(x, axis=-1, keepdims=True)
+        center = x - mean
+        spread = lax.rsqrt(jnp.mean(center * center, axis=-1, keepdims=True) + EPS)
+        for place in range(8):
+            piece = x_ref[micro, :, block_at(order_ref, place, width)].astype(jnp.float32)
+            span = slice(place * width, (place + 1) * width)
+            value = (piece - mean) * spread * gains_ref[0:1, span]
+            norm_ref[micro * rows : (micro + 1) * rows, span] = value.astype(jnp.bfloat16)
+    raw = mm(w_ref[:wide, :], norm_ref[...], NT)
+    cosine, sine = table_ref[:half, :], table_ref[half:, :]
+    for head in range(heads):
+        base = head * 3 * HD
+        for kind in range(2):
+            upper = raw[base + kind * HD : base + kind * HD + half]
+            lower = raw[base + kind * HD + half : base + (kind + 1) * HD]
+            first = (upper * cosine - lower * sine).astype(jnp.bfloat16)
+            second = (lower * cosine + upper * sine).astype(jnp.bfloat16)
+            for micro in range(2):
+                span = slice(micro * rows, (micro + 1) * rows)
+                send_ref[micro * heads + head, kind * HD : kind * HD + half, :] = first[:, span]
+                send_ref[micro * heads + head, kind * HD + half : (kind + 1) * HD, :] = second[:, span]
+        value = raw[base + 2 * HD : base + 3 * HD].astype(jnp.bfloat16)
+        for micro in range(2):
+            send_ref[micro * heads + head, 2 * HD :, :] = value[:, micro * rows : (micro + 1) * rows]
+
+
+def key_range(lens_ref, low, high):
+    first = jnp.int32(0)
+    last = jnp.int32(0)
+    total = jnp.int32(0)
+    for index in range(lens_ref.shape[0]):
+        start = total
+        total = total + lens_ref[index]
+        first = jnp.where((start <= low) & (low < total), start, first)
+        last = jnp.where((start <= high) & (high < total), total, last)
+    return first, last
+
+
+def query_bounds(lens_ref, base, width):
+    place = base + lax.broadcasted_iota(jnp.int32, (1, width), 1)
+    first = jnp.zeros((1, width), jnp.int32)
+    last = jnp.zeros((1, width), jnp.int32)
+    total = jnp.int32(0)
+    for index in range(lens_ref.shape[0]):
+        start = total
+        total = total + lens_ref[index]
+        inside = (place >= start) & (place < total)
+        first = jnp.where(inside, start, first)
+        last = jnp.where(inside, total, last)
+    return first, last
+
+
+def lanes(ref, index, count, rows):
+    return jnp.concatenate([ref[index * count + at, rows, :] for at in range(count)], axis=1)
+
+
+def attend_kernel(lens_ref, qkv_ref, mixed_ref, exact_ref, log_ref, key_ref):
+    blocks, _, small = qkv_ref.shape
+    wide = JOIN * small
+    for at in range(blocks):
+        block = qkv_ref[at, HD : 2 * HD, :].astype(jnp.float32)
+        key_ref[at * small : (at + 1) * small, :] = jnp.transpose(block).astype(jnp.bfloat16)
+
+    def one_query(index, carry):
+        base = index * wide
+        first, last = key_range(lens_ref, base, base + wide - 1)
+        low, high = query_bounds(lens_ref, base, wide)
+        query = lanes(qkv_ref, index, JOIN, slice(0, HD)) * jnp.bfloat16(HD**-0.5)
+
+        def one_key(at, state):
+            peak, total, acc = state
+            start = pl.multiple_of(at * wide, wide)
+            scores = mm(key_ref[pl.ds(start, wide), :], query, NN)
+            place = start + lax.broadcasted_iota(jnp.int32, (wide, wide), 0)
+            scores = jnp.where((place >= low) & (place < high), scores, FAR)
+            top = jnp.maximum(peak, jnp.max(scores, axis=0, keepdims=True))
+            weights = jnp.exp(scores - top)
+            fade = jnp.exp(peak - top)
+            total = total * fade + jnp.sum(weights, axis=0, keepdims=True)
+            value = lanes(qkv_ref, at, JOIN, slice(2 * HD, 3 * HD))
+            acc = acc * fade + mm(value, weights.astype(jnp.bfloat16), NN)
+            return top, total, acc
+
+        peak, total, acc = lax.fori_loop(
+            first // wide,
+            (last + wide - 1) // wide,
+            one_key,
+            (
+                jnp.full((1, wide), FAR, jnp.float32),
+                jnp.zeros((1, wide), jnp.float32),
+                jnp.zeros((HD, wide), jnp.float32),
+            ),
+        )
+        result = acc / total
+        logs = peak + jnp.log(total)
+        for at in range(JOIN):
+            span = slice(at * small, (at + 1) * small)
+            mixed_ref[index * JOIN + at] = result[:, span].astype(jnp.bfloat16)
+            exact_ref[index * JOIN + at] = result[:, span]
+            log_ref[index * JOIN + at] = logs[:, span]
+        return carry
+
+    lax.fori_loop(0, blocks // JOIN, one_query, 0)
+
+
+def attend_back_kernel(
+    lens_ref, qkv_ref, exact_ref, log_ref, grad_ref, table_ref, raw_ref, pair_ref, dkey_ref, dvalue_ref
+):
+    blocks, _, small = qkv_ref.shape
+    wide = JOIN * small
+    half = HD // 2
+    for at in range(blocks):
+        block = qkv_ref[at, HD : 3 * HD, :].astype(jnp.float32)
+        pair_ref[at * small : (at + 1) * small, :] = jnp.transpose(block).astype(jnp.bfloat16)
+    dkey_ref[...] = jnp.zeros(dkey_ref.shape, jnp.float32)
+    dvalue_ref[...] = jnp.zeros(dvalue_ref.shape, jnp.float32)
+
+    def unturn(index, grad):
+        cosine = table_ref[index, :half, :]
+        sine = table_ref[index, half:, :]
+        upper, lower = grad[:half], grad[half:]
+        return upper * cosine + lower * sine, lower * cosine - upper * sine
+
+    def one_query(index, carry):
+        base = index * wide
+        first, last = key_range(lens_ref, base, base + wide - 1)
+        low, high = query_bounds(lens_ref, base, wide)
+        query = lanes(qkv_ref, index, JOIN, slice(0, HD)) * jnp.bfloat16(HD**-0.5)
+        grad = lanes(grad_ref, index, JOIN, slice(0, HD))
+        logs = lanes(log_ref, index, JOIN, slice(0, 1))
+        exact = lanes(exact_ref, index, JOIN, slice(0, HD))
+        delta = jnp.sum(grad.astype(jnp.float32) * exact, axis=0, keepdims=True)
+
+        def one_key(at, dquery):
+            start = pl.multiple_of(at * wide, wide)
+            span = pl.ds(start, wide)
+            scores = mm(pair_ref[span, :HD], query, NN)
+            dweights = mm(pair_ref[span, HD:], grad, NN)
+            place = start + lax.broadcasted_iota(jnp.int32, (wide, wide), 0)
+            weights = jnp.where((place >= low) & (place < high), jnp.exp(scores - logs), 0.0)
+            dscores = (weights * (dweights - delta)).astype(jnp.bfloat16)
+            dkey_ref[:, span] += mm(query, dscores, NT)
+            dvalue_ref[:, span] += mm(grad, weights.astype(jnp.bfloat16), NT)
+            return dquery + mm(lanes(qkv_ref, at, JOIN, slice(HD, 2 * HD)), dscores, NN)
+
+        dquery = lax.fori_loop(
+            first // wide,
+            (last + wide - 1) // wide,
+            one_key,
+            jnp.zeros((HD, wide), jnp.float32),
+        ) * (HD**-0.5)
+        for at in range(JOIN):
+            upper, lower = unturn(index * JOIN + at, dquery[:, at * small : (at + 1) * small])
+            raw_ref[index * JOIN + at, :half, :] = upper.astype(jnp.bfloat16)
+            raw_ref[index * JOIN + at, half:HD, :] = lower.astype(jnp.bfloat16)
+        return carry
+
+    lax.fori_loop(0, blocks // JOIN, one_query, 0)
+    for at in range(blocks):
+        span = slice(at * small, (at + 1) * small)
+        upper, lower = unturn(at, dkey_ref[:, span])
+        raw_ref[at, HD : HD + half, :] = upper.astype(jnp.bfloat16)
+        raw_ref[at, HD + half : 2 * HD, :] = lower.astype(jnp.bfloat16)
+        raw_ref[at, 2 * HD :, :] = dvalue_ref[:, span].astype(jnp.bfloat16)
+
+
+def mix_out_kernel(core_ref, order_ref, mixed_ref, all_ref, send_ref, keep_ref, w_ref, sem_ref):
+    last = all_ref.shape[1]
+    finish(gathered_copies(order_ref, all_ref, last - mixed_ref.shape[1], last, w_ref, sem_ref))
+    core = core_ref[0]
+    send_ref[...] = mm(mixed_ref[1 - core], w_ref[...], TN).astype(jnp.bfloat16)
+    keep_ref[...] = mm(mixed_ref[core], w_ref[...], TN)
+
+
+def norm_two_kernel(core_ref, order_ref, x_ref, half_ref, far_ref, gains_ref, hidden_ref, norm_ref):
+    core = core_ref[0]
+    width = x_ref.shape[2] // 8
+    for place in range(8):
+        span = slice(place * width, (place + 1) * width)
+        piece = x_ref[core, :, block_at(order_ref, place, width)].astype(jnp.float32)
+        branch = half_ref[:, span].astype(jnp.float32) + far_ref[:, span].astype(jnp.float32)
+        hidden_ref[:, span] = piece + branch
+    hidden = hidden_ref[...]
+    center = hidden - jnp.mean(hidden, axis=-1, keepdims=True)
+    spread = lax.rsqrt(jnp.mean(center * center, axis=-1, keepdims=True) + EPS)
+    norm_ref[...] = (center * spread * gains_ref[1:2, :]).astype(jnp.bfloat16)
+
+
+def feed_kernel(
+    order_ref, own_ref, other_ref, grad_ref, all_ref, send_ref, keep_ref, act_ref, dinp_ref, dgate_ref, w_ref, sem_ref
+):
+    units = w_ref.shape[0] // 3
+    inp_w, gate_w, down_w = [w_ref.at[pl.ds(at * units, units), :] for at in range(3)]
+    rows = own_ref.shape[0]
+    finish(gathered_copies(order_ref, all_ref, 0, 3 * units, w_ref, sem_ref))
+    for micro, norm_ref in ((1, other_ref), (0, own_ref)):
+        span = slice(micro * rows, (micro + 1) * rows)
+        inp = mm(norm_ref[...], inp_w[...], NT)
+        gate = mm(norm_ref[...], gate_w[...], NT)
+        dact = mm(grad_ref[micro], down_w[...], NT)
+        cdf = 0.5 * (1.0 + lax.erf(inp * (0.5**0.5)))
+        density = jnp.exp(-0.5 * inp * inp) * ((0.5 / jnp.pi) ** 0.5)
+        gelu = inp * cdf
+        act_ref[span, :] = (gelu * gate).astype(jnp.bfloat16)
+        dinp = (dact * gate * (cdf + inp * density)).astype(jnp.bfloat16)
+        dgate = (dact * gelu).astype(jnp.bfloat16)
+        dinp_ref[span, :] = dinp
+        dgate_ref[span, :] = dgate
+        part = mm(dinp, inp_w[...], NN) + mm(dgate, gate_w[...], NN)
+        if micro:
+            send_ref[...] = part.astype(jnp.bfloat16)
+        else:
+            keep_ref[...] = part
+
+
+def weight_grad_kernel(order_ref, dinp_ref, dgate_ref, act_ref, own_ref, other_ref, grad_ref, out_ref):
+    units = act_ref.shape[1]
+    rows = own_ref.shape[0]
+    width = out_ref.shape[2]
+    for at, (left_ref, rights) in enumerate((
+        (dinp_ref, (own_ref, other_ref)),
+        (dgate_ref, (own_ref, other_ref)),
+        (act_ref, (grad_ref.at[0], grad_ref.at[1])),
+    )):
+        total = mm(left_ref[:rows, :], rights[0][...], TN) + mm(left_ref[rows:, :], rights[1][...], TN)
+        for place in range(8):
+            piece = total[:, place * width : (place + 1) * width].astype(jnp.bfloat16)
+            out_ref[order_ref[place], at * units : (at + 1) * units, :] = piece
+
+
+def near_sum_kernel(near_ref, far_ref, own_ref, *low_refs):
+    own_ref[...] = near_ref[0] + far_ref[0].astype(jnp.float32)
+    for at, low_ref in enumerate(low_refs):
+        low_ref[...] = (near_ref[at + 1] + far_ref[at + 1].astype(jnp.float32)).astype(jnp.bfloat16)
+
+
+def down_kernel(order_ref, act_ref, all_ref, send_ref, keep_ref, w_ref, sem_ref):
+    rows = send_ref.shape[0]
+    units = w_ref.shape[0]
+    finish(gathered_copies(order_ref, all_ref, 2 * units, 3 * units, w_ref, sem_ref))
+    send_ref[...] = mm(act_ref[rows:, :], w_ref[...], NN).astype(jnp.bfloat16)
+    keep_ref[...] = mm(act_ref[:rows, :], w_ref[...], NN)
+
+
+def norm_two_back_kernel(hidden_ref, half_ref, far_ref, grad_ref, gains_ref, dhidden_ref, low_ref):
+    hidden = hidden_ref[...]
+    center = hidden - jnp.mean(hidden, axis=-1, keepdims=True)
+    spread = lax.rsqrt(jnp.mean(center * center, axis=-1, keepdims=True) + EPS)
+    xhat = center * spread
+    dnorm = half_ref[...].astype(jnp.float32) + far_ref[...].astype(jnp.float32)
+    scaled = dnorm * gains_ref[1:2, :]
+    inner = scaled - jnp.mean(scaled, axis=-1, keepdims=True)
+    inner = inner - xhat * jnp.mean(scaled * xhat, axis=-1, keepdims=True)
+    total = grad_ref[0].astype(jnp.float32) + inner * spread
+    dhidden_ref[...] = total
+    low_ref[...] = total.astype(jnp.bfloat16)
+
+
+def mix_back_kernel(core_ref, own_ref, other_ref, w_ref, send_ref):
+    cols = w_ref.shape[0]
+    heads = cols // HD
+    core = core_ref[0]
+    for micro, low_ref in ((core, own_ref), (1 - core, other_ref)):
+        total = mm(w_ref[...], low_ref[...], NT).astype(jnp.bfloat16)
+        for head in range(heads):
+            send_ref[micro * heads + head] = total[head * HD : (head + 1) * HD, :]
+
+
+def mix_grad_kernel(core_ref, mixed_ref, own_ref, other_ref, far_ref, near_ref):
+    core = core_ref[0]
+    width = far_ref.shape[2]
+    total = mm(mixed_ref[core], own_ref[...], NN) + mm(mixed_ref[1 - core], other_ref[...], NN)
+    for place in range(4):
+        near_ref[place] = total[:, place * width : (place + 1) * width]
+        far_ref[place] = total[:, (4 + place) * width : (5 + place) * width].astype(jnp.bfloat16)
+
+
+def project_back_kernel(core_ref, raw_ref, w_ref, send_ref, keep_ref):
+    core = core_ref[0]
+    weights = w_ref[: raw_ref.shape[1], :]
+    send_ref[...] = mm(raw_ref[1 - core], weights, TN).astype(jnp.bfloat16)
+    keep_ref[...] = mm(raw_ref[core], weights, TN)
+
+
+def project_grad_kernel(first, raw_ref, norm_ref, far_ref, near_ref):
+    count, width = far_ref.shape[1:]
+    rows = raw_ref.shape[2]
+    span = slice(first, first + count)
+    total = mm(raw_ref[0, span, :], norm_ref[:rows, :], NN) + mm(raw_ref[1, span, :], norm_ref[rows:, :], NN)
+    for place in range(4):
+        near_ref[place] = total[:, place * width : (place + 1) * width]
+        far_ref[place] = total[:, (4 + place) * width : (5 + place) * width].astype(jnp.bfloat16)
+
+
+def norm_one_back_kernel(
+    core_ref, order_ref, x_ref, half_ref, far_ref, dhidden_ref, gains_ref, grad_ref, xhat_ref
+):
+    core = core_ref[0]
+    width = x_ref.shape[2] // 8
+    x = x_ref[core].astype(jnp.float32)
+    mean = jnp.mean(x, axis=-1, keepdims=True)
+    center = x - mean
+    spread = lax.rsqrt(jnp.mean(center * center, axis=-1, keepdims=True) + EPS)
+    for place in range(8):
+        span = slice(place * width, (place + 1) * width)
+        piece = x_ref[core, :, block_at(order_ref, place, width)].astype(jnp.float32)
+        xhat_ref[:, span] = (piece - mean) * spread
+    xhat = xhat_ref[...]
+    dnorm = half_ref[...].astype(jnp.float32) + far_ref[...].astype(jnp.float32)
+    scaled = dnorm * gains_ref[0:1, :]
+    inner = scaled - jnp.mean(scaled, axis=-1, keepdims=True)
+    inner = inner - xhat * jnp.mean(scaled * xhat, axis=-1, keepdims=True)
+    total = (dhidden_ref[...] + inner * spread).astype(jnp.bfloat16)
+    for place in range(8):
+        grad_ref[:, block_at(order_ref, place, width)] = total[:, place * width : (place + 1) * width]
+
+
+def place_grad_kernel(core_ref, order_ref, local_ref, four_ref, grad_ref, natural_ref):
+    rows = grad_ref.shape[1]
+    width = grad_ref.shape[2] // 8
+    core = core_ref[0]
+    for at in range(2):
+        micro = core if at == 0 else 1 - core
+        place = lax.broadcasted_iota(jnp.int32, (rows, rows), 0)
+        onehot = jnp.where(local_ref[pl.ds(micro, 1), :] == place, 1.0, 0.0).astype(jnp.bfloat16)
+        natural_ref[...] = mm(onehot, four_ref[micro], NN).astype(jnp.bfloat16)
+        for block in range(8):
+            span = slice(block * width, (block + 1) * width)
+            grad_ref[at, :, span] = natural_ref[:, block_at(order_ref, block, width)]
+
+
+def result_kernel(order_ref, picks_ref, hidden_ref, half_ref, far_ref, packed_ref, natural_ref):
+    rows = hidden_ref.shape[0]
+    width = hidden_ref.shape[1] // 8
+    branch = half_ref[...].astype(jnp.float32) + far_ref[...].astype(jnp.float32)
+    total = (hidden_ref[...] + branch).astype(jnp.bfloat16)
+    for block in range(8):
+        natural_ref[:, block_at(order_ref, block, width)] = total[:, block * width : (block + 1) * width]
+    count = packed_ref.shape[0]
+    place = lax.broadcasted_iota(jnp.int32, (rows, count), 0)
+    onehot = jnp.where(picks_ref[...] == place, 1.0, 0.0).astype(jnp.bfloat16)
+    packed_ref[...] = mm(onehot, natural_ref[...], TN).astype(jnp.bfloat16)
+
+
+def positions(anchor, seq_lens):
+    ends = running_ends(seq_lens)
+    starts = ends - seq_lens
+    inside = (anchor[:, None] >= starts[None, :]) & (anchor[:, None] < ends[None, :])
+    return anchor - jnp.sum(jnp.where(inside, starts[None, :], 0), axis=1)
+
+
+def turn_tables(place):
+    freqs = jnp.power(THETA, -jnp.arange(HD // 2, dtype=jnp.float32) * 2.0 / HD)
+    angle = freqs[:, None] * place.astype(jnp.float32)[None, :]
+    return jnp.concatenate([jnp.cos(angle), jnp.sin(angle)], axis=0)
+
+
+def paired_layer(
+    tokens, cotangent, perm, lengths, w_qkv, w_attn_out, w_in, w_down, gain_one, gain_two
+):
+    f32, bf16, i32 = jnp.float32, jnp.bfloat16, jnp.int32
+    mine = lax.axis_index("fsdp")
+    part = lax.axis_index("tp")
+    core, side = part & 1, part >> 1
+    core_at = core.reshape(1).astype(i32)
+    rows = tokens.shape[1]
+    width = w_qkv.shape[0]
+    full = 8 * width
+    cols = w_qkv.shape[2]
+    heads = cols // HD
+    units = w_in.shape[2]
+    per_pair = rows // 8
+    order = jnp.bitwise_xor(jnp.array(ORDER, i32), mine)
+
+    def pick(value, index):
+        return lax.dynamic_index_in_dim(value, index, 0, keepdims=False)
+
+    def both(value, other):
+        return jnp.stack([jnp.where(core == 0, value, other), jnp.where(core == 0, other, value)])
+
+    def add_half(keep, got):
+        return (keep + got.astype(f32)).astype(bf16)
+
+    def near_sum(near, far, name):
+        shape = near.shape[1:]
+        own, *lows = local_call(near_sum_kernel, name, (), (near, far), [(shape, f32)] + [(shape, bf16)] * 3, far_in=(0, 1), far_out=(0,))
+        return own, lows
+
+    def y_join(same):
+        return same + [hop(jnp.concatenate(same, axis=0), 1)]
+
+    def z_send(lows):
+        return [hop(low, ORDER[at + 1]) for at, low in enumerate(lows)]
+
+    def far_sum(own, got):
+        return own + sum(one.astype(f32) for one in got)
+
+    turned = jnp.transpose(w_qkv.reshape(width, 3, heads, HD), (2, 1, 3, 0)).reshape(3 * cols, width)
+    gains_rows = jnp.concatenate([gain_one[None], gain_two[None], jnp.zeros((14, width), bf16)])
+    first_same = z_phase(jnp.concatenate([turned, gains_rows], axis=0))
+    first = first_same + y_phase(first_same)
+
+    slots = perm.reshape(2, 8, rows)
+    from_me = (slots // rows == mine).astype(f32)
+    slot_no = jnp.arange(rows, dtype=i32)
+    before = (slot_no[:, None] < slot_no[None, :]).astype(f32)
+    rank_me = jnp.einsum("mds,st->mdt", from_me, before).astype(i32)
+    ranks = jnp.arange(per_pair, dtype=i32)
+    chosen = (from_me[..., None] > 0) & (rank_me[..., None] == ranks)
+    local = jnp.sum(jnp.where(chosen, (slots % rows)[..., None], 0), axis=2)
+    my_slots = lax.dynamic_index_in_dim(slots, mine, 1, keepdims=False)
+    target = my_slots // rows
+    same = (target[:, :, None] == target[:, None, :]) & (slot_no[:, None] < slot_no[None, :])[None]
+    rank_own = jnp.sum(same.astype(i32), axis=1)
+    place_own = target * per_pair + rank_own
+    quarter = per_pair // 4
+    wanted = jnp.arange(8, dtype=i32)[:, None] * per_pair + part * quarter
+    wanted = (wanted + jnp.arange(quarter, dtype=i32)[None, :]).reshape(-1)
+    packer = (place_own[:, None, :] == wanted[None, :, None]).astype(bf16)
+    packed = jnp.einsum("mps,msd->mpd", packer, cotangent, preferred_element_type=f32).astype(bf16)
+    packed = jnp.transpose(packed.reshape(2, 8, quarter, full), (1, 0, 2, 3))
+    anchor = mine * rows + jnp.arange(rows, dtype=i32)
+    own_table = jnp.concatenate([turn_tables(positions(anchor, lengths[m])) for m in range(2)], axis=1)
+    inp_turned, gate_turned = jnp.transpose(w_in[:, 0]), jnp.transpose(w_in[:, 1])
+    second = jnp.concatenate([inp_turned, gate_turned, jnp.transpose(w_down), jnp.transpose(w_attn_out)], axis=0)
+    second_all = lax.all_gather(second, "fsdp", axis=0, tiled=False)
+    halfway = per_pair // 2
+    picks = lax.dynamic_slice_in_dim(pick(local, core), side * halfway, halfway, 1).reshape(1, -1)
+    unpack = (place_own[:, :, None] == slot_no[None, None, :]).astype(bf16)
+    my_lens = lengths[mine // heads]
+    all_anchor = jnp.arange(8 * rows, dtype=i32)
+    table = turn_tables(positions(all_anchor, my_lens))
+    table = jnp.transpose(table.reshape(HD, 8, rows), (1, 0, 2))
+    arrived = deal_out(packed)
+    first, arrived, own_table, picks, unpack, table, local, order, core_at, core, side, my_lens = sync(
+        (first, arrived, own_table, picks, unpack, table, local, order, core_at, core, side, my_lens)
+    )
+
+    norm_one, gains, outgoing, qkv_w = local_call(
+        project_kernel, "project", (order,), (tokens, own_table),
+        [((2 * rows, full), bf16), ((2, full), f32), ((2 * heads, 3 * HD, rows), bf16), ((3 * cols + 16, full), bf16)],
+        (), first, far_in=(0, 1), far_out=(0, 1, 2, 3),
+    )
+    near = twin(arrived)
+    outgoing, near = sync((outgoing, near))
+    qkv = deal_out(outgoing)
+    pair = jnp.stack([jnp.where(core == 0, arrived, near), jnp.where(core == 0, near, arrived)])
+    far = across(pair)
+    qkv, far = sync((qkv, far))
+
+    mixed_out, exact, logs = local_call(
+        attend_kernel, "attend", (my_lens,), (qkv,),
+        [((8, HD, rows), bf16), ((8, HD, rows), f32), ((8, 1, rows), f32)],
+        [((8 * rows, HD), bf16)], far_in=(0,), far_out=(0, 1, 2),
+    )
+    mixed_out, far = sync((mixed_out, far))
+    mixed = deal_out(mixed_out).reshape(2, cols, rows)
+    four = jnp.concatenate([jnp.where(side == 0, pair, far), jnp.where(side == 0, far, pair)])
+    four = jnp.transpose(four, (2, 1, 0, 3, 4)).reshape(2, rows, full)
+    grad = local_call(
+        place_grad_kernel, "place_grad", (core_at, order), (local.reshape(2, rows), four),
+        [((2, rows, full), bf16)], [((rows, full), bf16)],
+    )
+    mixed, grad = sync((mixed, grad))
+
+    send, keep, out_w = local_call(
+        mix_out_kernel, "mix_out", (core_at, order), (mixed,),
+        [((rows, full), bf16), ((rows, full), f32), ((cols, full), bf16)], (), (second_all,), far_in=(0,),
+    )
+    half = add_half(keep, twin(send))
+    far = across(half)
+    hidden, two_own = local_call(
+        norm_two_kernel, "norm_two", (core_at, order), (tokens, half, far, gains),
+        [((rows, full), f32), ((rows, full), bf16)], far_in=(0, 3),
+    )
+    two_other = twin(two_own)
+
+    send, keep, act, d_inp, d_gate = local_call(
+        feed_kernel, "feed", (order,), (two_own, two_other, grad),
+        [((rows, full), bf16), ((rows, full), f32)] + [((2 * rows, units), bf16)] * 3,
+        [((3 * units, full), bf16)], (second_all,),
+    )
+    half_two = add_half(keep, twin(send))
+    half_two, act, d_inp, d_gate = sync((half_two, act, d_inp, d_gate))
+    far_two = across(half_two)
+    feed_grad = local_call(
+        weight_grad_kernel, "feed_grad", (order,), (d_inp, d_gate, act, two_own, two_other, grad),
+        [((8, 3 * units, width), bf16)], far_out=(0,),
+    )
+    feed_sum = lax.psum_scatter(feed_grad, "fsdp", scatter_dimension=0, tiled=False)
+    far_two, feed_grad = sync((far_two, feed_grad))
+    d_hidden, low_own = local_call(
+        norm_two_back_kernel, "norm_two_back", (), (hidden, half_two, far_two, grad, gains),
+        [((rows, full), f32), ((rows, full), bf16)], far_in=(4,), far_out=(0,),
+    )
+    low_other = twin(low_own)
+    d_mixed = local_call(
+        mix_back_kernel, "mix_back", (core_at,), (low_own, low_other, out_w),
+        [((8, HD, rows), bf16)], far_out=(0,),
+    )
+    d_mixed, low_other, act = sync((d_mixed, low_other, act))
+    grad_mixed = deal_out(d_mixed)
+    send, keep = local_call(
+        down_kernel, "down", (order,), (act,),
+        [((rows, full), bf16), ((rows, full), f32)], [((units, full), bf16)], (second_all,),
+    )
+    res_half = add_half(keep, twin(send))
+    grad_mixed, res_half = sync((grad_mixed, res_half))
+
+    res_far = across(res_half)
+    d_raw_out = local_call(
+        attend_back_kernel, "attend_back", (my_lens,), (qkv, exact, logs, grad_mixed, table),
+        [((8, 3 * HD, rows), bf16)],
+        [((8 * rows, 2 * HD), bf16), ((HD, 8 * rows), f32), ((HD, 8 * rows), f32)],
+        far_in=(0, 1, 2, 3, 4), far_out=(0,),
+    )
+    d_raw_out, res_far = sync((d_raw_out, res_far))
+    d_raw = deal_out(d_raw_out).reshape(2, 3 * cols, rows)
+    out_far, out_near = local_call(
+        mix_grad_kernel, "mix_grad", (core_at,), (mixed, low_own, low_other),
+        [((4, cols, width), bf16), ((4, cols, width), f32)], far_in=(0, 1, 2), far_out=(1,),
+    )
+    out_got = hop(out_far, 1)
+    packed = local_call(
+        result_kernel, "result", (order,), (picks, hidden, res_half, res_far),
+        [((8 * halfway, full), bf16)], [((rows, full), bf16)], far_in=(1, 2, 3), far_out=(0,),
+    )
+    d_raw, out_got, packed = sync((d_raw, out_got, packed))
+
+    qkv_far, qkv_near = local_call(
+        partial(project_grad_kernel, 0), "project_grad", (), (d_raw, norm_one),
+        [((4, 3 * cols, width), bf16), ((4, 3 * cols, width), f32)], far_in=(0, 1), far_out=(1,),
+    )
+    qkv_far, d_raw = sync((qkv_far, d_raw))
+    qkv_got = hop(qkv_far, 1)
+    send, keep = local_call(
+        project_back_kernel, "project_back", (core_at,), (d_raw, qkv_w),
+        [((rows, full), bf16), ((rows, full), f32)], far_in=(0, 1),
+    )
+    half = add_half(keep, twin(send))
+    half, packed, out_got = sync((half, packed, out_got))
+    far = across(half)
+    arrived = deal_out(packed.reshape(8, halfway, full))
+    out_own, out_lows = near_sum(out_near, out_got, "out_near")
+    out_got = z_send(out_lows)
+    qkv_got, far, arrived, out_got = sync((qkv_got, far, arrived, out_got))
+    qkv_own, qkv_lows = near_sum(qkv_near, qkv_got, "qkv_near")
+    qkv_got = z_send(qkv_lows)
+    input_own = local_call(
+        norm_one_back_kernel, "norm_one_back", (core_at, order), (tokens, half, far, d_hidden, gains),
+        [((rows, full), bf16)], [((rows, full), f32)], far_in=(0, 3, 4),
+    )
+    input_grad = both(input_own, twin(input_own))
+    other_side = across(arrived)
+    whole = jnp.concatenate(
+        [jnp.where(side == 0, arrived, other_side), jnp.where(side == 0, other_side, arrived)], axis=1
+    ).reshape(rows, full)
+    whole = both(whole, twin(whole))
+    output = jnp.einsum("msp,mpd->msd", unpack, whole, preferred_element_type=f32).astype(bf16)
+    out_sum = far_sum(out_own, out_got)
+    qkv_got, output, input_grad, out_sum = sync((qkv_got, output, input_grad, out_sum))
+    qkv_sum = far_sum(qkv_own, qkv_got)
+    inp_sum, gate_sum, down_sum = [feed_sum[at * units : (at + 1) * units].astype(f32) for at in range(3)]
+
+    one_row = jnp.sum(qkv_sum * turned.astype(f32), axis=0) / gain_one.astype(f32)
+    two_row = jnp.sum(inp_sum * inp_turned.astype(f32) + gate_sum * gate_turned.astype(f32), axis=0)
+    gain_rows = jnp.stack([one_row, two_row / gain_two.astype(f32)])
+    gain_rows = gain_rows + twin(gain_rows)
+    gain_rows = gain_rows + across(gain_rows)
+    return (
+        output,
+        input_grad,
+        jnp.transpose(qkv_sum.reshape(heads, 3, HD, width), (3, 1, 0, 2)).reshape(width, 3, cols),
+        jnp.transpose(out_sum),
+        jnp.stack([jnp.transpose(inp_sum), jnp.transpose(gate_sum)], axis=1),
+        jnp.transpose(down_sum),
+        gain_rows[0],
+        gain_rows[1],
+    )
+
+
+def on_device(*operands):
+    micro_count, tok_rows = operands[0].shape[0], operands[0].shape[1]
+    groups, parts = lax.axis_size("fsdp"), lax.axis_size("tp")
+    heads = operands[4].shape[2] // HD
+    if groups == 8 and parts == 4 and micro_count == 2 and micro_count * heads == groups and tok_rows % 256 == 0:
+        return paired_layer(*operands)
+    return general_layer(*operands)
+
+
 def solution(mesh):
     placed = (
         P(None, "fsdp", None),

time: 1080 us -> 347 us (0.32)
  waiting for transfers between devices: 555 us -> 168 us
  blocking collectives: 222 us -> 0 us
  matrix products: 130 us -> 1.9 us
  other arithmetic: 71.9 us -> 16.5 us
  Pallas kernels: 0 us -> 50 us
  starting transfers between devices: 24 us -> 62 us
  local copies, waits for them, and re-layouts: 48.3 us -> 31.7 us
    reduce_scatter x4 -> x1, waiting for transfers between devices: 263 us -> 0.01 us  [paired_layer(): lax.psum_scatter(feed_grad, 'fsdp', scatter_dimension=0, tiled=False)]
    all_gather x11 -> x1, waiting for transfers between devices: 212 us -> 0.01 us  [paired_layer(): second_all = lax.all_gather(second, 'fsdp', axis=0, tiled=False)]
    all_gather x7 -> x0, blocking collectives: 200 us -> none  [the longest x2 64 us: on_device(): lax.all_gather(jnp.transpose(log_total), 'fsdp', axis=0, tiled=True)]
    dot_general x36 -> x3, matrix products: 130 us -> 1.9 us  [the longest x1 1.41 us: paired_layer(): jnp.einsum('msp,mpd->msd', unpack, whole, preferred_element_type=f32)]
    ppermute x0 -> x32, waiting for transfers between devices: none -> 91.5 us  [the longest x7 42.2 us: across(): return lax.ppermute(value, 'tp', [(i, i ^ 2) for i in range(4)])]
    psum x3 -> x0, waiting for transfers between devices: 61 us -> none  [the longest x1 33.2 us: on_device(): branch = lax.psum(attn_part.astype(jnp.bfloat16), 'tp').astype(jnp.float32)]
    all_to_all x4 -> x6, waiting for transfers between devices: 17.8 us -> 76.6 us  [deal_out(): return lax.all_to_all(value, 'fsdp', 0, 0, tiled=True)]
    pallas_call x0 -> x18, Pallas kernels: none -> 50 us  [local_call(): pl.pallas_call(body, in_specs=[pl.BlockSpec(memory_space=pltpu.SMEM)] * l...]
  transfers between devices with their start and end apart: 22 -> 40, of which waited for: 13 -> 27; matrix products, arithmetic and copies ran while one was open for 18% -> 5% of each run, Pallas kernels for 0% -> 11%
where the time goes in v2:
time: 347 us; the launch traced here: 345 us
  waiting for transfers between devices  168 us (48%)
  starting transfers between devices  62 us (18%)
  Pallas kernels  50 us (14%)
  local copies, waits for them, and re-layouts  31.7 us (9%)
  other arithmetic  16.5 us (5%)
  between operations  15 us (4%)
    all_to_all x6, waiting for transfers between devices, deal_out(): return lax.all_to_all(value, 'fsdp', 0, 0, tiled=True)  76.6 us
    pallas_call x18, Pallas kernels, local_call(): pl.pallas_call(body, in_specs=[pl.BlockSpec(memory_space=pltpu.SMEM)] * l...  50 us
    ppermute x7, waiting for transfers between devices, across(): return lax.ppermute(value, 'tp', [(i, i ^ 2) for i in range(4)])  42.2 us
    ppermute x15, waiting for transfers between devices, hop(): return lax.ppermute(value, 'fsdp', [(i, i ^ step) for i in range(8)])  40.8 us
    unnamed x115, local copies, waits for them, and re-layouts  28.7 us
    all_to_all x6, starting transfers between devices, deal_out(): return lax.all_to_all(value, 'fsdp', 0, 0, tiled=True)  28.6 us
    ppermute x15, starting transfers between devices, hop(): return lax.ppermute(value, 'fsdp', [(i, i ^ step) for i in range(8)])  24.8 us
    ppermute x10, waiting for transfers between devices, twin(): return lax.ppermute(value, 'tp', [(i, i ^ 1) for i in range(4)])  8.53 us
  transfers between devices with their start and end apart: 40, of which 27 were waited for; matrix products, arithmetic and copies ran while one was open for 5% of the time, Pallas kernels for 11%

profile of v2, /device:TPU:0, one launch (start us, length us, event | category | flops | bytes accessed | tf_op | source)
XLA Modules:
  0.0 345.2 jit_solution(10581413756312364056)
XLA Ops:
  20.6 4.9 %all-to-all-start = ((bf16[8,2,8,1024]{3,2,1,0:T(8,128)(2,1)}), bf16[8,2,8,1024]{3,2,1,0:T(8,128)(2,1)S(1)}, u32[]{:S(2)}, u32[]{:S(2)}) async-start(bf16[8,2,8,1024]{3,2,1,0:T(8,128)(2,1)} %bitcast.144), calls=%async_computation | async-start | bytes 524288 | tf_op jit(solution)/shard_map/all_to_all | solution.py:356
  31.9 4.4 %collective-permute-done.1.refs_5_ = bf16[784,128]{1,0:T(8,128)(2,1)S(1)} collective-permute-done((bf16[784,128]{1,0:T(8,128)(2,1)S(1)}, bf16[784,128]{1,0:T(8,128)(2,1)S(1)}, u32[]{:S(2)}, u32[]{:S(2)}) %collective-permute-start.1) | collective-permute-done | bytes 200736 | tf_op jit(solution)/shard_map/ppermute | solution.py:344
  39.4 4.4 %collective-permute-done.5.refs_9_ = bf16[784,128]{1,0:T(8,128)(2,1)S(1)} collective-permute-done((bf16[784,128]{1,0:T(8,128)(2,1)S(1)}, bf16[784,128]{1,0:T(8,128)(2,1)S(1)}, u32[]{:S(2)}, u32[]{:S(2)}) %collective-permute-start.5) | collective-permute-done | bytes 200736 | tf_op jit(solution)/shard_map/ppermute | solution.py:344
  46.1 12.3 %all-to-all-done = bf16[8,2,8,1024]{3,2,1,0:T(8,128)(2,1)S(1)} async-done(((bf16[8,2,8,1024]{3,2,1,0:T(8,128)(2,1)}), bf16[8,2,8,1024]{3,2,1,0:T(8,128)(2,1)S(1)}, u32[]{:S(2)}, u32[]{:S(2)}) %all-to-all-start) | async-done | bytes 262176 | tf_op jit(solution)/shard_map/all_to_all | solution.py:356
  58.3 4.1 %project.1 = (bf16[512,1024]{1,0:T(8,128)(2,1)S(1)}, f32[2,1024]{1,0:T(2,128)S(1)}, bf16[8,192,256]{2,1,0:T(8,128)(2,1)}, bf16[784,1024]{1,0:T(8,128)(2,1)S(1)}) custom-call(s32[8]{0:T(128)S(1)} %broadcast_xor_fusion.refs_0_.refs_1_, bf16[2,256,1024]{2,1,0:T(8,128)(2,1)S(1)} %copy-done.6, f32[64,512]{1,0:T(8,128)S(1)} %maximum_maximum_fusion.1.refs_2_, ...), custom_call_target="tpu_custom_call" | custom-call | tf_op jit(solution)/shard_map/project/pallas_call | solution.py:410
  64.7 5.7 %all-to-all-start.1 = ((bf16[8,192,256]{2,1,0:T(8,128)(2,1)}), bf16[8,192,256]{2,1,0:T(8,128)(2,1)S(1)}, u32[]{:S(2)}, u32[]{:S(2)}) async-start(bf16[8,192,256]{2,1,0:T(8,128)(2,1)} %get-tuple-element.115), calls=%async_computation.1 | async-start | bytes 1572864 | tf_op jit(solution)/shard_map/all_to_all | solution.py:356
  72.0 12.6 %collective-permute-done.8 = bf16[2,8,2,8,1024]{4,3,2,1,0:T(8,128)(2,1)S(1)} collective-permute-done((bf16[2,8,2,8,1024]{4,3,2,1,0:T(8,128)(2,1)S(1)}, bf16[2,8,2,8,1024]{4,3,2,1,0:T(8,128)(2,1)S(1)}, u32[]{:S(2)}, u32[]{:S(2)}) %collective-permute-start.8) | collective-permute-done | bytes 524320 | tf_op jit(solution)/shard_map/ppermute | solution.py:352
  84.6 29.2 %all-to-all-done.1.refs_1_ = bf16[8,192,256]{2,1,0:T(8,128)(2,1)S(1)} async-done(((bf16[8,192,256]{2,1,0:T(8,128)(2,1)}), bf16[8,192,256]{2,1,0:T(8,128)(2,1)S(1)}, u32[]{:S(2)}, u32[]{:S(2)}) %all-to-all-start.1) | async-done | bytes 786464 | tf_op jit(solution)/shard_map/all_to_all | solution.py:356
  113.7 7.0 %attend.1 = (bf16[8,64,256]{2,1,0:T(8,128)(2,1)}, f32[8,64,256]{2,1,0:T(8,128)S(1)}, f32[8,1,256]{2,1,0:T(1,128)S(1)}) custom-call(s32[8]{0:T(128)S(1)} %get-tuple-element.102.refs_0_, bf16[8,192,256]{2,1,0:T(8,128)(2,1)S(1)} %all-to-all-done.1.refs_1_), custom_call_target="tpu_custom_call" | custom-call | tf_op jit(solution)/shard_map/attend/pallas_call | solution.py:410
  121.6 5.4 %all-to-all-start.2 = ((bf16[8,64,256]{2,1,0:T(8,128)(2,1)}), bf16[8,64,256]{2,1,0:T(8,128)(2,1)S(1)}, u32[]{:S(2)}, u32[]{:S(2)}) async-start(bf16[8,64,256]{2,1,0:T(8,128)(2,1)} %get-tuple-element.124), calls=%async_computation.2 | async-start | bytes 524288 | tf_op jit(solution)/shard_map/all_to_all | solution.py:356
  128.6 7.7 %all-to-all-done.2 = bf16[8,64,256]{2,1,0:T(8,128)(2,1)S(1)} async-done(((bf16[8,64,256]{2,1,0:T(8,128)(2,1)}), bf16[8,64,256]{2,1,0:T(8,128)(2,1)S(1)}, u32[]{:S(2)}, u32[]{:S(2)}) %all-to-all-start.2) | async-done | bytes 262176 | tf_op jit(solution)/shard_map/all_to_all | solution.py:356
  143.7 12.5 %collective-permute-done.10.refs_4_ = bf16[256,1024]{1,0:T(8,128)(2,1)S(1)} collective-permute-done((bf16[256,1024]{1,0:T(8,128)(2,1)S(1)}, bf16[256,1024]{1,0:T(8,128)(2,1)S(1)}, u32[]{:S(2)}, u32[]{:S(2)}) %collective-permute-start.10) | collective-permute-done | bytes 524320 | tf_op jit(solution)/shard_map/ppermute | solution.py:352
  160.2 6.8 %feed.1 = (bf16[256,1024]{1,0:T(8,128)(2,1)S(1)}, f32[256,1024]{1,0:T(8,128)S(1)}, bf16[512,656]{1,0:T(8,128)(2,1)S(1)}, bf16[512,656]{1,0:T(8,128)(2,1)S(1)}, bf16[512,656]{1,0:T(8,128)(2,1)S(1)}) custom-call(s32[8]{0:T(128)S(1)} %broadcast_xor_fusion.refs_0_.refs_1_, bf16[256,1024]{1,0:T(8,128)(2,1)S(1)} %get-tuple-element.133.refs_1_.refs_4_, ...), custom_call_target="tpu_custom_call" | custom-call | tf_op jit(solution)/shard_map/feed/pallas_call | solution.py:410
  170.0 3.6 %feed_grad.1 = bf16[8,1968,128]{2,1,0:T(8,128)(2,1)S(1)} custom-call(s32[8]{0:T(128)S(1)} %broadcast_xor_fusion.refs_0_.refs_1_, bf16[512,656]{1,0:T(8,128)(2,1)S(1)} %get-tuple-element.141.refs_1_, bf16[512,656]{1,0:T(8,128)(2,1)S(1)} %get-tuple-element.142.refs_2_, bf16[512,656]{1,0:T(8,128)(2,1)S(1)} %get-tuple-element.148.refs_3_.refs_1_, ...), custom_call_target="tpu_custom_call" | custom-call | tf_op jit(solution)/shard_map/feed_grad/pallas_call | solution.py:410
  177.2 12.7 %collective-permute-done.13.refs_2_ = bf16[256,1024]{1,0:T(8,128)(2,1)S(1)} collective-permute-done((bf16[256,1024]{1,0:T(8,128)(2,1)}, bf16[256,1024]{1,0:T(8,128)(2,1)S(1)}, u32[]{:S(2)}, u32[]{:S(2)}) %collective-permute-start.13) | collective-permute-done | bytes 524320 | tf_op jit(solution)/shard_map/ppermute | solution.py:352
  204.7 3.6 %all-to-all-start.3 = ((bf16[8,64,256]{2,1,0:T(8,128)(2,1)}), bf16[8,64,256]{2,1,0:T(8,128)(2,1)S(1)}, u32[]{:S(2)}, u32[]{:S(2)}) async-start(bf16[8,64,256]{2,1,0:T(8,128)(2,1)} %mix_back.1), calls=%async_computation.3 | async-start | bytes 524288 | tf_op jit(solution)/shard_map/all_to_all | solution.py:356
  210.8 12.1 %all-to-all-done.3.refs_4_ = bf16[8,64,256]{2,1,0:T(8,128)(2,1)S(1)} async-done(((bf16[8,64,256]{2,1,0:T(8,128)(2,1)}), bf16[8,64,256]{2,1,0:T(8,128)(2,1)S(1)}, u32[]{:S(2)}, u32[]{:S(2)}) %all-to-all-start.3) | async-done | bytes 262176 | tf_op jit(solution)/shard_map/all_to_all | solution.py:356
  224.4 10.0 %attend_back.1 = bf16[8,192,256]{2,1,0:T(8,128)(2,1)} custom-call(s32[8]{0:T(128)S(1)} %get-tuple-element.102.refs_0_, bf16[8,192,256]{2,1,0:T(8,128)(2,1)S(1)} %all-to-all-done.1.refs_1_, f32[8,64,256]{2,1,0:T(8,128)S(1)} %copy-done.28, f32[8,1,256]{2,1,0:T(1,128)S(1)} %get-tuple-element.120.refs_3_, bf16[8,64,256]{2,1,0:T(8,128)(2,1)S(1)} %all-to-all-done.3.refs_4_, ...), custom_call_target="tpu_custom_call" | custom-call | tf_op jit(solution)/shard_map/attend_back/pallas_call | solution.py:410
  237.8 4.9 %all-to-all-start.4 = ((bf16[8,192,256]{2,1,0:T(8,128)(2,1)}), bf16[8,192,256]{2,1,0:T(8,128)(2,1)S(1)}, u32[]{:S(2)}, u32[]{:S(2)}) async-start(bf16[8,192,256]{2,1,0:T(8,128)(2,1)} %attend_back.1), calls=%async_computation.4 | async-start | bytes 1572864 | tf_op jit(solution)/shard_map/all_to_all | solution.py:356
  250.4 13.0 %collective-permute-done.17.refs_1_ = bf16[4,256,128]{2,1,0:T(8,128)(2,1)S(1)} collective-permute-done((bf16[4,256,128]{2,1,0:T(8,128)(2,1)S(1)}, bf16[4,256,128]{2,1,0:T(8,128)(2,1)S(1)}, u32[]{:S(2)}, u32[]{:S(2)}) %collective-permute-start.17) | collective-permute-done | bytes 262176 | tf_op jit(solution)/shard_map/ppermute | solution.py:344
  264.1 14.8 %all-to-all-done.4 = bf16[8,192,256]{2,1,0:T(8,128)(2,1)S(1)} async-done(((bf16[8,192,256]{2,1,0:T(8,128)(2,1)}), bf16[8,192,256]{2,1,0:T(8,128)(2,1)S(1)}, u32[]{:S(2)}, u32[]{:S(2)}) %all-to-all-start.4) | async-done | bytes 786464 | tf_op jit(solution)/shard_map/all_to_all | solution.py:356
  287.1 4.2 %all-to-all-start.5 = ((bf16[8,16,1024]{2,1,0:T(8,128)(2,1)}), bf16[8,16,1024]{2,1,0:T(8,128)(2,1)}, u32[]{:S(2)}, u32[]{:S(2)}) async-start(bf16[8,16,1024]{2,1,0:T(8,128)(2,1)} %bitcast.32), calls=%async_computation.5 | async-start | bytes 524288 | tf_op jit(solution)/shard_map/all_to_all | solution.py:356
  299.9 5.3 %collective-permute-done.22 = bf16[256,128]{1,0:T(8,128)(2,1)S(1)} collective-permute-done((bf16[256,128]{1,0:T(8,128)(2,1)S(1)}, bf16[256,128]{1,0:T(8,128)(2,1)S(1)}, u32[]{:S(2)}, u32[]{:S(2)}) %collective-permute-start.22) | collective-permute-done | bytes 65568 | tf_op jit(solution)/shard_map/ppermute | solution.py:344
  321.4 7.6 %collective-permute-done.25 = bf16[768,128]{1,0:T(8,128)(2,1)S(1)} collective-permute-done((bf16[768,128]{1,0:T(8,128)(2,1)S(1)}, bf16[768,128]{1,0:T(8,128)(2,1)S(1)}, u32[]{:S(2)}, u32[]{:S(2)}) %collective-permute-start.25) | collective-permute-done | bytes 196640 | tf_op jit(solution)/shard_map/ppermute | solution.py:344
  (260 shorter events, 121.3 us)
Async XLA Ops:
  7.2 129.1 %all-gather.3.cloned.1.call-start = ((), (), s32[]{:S(2)}) async-start(), calls=%async_computation.8 | async-start | bytes 5124096 | tf_op jit(solution)/shard_map/all_gather | solution.py:899
  11.6 18.2 %collective-permute-start = (bf16[784,128]{1,0:T(8,128)(2,1)S(1)}, bf16[784,128]{1,0:T(8,128)(2,1)S(1)}, u32[]{:S(2)}, u32[]{:S(2)}) collective-permute-start(bf16[784,128]{1,0:T(8,128)(2,1)S(1)} %maximum_maximum_fusion.refs_3_), channel_id=1, source_target_pairs={{0,8},{4,12},{8,0},{12,4},{16,24},{20,28},{24,16},{28,20},{1,9},{5... | collective-permute-start | bytes 602120 | tf_op jit(solution)/shard_map/ppermute | solution.py:344
  14.7 21.6 %collective-permute-start.1 = (bf16[784,128]{1,0:T(8,128)(2,1)S(1)}, bf16[784,128]{1,0:T(8,128)(2,1)S(1)}, u32[]{:S(2)}, u32[]{:S(2)}) collective-permute-start(bf16[784,128]{1,0:T(8,128)(2,1)S(1)} %maximum_maximum_fusion.refs_3_), channel_id=1, source_target_pairs={{0,16},{4,20},{8,24},{12,28},{16,0},{20,4},{24,8},{28,12},{1,17},{... | collective-permute-start | bytes 602120 | tf_op jit(solution)/shard_map/ppermute | solution.py:344
  17.3 22.0 %collective-permute-start.2 = (bf16[784,128]{1,0:T(8,128)(2,1)S(1)}, bf16[784,128]{1,0:T(8,128)(2,1)S(1)}, u32[]{:S(2)}, u32[]{:S(2)}) collective-permute-start(bf16[784,128]{1,0:T(8,128)(2,1)S(1)} %maximum_maximum_fusion.refs_3_), channel_id=1, source_target_pairs={{0,24},{4,28},{8,16},{12,20},{16,8},{20,12},{24,0},{28,4},{1,25},{... | collective-permute-start | bytes 602120 | tf_op jit(solution)/shard_map/ppermute | solution.py:344
  17.3 22.0 %collective-permute-start.3 = (bf16[784,128]{1,0:T(8,128)(2,1)S(1)}, bf16[784,128]{1,0:T(8,128)(2,1)S(1)}, u32[]{:S(2)}, u32[]{:S(2)}) collective-permute-start(bf16[784,128]{1,0:T(8,128)(2,1)S(1)} %maximum_maximum_fusion.refs_3_), channel_id=1, source_target_pairs={{0,4},{4,0},{8,12},{12,8},{16,20},{20,16},{24,28},{28,24},{1,5},{5... | collective-permute-start | bytes 602120 | tf_op jit(solution)/shard_map/ppermute | solution.py:344
  20.6 37.8 %all-to-all-start = ((bf16[8,2,8,1024]{3,2,1,0:T(8,128)(2,1)}), bf16[8,2,8,1024]{3,2,1,0:T(8,128)(2,1)S(1)}, u32[]{:S(2)}, u32[]{:S(2)}) async-start(bf16[8,2,8,1024]{3,2,1,0:T(8,128)(2,1)} %bitcast.144), calls=%async_computation | async-start | bytes 524288 | tf_op jit(solution)/shard_map/all_to_all | solution.py:356
  29.9 9.4 %collective-permute-start.4 = (bf16[784,128]{1,0:T(8,128)(2,1)S(1)}, bf16[784,128]{1,0:T(8,128)(2,1)S(1)}, u32[]{:S(2)}, u32[]{:S(2)}) collective-permute-start(bf16[784,128]{1,0:T(8,128)(2,1)S(1)} %collective-permute-done.refs_4_), channel_id=1, source_target_pairs={{0,4},{4,0},{8,12},{12,8},{16,20},{20,16},{24,28},{28,24},{1,5},{5... | collective-permute-start | bytes 602120 | tf_op jit(solution)/shard_map/ppermute | solution.py:344
  64.7 49.1 %all-to-all-start.1 = ((bf16[8,192,256]{2,1,0:T(8,128)(2,1)}), bf16[8,192,256]{2,1,0:T(8,128)(2,1)S(1)}, u32[]{:S(2)}, u32[]{:S(2)}) async-start(bf16[8,192,256]{2,1,0:T(8,128)(2,1)} %get-tuple-element.115), calls=%async_computation.1 | async-start | bytes 1572864 | tf_op jit(solution)/shard_map/all_to_all | solution.py:356
  70.4 14.1 %collective-permute-start.8 = (bf16[2,8,2,8,1024]{4,3,2,1,0:T(8,128)(2,1)S(1)}, bf16[2,8,2,8,1024]{4,3,2,1,0:T(8,128)(2,1)S(1)}, u32[]{:S(2)}, u32[]{:S(2)}) collective-permute-start(bf16[2,8,2,8,1024]{4,3,2,1,0:T(8,128)(2,1)S(1)} %pad_maximum_fusion.3), channel_id=1, source_target_pairs={{0,2},{1,3},{2,0},{3,1},{4,6},{5,7},{6,4},{7,5},{8,10},{9,11},{10,... | collective-permute-start | bytes 1572872 | tf_op jit(solution)/shard_map/ppermute | solution.py:352
  121.6 14.7 %all-to-all-start.2 = ((bf16[8,64,256]{2,1,0:T(8,128)(2,1)}), bf16[8,64,256]{2,1,0:T(8,128)(2,1)S(1)}, u32[]{:S(2)}, u32[]{:S(2)}) async-start(bf16[8,64,256]{2,1,0:T(8,128)(2,1)} %get-tuple-element.124), calls=%async_computation.2 | async-start | bytes 524288 | tf_op jit(solution)/shard_map/all_to_all | solution.py:356
  127.0 204.0 %reduce-scatter.2.cloned.1.call-start = ((), (), s32[]{:S(2)}) async-start(), calls=%async_computation.7 | async-start | bytes 4534272 | tf_op jit(solution)/shard_map/reduce_scatter | solution.py:963
  142.2 14.0 %collective-permute-start.10 = (bf16[256,1024]{1,0:T(8,128)(2,1)S(1)}, bf16[256,1024]{1,0:T(8,128)(2,1)S(1)}, u32[]{:S(2)}, u32[]{:S(2)}) collective-permute-start(bf16[256,1024]{1,0:T(8,128)(2,1)S(1)} %add_convert_fusion.3.refs_3_), channel_id=1, source_target_pairs={{0,2},{1,3},{2,0},{3,1},{4,6},{5,7},{6,4},{7,5},{8,10},{9,11},{10,... | collective-permute-start | bytes 1572872 | tf_op jit(solution)/shard_map/ppermute | solution.py:352
  175.6 14.2 %collective-permute-start.13 = (bf16[256,1024]{1,0:T(8,128)(2,1)}, bf16[256,1024]{1,0:T(8,128)(2,1)S(1)}, u32[]{:S(2)}, u32[]{:S(2)}) collective-permute-start(bf16[256,1024]{1,0:T(8,128)(2,1)} %add_convert_fusion.2.refs_1_), channel_id=1, source_target_pairs={{0,2},{1,3},{2,0},{3,1},{4,6},{5,7},{6,4},{7,5},{8,10},{9,11},{10,... | collective-permute-start | bytes 1572872 | tf_op jit(solution)/shard_map/ppermute | solution.py:352
  204.7 18.2 %all-to-all-start.3 = ((bf16[8,64,256]{2,1,0:T(8,128)(2,1)}), bf16[8,64,256]{2,1,0:T(8,128)(2,1)S(1)}, u32[]{:S(2)}, u32[]{:S(2)}) async-start(bf16[8,64,256]{2,1,0:T(8,128)(2,1)} %mix_back.1), calls=%async_computation.3 | async-start | bytes 524288 | tf_op jit(solution)/shard_map/all_to_all | solution.py:356
  222.9 14.1 %collective-permute-start.16 = (bf16[256,1024]{1,0:T(8,128)(2,1)}, bf16[256,1024]{1,0:T(8,128)(2,1)S(1)}, u32[]{:S(2)}, u32[]{:S(2)}) collective-permute-start(bf16[256,1024]{1,0:T(8,128)(2,1)} %add_convert_fusion.1.refs_3_), channel_id=1, source_target_pairs={{0,2},{1,3},{2,0},{3,1},{4,6},{5,7},{6,4},{7,5},{8,10},{9,11},{10,... | collective-permute-start | bytes 1572872 | tf_op jit(solution)/shard_map/ppermute | solution.py:352
  237.8 41.1 %all-to-all-start.4 = ((bf16[8,192,256]{2,1,0:T(8,128)(2,1)}), bf16[8,192,256]{2,1,0:T(8,128)(2,1)S(1)}, u32[]{:S(2)}, u32[]{:S(2)}) async-start(bf16[8,192,256]{2,1,0:T(8,128)(2,1)} %attend_back.1), calls=%async_computation.4 | async-start | bytes 1572864 | tf_op jit(solution)/shard_map/all_to_all | solution.py:356
  244.1 19.3 %collective-permute-start.17 = (bf16[4,256,128]{2,1,0:T(8,128)(2,1)S(1)}, bf16[4,256,128]{2,1,0:T(8,128)(2,1)S(1)}, u32[]{:S(2)}, u32[]{:S(2)}) collective-permute-start(bf16[4,256,128]{2,1,0:T(8,128)(2,1)S(1)} %get-tuple-element.156), channel_id=1, source_target_pairs={{0,4},{4,0},{8,12},{12,8},{16,20},{20,16},{24,28},{28,24},{1,5},{5... | collective-permute-start | bytes 786440 | tf_op jit(solution)/shard_map/ppermute | solution.py:344
  284.8 22.6 %collective-permute-start.18 = (bf16[4,768,128]{2,1,0:T(8,128)(2,1)}, bf16[4,768,128]{2,1,0:T(8,128)(2,1)S(1)}, u32[]{:S(2)}, u32[]{:S(2)}) collective-permute-start(bf16[4,768,128]{2,1,0:T(8,128)(2,1)} %get-tuple-element.163), channel_id=1, source_target_pairs={{0,4},{4,0},{8,12},{12,8},{16,20},{20,16},{24,28},{28,24},{1,5},{5... | collective-permute-start | bytes 2359304 | tf_op jit(solution)/shard_map/ppermute | solution.py:344
  286.9 21.0 %collective-permute-start.20 = (bf16[256,1024]{1,0:T(8,128)(2,1)S(1)}, bf16[256,1024]{1,0:T(8,128)(2,1)}, u32[]{:S(2)}, u32[]{:S(2)}) collective-permute-start(bf16[256,1024]{1,0:T(8,128)(2,1)S(1)} %add_convert_fusion.refs_3_), channel_id=1, source_target_pairs={{0,2},{1,3},{2,0},{3,1},{4,6},{5,7},{6,4},{7,5},{8,10},{9,11},{10,... | collective-permute-start | bytes 1572872 | tf_op jit(solution)/shard_map/ppermute | solution.py:352
  287.1 20.8 %all-to-all-start.5 = ((bf16[8,16,1024]{2,1,0:T(8,128)(2,1)}), bf16[8,16,1024]{2,1,0:T(8,128)(2,1)}, u32[]{:S(2)}, u32[]{:S(2)}) async-start(bf16[8,16,1024]{2,1,0:T(8,128)(2,1)} %bitcast.32), calls=%async_computation.5 | async-start | bytes 524288 | tf_op jit(solution)/shard_map/all_to_all | solution.py:356
  295.5 9.8 %collective-permute-start.22 = (bf16[256,128]{1,0:T(8,128)(2,1)S(1)}, bf16[256,128]{1,0:T(8,128)(2,1)S(1)}, u32[]{:S(2)}, u32[]{:S(2)}) collective-permute-start(bf16[256,128]{1,0:T(8,128)(2,1)S(1)} %get-tuple-element.175), channel_id=1, source_target_pairs={{0,16},{4,20},{8,24},{12,28},{16,0},{20,4},{24,8},{28,12},{1,17},{... | collective-permute-start | bytes 196616 | tf_op jit(solution)/shard_map/ppermute | solution.py:344
  311.2 10.2 %collective-permute-start.24 = (bf16[768,128]{1,0:T(8,128)(2,1)S(1)}, bf16[768,128]{1,0:T(8,128)(2,1)S(1)}, u32[]{:S(2)}, u32[]{:S(2)}) collective-permute-start(bf16[768,128]{1,0:T(8,128)(2,1)S(1)} %get-tuple-element.178), channel_id=1, source_target_pairs={{0,8},{4,12},{8,0},{12,4},{16,24},{20,28},{24,16},{28,20},{1,9},{5... | collective-permute-start | bytes 589832 | tf_op jit(solution)/shard_map/ppermute | solution.py:344
  312.0 17.1 %collective-permute-start.25 = (bf16[768,128]{1,0:T(8,128)(2,1)S(1)}, bf16[768,128]{1,0:T(8,128)(2,1)S(1)}, u32[]{:S(2)}, u32[]{:S(2)}) collective-permute-start(bf16[768,128]{1,0:T(8,128)(2,1)S(1)} %get-tuple-element.179), channel_id=1, source_target_pairs={{0,16},{4,20},{8,24},{12,28},{16,0},{20,4},{24,8},{28,12},{1,17},{... | collective-permute-start | bytes 589832 | tf_op jit(solution)/shard_map/ppermute | solution.py:344
  313.2 15.9 %collective-permute-start.26 = (bf16[768,128]{1,0:T(8,128)(2,1)S(1)}, bf16[768,128]{1,0:T(8,128)(2,1)S(1)}, u32[]{:S(2)}, u32[]{:S(2)}) collective-permute-start(bf16[768,128]{1,0:T(8,128)(2,1)S(1)} %get-tuple-element.180), channel_id=1, source_target_pairs={{0,24},{4,28},{8,16},{12,20},{16,8},{20,12},{24,0},{28,4},{1,25},{... | collective-permute-start | bytes 589832 | tf_op jit(solution)/shard_map/ppermute | solution.py:344
  (70 other events, 384.4 us)
Sparse Core Ops, SparseCore 0:
  11.3 110.4 all-gather.2
  175.8 104.3 reduce-scatter.1

commit v3 on v2

--- a/solution.py
+++ b/solution.py
@@ -324,6 +324,7 @@
 
 
 JOIN = 2
+COST = 5 * 10**9
 FAR = -1e30
 ORDER = (0, 2, 4, 6, 1, 3, 5, 7)
 NT = (((1,), (1,)), ((), ()))
@@ -372,7 +373,7 @@
     return [hop(one, 1) for one in shards]
 
 
-def local_call(kernel, name, scalars, arrays, outs, scratch=(), shards=(), copies=8, far_in=(), far_out=()):
+def local_call(kernel, name, scalars, arrays, outs, scratch=(), shards=(), copies=8, far_in=(), far_out=(), far_shards=True):
     shapes = [(one.shape, one.dtype) for one in arrays]
     staged = [shapes[at] for at in far_in] + [outs[at] for at in far_out]
     sems = [pltpu.SemaphoreType.DMA((copies,))] if shards else []
@@ -404,6 +405,9 @@
         for copy in outgoing:
             copy.wait()
 
+    arrays = [pltpu.with_memory_space_constraint(one, pltpu.HBM) if at in far_in else one for at, one in enumerate(arrays)]
+    shards = [pltpu.with_memory_space_constraint(one, pltpu.HBM) if far_shards else one for one in shards]
+
     def space(at, far):
         return pl.BlockSpec(memory_space=pltpu.HBM if at in far else pltpu.VMEM)
 
@@ -411,14 +415,18 @@
         body,
         in_specs=[pl.BlockSpec(memory_space=pltpu.SMEM)] * len(scalars)
         + [space(at, far_in) for at in range(len(arrays))]
-        + [pl.BlockSpec(memory_space=pl.ANY)] * len(shards),
+        + [pl.BlockSpec(memory_space=pltpu.HBM if far_shards else pl.ANY)] * len(shards),
         out_specs=[space(at, far_out) for at in range(len(outs))],
-        out_shape=[jax.ShapeDtypeStruct(shape, kind) for shape, kind in outs],
+        out_shape=[
+            pltpu.HBM(shape, kind) if at in far_out else jax.ShapeDtypeStruct(shape, kind)
+            for at, (shape, kind) in enumerate(outs)
+        ],
         scratch_shapes=[pltpu.VMEM(shape, kind) for shape, kind in scratch]
         + sems
         + [pltpu.VMEM(shape, kind) for shape, kind in staged]
         + ([pltpu.SemaphoreType.DMA((len(staged),))] if staged else []),
         compiler_params=pltpu.CompilerParams(vmem_limit_bytes=room),
+        cost_estimate=pl.CostEstimate(flops=COST, transcendentals=0, bytes_accessed=8 * 1024 * 1024),
         name=name,
     )(*scalars, *arrays, *shards)
     return result if len(outs) > 1 else result[0]
@@ -439,7 +447,7 @@
     return copies
 
 
-def gathered_copies(order_ref, source, low, high, into_ref, sem_ref):
+def gathered_copies(order_ref, source, low, high, into_ref, sem_ref, base=0):
     width = source.shape[2]
     copies = []
     for place in range(8):
@@ -447,7 +455,7 @@
             pltpu.make_async_copy(
                 source.at[order_ref[place], pl.ds(low, high - low), :],
                 into_ref.at[:, pl.ds(place * width, width)],
-                sem_ref.at[place],
+                sem_ref.at[base + place],
             )
         )
         copies[-1].start()
@@ -660,12 +668,14 @@
 
 
 def feed_kernel(
-    order_ref, own_ref, other_ref, grad_ref, all_ref, send_ref, keep_ref, act_ref, dinp_ref, dgate_ref, w_ref, sem_ref
+    order_ref, own_ref, other_ref, grad_ref, all_ref, down_ref, send_ref, keep_ref, act_ref, dinp_ref, dgate_ref, w_ref, sem_ref
 ):
     units = w_ref.shape[0] // 3
     inp_w, gate_w, down_w = [w_ref.at[pl.ds(at * units, units), :] for at in range(3)]
     rows = own_ref.shape[0]
-    finish(gathered_copies(order_ref, all_ref, 0, 3 * units, w_ref, sem_ref))
+    first_copies = gathered_copies(order_ref, all_ref, 0, 2 * units, w_ref.at[pl.ds(0, 2 * units), :], sem_ref)
+    finish(gathered_copies(order_ref, down_ref, 0, units, down_w, sem_ref, 8))
+    finish(first_copies)
     for micro, norm_ref in ((1, other_ref), (0, own_ref)):
         span = slice(micro * rows, (micro + 1) * rows)
         inp = mm(norm_ref[...], inp_w[...], NT)
@@ -710,7 +720,7 @@
 def down_kernel(order_ref, act_ref, all_ref, send_ref, keep_ref, w_ref, sem_ref):
     rows = send_ref.shape[0]
     units = w_ref.shape[0]
-    finish(gathered_copies(order_ref, all_ref, 2 * units, 3 * units, w_ref, sem_ref))
+    finish(gathered_copies(order_ref, all_ref, 0, units, w_ref, sem_ref))
     send_ref[...] = mm(act_ref[rows:, :], w_ref[...], NN).astype(jnp.bfloat16)
     keep_ref[...] = mm(act_ref[:rows, :], w_ref[...], NN)
 
@@ -766,7 +776,7 @@
 
 
 def norm_one_back_kernel(
-    core_ref, order_ref, x_ref, half_ref, far_ref, dhidden_ref, gains_ref, grad_ref, xhat_ref
+    core_ref, order_ref, x_ref, half_ref, far_ref, dhidden_ref, gains_ref, grad_ref, dgain_ref, xhat_ref
 ):
     core = core_ref[0]
     width = x_ref.shape[2] // 8
@@ -780,6 +790,7 @@
         xhat_ref[:, span] = (piece - mean) * spread
     xhat = xhat_ref[...]
     dnorm = half_ref[...].astype(jnp.float32) + far_ref[...].astype(jnp.float32)
+    dgain_ref[...] = jnp.sum(dnorm * xhat, axis=0, keepdims=True)
     scaled = dnorm * gains_ref[0:1, :]
     inner = scaled - jnp.mean(scaled, axis=-1, keepdims=True)
     inner = inner - xhat * jnp.mean(scaled * xhat, axis=-1, keepdims=True)
@@ -887,16 +898,20 @@
     rank_own = jnp.sum(same.astype(i32), axis=1)
     place_own = target * per_pair + rank_own
     quarter = per_pair // 4
-    wanted = jnp.arange(8, dtype=i32)[:, None] * per_pair + part * quarter
+    wanted = order[:, None] * per_pair + part * quarter
     wanted = (wanted + jnp.arange(quarter, dtype=i32)[None, :]).reshape(-1)
     packer = (place_own[:, None, :] == wanted[None, :, None]).astype(bf16)
     packed = jnp.einsum("mps,msd->mpd", packer, cotangent, preferred_element_type=f32).astype(bf16)
-    packed = jnp.transpose(packed.reshape(2, 8, quarter, full), (1, 0, 2, 3))
+    packed = packed.reshape(2, 8, quarter, full)
+    packed = [packed[:, at] for at in range(8)]
+    chosen = order[:, None] == jnp.arange(8, dtype=i32)[None, :]
+    local_own = jnp.sum(jnp.where(chosen[None, :, :, None], local[:, None], 0), axis=2)
     anchor = mine * rows + jnp.arange(rows, dtype=i32)
     own_table = jnp.concatenate([turn_tables(positions(anchor, lengths[m])) for m in range(2)], axis=1)
     inp_turned, gate_turned = jnp.transpose(w_in[:, 0]), jnp.transpose(w_in[:, 1])
-    second = jnp.concatenate([inp_turned, gate_turned, jnp.transpose(w_down), jnp.transpose(w_attn_out)], axis=0)
+    second = jnp.concatenate([jnp.transpose(w_down), jnp.transpose(w_attn_out)], axis=0)
     second_all = lax.all_gather(second, "fsdp", axis=0, tiled=False)
+    third_all = lax.all_gather(jnp.concatenate([inp_turned, gate_turned], axis=0), "fsdp", axis=0, tiled=False)
     halfway = per_pair // 2
     picks = lax.dynamic_slice_in_dim(pick(local, core), side * halfway, halfway, 1).reshape(1, -1)
     unpack = (place_own[:, :, None] == slot_no[None, None, :]).astype(bf16)
@@ -904,37 +919,37 @@
     all_anchor = jnp.arange(8 * rows, dtype=i32)
     table = turn_tables(positions(all_anchor, my_lens))
     table = jnp.transpose(table.reshape(HD, 8, rows), (1, 0, 2))
-    arrived = deal_out(packed)
-    first, arrived, own_table, picks, unpack, table, local, order, core_at, core, side, my_lens = sync(
-        (first, arrived, own_table, picks, unpack, table, local, order, core_at, core, side, my_lens)
+    first, packed, own_table, picks, unpack, table, local_own, order, core_at, core, side, my_lens = sync(
+        (first, packed, own_table, picks, unpack, table, local_own, order, core_at, core, side, my_lens)
     )
 
     norm_one, gains, outgoing, qkv_w = local_call(
         project_kernel, "project", (order,), (tokens, own_table),
         [((2 * rows, full), bf16), ((2, full), f32), ((2 * heads, 3 * HD, rows), bf16), ((3 * cols + 16, full), bf16)],
-        (), first, far_in=(0, 1), far_out=(0, 1, 2, 3),
-    )
-    near = twin(arrived)
-    outgoing, near = sync((outgoing, near))
+        (), first, far_in=(0, 1), far_out=(0, 1, 2, 3), far_shards=False,
+    )
+    outgoing, packed = sync((outgoing, packed))
     qkv = deal_out(outgoing)
-    pair = jnp.stack([jnp.where(core == 0, arrived, near), jnp.where(core == 0, near, arrived)])
-    far = across(pair)
-    qkv, far = sync((qkv, far))
-
+    arrived = [hop(one, ORDER[at]) if at else one for at, one in enumerate(packed)]
+    qkv = sync((qkv,))[0]
     mixed_out, exact, logs = local_call(
         attend_kernel, "attend", (my_lens,), (qkv,),
         [((8, HD, rows), bf16), ((8, HD, rows), f32), ((8, 1, rows), f32)],
         [((8 * rows, HD), bf16)], far_in=(0,), far_out=(0, 1, 2),
     )
-    mixed_out, far = sync((mixed_out, far))
+    mixed_out, arrived = sync((mixed_out, arrived))
     mixed = deal_out(mixed_out).reshape(2, cols, rows)
+    arrived = jnp.stack(arrived)
+    near = twin(arrived)
+    pair = jnp.stack([jnp.where(core == 0, arrived, near), jnp.where(core == 0, near, arrived)])
+    far = across(pair)
+    mixed, far = sync((mixed, far))
     four = jnp.concatenate([jnp.where(side == 0, pair, far), jnp.where(side == 0, far, pair)])
     four = jnp.transpose(four, (2, 1, 0, 3, 4)).reshape(2, rows, full)
     grad = local_call(
-        place_grad_kernel, "place_grad", (core_at, order), (local.reshape(2, rows), four),
+        place_grad_kernel, "place_grad", (core_at, order), (local_own.reshape(2, rows), four),
         [((2, rows, full), bf16)], [((rows, full), bf16)],
     )
-    mixed, grad = sync((mixed, grad))
 
     send, keep, out_w = local_call(
         mix_out_kernel, "mix_out", (core_at, order), (mixed,),
@@ -942,6 +957,7 @@
     )
     half = add_half(keep, twin(send))
     far = across(half)
+    far, grad = sync((far, grad))
     hidden, two_own = local_call(
         norm_two_kernel, "norm_two", (core_at, order), (tokens, half, far, gains),
         [((rows, full), f32), ((rows, full), bf16)], far_in=(0, 3),
@@ -951,7 +967,7 @@
     send, keep, act, d_inp, d_gate = local_call(
         feed_kernel, "feed", (order,), (two_own, two_other, grad),
         [((rows, full), bf16), ((rows, full), f32)] + [((2 * rows, units), bf16)] * 3,
-        [((3 * units, full), bf16)], (second_all,),
+        [((3 * units, full), bf16)], (third_all, second_all), copies=16,
     )
     half_two = add_half(keep, twin(send))
     half_two, act, d_inp, d_gate = sync((half_two, act, d_inp, d_gate))
@@ -961,7 +977,12 @@
         [((8, 3 * units, width), bf16)], far_out=(0,),
     )
     feed_sum = lax.psum_scatter(feed_grad, "fsdp", scatter_dimension=0, tiled=False)
-    far_two, feed_grad = sync((far_two, feed_grad))
+    send, keep = local_call(
+        down_kernel, "down", (order,), (act,),
+        [((rows, full), bf16), ((rows, full), f32)], [((units, full), bf16)], (second_all,),
+    )
+    res_half = add_half(keep, twin(send))
+    far_two, feed_grad, res_half = sync((far_two, feed_grad, res_half))
     d_hidden, low_own = local_call(
         norm_two_back_kernel, "norm_two_back", (), (hidden, half_two, far_two, grad, gains),
         [((rows, full), f32), ((rows, full), bf16)], far_in=(4,), far_out=(0,),
@@ -971,34 +992,30 @@
         mix_back_kernel, "mix_back", (core_at,), (low_own, low_other, out_w),
         [((8, HD, rows), bf16)], far_out=(0,),
     )
-    d_mixed, low_other, act = sync((d_mixed, low_other, act))
+    out_far, out_near = local_call(
+        mix_grad_kernel, "mix_grad", (core_at,), (mixed, low_own, low_other),
+        [((4, cols, width), bf16), ((4, cols, width), f32)], far_in=(0,), far_out=(1,),
+    )
+    d_mixed, out_far = sync((d_mixed, out_far))
     grad_mixed = deal_out(d_mixed)
-    send, keep = local_call(
-        down_kernel, "down", (order,), (act,),
-        [((rows, full), bf16), ((rows, full), f32)], [((units, full), bf16)], (second_all,),
-    )
-    res_half = add_half(keep, twin(send))
-    grad_mixed, res_half = sync((grad_mixed, res_half))
-
     res_far = across(res_half)
+    grad_mixed, res_far = sync((grad_mixed, res_far))
+
+    out_got = hop(out_far, 1)
     d_raw_out = local_call(
         attend_back_kernel, "attend_back", (my_lens,), (qkv, exact, logs, grad_mixed, table),
         [((8, 3 * HD, rows), bf16)],
         [((8 * rows, 2 * HD), bf16), ((HD, 8 * rows), f32), ((HD, 8 * rows), f32)],
         far_in=(0, 1, 2, 3, 4), far_out=(0,),
     )
-    d_raw_out, res_far = sync((d_raw_out, res_far))
+    d_raw_out, out_got = sync((d_raw_out, out_got))
     d_raw = deal_out(d_raw_out).reshape(2, 3 * cols, rows)
-    out_far, out_near = local_call(
-        mix_grad_kernel, "mix_grad", (core_at,), (mixed, low_own, low_other),
-        [((4, cols, width), bf16), ((4, cols, width), f32)], far_in=(0, 1, 2), far_out=(1,),
-    )
-    out_got = hop(out_far, 1)
+    out_own, out_lows = near_sum(out_near, out_got, "out_near")
     packed = local_call(
         result_kernel, "result", (order,), (picks, hidden, res_half, res_far),
         [((8 * halfway, full), bf16)], [((rows, full), bf16)], far_in=(1, 2, 3), far_out=(0,),
     )
-    d_raw, out_got, packed = sync((d_raw, out_got, packed))
+    d_raw, out_lows, packed = sync((d_raw, out_lows, packed))
 
     qkv_far, qkv_near = local_call(
         partial(project_grad_kernel, 0), "project_grad", (), (d_raw, norm_one),
@@ -1011,19 +1028,26 @@
         [((rows, full), bf16), ((rows, full), f32)], far_in=(0, 1),
     )
     half = add_half(keep, twin(send))
-    half, packed, out_got = sync((half, packed, out_got))
+    half, packed, out_lows = sync((half, packed, out_lows))
     far = across(half)
     arrived = deal_out(packed.reshape(8, halfway, full))
-    out_own, out_lows = near_sum(out_near, out_got, "out_near")
     out_got = z_send(out_lows)
-    qkv_got, far, arrived, out_got = sync((qkv_got, far, arrived, out_got))
+    qkv_got, far, arrived = sync((qkv_got, far, arrived))
     qkv_own, qkv_lows = near_sum(qkv_near, qkv_got, "qkv_near")
     qkv_got = z_send(qkv_lows)
-    input_own = local_call(
+    input_own, d_gain_one = local_call(
         norm_one_back_kernel, "norm_one_back", (core_at, order), (tokens, half, far, d_hidden, gains),
-        [((rows, full), bf16)], [((rows, full), f32)], far_in=(0, 3, 4),
+        [((rows, full), bf16), ((1, full), f32)], [((rows, full), f32)], far_in=(0, 3, 4),
     )
     input_grad = both(input_own, twin(input_own))
+    high = d_gain_one.astype(bf16).astype(f32)
+    gain_parts = jnp.concatenate([high, d_gain_one - high, jnp.zeros((14, full), f32)], axis=0)
+    gain_parts = jnp.transpose(gain_parts.reshape(16, 8, width), (1, 0, 2))
+    gain_near = gain_parts[:4] + hop(gain_parts[4:].astype(bf16), 1).astype(f32)
+    gain_got = z_send([gain_near[at].astype(bf16) for at in range(1, 4)])
+    gain_row = far_sum(gain_near[0], gain_got)
+    gain_row = gain_row[0] + gain_row[1]
+    grad_gain_one = gain_row + twin(gain_row)
     other_side = across(arrived)
     whole = jnp.concatenate(
         [jnp.where(side == 0, arrived, other_side), jnp.where(side == 0, other_side, arrived)], axis=1
@@ -1031,24 +1055,26 @@
     whole = both(whole, twin(whole))
     output = jnp.einsum("msp,mpd->msd", unpack, whole, preferred_element_type=f32).astype(bf16)
     out_sum = far_sum(out_own, out_got)
-    qkv_got, output, input_grad, out_sum = sync((qkv_got, output, input_grad, out_sum))
+    inp_sum, gate_sum, down_sum = [feed_sum[at * units : (at + 1) * units].astype(f32) for at in range(3)]
+    two_row = jnp.sum(inp_sum * inp_turned.astype(f32) + gate_sum * gate_turned.astype(f32), axis=0)
+    two_row = two_row + twin(two_row)
+    grad_gain_two = (two_row + across(two_row)) / gain_two.astype(f32)
+    grad_attn_out = jnp.transpose(out_sum)
+    grad_in = jnp.stack([jnp.transpose(inp_sum), jnp.transpose(gate_sum)], axis=1)
+    grad_down = jnp.transpose(down_sum)
+    qkv_got, output, input_grad, grad_attn_out, grad_in, grad_down, grad_gain_one, grad_gain_two = sync(
+        (qkv_got, output, input_grad, grad_attn_out, grad_in, grad_down, grad_gain_one, grad_gain_two)
+    )
     qkv_sum = far_sum(qkv_own, qkv_got)
-    inp_sum, gate_sum, down_sum = [feed_sum[at * units : (at + 1) * units].astype(f32) for at in range(3)]
-
-    one_row = jnp.sum(qkv_sum * turned.astype(f32), axis=0) / gain_one.astype(f32)
-    two_row = jnp.sum(inp_sum * inp_turned.astype(f32) + gate_sum * gate_turned.astype(f32), axis=0)
-    gain_rows = jnp.stack([one_row, two_row / gain_two.astype(f32)])
-    gain_rows = gain_rows + twin(gain_rows)
-    gain_rows = gain_rows + across(gain_rows)
     return (
         output,
         input_grad,
         jnp.transpose(qkv_sum.reshape(heads, 3, HD, width), (3, 1, 0, 2)).reshape(width, 3, cols),
-        jnp.transpose(out_sum),
-        jnp.stack([jnp.transpose(inp_sum), jnp.transpose(gate_sum)], axis=1),
-        jnp.transpose(down_sum),
-        gain_rows[0],
-        gain_rows[1],
+        grad_attn_out,
+        grad_in,
+        grad_down,
+        grad_gain_one,
+        grad_gain_two,
     )
 
 

time: 347 us -> 332 us (0.957)
  waiting for transfers between devices: 168 us -> 126 us
  Pallas kernels: 50 us -> 77.7 us
  local copies, waits for them, and re-layouts: 31.7 us -> 10.3 us
  blocking collectives: 0 us -> 12.5 us
  other arithmetic: 16.5 us -> 20.8 us
  starting transfers between devices: 62 us -> 66 us
    pallas_call x18, Pallas kernels: 50 us -> 77.7 us  [local_call(): pl.pallas_call(body, in_specs=[pl.BlockSpec(memory_space=pltpu.SMEM)] * l...]
    unnamed x115 -> x64, local copies, waits for them, and re-layouts: 28.7 us -> 9.72 us
    all_to_all x6 -> x4, waiting for transfers between devices: 76.6 us -> 58.5 us  [deal_out(): return lax.all_to_all(value, 'fsdp', 0, 0, tiled=True)]
    ppermute x7, waiting for transfers between devices: 42.2 us -> 25.7 us  [across(): return lax.ppermute(value, 'tp', [(i, i ^ 2) for i in range(4)])]
    ppermute x15 -> x26, starting transfers between devices: 24.8 us -> 38.1 us  [hop(): return lax.ppermute(value, 'fsdp', [(i, i ^ step) for i in range(8)])]
    all_to_all x6 -> x4, starting transfers between devices: 28.6 us -> 16 us  [deal_out(): return lax.all_to_all(value, 'fsdp', 0, 0, tiled=True)]
    all_to_all x0 -> x1, blocking collectives: none -> 12.5 us  [deal_out(): return lax.all_to_all(value, 'fsdp', 0, 0, tiled=True)]
    ppermute x15 -> x26, waiting for transfers between devices: 40.8 us -> 32.3 us  [hop(): return lax.ppermute(value, 'fsdp', [(i, i ^ step) for i in range(8)])]
  transfers between devices with their start and end apart: 40 -> 51, of which waited for: 27 -> 22; matrix products, arithmetic and copies ran while one was open for 5% -> 7% of each run, Pallas kernels for 11% -> 19%
where the time goes in v3:
time: 332 us; the launch traced here: 330 us
  waiting for transfers between devices  126 us (38%)
  Pallas kernels  77.7 us (23%)
  starting transfers between devices  66 us (20%)
  other arithmetic  20.8 us (6%)
  between operations  14.7 us (4%)
  blocking collectives  12.5 us (4%)
  local copies, waits for them, and re-layouts  10.3 us (3%)
    pallas_call x18, Pallas kernels, local_call(): pl.pallas_call(body, in_specs=[pl.BlockSpec(memory_space=pltpu.SMEM)] * l...  77.7 us
    all_to_all x4, waiting for transfers between devices, deal_out(): return lax.all_to_all(value, 'fsdp', 0, 0, tiled=True)  58.5 us
    ppermute x26, starting transfers between devices, hop(): return lax.ppermute(value, 'fsdp', [(i, i ^ step) for i in range(8)])  38.1 us
    ppermute x26, waiting for transfers between devices, hop(): return lax.ppermute(value, 'fsdp', [(i, i ^ step) for i in range(8)])  32.3 us
    ppermute x7, waiting for transfers between devices, across(): return lax.ppermute(value, 'tp', [(i, i ^ 2) for i in range(4)])  25.7 us
    all_to_all x4, starting transfers between devices, deal_out(): return lax.all_to_all(value, 'fsdp', 0, 0, tiled=True)  16 us
    all_to_all x1, blocking collectives, deal_out(): return lax.all_to_all(value, 'fsdp', 0, 0, tiled=True)  12.5 us
    ppermute x7, starting transfers between devices, across(): return lax.ppermute(value, 'tp', [(i, i ^ 2) for i in range(4)])  10.3 us
  transfers between devices with their start and end apart: 51, of which 22 were waited for; matrix products, arithmetic and copies ran while one was open for 7% of the time, Pallas kernels for 19%

profile of v3, /device:TPU:0, one launch (start us, length us, event | category | flops | bytes accessed | tf_op | source)
XLA Modules:
  0.0 329.7 jit_solution(13028196448733370327)
XLA Ops:
  12.4 3.6 %collective-permute-start.2 = (bf16[784,128]{1,0:T(8,128)(2,1)S(1)}, bf16[784,128]{1,0:T(8,128)(2,1)S(1)}, u32[]{:S(2)}, u32[]{:S(2)}) collective-permute-start(bf16[784,128]{1,0:T(8,128)(2,1)S(1)} %maximum_maximum_fusion.refs_3_), channel_id=1, source_target_pairs={{0,24},{4,28},{8,16},{12,20},{16,8},{20,12},{24,0},{28,4},{1,25},{... | collective-permute-start | bytes 602120 | tf_op jit(solution)/shard_map/ppermute | solution.py:345
  25.0 10.5 %collective-permute-done.1.refs_5_ = bf16[784,128]{1,0:T(8,128)(2,1)S(1)} collective-permute-done((bf16[784,128]{1,0:T(8,128)(2,1)S(1)}, bf16[784,128]{1,0:T(8,128)(2,1)S(1)}, u32[]{:S(2)}, u32[]{:S(2)}) %collective-permute-start.1) | collective-permute-done | bytes 200736 | tf_op jit(solution)/shard_map/ppermute | solution.py:345
  43.4 5.6 %project.1 = (bf16[512,1024]{1,0:T(8,128)(2,1)}, f32[2,1024]{1,0:T(2,128)}, bf16[8,192,256]{2,1,0:T(8,128)(2,1)}, bf16[784,1024]{1,0:T(8,128)(2,1)}) custom-call(s32[8]{0:T(128)S(1)} %get-tuple-element.131.refs_0_.refs_1_, bf16[2,256,1024]{2,1,0:T(8,128)(2,1)} %refs_2_.3, f32[64,512]{1,0:T(8,128)} %maximum_maximum_fusion.1.refs_2_, ...), custom_call_target="tpu_custom_call" | custom-call | flops 5000000000 | bytes 8388608 | tf_op jit(solution)/shard_map/project/pallas_call | solution.py:414
  49.0 5.1 %all-to-all-start = ((bf16[8,192,256]{2,1,0:T(8,128)(2,1)}), bf16[8,192,256]{2,1,0:T(8,128)(2,1)S(1)}, u32[]{:S(2)}, u32[]{:S(2)}) async-start(bf16[8,192,256]{2,1,0:T(8,128)(2,1)} %get-tuple-element.150), calls=%async_computation | async-start | bytes 1572864 | tf_op jit(solution)/shard_map/all_to_all | solution.py:357
  61.9 22.6 %all-to-all-done.refs_1_ = bf16[8,192,256]{2,1,0:T(8,128)(2,1)S(1)} async-done(((bf16[8,192,256]{2,1,0:T(8,128)(2,1)}), bf16[8,192,256]{2,1,0:T(8,128)(2,1)S(1)}, u32[]{:S(2)}, u32[]{:S(2)}) %all-to-all-start) | async-done | bytes 786464 | tf_op jit(solution)/shard_map/all_to_all | solution.py:357
  87.2 10.9 %attend.1 = (bf16[8,64,256]{2,1,0:T(8,128)(2,1)}, f32[8,64,256]{2,1,0:T(8,128)}, f32[8,1,256]{2,1,0:T(1,128)}) custom-call(s32[8]{0:T(128)S(1)} %get-tuple-element.130.refs_0_, bf16[8,192,256]{2,1,0:T(8,128)(2,1)} %copy-done.10), custom_call_target="tpu_custom_call" | custom-call | flops 5000000000 | bytes 8388608 | tf_op jit(solution)/shard_map/attend/pallas_call | solution.py:414
  101.5 12.5 %all_to_all.25 = bf16[8,64,256]{2,1,0:T(8,128)(2,1)} all-to-all(bf16[8,64,256]{2,1,0:T(8,128)(2,1)S(1)} %copy-done.14), channel_id=1, replica_groups=mesh['fsdp'=8,'tp'=4] {'fsdp'}, dimensions={0} | all-to-all | bytes 524288 | tf_op jit(solution)/shard_map/all_to_all | solution.py:357
  124.0 11.2 %collective-permute-done.17.refs_4_ = bf16[256,1024]{1,0:T(8,128)(2,1)S(1)} collective-permute-done((bf16[256,1024]{1,0:T(8,128)(2,1)S(1)}, bf16[256,1024]{1,0:T(8,128)(2,1)S(1)}, u32[]{:S(2)}, u32[]{:S(2)}) %collective-permute-start.17) | collective-permute-done | bytes 524320 | tf_op jit(solution)/shard_map/ppermute | solution.py:353
  140.4 7.8 %feed.1 = (bf16[256,1024]{1,0:T(8,128)(2,1)S(1)}, f32[256,1024]{1,0:T(8,128)S(1)}, bf16[512,656]{1,0:T(8,128)(2,1)S(1)}, bf16[512,656]{1,0:T(8,128)(2,1)S(1)}, bf16[512,656]{1,0:T(8,128)(2,1)S(1)}) custom-call(s32[8]{0:T(128)S(1)} %get-tuple-element.131.refs_0_.refs_1_, bf16[256,1024]{1,0:T(8,128)(2,1)S(1)} %get-tuple-element.182.refs_1_.refs_4_, ...), custom_call_target="tpu_custom_call" | custom-call | flops 5000000000 | bytes 8388608 | tf_op jit(solution)/shard_map/feed/pallas_call | solution.py:414
  150.4 3.4 %down.1 = (bf16[256,1024]{1,0:T(8,128)(2,1)}, f32[256,1024]{1,0:T(8,128)S(1)}) custom-call(s32[8]{0:T(128)S(1)} %get-tuple-element.131.refs_0_.refs_1_, bf16[512,656]{1,0:T(8,128)(2,1)S(1)} %get-tuple-element.192.refs_3_.refs_1_, bf16[8,912,128]{2,1,0:T(8,128)(2,1)} %bitcast.236), custom_call_target="tpu_custom_call" | custom-call | flops 5000000000 | bytes 8388608 | tf_op jit(solution)/shard_map/down/pallas_call | solution.py:414
  155.5 5.2 %feed_grad.1 = bf16[8,1968,128]{2,1,0:T(8,128)(2,1)} custom-call(s32[8]{0:T(128)S(1)} %get-tuple-element.131.refs_0_.refs_1_, bf16[512,656]{1,0:T(8,128)(2,1)S(1)} %get-tuple-element.190.refs_1_, bf16[512,656]{1,0:T(8,128)(2,1)S(1)} %get-tuple-element.191.refs_2_, bf16[512,656]{1,0:T(8,128)(2,1)S(1)} %get-tuple-element.192.refs_3_.refs_1_, ...), custom_call_target="tpu_custom_call" | custom-call | flops 5000000000 | bytes 8388608 | tf_op jit(solution)/shard_map/feed_grad/pallas_call | solution.py:414
  162.7 5.5 %collective-permute-done.20.refs_2_ = bf16[256,1024]{1,0:T(8,128)(2,1)S(1)} collective-permute-done((bf16[256,1024]{1,0:T(8,128)(2,1)S(1)}, bf16[256,1024]{1,0:T(8,128)(2,1)S(1)}, u32[]{:S(2)}, u32[]{:S(2)}) %collective-permute-start.20) | collective-permute-done | bytes 524320 | tf_op jit(solution)/shard_map/ppermute | solution.py:353
  178.5 3.7 %all-to-all-start.2 = ((bf16[8,64,256]{2,1,0:T(8,128)(2,1)}), bf16[8,64,256]{2,1,0:T(8,128)(2,1)S(1)}, u32[]{:S(2)}, u32[]{:S(2)}) async-start(bf16[8,64,256]{2,1,0:T(8,128)(2,1)} %mix_back.1), calls=%async_computation.2 | async-start | bytes 524288 | tf_op jit(solution)/shard_map/all_to_all | solution.py:357
  187.8 3.7 %all-to-all-done.2.refs_4_ = bf16[8,64,256]{2,1,0:T(8,128)(2,1)S(1)} async-done(((bf16[8,64,256]{2,1,0:T(8,128)(2,1)}), bf16[8,64,256]{2,1,0:T(8,128)(2,1)S(1)}, u32[]{:S(2)}, u32[]{:S(2)}) %all-to-all-start.2) | async-done | bytes 262176 | tf_op jit(solution)/shard_map/all_to_all | solution.py:357
  192.2 15.4 %attend_back.1 = bf16[8,192,256]{2,1,0:T(8,128)(2,1)} custom-call(s32[8]{0:T(128)S(1)} %get-tuple-element.130.refs_0_, bf16[8,192,256]{2,1,0:T(8,128)(2,1)} %copy-done.10, f32[8,64,256]{2,1,0:T(8,128)} %get-tuple-element.151.refs_2_, f32[8,1,256]{2,1,0:T(1,128)} %get-tuple-element.152.refs_3_, bf16[8,64,256]{2,1,0:T(8,128)(2,1)} %copy-done.15, ...), custom_call_target="tpu_custom_call" | custom-call | flops 5000000000 | bytes 8388608 | tf_op jit(solution)/shard_map/attend_back/pallas_call | solution.py:414
  207.6 3.6 %all-to-all-start.3 = ((bf16[8,192,256]{2,1,0:T(8,128)(2,1)}), bf16[8,192,256]{2,1,0:T(8,128)(2,1)S(1)}, u32[]{:S(2)}, u32[]{:S(2)}) async-start(bf16[8,192,256]{2,1,0:T(8,128)(2,1)} %attend_back.1), calls=%async_computation.3 | async-start | bytes 1572864 | tf_op jit(solution)/shard_map/all_to_all | solution.py:357
  211.2 3.5 %result.1 = bf16[128,1024]{1,0:T(8,128)(2,1)} custom-call(s32[8]{0:T(128)S(1)} %get-tuple-element.131.refs_0_.refs_1_, s32[1,128]{1,0:T(1,128)S(1)} %reshape.288.refs_1_, f32[256,1024]{1,0:T(8,128)} %copy-done.5, bf16[256,1024]{1,0:T(8,128)(2,1)} %add_convert_fusion.1.refs_3_, bf16[256,1024]{1,0:T(8,128)(2,1)} %copy-done.21), custom_call_target="tpu_custom_call" | custom-call | flops 5000000000 | bytes 8388608 | tf_op jit(solution)/shard_map/result/pallas_call | solution.py:414
  216.5 30.9 %all-to-all-done.3 = bf16[8,192,256]{2,1,0:T(8,128)(2,1)S(1)} async-done(((bf16[8,192,256]{2,1,0:T(8,128)(2,1)}), bf16[8,192,256]{2,1,0:T(8,128)(2,1)S(1)}, u32[]{:S(2)}, u32[]{:S(2)}) %all-to-all-start.3) | async-done | bytes 786464 | tf_op jit(solution)/shard_map/all_to_all | solution.py:357
  248.3 3.5 %project_grad.1 = (bf16[4,768,128]{2,1,0:T(8,128)(2,1)S(1)}, f32[4,768,128]{2,1,0:T(8,128)}) custom-call(bf16[2,768,256]{2,1,0:T(8,128)(2,1)} %bitcast.211, bf16[512,1024]{1,0:T(8,128)(2,1)} %get-tuple-element.213.refs_1_), custom_call_target="tpu_custom_call" | custom-call | flops 5000000000 | bytes 8388608 | tf_op jit(solution)/shard_map/project_grad/pallas_call | solution.py:414
  258.2 3.7 %all-to-all-start.4 = ((bf16[8,16,1024]{2,1,0:T(8,128)(2,1)}), bf16[8,16,1024]{2,1,0:T(8,128)(2,1)S(1)}, u32[]{:S(2)}, u32[]{:S(2)}) async-start(bf16[8,16,1024]{2,1,0:T(8,128)(2,1)} %bitcast.49), calls=%async_computation.4 | async-start | bytes 524288 | tf_op jit(solution)/shard_map/all_to_all | solution.py:357
  266.4 16.0 %collective-permute-done.25.refs_1_ = bf16[4,768,128]{2,1,0:T(8,128)(2,1)} collective-permute-done((bf16[4,768,128]{2,1,0:T(8,128)(2,1)S(1)}, bf16[4,768,128]{2,1,0:T(8,128)(2,1)}, u32[]{:S(2)}, u32[]{:S(2)}) %collective-permute-start.25) | collective-permute-done | bytes 786464 | tf_op jit(solution)/shard_map/ppermute | solution.py:345
  283.6 3.2 norm_one_back.1
  291.4 3.4 %collective-permute-start.38 = (bf16[16,128]{1,0:T(8,128)(2,1)S(1)}, bf16[16,128]{1,0:T(8,128)(2,1)S(1)}, u32[]{:S(2)}, u32[]{:S(2)}) collective-permute-start(bf16[16,128]{1,0:T(8,128)(2,1)S(1)} %bitcast.228), channel_id=1, source_target_pairs={{0,8},{4,12},{8,0},{12,4},{16,24},{20,28},{24,16},{28,20},{1,9},{5... | collective-permute-start | bytes 12296 | tf_op jit(solution)/shard_map/ppermute | solution.py:345
  303.2 4.9 %collective-permute-done.31 = bf16[8,16,1024]{2,1,0:T(8,128)(2,1)S(1)} collective-permute-done((bf16[8,16,1024]{2,1,0:T(8,128)(2,1)S(1)}, bf16[8,16,1024]{2,1,0:T(8,128)(2,1)S(1)}, u32[]{:S(2)}, u32[]{:S(2)}) %collective-permute-start.31) | collective-permute-done | bytes 262176 | tf_op jit(solution)/shard_map/ppermute | solution.py:353
  (242 shorter events, 115.8 us)
Async XLA Ops:
  7.2 106.8 %all-gather.5.cloned.1.call-start = ((), (), s32[]{:S(2)}) async-start(), calls=%async_computation.7 | async-start | bytes 2101248 | tf_op jit(solution)/shard_map/all_gather | solution.py:913
  9.4 29.0 %collective-permute-start.3 = (bf16[784,128]{1,0:T(8,128)(2,1)S(1)}, bf16[784,128]{1,0:T(8,128)(2,1)S(1)}, u32[]{:S(2)}, u32[]{:S(2)}) collective-permute-start(bf16[784,128]{1,0:T(8,128)(2,1)S(1)} %maximum_maximum_fusion.refs_3_), channel_id=1, source_target_pairs={{0,4},{4,0},{8,12},{12,8},{16,20},{20,16},{24,28},{28,24},{1,5},{5... | collective-permute-start | bytes 602120 | tf_op jit(solution)/shard_map/ppermute | solution.py:345
  16.0 19.5 %collective-permute-start.1 = (bf16[784,128]{1,0:T(8,128)(2,1)S(1)}, bf16[784,128]{1,0:T(8,128)(2,1)S(1)}, u32[]{:S(2)}, u32[]{:S(2)}) collective-permute-start(bf16[784,128]{1,0:T(8,128)(2,1)S(1)} %maximum_maximum_fusion.refs_3_), channel_id=1, source_target_pairs={{0,16},{4,20},{8,24},{12,28},{16,0},{20,4},{24,8},{28,12},{1,17},{... | collective-permute-start | bytes 602120 | tf_op jit(solution)/shard_map/ppermute | solution.py:345
  16.0 19.5 %collective-permute-start = (bf16[784,128]{1,0:T(8,128)(2,1)S(1)}, bf16[784,128]{1,0:T(8,128)(2,1)S(1)}, u32[]{:S(2)}, u32[]{:S(2)}) collective-permute-start(bf16[784,128]{1,0:T(8,128)(2,1)S(1)} %maximum_maximum_fusion.refs_3_), channel_id=1, source_target_pairs={{0,8},{4,12},{8,0},{12,4},{16,24},{20,28},{24,16},{28,20},{1,9},{5... | collective-permute-start | bytes 602120 | tf_op jit(solution)/shard_map/ppermute | solution.py:345
  49.0 35.5 %all-to-all-start = ((bf16[8,192,256]{2,1,0:T(8,128)(2,1)}), bf16[8,192,256]{2,1,0:T(8,128)(2,1)S(1)}, u32[]{:S(2)}, u32[]{:S(2)}) async-start(bf16[8,192,256]{2,1,0:T(8,128)(2,1)} %get-tuple-element.150), calls=%async_computation | async-start | bytes 1572864 | tf_op jit(solution)/shard_map/all_to_all | solution.py:357
  54.0 85.1 %all-gather.7.cloned.1.call-start = ((), (), s32[]{:S(2)}) async-start(), calls=%async_computation.8 | async-start | bytes 3022848 | tf_op jit(solution)/shard_map/all_gather | solution.py:914
  54.1 30.4 %collective-permute-start.7 = (bf16[2,8,1024]{2,1,0:T(8,128)(2,1)S(1)}, bf16[2,8,1024]{2,1,0:T(8,128)(2,1)S(1)}, u32[]{:S(2)}, u32[]{:S(2)}) collective-permute-start(bf16[2,8,1024]{2,1,0:T(8,128)(2,1)S(1)} %get-tuple-element.156), channel_id=1, source_target_pairs={{0,8},{4,12},{8,0},{12,4},{16,24},{20,28},{24,16},{28,20},{1,9},{5... | collective-permute-start | bytes 98312 | tf_op jit(solution)/shard_map/ppermute | solution.py:345
  56.2 28.7 %collective-permute-start.8 = (bf16[2,8,1024]{2,1,0:T(8,128)(2,1)S(1)}, bf16[2,8,1024]{2,1,0:T(8,128)(2,1)S(1)}, u32[]{:S(2)}, u32[]{:S(2)}) collective-permute-start(bf16[2,8,1024]{2,1,0:T(8,128)(2,1)S(1)} %get-tuple-element.157), channel_id=1, source_target_pairs={{0,16},{4,20},{8,24},{12,28},{16,0},{20,4},{24,8},{28,12},{1,17},{... | collective-permute-start | bytes 98312 | tf_op jit(solution)/shard_map/ppermute | solution.py:345
  59.3 38.8 %collective-permute-start.9 = (bf16[2,8,1024]{2,1,0:T(8,128)(2,1)S(1)}, bf16[2,8,1024]{2,1,0:T(8,128)(2,1)S(1)}, u32[]{:S(2)}, u32[]{:S(2)}) collective-permute-start(bf16[2,8,1024]{2,1,0:T(8,128)(2,1)S(1)} %get-tuple-element.158), channel_id=1, source_target_pairs={{0,24},{4,28},{8,16},{12,20},{16,8},{20,12},{24,0},{28,4},{1,25},{... | collective-permute-start | bytes 98312 | tf_op jit(solution)/shard_map/ppermute | solution.py:345
  59.4 38.7 %collective-permute-start.10 = (bf16[2,8,1024]{2,1,0:T(8,128)(2,1)S(1)}, bf16[2,8,1024]{2,1,0:T(8,128)(2,1)S(1)}, u32[]{:S(2)}, u32[]{:S(2)}) collective-permute-start(bf16[2,8,1024]{2,1,0:T(8,128)(2,1)S(1)} %get-tuple-element.159), channel_id=1, source_target_pairs={{0,4},{4,0},{8,12},{12,8},{16,20},{20,16},{24,28},{28,24},{1,5},{5... | collective-permute-start | bytes 98312 | tf_op jit(solution)/shard_map/ppermute | solution.py:345
  61.4 36.8 %collective-permute-start.11 = (bf16[2,8,1024]{2,1,0:T(8,128)(2,1)S(1)}, bf16[2,8,1024]{2,1,0:T(8,128)(2,1)S(1)}, u32[]{:S(2)}, u32[]{:S(2)}) collective-permute-start(bf16[2,8,1024]{2,1,0:T(8,128)(2,1)S(1)} %get-tuple-element.160), channel_id=1, source_target_pairs={{0,12},{4,8},{8,4},{12,0},{16,28},{20,24},{24,20},{28,16},{1,13},{... | collective-permute-start | bytes 98312 | tf_op jit(solution)/shard_map/ppermute | solution.py:345
  173.3 14.6 %collective-permute-start.23 = (bf16[256,1024]{1,0:T(8,128)(2,1)}, bf16[256,1024]{1,0:T(8,128)(2,1)S(1)}, u32[]{:S(2)}, u32[]{:S(2)}) collective-permute-start(bf16[256,1024]{1,0:T(8,128)(2,1)} %add_convert_fusion.1.refs_3_), channel_id=1, source_target_pairs={{0,2},{1,3},{2,0},{3,1},{4,6},{5,7},{6,4},{7,5},{8,10},{9,11},{10,... | collective-permute-start | bytes 1572872 | tf_op jit(solution)/shard_map/ppermute | solution.py:353
  182.2 130.6 %reduce-scatter.2.cloned.1.call-start = ((), (), s32[]{:S(2)}) async-start(), calls=%async_computation.6 | async-start | bytes 4534272 | tf_op jit(solution)/shard_map/reduce_scatter | solution.py:979
  182.9 24.7 %collective-permute-start.24 = (bf16[4,256,128]{2,1,0:T(8,128)(2,1)S(1)}, bf16[4,256,128]{2,1,0:T(8,128)(2,1)S(1)}, u32[]{:S(2)}, u32[]{:S(2)}) collective-permute-start(bf16[4,256,128]{2,1,0:T(8,128)(2,1)S(1)} %get-tuple-element.203), channel_id=1, source_target_pairs={{0,4},{4,0},{8,12},{12,8},{16,20},{20,16},{24,28},{28,24},{1,5},{5... | collective-permute-start | bytes 786440 | tf_op jit(solution)/shard_map/ppermute | solution.py:345
  207.6 39.8 %all-to-all-start.3 = ((bf16[8,192,256]{2,1,0:T(8,128)(2,1)}), bf16[8,192,256]{2,1,0:T(8,128)(2,1)S(1)}, u32[]{:S(2)}, u32[]{:S(2)}) async-start(bf16[8,192,256]{2,1,0:T(8,128)(2,1)} %attend_back.1), calls=%async_computation.3 | async-start | bytes 1572864 | tf_op jit(solution)/shard_map/all_to_all | solution.py:357
  254.6 27.7 %collective-permute-start.25 = (bf16[4,768,128]{2,1,0:T(8,128)(2,1)S(1)}, bf16[4,768,128]{2,1,0:T(8,128)(2,1)}, u32[]{:S(2)}, u32[]{:S(2)}) collective-permute-start(bf16[4,768,128]{2,1,0:T(8,128)(2,1)S(1)} %get-tuple-element.216), channel_id=1, source_target_pairs={{0,4},{4,0},{8,12},{12,8},{16,20},{20,16},{24,28},{28,24},{1,5},{5... | collective-permute-start | bytes 2359304 | tf_op jit(solution)/shard_map/ppermute | solution.py:345
  256.6 27.0 %collective-permute-start.27 = (bf16[256,1024]{1,0:T(8,128)(2,1)S(1)}, bf16[256,1024]{1,0:T(8,128)(2,1)S(1)}, u32[]{:S(2)}, u32[]{:S(2)}) collective-permute-start(bf16[256,1024]{1,0:T(8,128)(2,1)S(1)} %add_convert_fusion.refs_3_), channel_id=1, source_target_pairs={{0,2},{1,3},{2,0},{3,1},{4,6},{5,7},{6,4},{7,5},{8,10},{9,11},{10,... | collective-permute-start | bytes 1572872 | tf_op jit(solution)/shard_map/ppermute | solution.py:353
  258.2 25.5 %all-to-all-start.4 = ((bf16[8,16,1024]{2,1,0:T(8,128)(2,1)}), bf16[8,16,1024]{2,1,0:T(8,128)(2,1)S(1)}, u32[]{:S(2)}, u32[]{:S(2)}) async-start(bf16[8,16,1024]{2,1,0:T(8,128)(2,1)} %bitcast.49), calls=%async_computation.4 | async-start | bytes 524288 | tf_op jit(solution)/shard_map/all_to_all | solution.py:357
  261.9 27.5 %collective-permute-start.34 = (bf16[256,128]{1,0:T(8,128)(2,1)S(1)}, bf16[256,128]{1,0:T(8,128)(2,1)S(1)}, u32[]{:S(2)}, u32[]{:S(2)}) collective-permute-start(bf16[256,128]{1,0:T(8,128)(2,1)S(1)} %get-tuple-element.237), channel_id=1, source_target_pairs={{0,8},{4,12},{8,0},{12,4},{16,24},{20,28},{24,16},{28,20},{1,9},{5... | collective-permute-start | bytes 196616 | tf_op jit(solution)/shard_map/ppermute | solution.py:345
  263.9 25.5 %collective-permute-start.35 = (bf16[256,128]{1,0:T(8,128)(2,1)S(1)}, bf16[256,128]{1,0:T(8,128)(2,1)S(1)}, u32[]{:S(2)}, u32[]{:S(2)}) collective-permute-start(bf16[256,128]{1,0:T(8,128)(2,1)S(1)} %get-tuple-element.238), channel_id=1, source_target_pairs={{0,16},{4,20},{8,24},{12,28},{16,0},{20,4},{24,8},{28,12},{1,17},{... | collective-permute-start | bytes 196616 | tf_op jit(solution)/shard_map/ppermute | solution.py:345
  266.3 23.2 %collective-permute-start.36 = (bf16[256,128]{1,0:T(8,128)(2,1)S(1)}, bf16[256,128]{1,0:T(8,128)(2,1)}, u32[]{:S(2)}, u32[]{:S(2)}) collective-permute-start(bf16[256,128]{1,0:T(8,128)(2,1)S(1)} %get-tuple-element.239), channel_id=1, source_target_pairs={{0,24},{4,28},{8,16},{12,20},{16,8},{20,12},{24,0},{28,4},{1,25},{... | collective-permute-start | bytes 196616 | tf_op jit(solution)/shard_map/ppermute | solution.py:345
  297.2 23.0 %collective-permute-start.28 = (bf16[768,128]{1,0:T(8,128)(2,1)S(1)}, bf16[768,128]{1,0:T(8,128)(2,1)}, u32[]{:S(2)}, u32[]{:S(2)}) collective-permute-start(bf16[768,128]{1,0:T(8,128)(2,1)S(1)} %get-tuple-element.228), channel_id=1, source_target_pairs={{0,8},{4,12},{8,0},{12,4},{16,24},{20,28},{24,16},{28,20},{1,9},{5... | collective-permute-start | bytes 589832 | tf_op jit(solution)/shard_map/ppermute | solution.py:345
  297.3 23.0 %collective-permute-start.29 = (bf16[768,128]{1,0:T(8,128)(2,1)S(1)}, bf16[768,128]{1,0:T(8,128)(2,1)}, u32[]{:S(2)}, u32[]{:S(2)}) collective-permute-start(bf16[768,128]{1,0:T(8,128)(2,1)S(1)} %get-tuple-element.229), channel_id=1, source_target_pairs={{0,16},{4,20},{8,24},{12,28},{16,0},{20,4},{24,8},{28,12},{1,17},{... | collective-permute-start | bytes 589832 | tf_op jit(solution)/shard_map/ppermute | solution.py:345
  298.7 21.5 %collective-permute-start.30 = (bf16[768,128]{1,0:T(8,128)(2,1)S(1)}, bf16[768,128]{1,0:T(8,128)(2,1)}, u32[]{:S(2)}, u32[]{:S(2)}) collective-permute-start(bf16[768,128]{1,0:T(8,128)(2,1)S(1)} %get-tuple-element.230), channel_id=1, source_target_pairs={{0,24},{4,28},{8,16},{12,20},{16,8},{20,12},{24,0},{28,4},{1,25},{... | collective-permute-start | bytes 589832 | tf_op jit(solution)/shard_map/ppermute | solution.py:345
  (50 other events, 352.4 us)
Sparse Core Ops, SparseCore 0:
  19.5 63.5 all-gather.4
  85.9 53.1 all-gather.6
  186.6 109.9 reduce-scatter.1

commit v4 on v3

--- a/solution.py
+++ b/solution.py
@@ -324,7 +324,7 @@
 
 
 JOIN = 2
-COST = 5 * 10**9
+COSTS = {"attend": 10, "attend_back": 15, "feed": 8, "feed_grad": 5, "down": 3}
 FAR = -1e30
 ORDER = (0, 2, 4, 6, 1, 3, 5, 7)
 NT = (((1,), (1,)), ((), ()))
@@ -426,7 +426,7 @@
         + [pltpu.VMEM(shape, kind) for shape, kind in staged]
         + ([pltpu.SemaphoreType.DMA((len(staged),))] if staged else []),
         compiler_params=pltpu.CompilerParams(vmem_limit_bytes=room),
-        cost_estimate=pl.CostEstimate(flops=COST, transcendentals=0, bytes_accessed=8 * 1024 * 1024),
+        cost_estimate=pl.CostEstimate(flops=COSTS.get(name, 3) * 10**9, transcendentals=0, bytes_accessed=8 * 1024 * 1024),
         name=name,
     )(*scalars, *arrays, *shards)
     return result if len(outs) > 1 else result[0]
@@ -776,7 +776,7 @@
 
 
 def norm_one_back_kernel(
-    core_ref, order_ref, x_ref, half_ref, far_ref, dhidden_ref, gains_ref, grad_ref, dgain_ref, xhat_ref
+    core_ref, order_ref, x_ref, half_ref, far_ref, dhidden_ref, gains_ref, grad_ref, xhat_ref
 ):
     core = core_ref[0]
     width = x_ref.shape[2] // 8
@@ -790,7 +790,6 @@
         xhat_ref[:, span] = (piece - mean) * spread
     xhat = xhat_ref[...]
     dnorm = half_ref[...].astype(jnp.float32) + far_ref[...].astype(jnp.float32)
-    dgain_ref[...] = jnp.sum(dnorm * xhat, axis=0, keepdims=True)
     scaled = dnorm * gains_ref[0:1, :]
     inner = scaled - jnp.mean(scaled, axis=-1, keepdims=True)
     inner = inner - xhat * jnp.mean(scaled * xhat, axis=-1, keepdims=True)
@@ -913,8 +912,9 @@
     second_all = lax.all_gather(second, "fsdp", axis=0, tiled=False)
     third_all = lax.all_gather(jnp.concatenate([inp_turned, gate_turned], axis=0), "fsdp", axis=0, tiled=False)
     halfway = per_pair // 2
-    picks = lax.dynamic_slice_in_dim(pick(local, core), side * halfway, halfway, 1).reshape(1, -1)
-    unpack = (place_own[:, :, None] == slot_no[None, None, :]).astype(bf16)
+    picks = lax.dynamic_slice_in_dim(pick(local_own, core), side * halfway, halfway, 1).reshape(1, -1)
+    row_of = (order[:, None] * per_pair + jnp.arange(per_pair, dtype=i32)[None, :]).reshape(-1)
+    unpack = (place_own[:, :, None] == row_of[None, None, :]).astype(bf16)
     my_lens = lengths[mine // heads]
     all_anchor = jnp.arange(8 * rows, dtype=i32)
     table = turn_tables(positions(all_anchor, my_lens))
@@ -1015,7 +1015,9 @@
         result_kernel, "result", (order,), (picks, hidden, res_half, res_far),
         [((8 * halfway, full), bf16)], [((rows, full), bf16)], far_in=(1, 2, 3), far_out=(0,),
     )
-    d_raw, out_lows, packed = sync((d_raw, out_lows, packed))
+    packed = packed.reshape(8, halfway, full)
+    arrived = [hop(packed[at], ORDER[at]) if at else packed[at] for at in range(8)]
+    d_raw, out_lows, arrived = sync((d_raw, out_lows, arrived))
 
     qkv_far, qkv_near = local_call(
         partial(project_grad_kernel, 0), "project_grad", (), (d_raw, norm_one),
@@ -1028,44 +1030,40 @@
         [((rows, full), bf16), ((rows, full), f32)], far_in=(0, 1),
     )
     half = add_half(keep, twin(send))
-    half, packed, out_lows = sync((half, packed, out_lows))
     far = across(half)
-    arrived = deal_out(packed.reshape(8, halfway, full))
     out_got = z_send(out_lows)
+    arrived = jnp.stack(arrived)
     qkv_got, far, arrived = sync((qkv_got, far, arrived))
     qkv_own, qkv_lows = near_sum(qkv_near, qkv_got, "qkv_near")
-    qkv_got = z_send(qkv_lows)
-    input_own, d_gain_one = local_call(
+    qkv_lows, arrived, far, feed_sum, out_got = sync((qkv_lows, arrived, far, feed_sum, out_got))
+    input_own = local_call(
         norm_one_back_kernel, "norm_one_back", (core_at, order), (tokens, half, far, d_hidden, gains),
-        [((rows, full), bf16), ((1, full), f32)], [((rows, full), f32)], far_in=(0, 3, 4),
-    )
+        [((rows, full), bf16)], [((rows, full), f32)], far_in=(0, 3, 4),
+    )
+    input_own, feed_sum, out_got = sync((input_own, feed_sum, out_got))
     input_grad = both(input_own, twin(input_own))
-    high = d_gain_one.astype(bf16).astype(f32)
-    gain_parts = jnp.concatenate([high, d_gain_one - high, jnp.zeros((14, full), f32)], axis=0)
-    gain_parts = jnp.transpose(gain_parts.reshape(16, 8, width), (1, 0, 2))
-    gain_near = gain_parts[:4] + hop(gain_parts[4:].astype(bf16), 1).astype(f32)
-    gain_got = z_send([gain_near[at].astype(bf16) for at in range(1, 4)])
-    gain_row = far_sum(gain_near[0], gain_got)
-    gain_row = gain_row[0] + gain_row[1]
-    grad_gain_one = gain_row + twin(gain_row)
+    out_sum = far_sum(out_own, out_got)
+    inp_sum, gate_sum, down_sum = [feed_sum[at * units : (at + 1) * units].astype(f32) for at in range(3)]
+    two_row = jnp.sum(inp_sum * inp_turned.astype(f32) + gate_sum * gate_turned.astype(f32), axis=0)
+    grad_attn_out = jnp.transpose(out_sum)
+    grad_in = jnp.stack([jnp.transpose(inp_sum), jnp.transpose(gate_sum)], axis=1)
+    grad_down = jnp.transpose(down_sum)
     other_side = across(arrived)
     whole = jnp.concatenate(
         [jnp.where(side == 0, arrived, other_side), jnp.where(side == 0, other_side, arrived)], axis=1
     ).reshape(rows, full)
     whole = both(whole, twin(whole))
     output = jnp.einsum("msp,mpd->msd", unpack, whole, preferred_element_type=f32).astype(bf16)
-    out_sum = far_sum(out_own, out_got)
-    inp_sum, gate_sum, down_sum = [feed_sum[at * units : (at + 1) * units].astype(f32) for at in range(3)]
-    two_row = jnp.sum(inp_sum * inp_turned.astype(f32) + gate_sum * gate_turned.astype(f32), axis=0)
-    two_row = two_row + twin(two_row)
-    grad_gain_two = (two_row + across(two_row)) / gain_two.astype(f32)
-    grad_attn_out = jnp.transpose(out_sum)
-    grad_in = jnp.stack([jnp.transpose(inp_sum), jnp.transpose(gate_sum)], axis=1)
-    grad_down = jnp.transpose(down_sum)
-    qkv_got, output, input_grad, grad_attn_out, grad_in, grad_down, grad_gain_one, grad_gain_two = sync(
-        (qkv_got, output, input_grad, grad_attn_out, grad_in, grad_down, grad_gain_one, grad_gain_two)
+    qkv_got = z_send(qkv_lows)
+    qkv_got, output, input_grad, grad_attn_out, grad_in, grad_down, two_row = sync(
+        (qkv_got, output, input_grad, grad_attn_out, grad_in, grad_down, two_row)
     )
     qkv_sum = far_sum(qkv_own, qkv_got)
+    one_row = jnp.sum(qkv_sum * turned.astype(f32), axis=0)
+    gain_rows = jnp.stack([one_row / gain_one.astype(f32), two_row / gain_two.astype(f32)])
+    beyond = lax.ppermute(gain_rows, "tp", [(i, i ^ 3) for i in range(4)])
+    gain_rows = (gain_rows + twin(gain_rows)) + (across(gain_rows) + beyond)
+    grad_gain_one, grad_gain_two = gain_rows[0], gain_rows[1]
     return (
         output,
         input_grad,

time: 332 us -> 318 us (0.958)
  waiting for transfers between devices: 126 us -> 117 us
  Pallas kernels: 77.7 us -> 71.1 us
  starting transfers between devices: 66 us -> 72.2 us
  other arithmetic: 20.8 us -> 14.9 us
    all_to_all x4 -> x3, waiting for transfers between devices: 58.5 us -> 34.4 us  [deal_out(): return lax.all_to_all(value, 'fsdp', 0, 0, tiled=True)]
    ppermute x26 -> x29, waiting for transfers between devices: 32.3 us -> 49.3 us  [hop(): return lax.ppermute(value, 'fsdp', [(i, i ^ step) for i in range(8)])]
    ppermute x26 -> x29, starting transfers between devices: 38.1 us -> 47.4 us  [hop(): return lax.ppermute(value, 'fsdp', [(i, i ^ step) for i in range(8)])]
    pallas_call x18, Pallas kernels: 77.7 us -> 71.1 us  [local_call(): pl.pallas_call(body, in_specs=[pl.BlockSpec(memory_space=pltpu.SMEM)] * l...]
    ppermute x7, starting transfers between devices: 10.3 us -> 6.98 us  [across(): return lax.ppermute(value, 'tp', [(i, i ^ 2) for i in range(4)])]
    unnamed x64 -> x77, local copies, waits for them, and re-layouts: 9.72 us -> 7.32 us
    ppermute x11 -> x10, waiting for transfers between devices: 8.21 us -> 8.69 us  [twin(): return lax.ppermute(value, 'tp', [(i, i ^ 1) for i in range(4)])]
    all_to_all x4 -> x3, starting transfers between devices: 16 us -> 15.6 us  [deal_out(): return lax.all_to_all(value, 'fsdp', 0, 0, tiled=True)]
  transfers between devices with their start and end apart: 51 -> 53, of which waited for: 22 -> 23; matrix products, arithmetic and copies ran while one was open for 7% -> 6% of each run, Pallas kernels for 19% -> 18%
where the time goes in v4:
time: 318 us; the launch traced here: 316 us
  waiting for transfers between devices  117 us (37%)
  starting transfers between devices  72.2 us (23%)
  Pallas kernels  71.1 us (22%)
  blocking collectives  15.2 us (5%)
  other arithmetic  14.9 us (5%)
  between operations  14.8 us (5%)
  local copies, waits for them, and re-layouts  9.31 us (3%)
    pallas_call x18, Pallas kernels, local_call(): pl.pallas_call(body, in_specs=[pl.BlockSpec(memory_space=pltpu.SMEM)] * l...  71.1 us
    ppermute x29, waiting for transfers between devices, hop(): return lax.ppermute(value, 'fsdp', [(i, i ^ step) for i in range(8)])  49.3 us
    ppermute x29, starting transfers between devices, hop(): return lax.ppermute(value, 'fsdp', [(i, i ^ step) for i in range(8)])  47.4 us
    all_to_all x3, waiting for transfers between devices, deal_out(): return lax.all_to_all(value, 'fsdp', 0, 0, tiled=True)  34.4 us
    ppermute x7, waiting for transfers between devices, across(): return lax.ppermute(value, 'tp', [(i, i ^ 2) for i in range(4)])  23.6 us
    all_to_all x3, starting transfers between devices, deal_out(): return lax.all_to_all(value, 'fsdp', 0, 0, tiled=True)  15.6 us
    all_to_all x1, blocking collectives, deal_out(): return lax.all_to_all(value, 'fsdp', 0, 0, tiled=True)  15.2 us
    ppermute x10, waiting for transfers between devices, twin(): return lax.ppermute(value, 'tp', [(i, i ^ 1) for i in range(4)])  8.69 us
  transfers between devices with their start and end apart: 53, of which 23 were waited for; matrix products, arithmetic and copies ran while one was open for 6% of the time, Pallas kernels for 18%

profile of v4, /device:TPU:0, one launch (start us, length us, event | category | flops | bytes accessed | tf_op | source)
XLA Modules:
  0.0 315.9 jit_solution(12223594091264522720)
XLA Ops:
  12.4 3.6 %collective-permute-start.2 = (bf16[784,128]{1,0:T(8,128)(2,1)S(1)}, bf16[784,128]{1,0:T(8,128)(2,1)S(1)}, u32[]{:S(2)}, u32[]{:S(2)}) collective-permute-start(bf16[784,128]{1,0:T(8,128)(2,1)S(1)} %maximum_maximum_fusion.refs_3_), channel_id=1, source_target_pairs={{0,24},{4,28},{8,16},{12,20},{16,8},{20,12},{24,0},{28,4},{1,25},{... | collective-permute-start | bytes 602120 | tf_op jit(solution)/shard_map/ppermute | solution.py:345
  25.1 10.4 %collective-permute-done.1.refs_5_ = bf16[784,128]{1,0:T(8,128)(2,1)S(1)} collective-permute-done((bf16[784,128]{1,0:T(8,128)(2,1)S(1)}, bf16[784,128]{1,0:T(8,128)(2,1)S(1)}, u32[]{:S(2)}, u32[]{:S(2)}) %collective-permute-start.1) | collective-permute-done | bytes 200736 | tf_op jit(solution)/shard_map/ppermute | solution.py:345
  43.4 5.6 %project.1 = (bf16[512,1024]{1,0:T(8,128)(2,1)}, f32[2,1024]{1,0:T(2,128)}, bf16[8,192,256]{2,1,0:T(8,128)(2,1)}, bf16[784,1024]{1,0:T(8,128)(2,1)}) custom-call(s32[8]{0:T(128)S(1)} %get-tuple-element.144.refs_0_.refs_1_, bf16[2,256,1024]{2,1,0:T(8,128)(2,1)} %refs_2_.3, f32[64,512]{1,0:T(8,128)} %maximum_maximum_fusion.1.refs_2_, ...), custom_call_target="tpu_custom_call" | custom-call | flops 3000000000 | bytes 8388608 | tf_op jit(solution)/shard_map/project/pallas_call | solution.py:414
  49.0 5.1 %all-to-all-start = ((bf16[8,192,256]{2,1,0:T(8,128)(2,1)}), bf16[8,192,256]{2,1,0:T(8,128)(2,1)S(1)}, u32[]{:S(2)}, u32[]{:S(2)}) async-start(bf16[8,192,256]{2,1,0:T(8,128)(2,1)} %get-tuple-element.163), calls=%async_computation | async-start | bytes 1572864 | tf_op jit(solution)/shard_map/all_to_all | solution.py:357
  62.0 22.5 %all-to-all-done.refs_1_ = bf16[8,192,256]{2,1,0:T(8,128)(2,1)S(1)} async-done(((bf16[8,192,256]{2,1,0:T(8,128)(2,1)}), bf16[8,192,256]{2,1,0:T(8,128)(2,1)S(1)}, u32[]{:S(2)}, u32[]{:S(2)}) %all-to-all-start) | async-done | bytes 786464 | tf_op jit(solution)/shard_map/all_to_all | solution.py:357
  87.2 8.3 %attend.1 = (bf16[8,64,256]{2,1,0:T(8,128)(2,1)}, f32[8,64,256]{2,1,0:T(8,128)}, f32[8,1,256]{2,1,0:T(1,128)}) custom-call(s32[8]{0:T(128)S(1)} %get-tuple-element.143.refs_0_, bf16[8,192,256]{2,1,0:T(8,128)(2,1)} %copy-done.12), custom_call_target="tpu_custom_call" | custom-call | flops 10000000000 | bytes 8388608 | tf_op jit(solution)/shard_map/attend/pallas_call | solution.py:414
  98.9 15.2 %all_to_all.20 = bf16[8,64,256]{2,1,0:T(8,128)(2,1)} all-to-all(bf16[8,64,256]{2,1,0:T(8,128)(2,1)S(1)} %copy-done.17), channel_id=1, replica_groups=mesh['fsdp'=8,'tp'=4] {'fsdp'}, dimensions={0} | all-to-all | bytes 524288 | tf_op jit(solution)/shard_map/all_to_all | solution.py:357
  123.2 12.1 %collective-permute-done.17.refs_4_ = bf16[256,1024]{1,0:T(8,128)(2,1)S(1)} collective-permute-done((bf16[256,1024]{1,0:T(8,128)(2,1)S(1)}, bf16[256,1024]{1,0:T(8,128)(2,1)S(1)}, u32[]{:S(2)}, u32[]{:S(2)}) %collective-permute-start.17) | collective-permute-done | bytes 524320 | tf_op jit(solution)/shard_map/ppermute | solution.py:353
  140.4 7.8 %feed.1 = (bf16[256,1024]{1,0:T(8,128)(2,1)S(1)}, f32[256,1024]{1,0:T(8,128)S(1)}, bf16[512,656]{1,0:T(8,128)(2,1)S(1)}, bf16[512,656]{1,0:T(8,128)(2,1)S(1)}, bf16[512,656]{1,0:T(8,128)(2,1)S(1)}) custom-call(s32[8]{0:T(128)S(1)} %get-tuple-element.144.refs_0_.refs_1_, bf16[256,1024]{1,0:T(8,128)(2,1)S(1)} %get-tuple-element.195.refs_1_.refs_4_, ...), custom_call_target="tpu_custom_call" | custom-call | flops 8000000000 | bytes 8388608 | tf_op jit(solution)/shard_map/feed/pallas_call | solution.py:414
  154.6 5.2 %feed_grad.1 = bf16[8,1968,128]{2,1,0:T(8,128)(2,1)} custom-call(s32[8]{0:T(128)S(1)} %get-tuple-element.144.refs_0_.refs_1_, bf16[512,656]{1,0:T(8,128)(2,1)S(1)} %get-tuple-element.203.refs_1_, bf16[512,656]{1,0:T(8,128)(2,1)S(1)} %get-tuple-element.204.refs_2_, bf16[512,656]{1,0:T(8,128)(2,1)S(1)} %get-tuple-element.205.refs_3_.refs_1_, ...), custom_call_target="tpu_custom_call" | custom-call | flops 5000000000 | bytes 8388608 | tf_op jit(solution)/shard_map/feed_grad/pallas_call | solution.py:414
  161.2 7.0 %collective-permute-done.20.refs_2_ = bf16[256,1024]{1,0:T(8,128)(2,1)S(1)} collective-permute-done((bf16[256,1024]{1,0:T(8,128)(2,1)S(1)}, bf16[256,1024]{1,0:T(8,128)(2,1)S(1)}, u32[]{:S(2)}, u32[]{:S(2)}) %collective-permute-start.20) | collective-permute-done | bytes 524320 | tf_op jit(solution)/shard_map/ppermute | solution.py:353
  176.1 3.6 %all-to-all-start.2 = ((bf16[8,64,256]{2,1,0:T(8,128)(2,1)}), bf16[8,64,256]{2,1,0:T(8,128)(2,1)S(1)}, u32[]{:S(2)}, u32[]{:S(2)}) async-start(bf16[8,64,256]{2,1,0:T(8,128)(2,1)} %mix_back.1), calls=%async_computation.2 | async-start | bytes 524288 | tf_op jit(solution)/shard_map/all_to_all | solution.py:357
  185.2 11.9 %all-to-all-done.2.refs_4_ = bf16[8,64,256]{2,1,0:T(8,128)(2,1)S(1)} async-done(((bf16[8,64,256]{2,1,0:T(8,128)(2,1)}), bf16[8,64,256]{2,1,0:T(8,128)(2,1)S(1)}, u32[]{:S(2)}, u32[]{:S(2)}) %all-to-all-start.2) | async-done | bytes 262176 | tf_op jit(solution)/shard_map/all_to_all | solution.py:357
  197.8 11.5 %attend_back.1 = bf16[8,192,256]{2,1,0:T(8,128)(2,1)} custom-call(s32[8]{0:T(128)S(1)} %get-tuple-element.143.refs_0_, bf16[8,192,256]{2,1,0:T(8,128)(2,1)} %copy-done.12, f32[8,64,256]{2,1,0:T(8,128)} %get-tuple-element.164.refs_2_, f32[8,1,256]{2,1,0:T(1,128)} %get-tuple-element.165.refs_3_, bf16[8,64,256]{2,1,0:T(8,128)(2,1)} %copy-done.18, ...), custom_call_target="tpu_custom_call" | custom-call | flops 15000000512 | bytes 8388608 | tf_op jit(solution)/shard_map/attend_back/pallas_call | solution.py:414
  209.3 6.9 %all-to-all-start.3 = ((bf16[8,192,256]{2,1,0:T(8,128)(2,1)}), bf16[8,192,256]{2,1,0:T(8,128)(2,1)S(1)}, u32[]{:S(2)}, u32[]{:S(2)}) async-start(bf16[8,192,256]{2,1,0:T(8,128)(2,1)} %attend_back.1), calls=%async_computation.3 | async-start | bytes 1572864 | tf_op jit(solution)/shard_map/all_to_all | solution.py:357
  220.6 4.8 %collective-permute-start.31 = (bf16[16,1024]{1,0:T(8,128)(2,1)S(1)}, bf16[16,1024]{1,0:T(8,128)(2,1)S(1)}, u32[]{:S(2)}, u32[]{:S(2)}) collective-permute-start(bf16[16,1024]{1,0:T(8,128)(2,1)S(1)} %get-tuple-element.333), channel_id=1, source_target_pairs={{0,28},{4,24},{8,20},{12,16},{16,12},{20,8},{24,4},{28,0},{1,29},{... | collective-permute-start | bytes 98312 | tf_op jit(solution)/shard_map/ppermute | solution.py:345
  227.5 3.8 %collective-permute-start.27 = (bf16[16,1024]{1,0:T(8,128)(2,1)S(1)}, bf16[16,1024]{1,0:T(8,128)(2,1)S(1)}, u32[]{:S(2)}, u32[]{:S(2)}) collective-permute-start(bf16[16,1024]{1,0:T(8,128)(2,1)S(1)} %get-tuple-element.337), channel_id=1, source_target_pairs={{0,24},{4,28},{8,16},{12,20},{16,8},{20,12},{24,0},{28,4},{1,25},{... | collective-permute-start | bytes 98312 | tf_op jit(solution)/shard_map/ppermute | solution.py:345
  231.2 4.2 %collective-permute-done.31 = bf16[16,1024]{1,0:T(8,128)(2,1)S(1)} collective-permute-done((bf16[16,1024]{1,0:T(8,128)(2,1)S(1)}, bf16[16,1024]{1,0:T(8,128)(2,1)S(1)}, u32[]{:S(2)}, u32[]{:S(2)}) %collective-permute-start.31) | collective-permute-done | bytes 32800 | tf_op jit(solution)/shard_map/ppermute | solution.py:345
  235.4 4.9 %collective-permute-start.26 = (bf16[16,1024]{1,0:T(8,128)(2,1)S(1)}, bf16[16,1024]{1,0:T(8,128)(2,1)S(1)}, u32[]{:S(2)}, u32[]{:S(2)}) collective-permute-start(bf16[16,1024]{1,0:T(8,128)(2,1)S(1)} %get-tuple-element.338), channel_id=1, source_target_pairs={{0,16},{4,20},{8,24},{12,28},{16,0},{20,4},{24,8},{28,12},{1,17},{... | collective-permute-start | bytes 98312 | tf_op jit(solution)/shard_map/ppermute | solution.py:345
  246.9 4.1 %collective-permute-start.36 = (bf16[256,128]{1,0:T(8,128)(2,1)S(1)}, bf16[256,128]{1,0:T(8,128)(2,1)S(1)}, u32[]{:S(2)}, u32[]{:S(2)}) collective-permute-start(bf16[256,128]{1,0:T(8,128)(2,1)S(1)} %get-tuple-element.249), channel_id=1, source_target_pairs={{0,16},{4,20},{8,24},{12,28},{16,0},{20,4},{24,8},{28,12},{1,17},{... | collective-permute-start | bytes 196616 | tf_op jit(solution)/shard_map/ppermute | solution.py:345
  251.1 3.5 %project_grad.1 = (bf16[4,768,128]{2,1,0:T(8,128)(2,1)S(1)}, f32[4,768,128]{2,1,0:T(8,128)}) custom-call(bf16[2,768,256]{2,1,0:T(8,128)(2,1)} %bitcast.201, bf16[512,1024]{1,0:T(8,128)(2,1)} %get-tuple-element.226.refs_1_), custom_call_target="tpu_custom_call" | custom-call | flops 3000000000 | bytes 8388608 | tf_op jit(solution)/shard_map/project_grad/pallas_call | solution.py:414
  260.9 16.5 %collective-permute-done.32.refs_1_ = bf16[4,768,128]{2,1,0:T(8,128)(2,1)S(1)} collective-permute-done((bf16[4,768,128]{2,1,0:T(8,128)(2,1)S(1)}, bf16[4,768,128]{2,1,0:T(8,128)(2,1)S(1)}, u32[]{:S(2)}, u32[]{:S(2)}) %collective-permute-start.32) | collective-permute-done | bytes 786464 | tf_op jit(solution)/shard_map/ppermute | solution.py:345
  286.7 3.8 %collective-permute-start.39 = (bf16[768,128]{1,0:T(8,128)(2,1)S(1)}, bf16[768,128]{1,0:T(8,128)(2,1)S(1)}, u32[]{:S(2)}, u32[]{:S(2)}) collective-permute-start(bf16[768,128]{1,0:T(8,128)(2,1)S(1)} %get-tuple-element.252), channel_id=1, source_target_pairs={{0,16},{4,20},{8,24},{12,28},{16,0},{20,4},{24,8},{28,12},{1,17},{... | collective-permute-start | bytes 589832 | tf_op jit(solution)/shard_map/ppermute | solution.py:345
  297.5 7.2 %collective-permute-done.39 = bf16[768,128]{1,0:T(8,128)(2,1)S(1)} collective-permute-done((bf16[768,128]{1,0:T(8,128)(2,1)S(1)}, bf16[768,128]{1,0:T(8,128)(2,1)S(1)}, u32[]{:S(2)}, u32[]{:S(2)}) %collective-permute-start.39) | collective-permute-done | bytes 196640 | tf_op jit(solution)/shard_map/ppermute | solution.py:345
  (255 shorter events, 111.7 us)
Async XLA Ops:
  7.2 106.9 %all-gather.5.cloned.1.call-start = ((), (), s32[]{:S(2)}) async-start(), calls=%async_computation.6 | async-start | bytes 2101248 | tf_op jit(solution)/shard_map/all_gather | solution.py:912
  9.4 29.0 %collective-permute-start.3 = (bf16[784,128]{1,0:T(8,128)(2,1)S(1)}, bf16[784,128]{1,0:T(8,128)(2,1)S(1)}, u32[]{:S(2)}, u32[]{:S(2)}) collective-permute-start(bf16[784,128]{1,0:T(8,128)(2,1)S(1)} %maximum_maximum_fusion.refs_3_), channel_id=1, source_target_pairs={{0,4},{4,0},{8,12},{12,8},{16,20},{20,16},{24,28},{28,24},{1,5},{5... | collective-permute-start | bytes 602120 | tf_op jit(solution)/shard_map/ppermute | solution.py:345
  16.0 19.5 %collective-permute-start.1 = (bf16[784,128]{1,0:T(8,128)(2,1)S(1)}, bf16[784,128]{1,0:T(8,128)(2,1)S(1)}, u32[]{:S(2)}, u32[]{:S(2)}) collective-permute-start(bf16[784,128]{1,0:T(8,128)(2,1)S(1)} %maximum_maximum_fusion.refs_3_), channel_id=1, source_target_pairs={{0,16},{4,20},{8,24},{12,28},{16,0},{20,4},{24,8},{28,12},{1,17},{... | collective-permute-start | bytes 602120 | tf_op jit(solution)/shard_map/ppermute | solution.py:345
  16.0 19.5 %collective-permute-start = (bf16[784,128]{1,0:T(8,128)(2,1)S(1)}, bf16[784,128]{1,0:T(8,128)(2,1)S(1)}, u32[]{:S(2)}, u32[]{:S(2)}) collective-permute-start(bf16[784,128]{1,0:T(8,128)(2,1)S(1)} %maximum_maximum_fusion.refs_3_), channel_id=1, source_target_pairs={{0,8},{4,12},{8,0},{12,4},{16,24},{20,28},{24,16},{28,20},{1,9},{5... | collective-permute-start | bytes 602120 | tf_op jit(solution)/shard_map/ppermute | solution.py:345
  49.0 35.5 %all-to-all-start = ((bf16[8,192,256]{2,1,0:T(8,128)(2,1)}), bf16[8,192,256]{2,1,0:T(8,128)(2,1)S(1)}, u32[]{:S(2)}, u32[]{:S(2)}) async-start(bf16[8,192,256]{2,1,0:T(8,128)(2,1)} %get-tuple-element.163), calls=%async_computation | async-start | bytes 1572864 | tf_op jit(solution)/shard_map/all_to_all | solution.py:357
  54.0 84.9 %all-gather.7.cloned.1.call-start = ((), (), s32[]{:S(2)}) async-start(), calls=%async_computation.7 | async-start | bytes 3022848 | tf_op jit(solution)/shard_map/all_gather | solution.py:913
  54.1 30.4 %collective-permute-start.7 = (bf16[2,8,1024]{2,1,0:T(8,128)(2,1)S(1)}, bf16[2,8,1024]{2,1,0:T(8,128)(2,1)S(1)}, u32[]{:S(2)}, u32[]{:S(2)}) collective-permute-start(bf16[2,8,1024]{2,1,0:T(8,128)(2,1)S(1)} %get-tuple-element.169), channel_id=1, source_target_pairs={{0,8},{4,12},{8,0},{12,4},{16,24},{20,28},{24,16},{28,20},{1,9},{5... | collective-permute-start | bytes 98312 | tf_op jit(solution)/shard_map/ppermute | solution.py:345
  56.2 28.7 %collective-permute-start.8 = (bf16[2,8,1024]{2,1,0:T(8,128)(2,1)S(1)}, bf16[2,8,1024]{2,1,0:T(8,128)(2,1)S(1)}, u32[]{:S(2)}, u32[]{:S(2)}) collective-permute-start(bf16[2,8,1024]{2,1,0:T(8,128)(2,1)S(1)} %get-tuple-element.170), channel_id=1, source_target_pairs={{0,16},{4,20},{8,24},{12,28},{16,0},{20,4},{24,8},{28,12},{1,17},{... | collective-permute-start | bytes 98312 | tf_op jit(solution)/shard_map/ppermute | solution.py:345
  59.3 221.4 %reduce-scatter.2.cloned.1.call-start = ((), (), s32[]{:S(2)}) async-start(), calls=%async_computation.5 | async-start | bytes 4534272 | tf_op jit(solution)/shard_map/reduce_scatter | solution.py:979
  59.4 36.2 %collective-permute-start.9 = (bf16[2,8,1024]{2,1,0:T(8,128)(2,1)S(1)}, bf16[2,8,1024]{2,1,0:T(8,128)(2,1)S(1)}, u32[]{:S(2)}, u32[]{:S(2)}) collective-permute-start(bf16[2,8,1024]{2,1,0:T(8,128)(2,1)S(1)} %get-tuple-element.171), channel_id=1, source_target_pairs={{0,24},{4,28},{8,16},{12,20},{16,8},{20,12},{24,0},{28,4},{1,25},{... | collective-permute-start | bytes 98312 | tf_op jit(solution)/shard_map/ppermute | solution.py:345
  59.5 36.0 %collective-permute-start.10 = (bf16[2,8,1024]{2,1,0:T(8,128)(2,1)S(1)}, bf16[2,8,1024]{2,1,0:T(8,128)(2,1)S(1)}, u32[]{:S(2)}, u32[]{:S(2)}) collective-permute-start(bf16[2,8,1024]{2,1,0:T(8,128)(2,1)S(1)} %get-tuple-element.172), channel_id=1, source_target_pairs={{0,4},{4,0},{8,12},{12,8},{16,20},{20,16},{24,28},{28,24},{1,5},{5... | collective-permute-start | bytes 98312 | tf_op jit(solution)/shard_map/ppermute | solution.py:345
  61.5 34.1 %collective-permute-start.11 = (bf16[2,8,1024]{2,1,0:T(8,128)(2,1)S(1)}, bf16[2,8,1024]{2,1,0:T(8,128)(2,1)S(1)}, u32[]{:S(2)}, u32[]{:S(2)}) collective-permute-start(bf16[2,8,1024]{2,1,0:T(8,128)(2,1)S(1)} %get-tuple-element.173), channel_id=1, source_target_pairs={{0,12},{4,8},{8,4},{12,0},{16,28},{20,24},{24,20},{28,16},{1,13},{... | collective-permute-start | bytes 98312 | tf_op jit(solution)/shard_map/ppermute | solution.py:345
  97.4 16.7 %collective-permute-start.15 = (bf16[2,8,2,8,1024]{4,3,0,1,2:T(8,128)(2,1)S(1)}, bf16[2,8,2,8,1024]{4,3,0,1,2:T(8,128)(2,1)S(1)}, u32[]{:S(2)}, u32[]{:S(2)}) collective-permute-start(bf16[2,8,2,8,1024]{4,3,0,1,2:T(8,128)(2,1)S(1)} %pad_maximum_fusion.3), channel_id=1, source_target_pairs={{0,2},{1,3},{2,0},{3,1},{4,6},{5,7},{6,4},{7,5},{8,10},{9,11},{10,... | collective-permute-start | bytes 1572872 | tf_op jit(solution)/shard_map/ppermute | solution.py:353
  176.1 21.0 %all-to-all-start.2 = ((bf16[8,64,256]{2,1,0:T(8,128)(2,1)}), bf16[8,64,256]{2,1,0:T(8,128)(2,1)S(1)}, u32[]{:S(2)}, u32[]{:S(2)}) async-start(bf16[8,64,256]{2,1,0:T(8,128)(2,1)} %mix_back.1), calls=%async_computation.2 | async-start | bytes 524288 | tf_op jit(solution)/shard_map/all_to_all | solution.py:357
  179.7 29.6 %collective-permute-start.24 = (bf16[4,256,128]{2,1,0:T(8,128)(2,1)S(1)}, bf16[4,256,128]{2,1,0:T(8,128)(2,1)S(1)}, u32[]{:S(2)}, u32[]{:S(2)}) collective-permute-start(bf16[4,256,128]{2,1,0:T(8,128)(2,1)S(1)} %get-tuple-element.216), channel_id=1, source_target_pairs={{0,4},{4,0},{8,12},{12,8},{16,20},{20,16},{24,28},{28,24},{1,5},{5... | collective-permute-start | bytes 786440 | tf_op jit(solution)/shard_map/ppermute | solution.py:345
  209.3 37.3 %all-to-all-start.3 = ((bf16[8,192,256]{2,1,0:T(8,128)(2,1)}), bf16[8,192,256]{2,1,0:T(8,128)(2,1)S(1)}, u32[]{:S(2)}, u32[]{:S(2)}) async-start(bf16[8,192,256]{2,1,0:T(8,128)(2,1)} %attend_back.1), calls=%async_computation.3 | async-start | bytes 1572864 | tf_op jit(solution)/shard_map/all_to_all | solution.py:357
  225.4 15.8 %collective-permute-start.30 = (bf16[16,1024]{1,0:T(8,128)(2,1)S(1)}, bf16[16,1024]{1,0:T(8,128)(2,1)S(1)}, u32[]{:S(2)}, u32[]{:S(2)}) collective-permute-start(bf16[16,1024]{1,0:T(8,128)(2,1)S(1)} %get-tuple-element.334), channel_id=1, source_target_pairs={{0,20},{4,16},{8,28},{12,24},{16,4},{20,0},{24,12},{28,8},{1,21},{... | collective-permute-start | bytes 98312 | tf_op jit(solution)/shard_map/ppermute | solution.py:345
  225.4 17.8 %collective-permute-start.29 = (bf16[16,1024]{1,0:T(8,128)(2,1)S(1)}, bf16[16,1024]{1,0:T(8,128)(2,1)S(1)}, u32[]{:S(2)}, u32[]{:S(2)}) collective-permute-start(bf16[16,1024]{1,0:T(8,128)(2,1)S(1)} %get-tuple-element.335), channel_id=1, source_target_pairs={{0,12},{4,8},{8,4},{12,0},{16,28},{20,24},{24,20},{28,16},{1,13},{... | collective-permute-start | bytes 98312 | tf_op jit(solution)/shard_map/ppermute | solution.py:345
  246.6 34.1 %collective-permute-start.35 = (bf16[256,128]{1,0:T(8,128)(2,1)S(1)}, bf16[256,128]{1,0:T(8,128)(2,1)S(1)}, u32[]{:S(2)}, u32[]{:S(2)}) collective-permute-start(bf16[256,128]{1,0:T(8,128)(2,1)S(1)} %get-tuple-element.248), channel_id=1, source_target_pairs={{0,8},{4,12},{8,0},{12,4},{16,24},{20,28},{24,16},{28,20},{1,9},{5... | collective-permute-start | bytes 196616 | tf_op jit(solution)/shard_map/ppermute | solution.py:345
  246.9 33.7 %collective-permute-start.36 = (bf16[256,128]{1,0:T(8,128)(2,1)S(1)}, bf16[256,128]{1,0:T(8,128)(2,1)S(1)}, u32[]{:S(2)}, u32[]{:S(2)}) collective-permute-start(bf16[256,128]{1,0:T(8,128)(2,1)S(1)} %get-tuple-element.249), channel_id=1, source_target_pairs={{0,16},{4,20},{8,24},{12,28},{16,0},{20,4},{24,8},{28,12},{1,17},{... | collective-permute-start | bytes 196616 | tf_op jit(solution)/shard_map/ppermute | solution.py:345
  251.1 29.6 %collective-permute-start.37 = (bf16[256,128]{1,0:T(8,128)(2,1)S(1)}, bf16[256,128]{1,0:T(8,128)(2,1)S(1)}, u32[]{:S(2)}, u32[]{:S(2)}) collective-permute-start(bf16[256,128]{1,0:T(8,128)(2,1)S(1)} %get-tuple-element.250), channel_id=1, source_target_pairs={{0,24},{4,28},{8,16},{12,20},{16,8},{20,12},{24,0},{28,4},{1,25},{... | collective-permute-start | bytes 196616 | tf_op jit(solution)/shard_map/ppermute | solution.py:345
  257.4 20.0 %collective-permute-start.32 = (bf16[4,768,128]{2,1,0:T(8,128)(2,1)S(1)}, bf16[4,768,128]{2,1,0:T(8,128)(2,1)S(1)}, u32[]{:S(2)}, u32[]{:S(2)}) collective-permute-start(bf16[4,768,128]{2,1,0:T(8,128)(2,1)S(1)} %get-tuple-element.229), channel_id=1, source_target_pairs={{0,4},{4,0},{8,12},{12,8},{16,20},{20,16},{24,28},{28,24},{1,5},{5... | collective-permute-start | bytes 2359304 | tf_op jit(solution)/shard_map/ppermute | solution.py:345
  259.4 17.9 %collective-permute-start.34 = (bf16[256,1024]{1,0:T(8,128)(2,1)S(1)}, bf16[256,1024]{1,0:T(8,128)(2,1)S(1)}, u32[]{:S(2)}, u32[]{:S(2)}) collective-permute-start(bf16[256,1024]{1,0:T(8,128)(2,1)S(1)} %add_convert_fusion.refs_3_), channel_id=1, source_target_pairs={{0,2},{1,3},{2,0},{3,1},{4,6},{5,7},{6,4},{7,5},{8,10},{9,11},{10,... | collective-permute-start | bytes 1572872 | tf_op jit(solution)/shard_map/ppermute | solution.py:353
  286.7 18.0 %collective-permute-start.39 = (bf16[768,128]{1,0:T(8,128)(2,1)S(1)}, bf16[768,128]{1,0:T(8,128)(2,1)S(1)}, u32[]{:S(2)}, u32[]{:S(2)}) collective-permute-start(bf16[768,128]{1,0:T(8,128)(2,1)S(1)} %get-tuple-element.252), channel_id=1, source_target_pairs={{0,16},{4,20},{8,24},{12,28},{16,0},{20,4},{24,8},{28,12},{1,17},{... | collective-permute-start | bytes 589832 | tf_op jit(solution)/shard_map/ppermute | solution.py:345
  (57 other events, 459.7 us)
Sparse Core Ops, SparseCore 0:
  19.5 63.5 all-gather.4
  85.9 53.0 all-gather.6
  159.9 104.6 reduce-scatter.1

commit v5 on v4

--- a/solution.py
+++ b/solution.py
@@ -324,7 +324,7 @@
 
 
 JOIN = 2
-COSTS = {"attend": 10, "attend_back": 15, "feed": 8, "feed_grad": 5, "down": 3}
+COSTS = {"attend": 10, "attend_back": 28, "feed": 8, "feed_grad": 5}
 FAR = -1e30
 ORDER = (0, 2, 4, 6, 1, 3, 5, 7)
 NT = (((1,), (1,)), ((), ()))
@@ -668,7 +668,8 @@
 
 
 def feed_kernel(
-    order_ref, own_ref, other_ref, grad_ref, all_ref, down_ref, send_ref, keep_ref, act_ref, dinp_ref, dgate_ref, w_ref, sem_ref
+    order_ref, own_ref, other_ref, grad_ref, all_ref, down_ref,
+    send_ref, keep_ref, act_ref, dinp_ref, dgate_ref, result_send_ref, result_keep_ref, w_ref, sem_ref
 ):
     units = w_ref.shape[0] // 3
     inp_w, gate_w, down_w = [w_ref.at[pl.ds(at * units, units), :] for at in range(3)]
@@ -684,16 +685,20 @@
         cdf = 0.5 * (1.0 + lax.erf(inp * (0.5**0.5)))
         density = jnp.exp(-0.5 * inp * inp) * ((0.5 / jnp.pi) ** 0.5)
         gelu = inp * cdf
-        act_ref[span, :] = (gelu * gate).astype(jnp.bfloat16)
+        act = (gelu * gate).astype(jnp.bfloat16)
+        act_ref[span, :] = act
         dinp = (dact * gate * (cdf + inp * density)).astype(jnp.bfloat16)
         dgate = (dact * gelu).astype(jnp.bfloat16)
         dinp_ref[span, :] = dinp
         dgate_ref[span, :] = dgate
         part = mm(dinp, inp_w[...], NN) + mm(dgate, gate_w[...], NN)
+        result = mm(act, down_w[...], NN)
         if micro:
             send_ref[...] = part.astype(jnp.bfloat16)
+            result_send_ref[...] = result.astype(jnp.bfloat16)
         else:
             keep_ref[...] = part
+            result_keep_ref[...] = result
 
 
 def weight_grad_kernel(order_ref, dinp_ref, dgate_ref, act_ref, own_ref, other_ref, grad_ref, out_ref):
@@ -717,14 +722,6 @@
         low_ref[...] = (near_ref[at + 1] + far_ref[at + 1].astype(jnp.float32)).astype(jnp.bfloat16)
 
 
-def down_kernel(order_ref, act_ref, all_ref, send_ref, keep_ref, w_ref, sem_ref):
-    rows = send_ref.shape[0]
-    units = w_ref.shape[0]
-    finish(gathered_copies(order_ref, all_ref, 0, units, w_ref, sem_ref))
-    send_ref[...] = mm(act_ref[rows:, :], w_ref[...], NN).astype(jnp.bfloat16)
-    keep_ref[...] = mm(act_ref[:rows, :], w_ref[...], NN)
-
-
 def norm_two_back_kernel(hidden_ref, half_ref, far_ref, grad_ref, gains_ref, dhidden_ref, low_ref):
     hidden = hidden_ref[...]
     center = hidden - jnp.mean(hidden, axis=-1, keepdims=True)
@@ -758,21 +755,16 @@
         far_ref[place] = total[:, (4 + place) * width : (5 + place) * width].astype(jnp.bfloat16)
 
 
-def project_back_kernel(core_ref, raw_ref, w_ref, send_ref, keep_ref):
+def project_back_kernel(core_ref, raw_ref, norm_ref, w_ref, far_ref, near_ref, send_ref, keep_ref):
+    wide, width = far_ref.shape[1:]
+    rows = raw_ref.shape[2]
     core = core_ref[0]
-    weights = w_ref[: raw_ref.shape[1], :]
-    send_ref[...] = mm(raw_ref[1 - core], weights, TN).astype(jnp.bfloat16)
-    keep_ref[...] = mm(raw_ref[core], weights, TN)
-
-
-def project_grad_kernel(first, raw_ref, norm_ref, far_ref, near_ref):
-    count, width = far_ref.shape[1:]
-    rows = raw_ref.shape[2]
-    span = slice(first, first + count)
-    total = mm(raw_ref[0, span, :], norm_ref[:rows, :], NN) + mm(raw_ref[1, span, :], norm_ref[rows:, :], NN)
+    total = mm(raw_ref[0], norm_ref[:rows, :], NN) + mm(raw_ref[1], norm_ref[rows:, :], NN)
     for place in range(4):
         near_ref[place] = total[:, place * width : (place + 1) * width]
         far_ref[place] = total[:, (4 + place) * width : (5 + place) * width].astype(jnp.bfloat16)
+    send_ref[...] = mm(raw_ref[1 - core], w_ref[:wide, :], TN).astype(jnp.bfloat16)
+    keep_ref[...] = mm(raw_ref[core], w_ref[:wide, :], TN)
 
 
 def norm_one_back_kernel(
@@ -912,9 +904,8 @@
     second_all = lax.all_gather(second, "fsdp", axis=0, tiled=False)
     third_all = lax.all_gather(jnp.concatenate([inp_turned, gate_turned], axis=0), "fsdp", axis=0, tiled=False)
     halfway = per_pair // 2
-    picks = lax.dynamic_slice_in_dim(pick(local_own, core), side * halfway, halfway, 1).reshape(1, -1)
-    row_of = (order[:, None] * per_pair + jnp.arange(per_pair, dtype=i32)[None, :]).reshape(-1)
-    unpack = (place_own[:, :, None] == row_of[None, None, :]).astype(bf16)
+    picks = lax.dynamic_slice_in_dim(pick(local, core), side * halfway, halfway, 1).reshape(1, -1)
+    unpack = (place_own[:, :, None] == slot_no[None, None, :]).astype(bf16)
     my_lens = lengths[mine // heads]
     all_anchor = jnp.arange(8 * rows, dtype=i32)
     table = turn_tables(positions(all_anchor, my_lens))
@@ -964,10 +955,12 @@
     )
     two_other = twin(two_own)
 
-    send, keep, act, d_inp, d_gate = local_call(
+    send, keep, act, d_inp, d_gate, result_send, result_keep = local_call(
         feed_kernel, "feed", (order,), (two_own, two_other, grad),
-        [((rows, full), bf16), ((rows, full), f32)] + [((2 * rows, units), bf16)] * 3,
-        [((3 * units, full), bf16)], (third_all, second_all), copies=16,
+        [((rows, full), bf16), ((rows, full), f32)]
+        + [((2 * rows, units), bf16)] * 3
+        + [((rows, full), bf16), ((rows, full), f32)],
+        [((3 * units, full), bf16)], (third_all, second_all), copies=16, far_out=(5, 6),
     )
     half_two = add_half(keep, twin(send))
     half_two, act, d_inp, d_gate = sync((half_two, act, d_inp, d_gate))
@@ -977,12 +970,7 @@
         [((8, 3 * units, width), bf16)], far_out=(0,),
     )
     feed_sum = lax.psum_scatter(feed_grad, "fsdp", scatter_dimension=0, tiled=False)
-    send, keep = local_call(
-        down_kernel, "down", (order,), (act,),
-        [((rows, full), bf16), ((rows, full), f32)], [((units, full), bf16)], (second_all,),
-    )
-    res_half = add_half(keep, twin(send))
-    far_two, feed_grad, res_half = sync((far_two, feed_grad, res_half))
+    far_two, feed_grad = sync((far_two, feed_grad))
     d_hidden, low_own = local_call(
         norm_two_back_kernel, "norm_two_back", (), (hidden, half_two, far_two, grad, gains),
         [((rows, full), f32), ((rows, full), bf16)], far_in=(4,), far_out=(0,),
@@ -992,47 +980,44 @@
         mix_back_kernel, "mix_back", (core_at,), (low_own, low_other, out_w),
         [((8, HD, rows), bf16)], far_out=(0,),
     )
+    d_mixed, low_own, low_other, result_send, result_keep = sync(
+        (d_mixed, low_own, low_other, result_send, result_keep)
+    )
+    grad_mixed = deal_out(d_mixed)
     out_far, out_near = local_call(
         mix_grad_kernel, "mix_grad", (core_at,), (mixed, low_own, low_other),
-        [((4, cols, width), bf16), ((4, cols, width), f32)], far_in=(0,), far_out=(1,),
-    )
-    d_mixed, out_far = sync((d_mixed, out_far))
-    grad_mixed = deal_out(d_mixed)
+        [((4, cols, width), bf16), ((4, cols, width), f32)], far_in=(0, 1, 2), far_out=(1,),
+    )
+    res_half = add_half(result_keep, twin(result_send))
+    grad_mixed, out_far, res_half = sync((grad_mixed, out_far, res_half))
+
+    out_got = hop(out_far, 1)
     res_far = across(res_half)
-    grad_mixed, res_far = sync((grad_mixed, res_far))
-
-    out_got = hop(out_far, 1)
     d_raw_out = local_call(
         attend_back_kernel, "attend_back", (my_lens,), (qkv, exact, logs, grad_mixed, table),
         [((8, 3 * HD, rows), bf16)],
         [((8 * rows, 2 * HD), bf16), ((HD, 8 * rows), f32), ((HD, 8 * rows), f32)],
         far_in=(0, 1, 2, 3, 4), far_out=(0,),
     )
-    d_raw_out, out_got = sync((d_raw_out, out_got))
+    d_raw_out, out_got, res_far = sync((d_raw_out, out_got, res_far))
     d_raw = deal_out(d_raw_out).reshape(2, 3 * cols, rows)
     out_own, out_lows = near_sum(out_near, out_got, "out_near")
     packed = local_call(
         result_kernel, "result", (order,), (picks, hidden, res_half, res_far),
         [((8 * halfway, full), bf16)], [((rows, full), bf16)], far_in=(1, 2, 3), far_out=(0,),
     )
-    packed = packed.reshape(8, halfway, full)
-    arrived = [hop(packed[at], ORDER[at]) if at else packed[at] for at in range(8)]
-    d_raw, out_lows, arrived = sync((d_raw, out_lows, arrived))
-
-    qkv_far, qkv_near = local_call(
-        partial(project_grad_kernel, 0), "project_grad", (), (d_raw, norm_one),
-        [((4, 3 * cols, width), bf16), ((4, 3 * cols, width), f32)], far_in=(0, 1), far_out=(1,),
-    )
-    qkv_far, d_raw = sync((qkv_far, d_raw))
+    d_raw, out_lows, packed = sync((d_raw, out_lows, packed))
+
+    qkv_far, qkv_near, send, keep = local_call(
+        project_back_kernel, "project_back", (core_at,), (d_raw, norm_one, qkv_w),
+        [((4, 3 * cols, width), bf16), ((4, 3 * cols, width), f32), ((rows, full), bf16), ((rows, full), f32)],
+        far_in=(0, 1, 2), far_out=(1,),
+    )
     qkv_got = hop(qkv_far, 1)
-    send, keep = local_call(
-        project_back_kernel, "project_back", (core_at,), (d_raw, qkv_w),
-        [((rows, full), bf16), ((rows, full), f32)], far_in=(0, 1),
-    )
     half = add_half(keep, twin(send))
     far = across(half)
     out_got = z_send(out_lows)
-    arrived = jnp.stack(arrived)
+    arrived = deal_out(packed.reshape(8, halfway, full))
     qkv_got, far, arrived = sync((qkv_got, far, arrived))
     qkv_own, qkv_lows = near_sum(qkv_near, qkv_got, "qkv_near")
     qkv_lows, arrived, far, feed_sum, out_got = sync((qkv_lows, arrived, far, feed_sum, out_got))

time: 318 us -> 304 us (0.956)
  starting transfers between devices: 72.2 us -> 58.9 us
  Pallas kernels: 71.1 us -> 66.9 us
  local copies, waits for them, and re-layouts: 9.31 us -> 13.1 us
    all_to_all x3 -> x4, waiting for transfers between devices: 34.4 us -> 61.8 us  [deal_out(): return lax.all_to_all(value, 'fsdp', 0, 0, tiled=True)]
    ppermute x29 -> x22, waiting for transfers between devices: 49.3 us -> 21.9 us  [hop(): return lax.ppermute(value, 'fsdp', [(i, i ^ step) for i in range(8)])]
    ppermute x29 -> x22, starting transfers between devices: 47.4 us -> 31.3 us  [hop(): return lax.ppermute(value, 'fsdp', [(i, i ^ step) for i in range(8)])]
    unnamed x77 -> x78, local copies, waits for them, and re-layouts: 7.32 us -> 12.1 us
    pallas_call x18 -> x16, Pallas kernels: 71.1 us -> 66.9 us  [local_call(): pl.pallas_call(body, in_specs=[pl.BlockSpec(memory_space=pltpu.SMEM)] * l...]
    all_to_all x3 -> x4, starting transfers between devices: 15.6 us -> 19.1 us  [deal_out(): return lax.all_to_all(value, 'fsdp', 0, 0, tiled=True)]
  transfers between devices with their start and end apart: 53 -> 47, of which waited for: 23 -> 18; matrix products, arithmetic and copies ran while one was open for 6% -> 6% of each run, Pallas kernels for 18% -> 18%
where the time goes in v5:
time: 304 us; the launch traced here: 301 us
  waiting for transfers between devices  115 us (38%)
  Pallas kernels  66.9 us (22%)
  starting transfers between devices  58.9 us (19%)
  other arithmetic  15.5 us (5%)
  blocking collectives  15.2 us (5%)
  between operations  14.7 us (5%)
  local copies, waits for them, and re-layouts  13.1 us (4%)
    pallas_call x16, Pallas kernels, local_call(): pl.pallas_call(body, in_specs=[pl.BlockSpec(memory_space=pltpu.SMEM)] * l...  66.9 us
    all_to_all x4, waiting for transfers between devices, deal_out(): return lax.all_to_all(value, 'fsdp', 0, 0, tiled=True)  61.8 us
    ppermute x22, starting transfers between devices, hop(): return lax.ppermute(value, 'fsdp', [(i, i ^ step) for i in range(8)])  31.3 us
    ppermute x22, waiting for transfers between devices, hop(): return lax.ppermute(value, 'fsdp', [(i, i ^ step) for i in range(8)])  21.9 us
    ppermute x7, waiting for transfers between devices, across(): return lax.ppermute(value, 'tp', [(i, i ^ 2) for i in range(4)])  21.2 us
    all_to_all x4, starting transfers between devices, deal_out(): return lax.all_to_all(value, 'fsdp', 0, 0, tiled=True)  19.1 us
    all_to_all x1, blocking collectives, deal_out(): return lax.all_to_all(value, 'fsdp', 0, 0, tiled=True)  15.2 us
    unnamed x78, local copies, waits for them, and re-layouts  12.1 us
  transfers between devices with their start and end apart: 47, of which 18 were waited for; matrix products, arithmetic and copies ran while one was open for 6% of the time, Pallas kernels for 18%

profile of v5, /device:TPU:0, one launch (start us, length us, event | category | flops | bytes accessed | tf_op | source)
XLA Modules:
  0.0 301.2 jit_solution(367399852671535029)
XLA Ops:
  9.4 3.0 %collective-permute-start.3 = (bf16[784,128]{1,0:T(8,128)(2,1)S(1)}, bf16[784,128]{1,0:T(8,128)(2,1)S(1)}, u32[]{:S(2)}, u32[]{:S(2)}) collective-permute-start(bf16[784,128]{1,0:T(8,128)(2,1)S(1)} %maximum_maximum_fusion.refs_3_), channel_id=1, source_target_pairs={{0,4},{4,0},{8,12},{12,8},{16,20},{20,16},{24,28},{28,24},{1,5},{5... | collective-permute-start | bytes 602120 | tf_op jit(solution)/shard_map/ppermute | solution.py:345
  12.4 3.6 %collective-permute-start.2 = (bf16[784,128]{1,0:T(8,128)(2,1)S(1)}, bf16[784,128]{1,0:T(8,128)(2,1)S(1)}, u32[]{:S(2)}, u32[]{:S(2)}) collective-permute-start(bf16[784,128]{1,0:T(8,128)(2,1)S(1)} %maximum_maximum_fusion.refs_3_), channel_id=1, source_target_pairs={{0,24},{4,28},{8,16},{12,20},{16,8},{20,12},{24,0},{28,4},{1,25},{... | collective-permute-start | bytes 602120 | tf_op jit(solution)/shard_map/ppermute | solution.py:345
  25.0 10.6 %collective-permute-done.1.refs_5_ = bf16[784,128]{1,0:T(8,128)(2,1)S(1)} collective-permute-done((bf16[784,128]{1,0:T(8,128)(2,1)S(1)}, bf16[784,128]{1,0:T(8,128)(2,1)S(1)}, u32[]{:S(2)}, u32[]{:S(2)}) %collective-permute-start.1) | collective-permute-done | bytes 200736 | tf_op jit(solution)/shard_map/ppermute | solution.py:345
  43.4 5.5 %project.1 = (bf16[512,1024]{1,0:T(8,128)(2,1)}, f32[2,1024]{1,0:T(2,128)}, bf16[8,192,256]{2,1,0:T(8,128)(2,1)}, bf16[784,1024]{1,0:T(8,128)(2,1)}) custom-call(s32[8]{0:T(128)S(1)} %get-tuple-element.140.refs_0_.refs_1_, bf16[2,256,1024]{2,1,0:T(8,128)(2,1)} %refs_2_.3, f32[64,512]{1,0:T(8,128)} %maximum_maximum_fusion.1.refs_2_, ...), custom_call_target="tpu_custom_call" | custom-call | flops 3000000000 | bytes 8388608 | tf_op jit(solution)/shard_map/project/pallas_call | solution.py:414
  48.9 5.1 %all-to-all-start = ((bf16[8,192,256]{2,1,0:T(8,128)(2,1)}), bf16[8,192,256]{2,1,0:T(8,128)(2,1)S(1)}, u32[]{:S(2)}, u32[]{:S(2)}) async-start(bf16[8,192,256]{2,1,0:T(8,128)(2,1)} %get-tuple-element.159), calls=%async_computation | async-start | bytes 1572864 | tf_op jit(solution)/shard_map/all_to_all | solution.py:357
  62.0 22.5 %all-to-all-done.refs_1_ = bf16[8,192,256]{2,1,0:T(8,128)(2,1)S(1)} async-done(((bf16[8,192,256]{2,1,0:T(8,128)(2,1)}), bf16[8,192,256]{2,1,0:T(8,128)(2,1)S(1)}, u32[]{:S(2)}, u32[]{:S(2)}) %all-to-all-start) | async-done | bytes 786464 | tf_op jit(solution)/shard_map/all_to_all | solution.py:357
  87.2 8.3 %attend.1 = (bf16[8,64,256]{2,1,0:T(8,128)(2,1)}, f32[8,64,256]{2,1,0:T(8,128)}, f32[8,1,256]{2,1,0:T(1,128)}) custom-call(s32[8]{0:T(128)S(1)} %get-tuple-element.139.refs_0_, bf16[8,192,256]{2,1,0:T(8,128)(2,1)} %copy-done.15), custom_call_target="tpu_custom_call" | custom-call | flops 10000000000 | bytes 8388608 | tf_op jit(solution)/shard_map/attend/pallas_call | solution.py:414
  98.9 15.2 %all_to_all.25 = bf16[8,64,256]{2,1,0:T(8,128)(2,1)} all-to-all(bf16[8,64,256]{2,1,0:T(8,128)(2,1)S(1)} %copy-done.22), channel_id=1, replica_groups=mesh['fsdp'=8,'tp'=4] {'fsdp'}, dimensions={0} | all-to-all | bytes 524288 | tf_op jit(solution)/shard_map/all_to_all | solution.py:357
  114.8 3.1 %mix_out.1 = (bf16[256,1024]{1,0:T(8,128)(2,1)S(1)}, f32[256,1024]{1,0:T(8,128)S(1)}, bf16[256,1024]{1,0:T(8,128)(2,1)S(1)}) custom-call(s32[1]{0:T(128)} %bitcast.25.refs_0_, s32[8]{0:T(128)S(1)} %get-tuple-element.140.refs_0_.refs_1_, bf16[2,256,256]{2,1,0:T(8,128)(2,1)} %bitcast.189, bf16[8,912,128]{2,1,0:T(8,128)(2,1)} %bitcast.202), custom_call_target="tpu_custom_call" | custom-call | flops 3000000000 | bytes 8388608 | tf_op jit(solution)/shard_map/mix_out/pallas_call | solution.py:414
  125.0 11.0 %collective-permute-done.17.refs_4_ = bf16[256,1024]{1,0:T(8,128)(2,1)S(1)} collective-permute-done((bf16[256,1024]{1,0:T(8,128)(2,1)S(1)}, bf16[256,1024]{1,0:T(8,128)(2,1)S(1)}, u32[]{:S(2)}, u32[]{:S(2)}) %collective-permute-start.17) | collective-permute-done | bytes 524320 | tf_op jit(solution)/shard_map/ppermute | solution.py:353
  142.4 9.0 %feed.1 = (bf16[256,1024]{1,0:T(8,128)(2,1)S(1)}, f32[256,1024]{1,0:T(8,128)S(1)}, bf16[512,656]{1,0:T(8,128)(2,1)S(1)}, bf16[512,656]{1,0:T(8,128)(2,1)S(1)}, b...) custom-call(s32[8]{0:T(128)S(1)} %get-tuple-element.140.refs_0_.refs_1_, ...), custom_call_target="tpu_custom_call" | custom-call | flops 8000000000 | bytes 8388608 | tf_op jit(solution)/shard_map/feed/pallas_call | solution.py:414
  154.1 5.2 %feed_grad.1 = bf16[8,1968,128]{2,1,0:T(8,128)(2,1)} custom-call(s32[8]{0:T(128)S(1)} %get-tuple-element.140.refs_0_.refs_1_, bf16[512,656]{1,0:T(8,128)(2,1)S(1)} %get-tuple-element.198.refs_1_, bf16[512,656]{1,0:T(8,128)(2,1)S(1)} %get-tuple-element.199.refs_2_, bf16[512,656]{1,0:T(8,128)(2,1)S(1)} %get-tuple-element.200.refs_3_, ...), custom_call_target="tpu_custom_call" | custom-call | flops 5000000000 | bytes 8388608 | tf_op jit(solution)/shard_map/feed_grad/pallas_call | solution.py:414
  159.4 8.2 %collective-permute-done.20.refs_2_ = bf16[256,1024]{1,0:T(8,128)(2,1)S(1)} collective-permute-done((bf16[256,1024]{1,0:T(8,128)(2,1)S(1)}, bf16[256,1024]{1,0:T(8,128)(2,1)S(1)}, u32[]{:S(2)}, u32[]{:S(2)}) %collective-permute-start.20) | collective-permute-done | bytes 524320 | tf_op jit(solution)/shard_map/ppermute | solution.py:353
  175.9 3.7 %all-to-all-start.2 = ((bf16[8,64,256]{2,1,0:T(8,128)(2,1)}), bf16[8,64,256]{2,1,0:T(8,128)(2,1)S(1)}, u32[]{:S(2)}, u32[]{:S(2)}) async-start(bf16[8,64,256]{2,1,0:T(8,128)(2,1)} %mix_back.1), calls=%async_computation.2 | async-start | bytes 524288 | tf_op jit(solution)/shard_map/all_to_all | solution.py:357
  183.4 13.4 %all-to-all-done.2.refs_4_ = bf16[8,64,256]{2,1,0:T(8,128)(2,1)S(1)} async-done(((bf16[8,64,256]{2,1,0:T(8,128)(2,1)}), bf16[8,64,256]{2,1,0:T(8,128)(2,1)S(1)}, u32[]{:S(2)}, u32[]{:S(2)}) %all-to-all-start.2) | async-done | bytes 262176 | tf_op jit(solution)/shard_map/all_to_all | solution.py:357
  199.7 11.4 %attend_back.1 = bf16[8,192,256]{2,1,0:T(8,128)(2,1)} custom-call(s32[8]{0:T(128)S(1)} %get-tuple-element.139.refs_0_, bf16[8,192,256]{2,1,0:T(8,128)(2,1)} %copy-done.15, f32[8,64,256]{2,1,0:T(8,128)} %get-tuple-element.160.refs_2_, f32[8,1,256]{2,1,0:T(1,128)} %get-tuple-element.161.refs_3_, bf16[8,64,256]{2,1,0:T(8,128)(2,1)} %copy-done.23, ...), custom_call_target="tpu_custom_call" | custom-call | flops 28000000000 | bytes 8388608 | tf_op jit(solution)/shard_map/attend_back/pallas_call | solution.py:414
  211.1 6.2 %all-to-all-start.3 = ((bf16[8,192,256]{2,1,0:T(8,128)(2,1)}), bf16[8,192,256]{2,1,0:T(8,128)(2,1)S(1)}, u32[]{:S(2)}, u32[]{:S(2)}) async-start(bf16[8,192,256]{2,1,0:T(8,128)(2,1)} %attend_back.1), calls=%async_computation.3 | async-start | bytes 1572864 | tf_op jit(solution)/shard_map/all_to_all | solution.py:357
  217.4 3.5 %result.1 = bf16[128,1024]{1,0:T(8,128)(2,1)} custom-call(s32[8]{0:T(128)S(1)} %get-tuple-element.140.refs_0_.refs_1_, s32[1,128]{1,0:T(1,128)S(1)} %reshape.272.refs_1_, f32[256,1024]{1,0:T(8,128)} %copy-done.3, bf16[256,1024]{1,0:T(8,128)(2,1)} %copy-done.19, bf16[256,1024]{1,0:T(8,128)(2,1)} %copy-done.30), custom_call_target="tpu_custom_call" | custom-call | flops 3000000000 | bytes 8388608 | tf_op jit(solution)/shard_map/result/pallas_call | solution.py:414
  222.7 14.4 %all-to-all-done.3 = bf16[8,192,256]{2,1,0:T(8,128)(2,1)S(1)} async-done(((bf16[8,192,256]{2,1,0:T(8,128)(2,1)}), bf16[8,192,256]{2,1,0:T(8,128)(2,1)S(1)}, u32[]{:S(2)}, u32[]{:S(2)}) %all-to-all-start.3) | async-done | bytes 786464 | tf_op jit(solution)/shard_map/all_to_all | solution.py:357
  237.9 3.9 %project_back.1 = (bf16[4,768,128]{2,1,0:T(8,128)(2,1)S(1)}, f32[4,768,128]{2,1,0:T(8,128)}, bf16[256,1024]{1,0:T(8,128)(2,1)S(1)}, f32[256,1024]{1,0:T(8,128)S(1)}) custom-call(s32[1]{0:T(128)} %bitcast.25.refs_0_, bf16[2,768,256]{2,1,0:T(8,128)(2,1)} %bitcast.186, bf16[512,1024]{1,0:T(8,128)(2,1)} %get-tuple-element.225.refs_2_, ...), custom_call_target="tpu_custom_call" | custom-call | flops 3000000000 | bytes 8388608 | tf_op jit(solution)/shard_map/project_back/pallas_call | solution.py:414
  244.8 4.1 %all-to-all-start.4 = ((bf16[8,16,1024]{2,1,0:T(8,128)(2,1)}), bf16[8,16,1024]{2,1,0:T(8,128)(2,1)}, u32[]{:S(2)}, u32[]{:S(2)}) async-start(bf16[8,16,1024]{2,1,0:T(8,128)(2,1)} %bitcast.191), calls=%async_computation.4 | async-start | bytes 524288 | tf_op jit(solution)/shard_map/all_to_all | solution.py:357
  253.3 11.6 %all-to-all-done.4 = bf16[8,16,1024]{2,1,0:T(8,128)(2,1)} async-done(((bf16[8,16,1024]{2,1,0:T(8,128)(2,1)}), bf16[8,16,1024]{2,1,0:T(8,128)(2,1)}, u32[]{:S(2)}, u32[]{:S(2)}) %all-to-all-start.4) | async-done | bytes 262176 | tf_op jit(solution)/shard_map/all_to_all | solution.py:357
  267.3 3.1 %norm_one_back.1 = bf16[256,1024]{1,0:T(8,128)(2,1)S(1)} custom-call(s32[1]{0:T(128)} %bitcast.25.refs_0_, s32[8]{0:T(128)S(1)} %get-tuple-element.140.refs_0_.refs_1_, bf16[2,256,1024]{2,1,0:T(8,128)(2,1)} %refs_2_.3, bf16[256,1024]{1,0:T(8,128)(2,1)S(1)} %add_convert_fusion.refs_3_, bf16[256,1024]{1,0:T(8,128)(2,1)S(1)} %collective-permute-done.27.refs_4_, ...), custom_call_target="tpu_custom_call" | custom-call | flops 3000000000 | bytes 8388608 | tf_op jit(solution)/shard_map/norm_one_back/pallas_call | solution.py:414
  283.3 6.3 %collective-permute-done.32 = bf16[768,128]{1,0:T(8,128)(2,1)S(1)} collective-permute-done((bf16[768,128]{1,0:T(8,128)(2,1)S(1)}, bf16[768,128]{1,0:T(8,128)(2,1)S(1)}, u32[]{:S(2)}, u32[]{:S(2)}) %collective-permute-start.32) | collective-permute-done | bytes 196640 | tf_op jit(solution)/shard_map/ppermute | solution.py:345
  (238 shorter events, 94.8 us)
Async XLA Ops:
  7.2 106.8 %all-gather.5.cloned.1.call-start = ((), (), s32[]{:S(2)}) async-start(), calls=%async_computation.7 | async-start | bytes 2101248 | tf_op jit(solution)/shard_map/all_gather | solution.py:904
  9.4 29.0 %collective-permute-start.3 = (bf16[784,128]{1,0:T(8,128)(2,1)S(1)}, bf16[784,128]{1,0:T(8,128)(2,1)S(1)}, u32[]{:S(2)}, u32[]{:S(2)}) collective-permute-start(bf16[784,128]{1,0:T(8,128)(2,1)S(1)} %maximum_maximum_fusion.refs_3_), channel_id=1, source_target_pairs={{0,4},{4,0},{8,12},{12,8},{16,20},{20,16},{24,28},{28,24},{1,5},{5... | collective-permute-start | bytes 602120 | tf_op jit(solution)/shard_map/ppermute | solution.py:345
  16.0 19.5 %collective-permute-start.1 = (bf16[784,128]{1,0:T(8,128)(2,1)S(1)}, bf16[784,128]{1,0:T(8,128)(2,1)S(1)}, u32[]{:S(2)}, u32[]{:S(2)}) collective-permute-start(bf16[784,128]{1,0:T(8,128)(2,1)S(1)} %maximum_maximum_fusion.refs_3_), channel_id=1, source_target_pairs={{0,16},{4,20},{8,24},{12,28},{16,0},{20,4},{24,8},{28,12},{1,17},{... | collective-permute-start | bytes 602120 | tf_op jit(solution)/shard_map/ppermute | solution.py:345
  16.0 19.5 %collective-permute-start = (bf16[784,128]{1,0:T(8,128)(2,1)S(1)}, bf16[784,128]{1,0:T(8,128)(2,1)S(1)}, u32[]{:S(2)}, u32[]{:S(2)}) collective-permute-start(bf16[784,128]{1,0:T(8,128)(2,1)S(1)} %maximum_maximum_fusion.refs_3_), channel_id=1, source_target_pairs={{0,8},{4,12},{8,0},{12,4},{16,24},{20,28},{24,16},{28,20},{1,9},{5... | collective-permute-start | bytes 602120 | tf_op jit(solution)/shard_map/ppermute | solution.py:345
  48.9 35.6 %all-to-all-start = ((bf16[8,192,256]{2,1,0:T(8,128)(2,1)}), bf16[8,192,256]{2,1,0:T(8,128)(2,1)S(1)}, u32[]{:S(2)}, u32[]{:S(2)}) async-start(bf16[8,192,256]{2,1,0:T(8,128)(2,1)} %get-tuple-element.159), calls=%async_computation | async-start | bytes 1572864 | tf_op jit(solution)/shard_map/all_to_all | solution.py:357
  54.0 85.2 %all-gather.7.cloned.1.call-start = ((), (), s32[]{:S(2)}) async-start(), calls=%async_computation.8 | async-start | bytes 3022848 | tf_op jit(solution)/shard_map/all_gather | solution.py:905
  54.1 30.4 %collective-permute-start.7 = (bf16[2,8,1024]{2,1,0:T(8,128)(2,1)S(1)}, bf16[2,8,1024]{2,1,0:T(8,128)(2,1)S(1)}, u32[]{:S(2)}, u32[]{:S(2)}) collective-permute-start(bf16[2,8,1024]{2,1,0:T(8,128)(2,1)S(1)} %get-tuple-element.164), channel_id=1, source_target_pairs={{0,8},{4,12},{8,0},{12,4},{16,24},{20,28},{24,16},{28,20},{1,9},{5... | collective-permute-start | bytes 98312 | tf_op jit(solution)/shard_map/ppermute | solution.py:345
  56.1 28.7 %collective-permute-start.8 = (bf16[2,8,1024]{2,1,0:T(8,128)(2,1)S(1)}, bf16[2,8,1024]{2,1,0:T(8,128)(2,1)S(1)}, u32[]{:S(2)}, u32[]{:S(2)}) collective-permute-start(bf16[2,8,1024]{2,1,0:T(8,128)(2,1)S(1)} %get-tuple-element.165), channel_id=1, source_target_pairs={{0,16},{4,20},{8,24},{12,28},{16,0},{20,4},{24,8},{28,12},{1,17},{... | collective-permute-start | bytes 98312 | tf_op jit(solution)/shard_map/ppermute | solution.py:345
  59.3 208.1 %reduce-scatter.2.cloned.1.call-start = ((), (), s32[]{:S(2)}) async-start(), calls=%async_computation.6 | async-start | bytes 4534272 | tf_op jit(solution)/shard_map/reduce_scatter | solution.py:972
  59.3 36.2 %collective-permute-start.9 = (bf16[2,8,1024]{2,1,0:T(8,128)(2,1)S(1)}, bf16[2,8,1024]{2,1,0:T(8,128)(2,1)S(1)}, u32[]{:S(2)}, u32[]{:S(2)}) collective-permute-start(bf16[2,8,1024]{2,1,0:T(8,128)(2,1)S(1)} %get-tuple-element.166), channel_id=1, source_target_pairs={{0,24},{4,28},{8,16},{12,20},{16,8},{20,12},{24,0},{28,4},{1,25},{... | collective-permute-start | bytes 98312 | tf_op jit(solution)/shard_map/ppermute | solution.py:345
  59.5 36.0 %collective-permute-start.10 = (bf16[2,8,1024]{2,1,0:T(8,128)(2,1)S(1)}, bf16[2,8,1024]{2,1,0:T(8,128)(2,1)S(1)}, u32[]{:S(2)}, u32[]{:S(2)}) collective-permute-start(bf16[2,8,1024]{2,1,0:T(8,128)(2,1)S(1)} %get-tuple-element.167), channel_id=1, source_target_pairs={{0,4},{4,0},{8,12},{12,8},{16,20},{20,16},{24,28},{28,24},{1,5},{5... | collective-permute-start | bytes 98312 | tf_op jit(solution)/shard_map/ppermute | solution.py:345
  61.4 34.1 %collective-permute-start.11 = (bf16[2,8,1024]{2,1,0:T(8,128)(2,1)S(1)}, bf16[2,8,1024]{2,1,0:T(8,128)(2,1)S(1)}, u32[]{:S(2)}, u32[]{:S(2)}) collective-permute-start(bf16[2,8,1024]{2,1,0:T(8,128)(2,1)S(1)} %get-tuple-element.168), channel_id=1, source_target_pairs={{0,12},{4,8},{8,4},{12,0},{16,28},{20,24},{24,20},{28,16},{1,13},{... | collective-permute-start | bytes 98312 | tf_op jit(solution)/shard_map/ppermute | solution.py:345
  97.3 16.7 %collective-permute-start.15 = (bf16[2,8,2,8,1024]{4,3,0,1,2:T(8,128)(2,1)S(1)}, bf16[2,8,2,8,1024]{4,3,0,1,2:T(8,128)(2,1)S(1)}, u32[]{:S(2)}, u32[]{:S(2)}) collective-permute-start(bf16[2,8,2,8,1024]{4,3,0,1,2:T(8,128)(2,1)S(1)} %pad_maximum_fusion.3), channel_id=1, source_target_pairs={{0,2},{1,3},{2,0},{3,1},{4,6},{5,7},{6,4},{7,5},{8,10},{9,11},{10,... | collective-permute-start | bytes 1572872 | tf_op jit(solution)/shard_map/ppermute | solution.py:353
  175.9 20.9 %all-to-all-start.2 = ((bf16[8,64,256]{2,1,0:T(8,128)(2,1)}), bf16[8,64,256]{2,1,0:T(8,128)(2,1)S(1)}, u32[]{:S(2)}, u32[]{:S(2)}) async-start(bf16[8,64,256]{2,1,0:T(8,128)(2,1)} %mix_back.1), calls=%async_computation.2 | async-start | bytes 524288 | tf_op jit(solution)/shard_map/all_to_all | solution.py:357
  196.8 14.3 %collective-permute-start.23 = (bf16[4,256,128]{2,1,0:T(8,128)(2,1)S(1)}, bf16[4,256,128]{2,1,0:T(8,128)(2,1)S(1)}, u32[]{:S(2)}, u32[]{:S(2)}) collective-permute-start(bf16[4,256,128]{2,1,0:T(8,128)(2,1)S(1)} %get-tuple-element.214), channel_id=1, source_target_pairs={{0,4},{4,0},{8,12},{12,8},{16,20},{20,16},{24,28},{28,24},{1,5},{5... | collective-permute-start | bytes 786440 | tf_op jit(solution)/shard_map/ppermute | solution.py:345
  211.1 25.9 %all-to-all-start.3 = ((bf16[8,192,256]{2,1,0:T(8,128)(2,1)}), bf16[8,192,256]{2,1,0:T(8,128)(2,1)S(1)}, u32[]{:S(2)}, u32[]{:S(2)}) async-start(bf16[8,192,256]{2,1,0:T(8,128)(2,1)} %attend_back.1), calls=%async_computation.3 | async-start | bytes 1572864 | tf_op jit(solution)/shard_map/all_to_all | solution.py:357
  242.0 22.9 %collective-permute-start.25 = (bf16[4,768,128]{2,1,0:T(8,128)(2,1)S(1)}, bf16[4,768,128]{2,1,0:T(8,128)(2,1)}, u32[]{:S(2)}, u32[]{:S(2)}) collective-permute-start(bf16[4,768,128]{2,1,0:T(8,128)(2,1)S(1)} %get-tuple-element.228), channel_id=1, source_target_pairs={{0,4},{4,0},{8,12},{12,8},{16,20},{20,16},{24,28},{28,24},{1,5},{5... | collective-permute-start | bytes 2359304 | tf_op jit(solution)/shard_map/ppermute | solution.py:345
  244.0 20.8 %collective-permute-start.27 = (bf16[256,1024]{1,0:T(8,128)(2,1)S(1)}, bf16[256,1024]{1,0:T(8,128)(2,1)S(1)}, u32[]{:S(2)}, u32[]{:S(2)}) collective-permute-start(bf16[256,1024]{1,0:T(8,128)(2,1)S(1)} %add_convert_fusion.refs_3_), channel_id=1, source_target_pairs={{0,2},{1,3},{2,0},{3,1},{4,6},{5,7},{6,4},{7,5},{8,10},{9,11},{10,... | collective-permute-start | bytes 1572872 | tf_op jit(solution)/shard_map/ppermute | solution.py:353
  244.8 20.1 %all-to-all-start.4 = ((bf16[8,16,1024]{2,1,0:T(8,128)(2,1)}), bf16[8,16,1024]{2,1,0:T(8,128)(2,1)}, u32[]{:S(2)}, u32[]{:S(2)}) async-start(bf16[8,16,1024]{2,1,0:T(8,128)(2,1)} %bitcast.191), calls=%async_computation.4 | async-start | bytes 524288 | tf_op jit(solution)/shard_map/all_to_all | solution.py:357
  248.8 18.4 %collective-permute-start.28 = (bf16[256,128]{1,0:T(8,128)(2,1)S(1)}, bf16[256,128]{1,0:T(8,128)(2,1)S(1)}, u32[]{:S(2)}, u32[]{:S(2)}) collective-permute-start(bf16[256,128]{1,0:T(8,128)(2,1)S(1)} %get-tuple-element.238), channel_id=1, source_target_pairs={{0,8},{4,12},{8,0},{12,4},{16,24},{20,28},{24,16},{28,20},{1,9},{5... | collective-permute-start | bytes 196616 | tf_op jit(solution)/shard_map/ppermute | solution.py:345
  250.7 16.6 %collective-permute-start.29 = (bf16[256,128]{1,0:T(8,128)(2,1)S(1)}, bf16[256,128]{1,0:T(8,128)(2,1)S(1)}, u32[]{:S(2)}, u32[]{:S(2)}) collective-permute-start(bf16[256,128]{1,0:T(8,128)(2,1)S(1)} %get-tuple-element.239), channel_id=1, source_target_pairs={{0,16},{4,20},{8,24},{12,28},{16,0},{20,4},{24,8},{28,12},{1,17},{... | collective-permute-start | bytes 196616 | tf_op jit(solution)/shard_map/ppermute | solution.py:345
  253.1 14.2 %collective-permute-start.30 = (bf16[256,128]{1,0:T(8,128)(2,1)S(1)}, bf16[256,128]{1,0:T(8,128)(2,1)S(1)}, u32[]{:S(2)}, u32[]{:S(2)}) collective-permute-start(bf16[256,128]{1,0:T(8,128)(2,1)S(1)} %get-tuple-element.240), channel_id=1, source_target_pairs={{0,24},{4,28},{8,16},{12,20},{16,8},{20,12},{24,0},{28,4},{1,25},{... | collective-permute-start | bytes 196616 | tf_op jit(solution)/shard_map/ppermute | solution.py:345
  272.6 17.1 %collective-permute-start.32 = (bf16[768,128]{1,0:T(8,128)(2,1)S(1)}, bf16[768,128]{1,0:T(8,128)(2,1)S(1)}, u32[]{:S(2)}, u32[]{:S(2)}) collective-permute-start(bf16[768,128]{1,0:T(8,128)(2,1)S(1)} %get-tuple-element.242), channel_id=1, source_target_pairs={{0,16},{4,20},{8,24},{12,28},{16,0},{20,4},{24,8},{28,12},{1,17},{... | collective-permute-start | bytes 589832 | tf_op jit(solution)/shard_map/ppermute | solution.py:345
  275.0 14.7 %collective-permute-start.33 = (bf16[768,128]{1,0:T(8,128)(2,1)S(1)}, bf16[768,128]{1,0:T(8,128)(2,1)S(1)}, u32[]{:S(2)}, u32[]{:S(2)}) collective-permute-start(bf16[768,128]{1,0:T(8,128)(2,1)S(1)} %get-tuple-element.243), channel_id=1, source_target_pairs={{0,24},{4,28},{8,16},{12,20},{16,8},{20,12},{24,0},{28,4},{1,25},{... | collective-permute-start | bytes 589832 | tf_op jit(solution)/shard_map/ppermute | solution.py:345
  (55 other events, 338.8 us)
Sparse Core Ops, SparseCore 0:
  19.5 63.5 all-gather.4
  85.9 53.0 all-gather.6
  159.5 97.8 reduce-scatter.1

commit v6 on v5

--- a/solution.py
+++ b/solution.py
@@ -324,7 +324,7 @@
 
 
 JOIN = 2
-COSTS = {"attend": 10, "attend_back": 28, "feed": 8, "feed_grad": 5}
+COSTS = {"attend": 10, "attend_back": 28, "feed": 8, "norm_one_back": 0, "qkv_near": 0, "feed_grad": 5}
 FAR = -1e30
 ORDER = (0, 2, 4, 6, 1, 3, 5, 7)
 NT = (((1,), (1,)), ((), ()))
@@ -373,7 +373,7 @@
     return [hop(one, 1) for one in shards]
 
 
-def local_call(kernel, name, scalars, arrays, outs, scratch=(), shards=(), copies=8, far_in=(), far_out=(), far_shards=True):
+def local_call(kernel, name, scalars, arrays, outs, scratch=(), shards=(), copies=8, far_in=(), far_out=(), far_shards=True, raw_out=()):
     shapes = [(one.shape, one.dtype) for one in arrays]
     staged = [shapes[at] for at in far_in] + [outs[at] for at in far_out]
     sems = [pltpu.SemaphoreType.DMA((copies,))] if shards else []
@@ -416,9 +416,9 @@
         in_specs=[pl.BlockSpec(memory_space=pltpu.SMEM)] * len(scalars)
         + [space(at, far_in) for at in range(len(arrays))]
         + [pl.BlockSpec(memory_space=pltpu.HBM if far_shards else pl.ANY)] * len(shards),
-        out_specs=[space(at, far_out) for at in range(len(outs))],
+        out_specs=[space(at, (*far_out, *raw_out)) for at in range(len(outs))],
         out_shape=[
-            pltpu.HBM(shape, kind) if at in far_out else jax.ShapeDtypeStruct(shape, kind)
+            pltpu.HBM(shape, kind) if at in (*far_out, *raw_out) else jax.ShapeDtypeStruct(shape, kind)
             for at, (shape, kind) in enumerate(outs)
         ],
         scratch_shapes=[pltpu.VMEM(shape, kind) for shape, kind in scratch]
@@ -469,13 +469,15 @@
 
 def project_kernel(order_ref, x_ref, table_ref, *refs):
     shards = refs[:8]
-    norm_ref, gains_ref, send_ref, w_ref, sem_ref = refs[8:]
+    norm_out_ref, gains_ref, send_ref, w_out_ref, norm_ref, w_ref, sem_ref = refs[8:]
     width = shards[0].shape[1]
     rows = x_ref.shape[1]
     wide = w_ref.shape[0] - 16
     heads = wide // (3 * HD)
     half = HD // 2
     finish(shard_copies(shards, 0, wide + 16, w_ref, sem_ref))
+    outgoing = [pltpu.make_async_copy(w_ref, w_out_ref, sem_ref.at[8]), pltpu.make_async_copy(norm_ref, norm_out_ref, sem_ref.at[9])]
+    outgoing[0].start()
     gains_ref[...] = w_ref[wide:, :].astype(jnp.float32)[:2]
     for micro in range(2):
         x = x_ref[micro].astype(jnp.float32)
@@ -487,6 +489,7 @@
             span = slice(place * width, (place + 1) * width)
             value = (piece - mean) * spread * gains_ref[0:1, span]
             norm_ref[micro * rows : (micro + 1) * rows, span] = value.astype(jnp.bfloat16)
+    outgoing[1].start()
     raw = mm(w_ref[:wide, :], norm_ref[...], NT)
     cosine, sine = table_ref[:half, :], table_ref[half:, :]
     for head in range(heads):
@@ -503,6 +506,7 @@
         value = raw[base + 2 * HD : base + 3 * HD].astype(jnp.bfloat16)
         for micro in range(2):
             send_ref[micro * heads + head, 2 * HD :, :] = value[:, micro * rows : (micro + 1) * rows]
+    finish(outgoing)
 
 
 def key_range(lens_ref, low, high):
@@ -668,19 +672,26 @@
 
 
 def feed_kernel(
-    order_ref, own_ref, other_ref, grad_ref, all_ref, down_ref,
-    send_ref, keep_ref, act_ref, dinp_ref, dgate_ref, result_send_ref, result_keep_ref, w_ref, sem_ref
+    order_ref, own_ref, other_ref, all_ref, down_ref, source_ref,
+    send_ref, keep_ref, act_ref, dinp_ref, dgate_ref, result_send_ref, result_keep_ref, w_ref, grad_ref, sem_ref
 ):
     units = w_ref.shape[0] // 3
     inp_w, gate_w, down_w = [w_ref.at[pl.ds(at * units, units), :] for at in range(3)]
     rows = own_ref.shape[0]
-    first_copies = gathered_copies(order_ref, all_ref, 0, 2 * units, w_ref.at[pl.ds(0, 2 * units), :], sem_ref)
-    finish(gathered_copies(order_ref, down_ref, 0, units, down_w, sem_ref, 8))
-    finish(first_copies)
+    inp_copies = gathered_copies(order_ref, all_ref, 0, units, inp_w, sem_ref)
+    grad_copy = pltpu.make_async_copy(source_ref, grad_ref, sem_ref.at[24])
+    grad_copy.start()
+    gate_copies = gathered_copies(order_ref, all_ref, units, 2 * units, gate_w, sem_ref, 16)
+    down_copies = gathered_copies(order_ref, down_ref, 0, units, down_w, sem_ref, 8)
+    finish(inp_copies)
     for micro, norm_ref in ((1, other_ref), (0, own_ref)):
         span = slice(micro * rows, (micro + 1) * rows)
         inp = mm(norm_ref[...], inp_w[...], NT)
+        if micro:
+            finish(gate_copies)
         gate = mm(norm_ref[...], gate_w[...], NT)
+        if micro:
+            finish(down_copies + [grad_copy])
         dact = mm(grad_ref[micro], down_w[...], NT)
         cdf = 0.5 * (1.0 + lax.erf(inp * (0.5**0.5)))
         density = jnp.exp(-0.5 * inp * inp) * ((0.5 / jnp.pi) ** 0.5)
@@ -716,8 +727,7 @@
             out_ref[order_ref[place], at * units : (at + 1) * units, :] = piece
 
 
-def near_sum_kernel(near_ref, far_ref, own_ref, *low_refs):
-    own_ref[...] = near_ref[0] + far_ref[0].astype(jnp.float32)
+def near_sum_kernel(near_ref, far_ref, *low_refs):
     for at, low_ref in enumerate(low_refs):
         low_ref[...] = (near_ref[at + 1] + far_ref[at + 1].astype(jnp.float32)).astype(jnp.bfloat16)
 
@@ -817,6 +827,27 @@
     packed_ref[...] = mm(onehot, natural_ref[...], TN).astype(jnp.bfloat16)
 
 
+def join_kernel(
+    core_ref, side_ref, place_ref, own_ref, far_ref, near_ref, cross_ref, input_own_ref, input_other_ref,
+    output_ref, input_ref,
+):
+    rows = output_ref.shape[1]
+    count = own_ref.shape[0]
+    halfway = count // 8
+    core, side = core_ref[0], side_ref[0]
+    row = lax.broadcasted_iota(jnp.int32, (count, rows), 0)
+    row = (row // halfway) * (2 * halfway) + row % halfway
+    for micro, pieces in ((core, (own_ref, far_ref)), (1 - core, (near_ref, cross_ref))):
+        total = jnp.zeros((rows, output_ref.shape[2]), jnp.float32)
+        for half, piece in ((side, pieces[0]), (1 - side, pieces[1])):
+            wanted = place_ref[pl.ds(micro, 1), :] - half * halfway
+            onehot = jnp.where(row == wanted, 1.0, 0.0).astype(jnp.bfloat16)
+            total = total + mm(onehot, piece[...], TN)
+        output_ref[micro] = total.astype(jnp.bfloat16)
+    input_ref[core] = input_own_ref[...]
+    input_ref[1 - core] = input_other_ref[...]
+
+
 def positions(anchor, seq_lens):
     ends = running_ends(seq_lens)
     starts = ends - seq_lens
@@ -838,6 +869,7 @@
     part = lax.axis_index("tp")
     core, side = part & 1, part >> 1
     core_at = core.reshape(1).astype(i32)
+    side_at = side.reshape(1).astype(i32)
     rows = tokens.shape[1]
     width = w_qkv.shape[0]
     full = 8 * width
@@ -850,19 +882,13 @@
     def pick(value, index):
         return lax.dynamic_index_in_dim(value, index, 0, keepdims=False)
 
-    def both(value, other):
-        return jnp.stack([jnp.where(core == 0, value, other), jnp.where(core == 0, other, value)])
-
     def add_half(keep, got):
         return (keep + got.astype(f32)).astype(bf16)
 
     def near_sum(near, far, name):
         shape = near.shape[1:]
-        own, *lows = local_call(near_sum_kernel, name, (), (near, far), [(shape, f32)] + [(shape, bf16)] * 3, far_in=(0, 1), far_out=(0,))
-        return own, lows
-
-    def y_join(same):
-        return same + [hop(jnp.concatenate(same, axis=0), 1)]
+        lows = local_call(near_sum_kernel, name, (), (near, far), [(shape, bf16)] * 3, far_in=(0, 1))
+        return near[0] + far[0].astype(f32), lows
 
     def z_send(lows):
         return [hop(low, ORDER[at + 1]) for at, low in enumerate(lows)]
@@ -905,19 +931,19 @@
     third_all = lax.all_gather(jnp.concatenate([inp_turned, gate_turned], axis=0), "fsdp", axis=0, tiled=False)
     halfway = per_pair // 2
     picks = lax.dynamic_slice_in_dim(pick(local, core), side * halfway, halfway, 1).reshape(1, -1)
-    unpack = (place_own[:, :, None] == slot_no[None, None, :]).astype(bf16)
     my_lens = lengths[mine // heads]
     all_anchor = jnp.arange(8 * rows, dtype=i32)
     table = turn_tables(positions(all_anchor, my_lens))
     table = jnp.transpose(table.reshape(HD, 8, rows), (1, 0, 2))
-    first, packed, own_table, picks, unpack, table, local_own, order, core_at, core, side, my_lens = sync(
-        (first, packed, own_table, picks, unpack, table, local_own, order, core_at, core, side, my_lens)
+    first, packed, own_table, picks, place_own, side_at, table, local_own, order, core_at, core, side, my_lens = sync(
+        (first, packed, own_table, picks, place_own, side_at, table, local_own, order, core_at, core, side, my_lens)
     )
 
     norm_one, gains, outgoing, qkv_w = local_call(
         project_kernel, "project", (order,), (tokens, own_table),
         [((2 * rows, full), bf16), ((2, full), f32), ((2 * heads, 3 * HD, rows), bf16), ((3 * cols + 16, full), bf16)],
-        (), first, far_in=(0, 1), far_out=(0, 1, 2, 3), far_shards=False,
+        [((2 * rows, full), bf16), ((3 * cols + 16, full), bf16)], first, copies=10,
+        far_in=(0, 1), far_out=(1, 2), far_shards=False, raw_out=(0, 3),
     )
     outgoing, packed = sync((outgoing, packed))
     qkv = deal_out(outgoing)
@@ -944,23 +970,23 @@
 
     send, keep, out_w = local_call(
         mix_out_kernel, "mix_out", (core_at, order), (mixed,),
-        [((rows, full), bf16), ((rows, full), f32), ((cols, full), bf16)], (), (second_all,), far_in=(0,),
+        [((rows, full), bf16), ((rows, full), f32), ((cols, full), bf16)], (), (second_all,), far_in=(0,), far_out=(2,),
     )
     half = add_half(keep, twin(send))
     far = across(half)
     far, grad = sync((far, grad))
     hidden, two_own = local_call(
         norm_two_kernel, "norm_two", (core_at, order), (tokens, half, far, gains),
-        [((rows, full), f32), ((rows, full), bf16)], far_in=(0, 3),
+        [((rows, full), f32), ((rows, full), bf16)], far_in=(0, 3), far_out=(0,),
     )
     two_other = twin(two_own)
 
     send, keep, act, d_inp, d_gate, result_send, result_keep = local_call(
-        feed_kernel, "feed", (order,), (two_own, two_other, grad),
+        feed_kernel, "feed", (order,), (two_own, two_other),
         [((rows, full), bf16), ((rows, full), f32)]
         + [((2 * rows, units), bf16)] * 3
         + [((rows, full), bf16), ((rows, full), f32)],
-        [((3 * units, full), bf16)], (third_all, second_all), copies=16, far_out=(5, 6),
+        [((3 * units, full), bf16), ((2, rows, full), bf16)], (third_all, second_all, grad), copies=25, far_out=(5, 6),
     )
     half_two = add_half(keep, twin(send))
     half_two, act, d_inp, d_gate = sync((half_two, act, d_inp, d_gate))
@@ -973,7 +999,7 @@
     far_two, feed_grad = sync((far_two, feed_grad))
     d_hidden, low_own = local_call(
         norm_two_back_kernel, "norm_two_back", (), (hidden, half_two, far_two, grad, gains),
-        [((rows, full), f32), ((rows, full), bf16)], far_in=(4,), far_out=(0,),
+        [((rows, full), f32), ((rows, full), bf16)], far_in=(0, 3, 4), far_out=(0,),
     )
     low_other = twin(low_own)
     d_mixed = local_call(
@@ -989,10 +1015,10 @@
         [((4, cols, width), bf16), ((4, cols, width), f32)], far_in=(0, 1, 2), far_out=(1,),
     )
     res_half = add_half(result_keep, twin(result_send))
-    grad_mixed, out_far, res_half = sync((grad_mixed, out_far, res_half))
-
     out_got = hop(out_far, 1)
     res_far = across(res_half)
+    grad_mixed, out_got, res_far = sync((grad_mixed, out_got, res_far))
+
     d_raw_out = local_call(
         attend_back_kernel, "attend_back", (my_lens,), (qkv, exact, logs, grad_mixed, table),
         [((8, 3 * HD, rows), bf16)],
@@ -1018,28 +1044,28 @@
     far = across(half)
     out_got = z_send(out_lows)
     arrived = deal_out(packed.reshape(8, halfway, full))
-    qkv_got, far, arrived = sync((qkv_got, far, arrived))
-    qkv_own, qkv_lows = near_sum(qkv_near, qkv_got, "qkv_near")
-    qkv_lows, arrived, far, feed_sum, out_got = sync((qkv_lows, arrived, far, feed_sum, out_got))
     input_own = local_call(
         norm_one_back_kernel, "norm_one_back", (core_at, order), (tokens, half, far, d_hidden, gains),
         [((rows, full), bf16)], [((rows, full), f32)], far_in=(0, 3, 4),
     )
-    input_own, feed_sum, out_got = sync((input_own, feed_sum, out_got))
-    input_grad = both(input_own, twin(input_own))
-    out_sum = far_sum(out_own, out_got)
+    qkv_got, input_own, out_got = sync((qkv_got, input_own, out_got))
+    qkv_own, qkv_lows = near_sum(qkv_near, qkv_got, "qkv_near")
+    qkv_lows = sync(qkv_lows)
+    qkv_got = z_send(qkv_lows)
+    qkv_got[0], arrived, input_own, feed_sum = sync((qkv_got[0], arrived, input_own, feed_sum))
+    input_other = twin(input_own)
+    grad_attn_out = jnp.transpose(far_sum(out_own, out_got))
     inp_sum, gate_sum, down_sum = [feed_sum[at * units : (at + 1) * units].astype(f32) for at in range(3)]
     two_row = jnp.sum(inp_sum * inp_turned.astype(f32) + gate_sum * gate_turned.astype(f32), axis=0)
-    grad_attn_out = jnp.transpose(out_sum)
     grad_in = jnp.stack([jnp.transpose(inp_sum), jnp.transpose(gate_sum)], axis=1)
     grad_down = jnp.transpose(down_sum)
+    arrived = arrived.reshape(8 * halfway, full)
     other_side = across(arrived)
-    whole = jnp.concatenate(
-        [jnp.where(side == 0, arrived, other_side), jnp.where(side == 0, other_side, arrived)], axis=1
-    ).reshape(rows, full)
-    whole = both(whole, twin(whole))
-    output = jnp.einsum("msp,mpd->msd", unpack, whole, preferred_element_type=f32).astype(bf16)
-    qkv_got = z_send(qkv_lows)
+    output, input_grad = local_call(
+        join_kernel, "join", (core_at, side_at),
+        (place_own, arrived, other_side, twin(arrived), twin(other_side), input_own, input_other),
+        [((2, rows, full), bf16), ((2, rows, full), bf16)],
+    )
     qkv_got, output, input_grad, grad_attn_out, grad_in, grad_down, two_row = sync(
         (qkv_got, output, input_grad, grad_attn_out, grad_in, grad_down, two_row)
     )

time: 304 us -> 298 us (0.980)
  Pallas kernels: 66.9 us -> 77.1 us
  waiting for transfers between devices: 115 us -> 107 us
  local copies, waits for them, and re-layouts: 13.1 us -> 7.59 us
    all_to_all x4, waiting for transfers between devices: 61.8 us -> 38.5 us  [deal_out(): return lax.all_to_all(value, 'fsdp', 0, 0, tiled=True)]
    ppermute x22, waiting for transfers between devices: 21.9 us -> 35 us  [hop(): return lax.ppermute(value, 'fsdp', [(i, i ^ step) for i in range(8)])]
    pallas_call x16 -> x17, Pallas kernels: 66.9 us -> 77.1 us  [local_call(): pl.pallas_call(body, in_specs=[pl.BlockSpec(memory_space=pltpu.SMEM)] * l...]
    unnamed x78 -> x68, local copies, waits for them, and re-layouts: 12.1 us -> 6.57 us
    ppermute x10 -> x11, waiting for transfers between devices: 9.57 us -> 9.03 us  [twin(): return lax.ppermute(value, 'tp', [(i, i ^ 1) for i in range(4)])]
  transfers between devices with their start and end apart: 47 -> 48, of which waited for: 18 -> 23; matrix products, arithmetic and copies ran while one was open for 6% -> 6% of each run, Pallas kernels for 18% -> 23%
where the time goes in v6:
time: 298 us; the launch traced here: 297 us
  waiting for transfers between devices  107 us (36%)
  Pallas kernels  77.1 us (26%)
  starting transfers between devices  61 us (20%)
  other arithmetic  16.8 us (6%)
  between operations  14.6 us (5%)
  blocking collectives  12.5 us (4%)
  local copies, waits for them, and re-layouts  7.59 us (3%)
    pallas_call x17, Pallas kernels, local_call(): pl.pallas_call(body, in_specs=[pl.BlockSpec(memory_space=pltpu.SMEM)] * l...  77.1 us
    all_to_all x4, waiting for transfers between devices, deal_out(): return lax.all_to_all(value, 'fsdp', 0, 0, tiled=True)  38.5 us
    ppermute x22, waiting for transfers between devices, hop(): return lax.ppermute(value, 'fsdp', [(i, i ^ step) for i in range(8)])  35 us
    ppermute x22, starting transfers between devices, hop(): return lax.ppermute(value, 'fsdp', [(i, i ^ step) for i in range(8)])  32 us
    ppermute x7, waiting for transfers between devices, across(): return lax.ppermute(value, 'tp', [(i, i ^ 2) for i in range(4)])  22.9 us
    all_to_all x4, starting transfers between devices, deal_out(): return lax.all_to_all(value, 'fsdp', 0, 0, tiled=True)  16.9 us
    all_to_all x1, blocking collectives, deal_out(): return lax.all_to_all(value, 'fsdp', 0, 0, tiled=True)  12.5 us
    ppermute x7, starting transfers between devices, across(): return lax.ppermute(value, 'tp', [(i, i ^ 2) for i in range(4)])  9.83 us
  transfers between devices with their start and end apart: 48, of which 23 were waited for; matrix products, arithmetic and copies ran while one was open for 6% of the time, Pallas kernels for 23%

profile of v6, /device:TPU:0, one launch (start us, length us, event | category | flops | bytes accessed | tf_op | source)
XLA Modules:
  0.0 297.0 jit_solution(16556725209092003516)
XLA Ops:
  12.4 3.6 %collective-permute-start.2 = (bf16[784,128]{1,0:T(8,128)(2,1)S(1)}, bf16[784,128]{1,0:T(8,128)(2,1)S(1)}, u32[]{:S(2)}, u32[]{:S(2)}) collective-permute-start(bf16[784,128]{1,0:T(8,128)(2,1)S(1)} %maximum_maximum_fusion.refs_3_), channel_id=1, source_target_pairs={{0,24},{4,28},{8,16},{12,20},{16,8},{20,12},{24,0},{28,4},{1,25},{... | collective-permute-start | bytes 602120 | tf_op jit(solution)/shard_map/ppermute | solution.py:345
  25.0 10.5 %collective-permute-done.1.refs_5_ = bf16[784,128]{1,0:T(8,128)(2,1)S(1)} collective-permute-done((bf16[784,128]{1,0:T(8,128)(2,1)S(1)}, bf16[784,128]{1,0:T(8,128)(2,1)S(1)}, u32[]{:S(2)}, u32[]{:S(2)}) %collective-permute-start.1) | collective-permute-done | bytes 200736 | tf_op jit(solution)/shard_map/ppermute | solution.py:345
  37.6 3.7 %collective-permute-done.5.refs_9_ = bf16[784,128]{1,0:T(8,128)(2,1)S(1)} collective-permute-done((bf16[784,128]{1,0:T(8,128)(2,1)S(1)}, bf16[784,128]{1,0:T(8,128)(2,1)S(1)}, u32[]{:S(2)}, u32[]{:S(2)}) %collective-permute-start.5) | collective-permute-done | bytes 200736 | tf_op jit(solution)/shard_map/ppermute | solution.py:345
  43.4 5.3 %project.1 = (bf16[512,1024]{1,0:T(8,128)(2,1)}, f32[2,1024]{1,0:T(2,128)}, bf16[8,192,256]{2,1,0:T(8,128)(2,1)}, bf16[784,1024]{1,0:T(8,128)(2,1)}) custom-call(s32[8]{0:T(128)S(1)} %get-tuple-element.133.refs_0_.refs_1_, bf16[2,256,1024]{2,1,0:T(8,128)(2,1)} %refs_2_.3, f32[64,512]{1,0:T(8,128)} %maximum_maximum_fusion.1.refs_2_, ...), custom_call_target="tpu_custom_call" | custom-call | flops 3000000000 | bytes 8388608 | tf_op jit(solution)/shard_map/project/pallas_call | solution.py:414
  48.7 5.0 %all-to-all-start = ((bf16[8,192,256]{2,1,0:T(8,128)(2,1)}), bf16[8,192,256]{2,1,0:T(8,128)(2,1)S(1)}, u32[]{:S(2)}, u32[]{:S(2)}) async-start(bf16[8,192,256]{2,1,0:T(8,128)(2,1)} %get-tuple-element.152), calls=%async_computation | async-start | bytes 1572864 | tf_op jit(solution)/shard_map/all_to_all | solution.py:357
  61.8 22.8 %all-to-all-done.refs_1_ = bf16[8,192,256]{2,1,0:T(8,128)(2,1)S(1)} async-done(((bf16[8,192,256]{2,1,0:T(8,128)(2,1)}), bf16[8,192,256]{2,1,0:T(8,128)(2,1)S(1)}, u32[]{:S(2)}, u32[]{:S(2)}) %all-to-all-start) | async-done | bytes 786464 | tf_op jit(solution)/shard_map/all_to_all | solution.py:357
  87.2 11.0 %attend.1 = (bf16[8,64,256]{2,1,0:T(8,128)(2,1)}, f32[8,64,256]{2,1,0:T(8,128)}, f32[8,1,256]{2,1,0:T(1,128)}) custom-call(s32[8]{0:T(128)S(1)} %get-tuple-element.132.refs_0_, bf16[8,192,256]{2,1,0:T(8,128)(2,1)} %copy-done.11), custom_call_target="tpu_custom_call" | custom-call | flops 10000000000 | bytes 8388608 | tf_op jit(solution)/shard_map/attend/pallas_call | solution.py:414
  101.5 12.5 %all_to_all.25 = bf16[8,64,256]{2,1,0:T(8,128)(2,1)} all-to-all(bf16[8,64,256]{2,1,0:T(8,128)(2,1)S(1)} %copy-done.14), channel_id=1, replica_groups=mesh['fsdp'=8,'tp'=4] {'fsdp'}, dimensions={0} | all-to-all | bytes 524288 | tf_op jit(solution)/shard_map/all_to_all | solution.py:357
  114.1 3.5 %mix_out.1 = (bf16[256,1024]{1,0:T(8,128)(2,1)S(1)}, f32[256,1024]{1,0:T(8,128)S(1)}, bf16[256,1024]{1,0:T(8,128)(2,1)}) custom-call(s32[1]{0:T(128)} %bitcast.26.refs_0_, s32[8]{0:T(128)S(1)} %get-tuple-element.133.refs_0_.refs_1_, bf16[2,256,256]{2,1,0:T(8,128)(2,1)} %bitcast.188, bf16[8,912,128]{2,1,0:T(8,128)(2,1)} %bitcast.200), custom_call_target="tpu_custom_call" | custom-call | flops 3000000000 | bytes 8388608 | tf_op jit(solution)/shard_map/mix_out/pallas_call | solution.py:414
  125.9 9.1 %collective-permute-done.17.refs_4_ = bf16[256,1024]{1,0:T(8,128)(2,1)S(1)} collective-permute-done((bf16[256,1024]{1,0:T(8,128)(2,1)S(1)}, bf16[256,1024]{1,0:T(8,128)(2,1)S(1)}, u32[]{:S(2)}, u32[]{:S(2)}) %collective-permute-start.17) | collective-permute-done | bytes 524320 | tf_op jit(solution)/shard_map/ppermute | solution.py:353
  139.9 9.1 %feed.1 = (bf16[256,1024]{1,0:T(8,128)(2,1)S(1)}, f32[256,1024]{1,0:T(8,128)S(1)}, bf16[512,656]{1,0:T(8,128)(2,1)S(1)}, bf16[512,656]{1,0:T(8,128)(2,1)S(1)}, b...) custom-call(s32[8]{0:T(128)S(1)} %get-tuple-element.133.refs_0_.refs_1_, ...), custom_call_target="tpu_custom_call" | custom-call | flops 8000000000 | bytes 8388608 | tf_op jit(solution)/shard_map/feed/pallas_call | solution.py:414
  152.7 5.2 %feed_grad.1 = bf16[8,1968,128]{2,1,0:T(8,128)(2,1)} custom-call(s32[8]{0:T(128)S(1)} %get-tuple-element.133.refs_0_.refs_1_, bf16[512,656]{1,0:T(8,128)(2,1)S(1)} %get-tuple-element.191.refs_1_, bf16[512,656]{1,0:T(8,128)(2,1)S(1)} %get-tuple-element.192.refs_2_, bf16[512,656]{1,0:T(8,128)(2,1)S(1)} %get-tuple-element.193.refs_3_, ...), custom_call_target="tpu_custom_call" | custom-call | flops 5000000000 | bytes 8388608 | tf_op jit(solution)/shard_map/feed_grad/pallas_call | solution.py:414
  157.9 7.3 %collective-permute-done.20.refs_2_ = bf16[256,1024]{1,0:T(8,128)(2,1)S(1)} collective-permute-done((bf16[256,1024]{1,0:T(8,128)(2,1)S(1)}, bf16[256,1024]{1,0:T(8,128)(2,1)S(1)}, u32[]{:S(2)}, u32[]{:S(2)}) %collective-permute-start.20) | collective-permute-done | bytes 524320 | tf_op jit(solution)/shard_map/ppermute | solution.py:353
  165.2 3.4 %norm_two_back.1 = (f32[256,1024]{1,0:T(8,128)}, bf16[256,1024]{1,0:T(8,128)(2,1)S(1)}) custom-call(f32[256,1024]{1,0:T(8,128)} %get-tuple-element.182.refs_0_.refs_2_, bf16[256,1024]{1,0:T(8,128)(2,1)S(1)} %add_convert_fusion.2.refs_1_, bf16[256,1024]{1,0:T(8,128)(2,1)S(1)} %collective-permute-done.20.refs_2_, bf16[2,256,1024]{2,1,0:T(8,128)(2,1)} %copy-done.3, ...), custom_call_target="tpu_custom_call" | custom-call | flops 3000000000 | bytes 8388608 | tf_op jit(solution)/shard_map/norm_two_back/pallas_call | solution.py:414
  172.0 3.8 %all-to-all-start.2 = ((bf16[8,64,256]{2,1,0:T(8,128)(2,1)}), bf16[8,64,256]{2,1,0:T(8,128)(2,1)S(1)}, u32[]{:S(2)}, u32[]{:S(2)}) async-start(bf16[8,64,256]{2,1,0:T(8,128)(2,1)} %mix_back.1), calls=%async_computation.2 | async-start | bytes 524288 | tf_op jit(solution)/shard_map/all_to_all | solution.py:357
  183.4 10.6 %collective-permute-done.22.refs_1_ = bf16[4,256,128]{2,1,0:T(8,128)(2,1)S(1)} collective-permute-done((bf16[4,256,128]{2,1,0:T(8,128)(2,1)S(1)}, bf16[4,256,128]{2,1,0:T(8,128)(2,1)S(1)}, u32[]{:S(2)}, u32[]{:S(2)}) %collective-permute-start.22) | collective-permute-done | bytes 262176 | tf_op jit(solution)/shard_map/ppermute | solution.py:345
  194.7 15.3 %attend_back.1 = bf16[8,192,256]{2,1,0:T(8,128)(2,1)} custom-call(s32[8]{0:T(128)S(1)} %get-tuple-element.132.refs_0_, bf16[8,192,256]{2,1,0:T(8,128)(2,1)} %copy-done.11, f32[8,64,256]{2,1,0:T(8,128)} %get-tuple-element.153.refs_2_, f32[8,1,256]{2,1,0:T(1,128)} %get-tuple-element.154.refs_3_, bf16[8,64,256]{2,1,0:T(8,128)(2,1)} %copy-done.15, ...), custom_call_target="tpu_custom_call" | custom-call | flops 28000000000 | bytes 8388608 | tf_op jit(solution)/shard_map/attend_back/pallas_call | solution.py:414
  210.1 4.5 %all-to-all-start.3 = ((bf16[8,192,256]{2,1,0:T(8,128)(2,1)}), bf16[8,192,256]{2,1,0:T(8,128)(2,1)S(1)}, u32[]{:S(2)}, u32[]{:S(2)}) async-start(bf16[8,192,256]{2,1,0:T(8,128)(2,1)} %attend_back.1), calls=%async_computation.3 | async-start | bytes 1572864 | tf_op jit(solution)/shard_map/all_to_all | solution.py:357
  214.5 3.5 %result.1 = bf16[128,1024]{1,0:T(8,128)(2,1)} custom-call(s32[8]{0:T(128)S(1)} %get-tuple-element.133.refs_0_.refs_1_, s32[1,128]{1,0:T(1,128)S(1)} %reshape.266.refs_1_, f32[256,1024]{1,0:T(8,128)} %get-tuple-element.182.refs_0_.refs_2_, bf16[256,1024]{1,0:T(8,128)(2,1)} %copy-done.13, bf16[256,1024]{1,0:T(8,128)(2,1)} %copy-done.26), custom_call_target="tpu_custom_call" | custom-call | flops 3000000000 | bytes 8388608 | tf_op jit(solution)/shard_map/result/pallas_call | solution.py:414
  219.2 15.7 %all-to-all-done.3 = bf16[8,192,256]{2,1,0:T(8,128)(2,1)S(1)} async-done(((bf16[8,192,256]{2,1,0:T(8,128)(2,1)}), bf16[8,192,256]{2,1,0:T(8,128)(2,1)S(1)}, u32[]{:S(2)}, u32[]{:S(2)}) %all-to-all-start.3) | async-done | bytes 786464 | tf_op jit(solution)/shard_map/all_to_all | solution.py:357
  235.8 5.0 %project_back.1 = (bf16[4,768,128]{2,1,0:T(8,128)(2,1)}, f32[4,768,128]{2,1,0:T(8,128)}, bf16[256,1024]{1,0:T(8,128)(2,1)S(1)}, f32[256,1024]{1,0:T(8,128)S(1)}) custom-call(s32[1]{0:T(128)} %bitcast.26.refs_0_, bf16[2,768,256]{2,1,0:T(8,128)(2,1)} %bitcast.185, bf16[512,1024]{1,0:T(8,128)(2,1)} %get-tuple-element.218.refs_2_, ...), custom_call_target="tpu_custom_call" | custom-call | flops 3000000000 | bytes 8388608 | tf_op jit(solution)/shard_map/project_back/pallas_call | solution.py:414
  244.1 3.6 %all-to-all-start.4 = ((bf16[8,16,1024]{2,1,0:T(8,128)(2,1)}), bf16[8,16,1024]{2,1,0:T(8,128)(2,1)S(1)}, u32[]{:S(2)}, u32[]{:S(2)}) async-start(bf16[8,16,1024]{2,1,0:T(8,128)(2,1)} %bitcast.50), calls=%async_computation.4 | async-start | bytes 524288 | tf_op jit(solution)/shard_map/all_to_all | solution.py:357
  252.1 4.8 %collective-permute-done.27.refs_4_ = bf16[256,1024]{1,0:T(8,128)(2,1)S(1)} collective-permute-done((bf16[256,1024]{1,0:T(8,128)(2,1)S(1)}, bf16[256,1024]{1,0:T(8,128)(2,1)S(1)}, u32[]{:S(2)}, u32[]{:S(2)}) %collective-permute-start.27) | collective-permute-done | bytes 524320 | tf_op jit(solution)/shard_map/ppermute | solution.py:353
  269.8 4.5 %collective-permute-done.31 = bf16[768,128]{1,0:T(8,128)(2,1)S(1)} collective-permute-done((bf16[768,128]{1,0:T(8,128)(2,1)S(1)}, bf16[768,128]{1,0:T(8,128)(2,1)S(1)}, u32[]{:S(2)}, u32[]{:S(2)}) %collective-permute-start.31) | collective-permute-done | bytes 196640 | tf_op jit(solution)/shard_map/ppermute | solution.py:345
  (224 shorter events, 99.3 us)
Async XLA Ops:
  7.2 106.9 %all-gather.5.cloned.1.call-start = ((), (), s32[]{:S(2)}) async-start(), calls=%async_computation.7 | async-start | bytes 2101248 | tf_op jit(solution)/shard_map/all_gather | solution.py:930
  9.4 28.2 %collective-permute-start.3 = (bf16[784,128]{1,0:T(8,128)(2,1)S(1)}, bf16[784,128]{1,0:T(8,128)(2,1)S(1)}, u32[]{:S(2)}, u32[]{:S(2)}) collective-permute-start(bf16[784,128]{1,0:T(8,128)(2,1)S(1)} %maximum_maximum_fusion.refs_3_), channel_id=1, source_target_pairs={{0,4},{4,0},{8,12},{12,8},{16,20},{20,16},{24,28},{28,24},{1,5},{5... | collective-permute-start | bytes 602120 | tf_op jit(solution)/shard_map/ppermute | solution.py:345
  16.0 19.5 %collective-permute-start.1 = (bf16[784,128]{1,0:T(8,128)(2,1)S(1)}, bf16[784,128]{1,0:T(8,128)(2,1)S(1)}, u32[]{:S(2)}, u32[]{:S(2)}) collective-permute-start(bf16[784,128]{1,0:T(8,128)(2,1)S(1)} %maximum_maximum_fusion.refs_3_), channel_id=1, source_target_pairs={{0,16},{4,20},{8,24},{12,28},{16,0},{20,4},{24,8},{28,12},{1,17},{... | collective-permute-start | bytes 602120 | tf_op jit(solution)/shard_map/ppermute | solution.py:345
  16.0 19.5 %collective-permute-start = (bf16[784,128]{1,0:T(8,128)(2,1)S(1)}, bf16[784,128]{1,0:T(8,128)(2,1)S(1)}, u32[]{:S(2)}, u32[]{:S(2)}) collective-permute-start(bf16[784,128]{1,0:T(8,128)(2,1)S(1)} %maximum_maximum_fusion.refs_3_), channel_id=1, source_target_pairs={{0,8},{4,12},{8,0},{12,4},{16,24},{20,28},{24,16},{28,20},{1,9},{5... | collective-permute-start | bytes 602120 | tf_op jit(solution)/shard_map/ppermute | solution.py:345
  48.7 35.8 %all-to-all-start = ((bf16[8,192,256]{2,1,0:T(8,128)(2,1)}), bf16[8,192,256]{2,1,0:T(8,128)(2,1)S(1)}, u32[]{:S(2)}, u32[]{:S(2)}) async-start(bf16[8,192,256]{2,1,0:T(8,128)(2,1)} %get-tuple-element.152), calls=%async_computation | async-start | bytes 1572864 | tf_op jit(solution)/shard_map/all_to_all | solution.py:357
  53.8 85.2 %all-gather.7.cloned.1.call-start = ((), (), s32[]{:S(2)}) async-start(), calls=%async_computation.8 | async-start | bytes 3022848 | tf_op jit(solution)/shard_map/all_gather | solution.py:931
  53.9 30.6 %collective-permute-start.7 = (bf16[2,8,1024]{2,1,0:T(8,128)(2,1)S(1)}, bf16[2,8,1024]{2,1,0:T(8,128)(2,1)S(1)}, u32[]{:S(2)}, u32[]{:S(2)}) collective-permute-start(bf16[2,8,1024]{2,1,0:T(8,128)(2,1)S(1)} %get-tuple-element.157), channel_id=1, source_target_pairs={{0,8},{4,12},{8,0},{12,4},{16,24},{20,28},{24,16},{28,20},{1,9},{5... | collective-permute-start | bytes 98312 | tf_op jit(solution)/shard_map/ppermute | solution.py:345
  55.9 29.0 %collective-permute-start.8 = (bf16[2,8,1024]{2,1,0:T(8,128)(2,1)S(1)}, bf16[2,8,1024]{2,1,0:T(8,128)(2,1)S(1)}, u32[]{:S(2)}, u32[]{:S(2)}) collective-permute-start(bf16[2,8,1024]{2,1,0:T(8,128)(2,1)S(1)} %get-tuple-element.158), channel_id=1, source_target_pairs={{0,16},{4,20},{8,24},{12,28},{16,0},{20,4},{24,8},{28,12},{1,17},{... | collective-permute-start | bytes 98312 | tf_op jit(solution)/shard_map/ppermute | solution.py:345
  59.0 215.3 %reduce-scatter.2.cloned.1.call-start = ((), (), s32[]{:S(2)}) async-start(), calls=%async_computation.6 | async-start | bytes 4534272 | tf_op jit(solution)/shard_map/reduce_scatter | solution.py:998
  59.1 39.1 %collective-permute-start.9 = (bf16[2,8,1024]{2,1,0:T(8,128)(2,1)S(1)}, bf16[2,8,1024]{2,1,0:T(8,128)(2,1)S(1)}, u32[]{:S(2)}, u32[]{:S(2)}) collective-permute-start(bf16[2,8,1024]{2,1,0:T(8,128)(2,1)S(1)} %get-tuple-element.159), channel_id=1, source_target_pairs={{0,24},{4,28},{8,16},{12,20},{16,8},{20,12},{24,0},{28,4},{1,25},{... | collective-permute-start | bytes 98312 | tf_op jit(solution)/shard_map/ppermute | solution.py:345
  59.2 38.9 %collective-permute-start.10 = (bf16[2,8,1024]{2,1,0:T(8,128)(2,1)S(1)}, bf16[2,8,1024]{2,1,0:T(8,128)(2,1)S(1)}, u32[]{:S(2)}, u32[]{:S(2)}) collective-permute-start(bf16[2,8,1024]{2,1,0:T(8,128)(2,1)S(1)} %get-tuple-element.160), channel_id=1, source_target_pairs={{0,4},{4,0},{8,12},{12,8},{16,20},{20,16},{24,28},{28,24},{1,5},{5... | collective-permute-start | bytes 98312 | tf_op jit(solution)/shard_map/ppermute | solution.py:345
  61.2 37.0 %collective-permute-start.11 = (bf16[2,8,1024]{2,1,0:T(8,128)(2,1)S(1)}, bf16[2,8,1024]{2,1,0:T(8,128)(2,1)S(1)}, u32[]{:S(2)}, u32[]{:S(2)}) collective-permute-start(bf16[2,8,1024]{2,1,0:T(8,128)(2,1)S(1)} %get-tuple-element.161), channel_id=1, source_target_pairs={{0,12},{4,8},{8,4},{12,0},{16,28},{20,24},{24,20},{28,16},{1,13},{... | collective-permute-start | bytes 98312 | tf_op jit(solution)/shard_map/ppermute | solution.py:345
  84.5 13.7 %collective-permute-start.12 = (bf16[2,8,1024]{2,1,0:T(8,128)(2,1)S(1)}, bf16[2,8,1024]{2,1,0:T(8,128)(2,1)S(1)}, u32[]{:S(2)}, u32[]{:S(2)}) collective-permute-start(bf16[2,8,1024]{2,1,0:T(8,128)(2,1)S(1)} %get-tuple-element.162), channel_id=1, source_target_pairs={{0,20},{4,16},{8,28},{12,24},{16,4},{20,0},{24,12},{28,8},{1,21},{... | collective-permute-start | bytes 98312 | tf_op jit(solution)/shard_map/ppermute | solution.py:345
  100.0 14.1 %collective-permute-start.15 = (bf16[2,8,2,8,1024]{4,3,0,1,2:T(8,128)(2,1)S(1)}, bf16[2,8,2,8,1024]{4,3,0,1,2:T(8,128)(2,1)}, u32[]{:S(2)}, u32[]{:S(2)}) collective-permute-start(bf16[2,8,2,8,1024]{4,3,0,1,2:T(8,128)(2,1)S(1)} %pad_maximum_fusion.2), channel_id=1, source_target_pairs={{0,2},{1,3},{2,0},{3,1},{4,6},{5,7},{6,4},{7,5},{8,10},{9,11},{10,... | collective-permute-start | bytes 1572872 | tf_op jit(solution)/shard_map/ppermute | solution.py:353
  120.9 14.0 %collective-permute-start.17 = (bf16[256,1024]{1,0:T(8,128)(2,1)S(1)}, bf16[256,1024]{1,0:T(8,128)(2,1)S(1)}, u32[]{:S(2)}, u32[]{:S(2)}) collective-permute-start(bf16[256,1024]{1,0:T(8,128)(2,1)S(1)} %add_convert_fusion.3.refs_3_), channel_id=1, source_target_pairs={{0,2},{1,3},{2,0},{3,1},{4,6},{5,7},{6,4},{7,5},{8,10},{9,11},{10,... | collective-permute-start | bytes 1572872 | tf_op jit(solution)/shard_map/ppermute | solution.py:353
  151.2 14.0 %collective-permute-start.20 = (bf16[256,1024]{1,0:T(8,128)(2,1)S(1)}, bf16[256,1024]{1,0:T(8,128)(2,1)S(1)}, u32[]{:S(2)}, u32[]{:S(2)}) collective-permute-start(bf16[256,1024]{1,0:T(8,128)(2,1)S(1)} %add_convert_fusion.2.refs_1_), channel_id=1, source_target_pairs={{0,2},{1,3},{2,0},{3,1},{4,6},{5,7},{6,4},{7,5},{8,10},{9,11},{10,... | collective-permute-start | bytes 1572872 | tf_op jit(solution)/shard_map/ppermute | solution.py:353
  172.0 22.0 %all-to-all-start.2 = ((bf16[8,64,256]{2,1,0:T(8,128)(2,1)}), bf16[8,64,256]{2,1,0:T(8,128)(2,1)S(1)}, u32[]{:S(2)}, u32[]{:S(2)}) async-start(bf16[8,64,256]{2,1,0:T(8,128)(2,1)} %mix_back.1), calls=%async_computation.2 | async-start | bytes 524288 | tf_op jit(solution)/shard_map/all_to_all | solution.py:357
  177.2 16.8 %collective-permute-start.24 = (bf16[256,1024]{1,0:T(8,128)(2,1)S(1)}, bf16[256,1024]{1,0:T(8,128)(2,1)S(1)}, u32[]{:S(2)}, u32[]{:S(2)}) collective-permute-start(bf16[256,1024]{1,0:T(8,128)(2,1)S(1)} %add_convert_fusion.1.refs_3_), channel_id=1, source_target_pairs={{0,2},{1,3},{2,0},{3,1},{4,6},{5,7},{6,4},{7,5},{8,10},{9,11},{10,... | collective-permute-start | bytes 1572872 | tf_op jit(solution)/shard_map/ppermute | solution.py:353
  210.1 24.8 %all-to-all-start.3 = ((bf16[8,192,256]{2,1,0:T(8,128)(2,1)}), bf16[8,192,256]{2,1,0:T(8,128)(2,1)S(1)}, u32[]{:S(2)}, u32[]{:S(2)}) async-start(bf16[8,192,256]{2,1,0:T(8,128)(2,1)} %attend_back.1), calls=%async_computation.3 | async-start | bytes 1572864 | tf_op jit(solution)/shard_map/all_to_all | solution.py:357
  240.8 22.7 %collective-permute-start.25 = (bf16[4,768,128]{2,1,0:T(8,128)(2,1)}, bf16[4,768,128]{2,1,0:T(8,128)(2,1)}, u32[]{:S(2)}, u32[]{:S(2)}) collective-permute-start(bf16[4,768,128]{2,1,0:T(8,128)(2,1)} %get-tuple-element.221), channel_id=1, source_target_pairs={{0,4},{4,0},{8,12},{12,8},{16,20},{20,16},{24,28},{28,24},{1,5},{5... | collective-permute-start | bytes 2359304 | tf_op jit(solution)/shard_map/ppermute | solution.py:345
  242.9 14.0 %collective-permute-start.27 = (bf16[256,1024]{1,0:T(8,128)(2,1)S(1)}, bf16[256,1024]{1,0:T(8,128)(2,1)S(1)}, u32[]{:S(2)}, u32[]{:S(2)}) collective-permute-start(bf16[256,1024]{1,0:T(8,128)(2,1)S(1)} %add_convert_fusion.refs_3_), channel_id=1, source_target_pairs={{0,2},{1,3},{2,0},{3,1},{4,6},{5,7},{6,4},{7,5},{8,10},{9,11},{10,... | collective-permute-start | bytes 1572872 | tf_op jit(solution)/shard_map/ppermute | solution.py:353
  244.1 25.8 %all-to-all-start.4 = ((bf16[8,16,1024]{2,1,0:T(8,128)(2,1)}), bf16[8,16,1024]{2,1,0:T(8,128)(2,1)S(1)}, u32[]{:S(2)}, u32[]{:S(2)}) async-start(bf16[8,16,1024]{2,1,0:T(8,128)(2,1)} %bitcast.50), calls=%async_computation.4 | async-start | bytes 524288 | tf_op jit(solution)/shard_map/all_to_all | solution.py:357
  266.0 18.3 %collective-permute-start.32 = (bf16[768,128]{1,0:T(8,128)(2,1)S(1)}, bf16[768,128]{1,0:T(8,128)(2,1)S(1)}, u32[]{:S(2)}, u32[]{:S(2)}) collective-permute-start(bf16[768,128]{1,0:T(8,128)(2,1)S(1)} %get-tuple-element.233), channel_id=1, source_target_pairs={{0,16},{4,20},{8,24},{12,28},{16,0},{20,4},{24,8},{28,12},{1,17},{... | collective-permute-start | bytes 589832 | tf_op jit(solution)/shard_map/ppermute | solution.py:345
  267.1 17.2 %collective-permute-start.33 = (bf16[768,128]{1,0:T(8,128)(2,1)S(1)}, bf16[768,128]{1,0:T(8,128)(2,1)S(1)}, u32[]{:S(2)}, u32[]{:S(2)}) collective-permute-start(bf16[768,128]{1,0:T(8,128)(2,1)S(1)} %get-tuple-element.234), channel_id=1, source_target_pairs={{0,24},{4,28},{8,16},{12,20},{16,8},{20,12},{24,0},{28,4},{1,25},{... | collective-permute-start | bytes 589832 | tf_op jit(solution)/shard_map/ppermute | solution.py:345
  (51 other events, 336.3 us)
Sparse Core Ops, SparseCore 0:
  19.6 63.5 all-gather.4
  85.9 53.0 all-gather.6
  158.0 95.7 reduce-scatter.1

commit v7 on v6

--- a/solution.py
+++ b/solution.py
@@ -589,8 +589,17 @@
 
 
 def attend_back_kernel(
-    lens_ref, qkv_ref, exact_ref, log_ref, grad_ref, table_ref, raw_ref, pair_ref, dkey_ref, dvalue_ref
+    lens_ref, qkv_in_ref, exact_in_ref, log_in_ref, grad_in_ref, table_in_ref, raw_out_ref,
+    qkv_ref, exact_ref, log_ref, grad_ref, table_ref, raw_ref, pair_ref, dkey_ref, dvalue_ref, sem_ref
 ):
+    pairs = (
+        (qkv_in_ref, qkv_ref), (exact_in_ref, exact_ref), (log_in_ref, log_ref), (grad_in_ref, grad_ref),
+        (table_in_ref, table_ref), (raw_ref, raw_out_ref),
+    )
+    copies = [pltpu.make_async_copy(one, two, sem_ref.at[at]) for at, (one, two) in enumerate(pairs)]
+    for copy in copies[:5]:
+        copy.start()
+    copies[0].wait()
     blocks, _, small = qkv_ref.shape
     wide = JOIN * small
     half = HD // 2
@@ -599,6 +608,7 @@
         pair_ref[at * small : (at + 1) * small, :] = jnp.transpose(block).astype(jnp.bfloat16)
     dkey_ref[...] = jnp.zeros(dkey_ref.shape, jnp.float32)
     dvalue_ref[...] = jnp.zeros(dvalue_ref.shape, jnp.float32)
+    finish(copies[1:5])
 
     def unturn(index, grad):
         cosine = table_ref[index, :half, :]
@@ -647,6 +657,8 @@
         raw_ref[at, HD : HD + half, :] = upper.astype(jnp.bfloat16)
         raw_ref[at, HD + half : 2 * HD, :] = lower.astype(jnp.bfloat16)
         raw_ref[at, 2 * HD :, :] = dvalue_ref[:, span].astype(jnp.bfloat16)
+    copies[5].start()
+    copies[5].wait()
 
 
 def mix_out_kernel(core_ref, order_ref, mixed_ref, all_ref, send_ref, keep_ref, w_ref, sem_ref):
@@ -673,7 +685,8 @@
 
 def feed_kernel(
     order_ref, own_ref, other_ref, all_ref, down_ref, source_ref,
-    send_ref, keep_ref, act_ref, dinp_ref, dgate_ref, result_send_ref, result_keep_ref, w_ref, grad_ref, sem_ref
+    send_ref, keep_ref, act_ref, dinp_ref, dgate_ref, result_send_out, result_keep_out, w_ref, grad_ref,
+    result_send_ref, result_keep_ref, sem_ref
 ):
     units = w_ref.shape[0] // 3
     inp_w, gate_w, down_w = [w_ref.at[pl.ds(at * units, units), :] for at in range(3)]
@@ -702,29 +715,46 @@
         dgate = (dact * gelu).astype(jnp.bfloat16)
         dinp_ref[span, :] = dinp
         dgate_ref[span, :] = dgate
-        part = mm(dinp, inp_w[...], NN) + mm(dgate, gate_w[...], NN)
         result = mm(act, down_w[...], NN)
         if micro:
+            result_send_ref[...] = result.astype(jnp.bfloat16)
+            outgoing = [pltpu.make_async_copy(result_send_ref, result_send_out, sem_ref.at[25])]
+        else:
+            result_keep_ref[...] = result
+            outgoing.append(pltpu.make_async_copy(result_keep_ref, result_keep_out, sem_ref.at[26]))
+        outgoing[-1].start()
+        part = mm(dinp, inp_w[...], NN) + mm(dgate, gate_w[...], NN)
+        if micro:
             send_ref[...] = part.astype(jnp.bfloat16)
-            result_send_ref[...] = result.astype(jnp.bfloat16)
         else:
             keep_ref[...] = part
-            result_keep_ref[...] = result
-
-
-def weight_grad_kernel(order_ref, dinp_ref, dgate_ref, act_ref, own_ref, other_ref, grad_ref, out_ref):
+    finish(outgoing)
+
+
+def weight_grad_kernel(
+    order_ref, dinp_ref, dgate_ref, act_ref, own_ref, other_ref, source_ref, result_ref, grad_ref, out_ref, sem_ref
+):
     units = act_ref.shape[1]
     rows = own_ref.shape[0]
     width = out_ref.shape[2]
+    grad_copy = pltpu.make_async_copy(source_ref, grad_ref, sem_ref.at[3])
+    grad_copy.start()
+    copies = []
     for at, (left_ref, rights) in enumerate((
         (dinp_ref, (own_ref, other_ref)),
         (dgate_ref, (own_ref, other_ref)),
         (act_ref, (grad_ref.at[0], grad_ref.at[1])),
     )):
+        if at == 2:
+            grad_copy.wait()
         total = mm(left_ref[:rows, :], rights[0][...], TN) + mm(left_ref[rows:, :], rights[1][...], TN)
         for place in range(8):
             piece = total[:, place * width : (place + 1) * width].astype(jnp.bfloat16)
             out_ref[order_ref[place], at * units : (at + 1) * units, :] = piece
+        span = pl.ds(at * units, units)
+        copies.append(pltpu.make_async_copy(out_ref.at[:, span, :], result_ref.at[:, span, :], sem_ref.at[at]))
+        copies[-1].start()
+    finish(copies)
 
 
 def near_sum_kernel(near_ref, far_ref, *low_refs):
@@ -765,7 +795,15 @@
         far_ref[place] = total[:, (4 + place) * width : (5 + place) * width].astype(jnp.bfloat16)
 
 
-def project_back_kernel(core_ref, raw_ref, norm_ref, w_ref, far_ref, near_ref, send_ref, keep_ref):
+def project_back_kernel(
+    core_ref, raw_in_ref, norm_in_ref, w_in_ref, far_ref, near_out_ref, send_ref, keep_ref,
+    raw_ref, norm_ref, w_ref, near_ref, sem_ref,
+):
+    pairs = ((raw_in_ref, raw_ref), (norm_in_ref, norm_ref), (w_in_ref, w_ref), (near_ref, near_out_ref))
+    copies = [pltpu.make_async_copy(one, two, sem_ref.at[at]) for at, (one, two) in enumerate(pairs)]
+    for copy in copies[:3]:
+        copy.start()
+    finish(copies[:2])
     wide, width = far_ref.shape[1:]
     rows = raw_ref.shape[2]
     core = core_ref[0]
@@ -773,8 +811,11 @@
     for place in range(4):
         near_ref[place] = total[:, place * width : (place + 1) * width]
         far_ref[place] = total[:, (4 + place) * width : (5 + place) * width].astype(jnp.bfloat16)
+    copies[3].start()
+    copies[2].wait()
     send_ref[...] = mm(raw_ref[1 - core], w_ref[:wide, :], TN).astype(jnp.bfloat16)
     keep_ref[...] = mm(raw_ref[core], w_ref[:wide, :], TN)
+    copies[3].wait()
 
 
 def norm_one_back_kernel(
@@ -986,14 +1027,16 @@
         [((rows, full), bf16), ((rows, full), f32)]
         + [((2 * rows, units), bf16)] * 3
         + [((rows, full), bf16), ((rows, full), f32)],
-        [((3 * units, full), bf16), ((2, rows, full), bf16)], (third_all, second_all, grad), copies=25, far_out=(5, 6),
+        [((3 * units, full), bf16), ((2, rows, full), bf16), ((rows, full), bf16), ((rows, full), f32)],
+        (third_all, second_all, grad), copies=27, raw_out=(5, 6),
     )
     half_two = add_half(keep, twin(send))
     half_two, act, d_inp, d_gate = sync((half_two, act, d_inp, d_gate))
     far_two = across(half_two)
     feed_grad = local_call(
-        weight_grad_kernel, "feed_grad", (order,), (d_inp, d_gate, act, two_own, two_other, grad),
-        [((8, 3 * units, width), bf16)], far_out=(0,),
+        weight_grad_kernel, "feed_grad", (order,), (d_inp, d_gate, act, two_own, two_other),
+        [((8, 3 * units, width), bf16)], [((2, rows, full), bf16), ((8, 3 * units, width), bf16)], (grad,),
+        copies=4, raw_out=(0,),
     )
     feed_sum = lax.psum_scatter(feed_grad, "fsdp", scatter_dimension=0, tiled=False)
     far_two, feed_grad = sync((far_two, feed_grad))
@@ -1020,10 +1063,14 @@
     grad_mixed, out_got, res_far = sync((grad_mixed, out_got, res_far))
 
     d_raw_out = local_call(
-        attend_back_kernel, "attend_back", (my_lens,), (qkv, exact, logs, grad_mixed, table),
+        attend_back_kernel, "attend_back", (my_lens,), (),
         [((8, 3 * HD, rows), bf16)],
-        [((8 * rows, 2 * HD), bf16), ((HD, 8 * rows), f32), ((HD, 8 * rows), f32)],
-        far_in=(0, 1, 2, 3, 4), far_out=(0,),
+        [
+            ((8, 3 * HD, rows), bf16), ((8, HD, rows), f32), ((8, 1, rows), f32), ((8, HD, rows), bf16),
+            ((8, HD, rows), f32), ((8, 3 * HD, rows), bf16),
+            ((8 * rows, 2 * HD), bf16), ((HD, 8 * rows), f32), ((HD, 8 * rows), f32),
+        ],
+        (qkv, exact, logs, grad_mixed, table), copies=6, raw_out=(0,),
     )
     d_raw_out, out_got, res_far = sync((d_raw_out, out_got, res_far))
     d_raw = deal_out(d_raw_out).reshape(2, 3 * cols, rows)
@@ -1035,9 +1082,13 @@
     d_raw, out_lows, packed = sync((d_raw, out_lows, packed))
 
     qkv_far, qkv_near, send, keep = local_call(
-        project_back_kernel, "project_back", (core_at,), (d_raw, norm_one, qkv_w),
+        project_back_kernel, "project_back", (core_at,), (),
         [((4, 3 * cols, width), bf16), ((4, 3 * cols, width), f32), ((rows, full), bf16), ((rows, full), f32)],
-        far_in=(0, 1, 2), far_out=(1,),
+        [
+            ((2, 3 * cols, rows), bf16), ((2 * rows, full), bf16), ((3 * cols + 16, full), bf16),
+            ((4, 3 * cols, width), f32),
+        ],
+        (d_raw, norm_one, qkv_w), copies=4, raw_out=(1,),
     )
     qkv_got = hop(qkv_far, 1)
     half = add_half(keep, twin(send))

time: 298 us -> 297 us (level)
    unnamed x68 -> x66, local copies, waits for them, and re-layouts: 6.57 us -> 6.55 us
where the time goes in v7:
time: 297 us; the launch traced here: 295 us
  waiting for transfers between devices  107 us (36%)
  Pallas kernels  74.9 us (25%)
  starting transfers between devices  61.6 us (21%)
  other arithmetic  16.8 us (6%)
  between operations  14.6 us (5%)
  blocking collectives  12.5 us (4%)
  local copies, waits for them, and re-layouts  7.58 us (3%)
    pallas_call x17, Pallas kernels, local_call(): pl.pallas_call(body, in_specs=[pl.BlockSpec(memory_space=pltpu.SMEM)] * l...  74.9 us
    all_to_all x4, waiting for transfers between devices, deal_out(): return lax.all_to_all(value, 'fsdp', 0, 0, tiled=True)  38.3 us
    ppermute x22, waiting for transfers between devices, hop(): return lax.ppermute(value, 'fsdp', [(i, i ^ step) for i in range(8)])  34.7 us
    ppermute x22, starting transfers between devices, hop(): return lax.ppermute(value, 'fsdp', [(i, i ^ step) for i in range(8)])  31.8 us
    ppermute x7, waiting for transfers between devices, across(): return lax.ppermute(value, 'tp', [(i, i ^ 2) for i in range(4)])  22.9 us
    all_to_all x4, starting transfers between devices, deal_out(): return lax.all_to_all(value, 'fsdp', 0, 0, tiled=True)  16.7 us
    all_to_all x1, blocking collectives, deal_out(): return lax.all_to_all(value, 'fsdp', 0, 0, tiled=True)  12.5 us
    ppermute x7, starting transfers between devices, across(): return lax.ppermute(value, 'tp', [(i, i ^ 2) for i in range(4)])  11.2 us
  transfers between devices with their start and end apart: 48, of which 23 were waited for; matrix products, arithmetic and copies ran while one was open for 6% of the time, Pallas kernels for 23%

profile of v7, /device:TPU:0, one launch (start us, length us, event | category | flops | bytes accessed | tf_op | source)
XLA Modules:
  0.0 295.4 jit_solution(12120501461467804481)
XLA Ops:
  12.4 3.6 %collective-permute-start.2 = (bf16[784,128]{1,0:T(8,128)(2,1)S(1)}, bf16[784,128]{1,0:T(8,128)(2,1)S(1)}, u32[]{:S(2)}, u32[]{:S(2)}) collective-permute-start(bf16[784,128]{1,0:T(8,128)(2,1)S(1)} %maximum_maximum_fusion.refs_3_), channel_id=1, source_target_pairs={{0,24},{4,28},{8,16},{12,20},{16,8},{20,12},{24,0},{28,4},{1,25},{... | collective-permute-start | bytes 602120 | tf_op jit(solution)/shard_map/ppermute | solution.py:345
  25.0 10.5 %collective-permute-done.1.refs_5_ = bf16[784,128]{1,0:T(8,128)(2,1)S(1)} collective-permute-done((bf16[784,128]{1,0:T(8,128)(2,1)S(1)}, bf16[784,128]{1,0:T(8,128)(2,1)S(1)}, u32[]{:S(2)}, u32[]{:S(2)}) %collective-permute-start.1) | collective-permute-done | bytes 200736 | tf_op jit(solution)/shard_map/ppermute | solution.py:345
  37.6 3.7 %collective-permute-done.5.refs_9_ = bf16[784,128]{1,0:T(8,128)(2,1)S(1)} collective-permute-done((bf16[784,128]{1,0:T(8,128)(2,1)S(1)}, bf16[784,128]{1,0:T(8,128)(2,1)S(1)}, u32[]{:S(2)}, u32[]{:S(2)}) %collective-permute-start.5) | collective-permute-done | bytes 200736 | tf_op jit(solution)/shard_map/ppermute | solution.py:345
  43.4 5.3 %project.1 = (bf16[512,1024]{1,0:T(8,128)(2,1)}, f32[2,1024]{1,0:T(2,128)}, bf16[8,192,256]{2,1,0:T(8,128)(2,1)}, bf16[784,1024]{1,0:T(8,128)(2,1)}) custom-call(s32[8]{0:T(128)S(1)} %get-tuple-element.133.refs_0_.refs_1_, bf16[2,256,1024]{2,1,0:T(8,128)(2,1)} %refs_2_.3, f32[64,512]{1,0:T(8,128)} %maximum_maximum_fusion.1.refs_2_, ...), custom_call_target="tpu_custom_call" | custom-call | flops 3000000000 | bytes 8388608 | tf_op jit(solution)/shard_map/project/pallas_call | solution.py:414
  48.7 5.0 %all-to-all-start = ((bf16[8,192,256]{2,1,0:T(8,128)(2,1)}), bf16[8,192,256]{2,1,0:T(8,128)(2,1)S(1)}, u32[]{:S(2)}, u32[]{:S(2)}) async-start(bf16[8,192,256]{2,1,0:T(8,128)(2,1)} %get-tuple-element.152), calls=%async_computation | async-start | bytes 1572864 | tf_op jit(solution)/shard_map/all_to_all | solution.py:357
  61.7 22.8 %all-to-all-done.refs_1_ = bf16[8,192,256]{2,1,0:T(8,128)(2,1)S(1)} async-done(((bf16[8,192,256]{2,1,0:T(8,128)(2,1)}), bf16[8,192,256]{2,1,0:T(8,128)(2,1)S(1)}, u32[]{:S(2)}, u32[]{:S(2)}) %all-to-all-start) | async-done | bytes 786464 | tf_op jit(solution)/shard_map/all_to_all | solution.py:357
  87.2 10.9 %attend.1 = (bf16[8,64,256]{2,1,0:T(8,128)(2,1)}, f32[8,64,256]{2,1,0:T(8,128)}, f32[8,1,256]{2,1,0:T(1,128)}) custom-call(s32[8]{0:T(128)S(1)} %get-tuple-element.132.refs_0_, bf16[8,192,256]{2,1,0:T(8,128)(2,1)} %copy-done.10), custom_call_target="tpu_custom_call" | custom-call | flops 10000000000 | bytes 8388608 | tf_op jit(solution)/shard_map/attend/pallas_call | solution.py:414
  101.5 12.5 %all_to_all.25 = bf16[8,64,256]{2,1,0:T(8,128)(2,1)} all-to-all(bf16[8,64,256]{2,1,0:T(8,128)(2,1)S(1)} %copy-done.13), channel_id=1, replica_groups=mesh['fsdp'=8,'tp'=4] {'fsdp'}, dimensions={0} | all-to-all | bytes 524288 | tf_op jit(solution)/shard_map/all_to_all | solution.py:357
  114.1 3.4 %mix_out.1 = (bf16[256,1024]{1,0:T(8,128)(2,1)S(1)}, f32[256,1024]{1,0:T(8,128)S(1)}, bf16[256,1024]{1,0:T(8,128)(2,1)}) custom-call(s32[1]{0:T(128)} %bitcast.26.refs_0_, s32[8]{0:T(128)S(1)} %get-tuple-element.133.refs_0_.refs_1_, bf16[2,256,256]{2,1,0:T(8,128)(2,1)} %bitcast.188, bf16[8,912,128]{2,1,0:T(8,128)(2,1)} %bitcast.200), custom_call_target="tpu_custom_call" | custom-call | flops 3000000000 | bytes 8388608 | tf_op jit(solution)/shard_map/mix_out/pallas_call | solution.py:414
  125.8 9.1 %collective-permute-done.17.refs_4_ = bf16[256,1024]{1,0:T(8,128)(2,1)S(1)} collective-permute-done((bf16[256,1024]{1,0:T(8,128)(2,1)S(1)}, bf16[256,1024]{1,0:T(8,128)(2,1)S(1)}, u32[]{:S(2)}, u32[]{:S(2)}) %collective-permute-start.17) | collective-permute-done | bytes 524320 | tf_op jit(solution)/shard_map/ppermute | solution.py:353
  139.9 8.3 %feed.1 = (bf16[256,1024]{1,0:T(8,128)(2,1)S(1)}, f32[256,1024]{1,0:T(8,128)S(1)}, bf16[512,656]{1,0:T(8,128)(2,1)S(1)}, bf16[512,656]{1,0:T(8,128)(2,1)S(1)}, b...) custom-call(s32[8]{0:T(128)S(1)} %get-tuple-element.133.refs_0_.refs_1_, ...), custom_call_target="tpu_custom_call" | custom-call | flops 8000000000 | bytes 8388608 | tf_op jit(solution)/shard_map/feed/pallas_call | solution.py:414
  151.9 4.5 %feed_grad.1 = bf16[8,1968,128]{2,1,0:T(8,128)(2,1)} custom-call(s32[8]{0:T(128)S(1)} %get-tuple-element.133.refs_0_.refs_1_, bf16[512,656]{1,0:T(8,128)(2,1)S(1)} %get-tuple-element.191.refs_1_, bf16[512,656]{1,0:T(8,128)(2,1)S(1)} %get-tuple-element.192.refs_2_, bf16[512,656]{1,0:T(8,128)(2,1)S(1)} %get-tuple-element.193.refs_3_, ...), custom_call_target="tpu_custom_call" | custom-call | flops 5000000000 | bytes 8388608 | tf_op jit(solution)/shard_map/feed_grad/pallas_call | solution.py:414
  156.4 8.0 %collective-permute-done.20.refs_2_ = bf16[256,1024]{1,0:T(8,128)(2,1)S(1)} collective-permute-done((bf16[256,1024]{1,0:T(8,128)(2,1)S(1)}, bf16[256,1024]{1,0:T(8,128)(2,1)S(1)}, u32[]{:S(2)}, u32[]{:S(2)}) %collective-permute-start.20) | collective-permute-done | bytes 524320 | tf_op jit(solution)/shard_map/ppermute | solution.py:353
  164.4 3.4 %norm_two_back.1 = (f32[256,1024]{1,0:T(8,128)}, bf16[256,1024]{1,0:T(8,128)(2,1)S(1)}) custom-call(f32[256,1024]{1,0:T(8,128)} %get-tuple-element.182.refs_0_.refs_2_, bf16[256,1024]{1,0:T(8,128)(2,1)S(1)} %add_convert_fusion.2.refs_1_, bf16[256,1024]{1,0:T(8,128)(2,1)S(1)} %collective-permute-done.20.refs_2_, bf16[2,256,1024]{2,1,0:T(8,128)(2,1)} %copy-done.3, ...), custom_call_target="tpu_custom_call" | custom-call | flops 3000000000 | bytes 8388608 | tf_op jit(solution)/shard_map/norm_two_back/pallas_call | solution.py:414
  171.2 3.7 %all-to-all-start.2 = ((bf16[8,64,256]{2,1,0:T(8,128)(2,1)}), bf16[8,64,256]{2,1,0:T(8,128)(2,1)S(1)}, u32[]{:S(2)}, u32[]{:S(2)}) async-start(bf16[8,64,256]{2,1,0:T(8,128)(2,1)} %mix_back.1), calls=%async_computation.2 | async-start | bytes 524288 | tf_op jit(solution)/shard_map/all_to_all | solution.py:357
  182.4 10.2 %collective-permute-done.22.refs_1_ = bf16[4,256,128]{2,1,0:T(8,128)(2,1)S(1)} collective-permute-done((bf16[4,256,128]{2,1,0:T(8,128)(2,1)S(1)}, bf16[4,256,128]{2,1,0:T(8,128)(2,1)S(1)}, u32[]{:S(2)}, u32[]{:S(2)}) %collective-permute-start.22) | collective-permute-done | bytes 262176 | tf_op jit(solution)/shard_map/ppermute | solution.py:345
  193.4 15.1 %attend_back.1 = bf16[8,192,256]{2,1,0:T(8,128)(2,1)} custom-call(s32[8]{0:T(128)S(1)} %get-tuple-element.132.refs_0_, bf16[8,192,256]{2,1,0:T(8,128)(2,1)} %copy-done.10, f32[8,64,256]{2,1,0:T(8,128)} %get-tuple-element.153.refs_2_, f32[8,1,256]{2,1,0:T(1,128)} %get-tuple-element.154.refs_3_, bf16[8,64,256]{2,1,0:T(8,128)(2,1)} %copy-done.14, ...), custom_call_target="tpu_custom_call" | custom-call | flops 28000000000 | bytes 8388608 | tf_op jit(solution)/shard_map/attend_back/pallas_call | solution.py:414
  208.6 4.4 %all-to-all-start.3 = ((bf16[8,192,256]{2,1,0:T(8,128)(2,1)}), bf16[8,192,256]{2,1,0:T(8,128)(2,1)S(1)}, u32[]{:S(2)}, u32[]{:S(2)}) async-start(bf16[8,192,256]{2,1,0:T(8,128)(2,1)} %attend_back.1), calls=%async_computation.3 | async-start | bytes 1572864 | tf_op jit(solution)/shard_map/all_to_all | solution.py:357
  212.9 3.5 %result.1 = bf16[128,1024]{1,0:T(8,128)(2,1)} custom-call(s32[8]{0:T(128)S(1)} %get-tuple-element.133.refs_0_.refs_1_, s32[1,128]{1,0:T(1,128)S(1)} %reshape.266.refs_1_, f32[256,1024]{1,0:T(8,128)} %get-tuple-element.182.refs_0_.refs_2_, bf16[256,1024]{1,0:T(8,128)(2,1)} %copy-done.12, bf16[256,1024]{1,0:T(8,128)(2,1)} %copy-done.25), custom_call_target="tpu_custom_call" | custom-call | flops 3000000000 | bytes 8388608 | tf_op jit(solution)/shard_map/result/pallas_call | solution.py:414
  217.6 15.5 %all-to-all-done.3 = bf16[8,192,256]{2,1,0:T(8,128)(2,1)S(1)} async-done(((bf16[8,192,256]{2,1,0:T(8,128)(2,1)}), bf16[8,192,256]{2,1,0:T(8,128)(2,1)S(1)}, u32[]{:S(2)}, u32[]{:S(2)}) %all-to-all-start.3) | async-done | bytes 786464 | tf_op jit(solution)/shard_map/all_to_all | solution.py:357
  234.0 4.4 %project_back.1 = (bf16[4,768,128]{2,1,0:T(8,128)(2,1)}, f32[4,768,128]{2,1,0:T(8,128)}, bf16[256,1024]{1,0:T(8,128)(2,1)S(1)}, f32[256,1024]{1,0:T(8,128)S(1)}) custom-call(s32[1]{0:T(128)} %bitcast.26.refs_0_, bf16[2,768,256]{2,1,0:T(8,128)(2,1)} %bitcast.185, bf16[512,1024]{1,0:T(8,128)(2,1)} %get-tuple-element.218.refs_2_, ...), custom_call_target="tpu_custom_call" | custom-call | flops 3000000000 | bytes 8388608 | tf_op jit(solution)/shard_map/project_back/pallas_call | solution.py:414
  241.9 3.6 %all-to-all-start.4 = ((bf16[8,16,1024]{2,1,0:T(8,128)(2,1)}), bf16[8,16,1024]{2,1,0:T(8,128)(2,1)S(1)}, u32[]{:S(2)}, u32[]{:S(2)}) async-start(bf16[8,16,1024]{2,1,0:T(8,128)(2,1)} %bitcast.50), calls=%async_computation.4 | async-start | bytes 524288 | tf_op jit(solution)/shard_map/all_to_all | solution.py:357
  249.9 4.6 %collective-permute-done.27.refs_4_ = bf16[256,1024]{1,0:T(8,128)(2,1)S(1)} collective-permute-done((bf16[256,1024]{1,0:T(8,128)(2,1)S(1)}, bf16[256,1024]{1,0:T(8,128)(2,1)S(1)}, u32[]{:S(2)}, u32[]{:S(2)}) %collective-permute-start.27) | collective-permute-done | bytes 524320 | tf_op jit(solution)/shard_map/ppermute | solution.py:353
  267.4 4.6 %collective-permute-done.31 = bf16[768,128]{1,0:T(8,128)(2,1)S(1)} collective-permute-done((bf16[768,128]{1,0:T(8,128)(2,1)S(1)}, bf16[768,128]{1,0:T(8,128)(2,1)S(1)}, u32[]{:S(2)}, u32[]{:S(2)}) %collective-permute-start.31) | collective-permute-done | bytes 196640 | tf_op jit(solution)/shard_map/ppermute | solution.py:345
  (222 shorter events, 100.1 us)
Async XLA Ops:
  7.2 106.9 %all-gather.5.cloned.1.call-start = ((), (), s32[]{:S(2)}) async-start(), calls=%async_computation.7 | async-start | bytes 2101248 | tf_op jit(solution)/shard_map/all_gather | solution.py:971
  9.4 28.2 %collective-permute-start.3 = (bf16[784,128]{1,0:T(8,128)(2,1)S(1)}, bf16[784,128]{1,0:T(8,128)(2,1)S(1)}, u32[]{:S(2)}, u32[]{:S(2)}) collective-permute-start(bf16[784,128]{1,0:T(8,128)(2,1)S(1)} %maximum_maximum_fusion.refs_3_), channel_id=1, source_target_pairs={{0,4},{4,0},{8,12},{12,8},{16,20},{20,16},{24,28},{28,24},{1,5},{5... | collective-permute-start | bytes 602120 | tf_op jit(solution)/shard_map/ppermute | solution.py:345
  16.0 19.5 %collective-permute-start.1 = (bf16[784,128]{1,0:T(8,128)(2,1)S(1)}, bf16[784,128]{1,0:T(8,128)(2,1)S(1)}, u32[]{:S(2)}, u32[]{:S(2)}) collective-permute-start(bf16[784,128]{1,0:T(8,128)(2,1)S(1)} %maximum_maximum_fusion.refs_3_), channel_id=1, source_target_pairs={{0,16},{4,20},{8,24},{12,28},{16,0},{20,4},{24,8},{28,12},{1,17},{... | collective-permute-start | bytes 602120 | tf_op jit(solution)/shard_map/ppermute | solution.py:345
  16.0 19.5 %collective-permute-start = (bf16[784,128]{1,0:T(8,128)(2,1)S(1)}, bf16[784,128]{1,0:T(8,128)(2,1)S(1)}, u32[]{:S(2)}, u32[]{:S(2)}) collective-permute-start(bf16[784,128]{1,0:T(8,128)(2,1)S(1)} %maximum_maximum_fusion.refs_3_), channel_id=1, source_target_pairs={{0,8},{4,12},{8,0},{12,4},{16,24},{20,28},{24,16},{28,20},{1,9},{5... | collective-permute-start | bytes 602120 | tf_op jit(solution)/shard_map/ppermute | solution.py:345
  48.7 35.8 %all-to-all-start = ((bf16[8,192,256]{2,1,0:T(8,128)(2,1)}), bf16[8,192,256]{2,1,0:T(8,128)(2,1)S(1)}, u32[]{:S(2)}, u32[]{:S(2)}) async-start(bf16[8,192,256]{2,1,0:T(8,128)(2,1)} %get-tuple-element.152), calls=%async_computation | async-start | bytes 1572864 | tf_op jit(solution)/shard_map/all_to_all | solution.py:357
  53.8 85.2 %all-gather.7.cloned.1.call-start = ((), (), s32[]{:S(2)}) async-start(), calls=%async_computation.8 | async-start | bytes 3022848 | tf_op jit(solution)/shard_map/all_gather | solution.py:972
  53.8 30.7 %collective-permute-start.7 = (bf16[2,8,1024]{2,1,0:T(8,128)(2,1)S(1)}, bf16[2,8,1024]{2,1,0:T(8,128)(2,1)S(1)}, u32[]{:S(2)}, u32[]{:S(2)}) collective-permute-start(bf16[2,8,1024]{2,1,0:T(8,128)(2,1)S(1)} %get-tuple-element.157), channel_id=1, source_target_pairs={{0,8},{4,12},{8,0},{12,4},{16,24},{20,28},{24,16},{28,20},{1,9},{5... | collective-permute-start | bytes 98312 | tf_op jit(solution)/shard_map/ppermute | solution.py:345
  55.9 29.0 %collective-permute-start.8 = (bf16[2,8,1024]{2,1,0:T(8,128)(2,1)S(1)}, bf16[2,8,1024]{2,1,0:T(8,128)(2,1)S(1)}, u32[]{:S(2)}, u32[]{:S(2)}) collective-permute-start(bf16[2,8,1024]{2,1,0:T(8,128)(2,1)S(1)} %get-tuple-element.158), channel_id=1, source_target_pairs={{0,16},{4,20},{8,24},{12,28},{16,0},{20,4},{24,8},{28,12},{1,17},{... | collective-permute-start | bytes 98312 | tf_op jit(solution)/shard_map/ppermute | solution.py:345
  59.0 213.0 %reduce-scatter.2.cloned.1.call-start = ((), (), s32[]{:S(2)}) async-start(), calls=%async_computation.6 | async-start | bytes 4534272 | tf_op jit(solution)/shard_map/reduce_scatter | solution.py:1041
  59.1 39.1 %collective-permute-start.9 = (bf16[2,8,1024]{2,1,0:T(8,128)(2,1)S(1)}, bf16[2,8,1024]{2,1,0:T(8,128)(2,1)S(1)}, u32[]{:S(2)}, u32[]{:S(2)}) collective-permute-start(bf16[2,8,1024]{2,1,0:T(8,128)(2,1)S(1)} %get-tuple-element.159), channel_id=1, source_target_pairs={{0,24},{4,28},{8,16},{12,20},{16,8},{20,12},{24,0},{28,4},{1,25},{... | collective-permute-start | bytes 98312 | tf_op jit(solution)/shard_map/ppermute | solution.py:345
  59.2 38.9 %collective-permute-start.10 = (bf16[2,8,1024]{2,1,0:T(8,128)(2,1)S(1)}, bf16[2,8,1024]{2,1,0:T(8,128)(2,1)S(1)}, u32[]{:S(2)}, u32[]{:S(2)}) collective-permute-start(bf16[2,8,1024]{2,1,0:T(8,128)(2,1)S(1)} %get-tuple-element.160), channel_id=1, source_target_pairs={{0,4},{4,0},{8,12},{12,8},{16,20},{20,16},{24,28},{28,24},{1,5},{5... | collective-permute-start | bytes 98312 | tf_op jit(solution)/shard_map/ppermute | solution.py:345
  61.2 37.0 %collective-permute-start.11 = (bf16[2,8,1024]{2,1,0:T(8,128)(2,1)S(1)}, bf16[2,8,1024]{2,1,0:T(8,128)(2,1)S(1)}, u32[]{:S(2)}, u32[]{:S(2)}) collective-permute-start(bf16[2,8,1024]{2,1,0:T(8,128)(2,1)S(1)} %get-tuple-element.161), channel_id=1, source_target_pairs={{0,12},{4,8},{8,4},{12,0},{16,28},{20,24},{24,20},{28,16},{1,13},{... | collective-permute-start | bytes 98312 | tf_op jit(solution)/shard_map/ppermute | solution.py:345
  84.5 13.7 %collective-permute-start.12 = (bf16[2,8,1024]{2,1,0:T(8,128)(2,1)S(1)}, bf16[2,8,1024]{2,1,0:T(8,128)(2,1)S(1)}, u32[]{:S(2)}, u32[]{:S(2)}) collective-permute-start(bf16[2,8,1024]{2,1,0:T(8,128)(2,1)S(1)} %get-tuple-element.162), channel_id=1, source_target_pairs={{0,20},{4,16},{8,28},{12,24},{16,4},{20,0},{24,12},{28,8},{1,21},{... | collective-permute-start | bytes 98312 | tf_op jit(solution)/shard_map/ppermute | solution.py:345
  100.0 14.1 %collective-permute-start.15 = (bf16[2,8,2,8,1024]{4,3,0,1,2:T(8,128)(2,1)S(1)}, bf16[2,8,2,8,1024]{4,3,0,1,2:T(8,128)(2,1)}, u32[]{:S(2)}, u32[]{:S(2)}) collective-permute-start(bf16[2,8,2,8,1024]{4,3,0,1,2:T(8,128)(2,1)S(1)} %pad_maximum_fusion.2), channel_id=1, source_target_pairs={{0,2},{1,3},{2,0},{3,1},{4,6},{5,7},{6,4},{7,5},{8,10},{9,11},{10,... | collective-permute-start | bytes 1572872 | tf_op jit(solution)/shard_map/ppermute | solution.py:353
  120.9 14.0 %collective-permute-start.17 = (bf16[256,1024]{1,0:T(8,128)(2,1)S(1)}, bf16[256,1024]{1,0:T(8,128)(2,1)S(1)}, u32[]{:S(2)}, u32[]{:S(2)}) collective-permute-start(bf16[256,1024]{1,0:T(8,128)(2,1)S(1)} %add_convert_fusion.3.refs_3_), channel_id=1, source_target_pairs={{0,2},{1,3},{2,0},{3,1},{4,6},{5,7},{6,4},{7,5},{8,10},{9,11},{10,... | collective-permute-start | bytes 1572872 | tf_op jit(solution)/shard_map/ppermute | solution.py:353
  150.3 14.0 %collective-permute-start.20 = (bf16[256,1024]{1,0:T(8,128)(2,1)S(1)}, bf16[256,1024]{1,0:T(8,128)(2,1)S(1)}, u32[]{:S(2)}, u32[]{:S(2)}) collective-permute-start(bf16[256,1024]{1,0:T(8,128)(2,1)S(1)} %add_convert_fusion.2.refs_1_), channel_id=1, source_target_pairs={{0,2},{1,3},{2,0},{3,1},{4,6},{5,7},{6,4},{7,5},{8,10},{9,11},{10,... | collective-permute-start | bytes 1572872 | tf_op jit(solution)/shard_map/ppermute | solution.py:353
  171.2 21.5 %all-to-all-start.2 = ((bf16[8,64,256]{2,1,0:T(8,128)(2,1)}), bf16[8,64,256]{2,1,0:T(8,128)(2,1)S(1)}, u32[]{:S(2)}, u32[]{:S(2)}) async-start(bf16[8,64,256]{2,1,0:T(8,128)(2,1)} %mix_back.1), calls=%async_computation.2 | async-start | bytes 524288 | tf_op jit(solution)/shard_map/all_to_all | solution.py:357
  176.3 16.4 %collective-permute-start.24 = (bf16[256,1024]{1,0:T(8,128)(2,1)S(1)}, bf16[256,1024]{1,0:T(8,128)(2,1)S(1)}, u32[]{:S(2)}, u32[]{:S(2)}) collective-permute-start(bf16[256,1024]{1,0:T(8,128)(2,1)S(1)} %add_convert_fusion.1.refs_3_), channel_id=1, source_target_pairs={{0,2},{1,3},{2,0},{3,1},{4,6},{5,7},{6,4},{7,5},{8,10},{9,11},{10,... | collective-permute-start | bytes 1572872 | tf_op jit(solution)/shard_map/ppermute | solution.py:353
  208.6 24.5 %all-to-all-start.3 = ((bf16[8,192,256]{2,1,0:T(8,128)(2,1)}), bf16[8,192,256]{2,1,0:T(8,128)(2,1)S(1)}, u32[]{:S(2)}, u32[]{:S(2)}) async-start(bf16[8,192,256]{2,1,0:T(8,128)(2,1)} %attend_back.1), calls=%async_computation.3 | async-start | bytes 1572864 | tf_op jit(solution)/shard_map/all_to_all | solution.py:357
  238.4 22.7 %collective-permute-start.25 = (bf16[4,768,128]{2,1,0:T(8,128)(2,1)}, bf16[4,768,128]{2,1,0:T(8,128)(2,1)}, u32[]{:S(2)}, u32[]{:S(2)}) collective-permute-start(bf16[4,768,128]{2,1,0:T(8,128)(2,1)} %get-tuple-element.221), channel_id=1, source_target_pairs={{0,4},{4,0},{8,12},{12,8},{16,20},{20,16},{24,28},{28,24},{1,5},{5... | collective-permute-start | bytes 2359304 | tf_op jit(solution)/shard_map/ppermute | solution.py:345
  240.5 14.0 %collective-permute-start.27 = (bf16[256,1024]{1,0:T(8,128)(2,1)S(1)}, bf16[256,1024]{1,0:T(8,128)(2,1)S(1)}, u32[]{:S(2)}, u32[]{:S(2)}) collective-permute-start(bf16[256,1024]{1,0:T(8,128)(2,1)S(1)} %add_convert_fusion.refs_3_), channel_id=1, source_target_pairs={{0,2},{1,3},{2,0},{3,1},{4,6},{5,7},{6,4},{7,5},{8,10},{9,11},{10,... | collective-permute-start | bytes 1572872 | tf_op jit(solution)/shard_map/ppermute | solution.py:353
  241.9 25.5 %all-to-all-start.4 = ((bf16[8,16,1024]{2,1,0:T(8,128)(2,1)}), bf16[8,16,1024]{2,1,0:T(8,128)(2,1)S(1)}, u32[]{:S(2)}, u32[]{:S(2)}) async-start(bf16[8,16,1024]{2,1,0:T(8,128)(2,1)} %bitcast.50), calls=%async_computation.4 | async-start | bytes 524288 | tf_op jit(solution)/shard_map/all_to_all | solution.py:357
  264.3 17.9 %collective-permute-start.32 = (bf16[768,128]{1,0:T(8,128)(2,1)S(1)}, bf16[768,128]{1,0:T(8,128)(2,1)S(1)}, u32[]{:S(2)}, u32[]{:S(2)}) collective-permute-start(bf16[768,128]{1,0:T(8,128)(2,1)S(1)} %get-tuple-element.233), channel_id=1, source_target_pairs={{0,16},{4,20},{8,24},{12,28},{16,0},{20,4},{24,8},{28,12},{1,17},{... | collective-permute-start | bytes 589832 | tf_op jit(solution)/shard_map/ppermute | solution.py:345
  264.6 17.5 %collective-permute-start.33 = (bf16[768,128]{1,0:T(8,128)(2,1)S(1)}, bf16[768,128]{1,0:T(8,128)(2,1)S(1)}, u32[]{:S(2)}, u32[]{:S(2)}) collective-permute-start(bf16[768,128]{1,0:T(8,128)(2,1)S(1)} %get-tuple-element.234), channel_id=1, source_target_pairs={{0,24},{4,28},{8,16},{12,20},{16,8},{20,12},{24,0},{28,4},{1,25},{... | collective-permute-start | bytes 589832 | tf_op jit(solution)/shard_map/ppermute | solution.py:345
  (50 other events, 331.0 us)
Sparse Core Ops, SparseCore 0:
  19.6 63.5 all-gather.4
  85.9 53.0 all-gather.6
  156.5 95.6 reduce-scatter.1

commit v8 on v7

--- a/solution.py
+++ b/solution.py
@@ -762,18 +762,29 @@
         low_ref[...] = (near_ref[at + 1] + far_ref[at + 1].astype(jnp.float32)).astype(jnp.bfloat16)
 
 
-def norm_two_back_kernel(hidden_ref, half_ref, far_ref, grad_ref, gains_ref, dhidden_ref, low_ref):
+def norm_two_back_kernel(
+    half_ref, far_ref, hidden_in_ref, grad_in_ref, gains_in_ref, result_ref, low_ref,
+    hidden_ref, grad_ref, gains_ref, dhidden_ref, sem_ref,
+):
+    pairs = ((hidden_in_ref, hidden_ref), (grad_in_ref.at[0], grad_ref), (gains_in_ref, gains_ref), (dhidden_ref, result_ref))
+    copies = [pltpu.make_async_copy(one, two, sem_ref.at[at]) for at, (one, two) in enumerate(pairs)]
+    for copy in copies[:3]:
+        copy.start()
+    copies[0].wait()
     hidden = hidden_ref[...]
     center = hidden - jnp.mean(hidden, axis=-1, keepdims=True)
     spread = lax.rsqrt(jnp.mean(center * center, axis=-1, keepdims=True) + EPS)
     xhat = center * spread
     dnorm = half_ref[...].astype(jnp.float32) + far_ref[...].astype(jnp.float32)
+    finish(copies[1:3])
     scaled = dnorm * gains_ref[1:2, :]
     inner = scaled - jnp.mean(scaled, axis=-1, keepdims=True)
     inner = inner - xhat * jnp.mean(scaled * xhat, axis=-1, keepdims=True)
-    total = grad_ref[0].astype(jnp.float32) + inner * spread
+    total = grad_ref[...].astype(jnp.float32) + inner * spread
     dhidden_ref[...] = total
+    copies[3].start()
     low_ref[...] = total.astype(jnp.bfloat16)
+    copies[3].wait()
 
 
 def mix_back_kernel(core_ref, own_ref, other_ref, w_ref, send_ref):
@@ -1041,8 +1052,10 @@
     feed_sum = lax.psum_scatter(feed_grad, "fsdp", scatter_dimension=0, tiled=False)
     far_two, feed_grad = sync((far_two, feed_grad))
     d_hidden, low_own = local_call(
-        norm_two_back_kernel, "norm_two_back", (), (hidden, half_two, far_two, grad, gains),
-        [((rows, full), f32), ((rows, full), bf16)], far_in=(0, 3, 4), far_out=(0,),
+        norm_two_back_kernel, "norm_two_back", (), (half_two, far_two),
+        [((rows, full), f32), ((rows, full), bf16)],
+        [((rows, full), f32), ((rows, full), bf16), ((2, full), f32), ((rows, full), f32)],
+        (hidden, grad, gains), copies=4, raw_out=(0,),
     )
     low_other = twin(low_own)
     d_mixed = local_call(

time: 297 us -> 298 us (level)
  transfers between devices with their start and end apart: 48 -> 48, of which waited for: 23 -> 22; matrix products, arithmetic and copies ran while one was open for 6% -> 6% of each run, Pallas kernels for 23% -> 22%
where the time goes in v8:
time: 298 us; the launch traced here: 296 us
  waiting for transfers between devices  108 us (36%)
  Pallas kernels  74.9 us (25%)
  starting transfers between devices  60.9 us (20%)
  other arithmetic  16.8 us (6%)
  between operations  14.6 us (5%)
  blocking collectives  12.5 us (4%)
  local copies, waits for them, and re-layouts  7.58 us (3%)
    pallas_call x17, Pallas kernels, local_call(): pl.pallas_call(body, in_specs=[pl.BlockSpec(memory_space=pltpu.SMEM)] * l...  74.9 us
    all_to_all x4, waiting for transfers between devices, deal_out(): return lax.all_to_all(value, 'fsdp', 0, 0, tiled=True)  38.6 us
    ppermute x22, waiting for transfers between devices, hop(): return lax.ppermute(value, 'fsdp', [(i, i ^ step) for i in range(8)])  35.6 us
    ppermute x22, starting transfers between devices, hop(): return lax.ppermute(value, 'fsdp', [(i, i ^ step) for i in range(8)])  31.9 us
    ppermute x7, waiting for transfers between devices, across(): return lax.ppermute(value, 'tp', [(i, i ^ 2) for i in range(4)])  23.4 us
    all_to_all x4, starting transfers between devices, deal_out(): return lax.all_to_all(value, 'fsdp', 0, 0, tiled=True)  16.1 us
    all_to_all x1, blocking collectives, deal_out(): return lax.all_to_all(value, 'fsdp', 0, 0, tiled=True)  12.5 us
    ppermute x7, starting transfers between devices, across(): return lax.ppermute(value, 'tp', [(i, i ^ 2) for i in range(4)])  10.9 us
  transfers between devices with their start and end apart: 48, of which 22 were waited for; matrix products, arithmetic and copies ran while one was open for 6% of the time, Pallas kernels for 22%

profile of v8, /device:TPU:0, one launch (start us, length us, event | category | flops | bytes accessed | tf_op | source)
XLA Modules:
  0.0 296.2 jit_solution(9104788274099125194)
XLA Ops:
  12.4 3.6 %collective-permute-start.2 = (bf16[784,128]{1,0:T(8,128)(2,1)S(1)}, bf16[784,128]{1,0:T(8,128)(2,1)S(1)}, u32[]{:S(2)}, u32[]{:S(2)}) collective-permute-start(bf16[784,128]{1,0:T(8,128)(2,1)S(1)} %maximum_maximum_fusion.refs_3_), channel_id=1, source_target_pairs={{0,24},{4,28},{8,16},{12,20},{16,8},{20,12},{24,0},{28,4},{1,25},{... | collective-permute-start | bytes 602120 | tf_op jit(solution)/shard_map/ppermute | solution.py:345
  25.0 10.5 %collective-permute-done.1.refs_5_ = bf16[784,128]{1,0:T(8,128)(2,1)S(1)} collective-permute-done((bf16[784,128]{1,0:T(8,128)(2,1)S(1)}, bf16[784,128]{1,0:T(8,128)(2,1)S(1)}, u32[]{:S(2)}, u32[]{:S(2)}) %collective-permute-start.1) | collective-permute-done | bytes 200736 | tf_op jit(solution)/shard_map/ppermute | solution.py:345
  37.6 3.7 %collective-permute-done.5.refs_9_ = bf16[784,128]{1,0:T(8,128)(2,1)S(1)} collective-permute-done((bf16[784,128]{1,0:T(8,128)(2,1)S(1)}, bf16[784,128]{1,0:T(8,128)(2,1)S(1)}, u32[]{:S(2)}, u32[]{:S(2)}) %collective-permute-start.5) | collective-permute-done | bytes 200736 | tf_op jit(solution)/shard_map/ppermute | solution.py:345
  43.4 5.3 %project.1 = (bf16[512,1024]{1,0:T(8,128)(2,1)}, f32[2,1024]{1,0:T(2,128)}, bf16[8,192,256]{2,1,0:T(8,128)(2,1)}, bf16[784,1024]{1,0:T(8,128)(2,1)}) custom-call(s32[8]{0:T(128)S(1)} %get-tuple-element.133.refs_0_.refs_1_, bf16[2,256,1024]{2,1,0:T(8,128)(2,1)} %refs_2_.3, f32[64,512]{1,0:T(8,128)} %maximum_maximum_fusion.1.refs_2_, ...), custom_call_target="tpu_custom_call" | custom-call | flops 3000000000 | bytes 8388608 | tf_op jit(solution)/shard_map/project/pallas_call | solution.py:414
  48.7 5.0 %all-to-all-start = ((bf16[8,192,256]{2,1,0:T(8,128)(2,1)}), bf16[8,192,256]{2,1,0:T(8,128)(2,1)S(1)}, u32[]{:S(2)}, u32[]{:S(2)}) async-start(bf16[8,192,256]{2,1,0:T(8,128)(2,1)} %get-tuple-element.152), calls=%async_computation | async-start | bytes 1572864 | tf_op jit(solution)/shard_map/all_to_all | solution.py:357
  61.7 22.8 %all-to-all-done.refs_1_ = bf16[8,192,256]{2,1,0:T(8,128)(2,1)S(1)} async-done(((bf16[8,192,256]{2,1,0:T(8,128)(2,1)}), bf16[8,192,256]{2,1,0:T(8,128)(2,1)S(1)}, u32[]{:S(2)}, u32[]{:S(2)}) %all-to-all-start) | async-done | bytes 786464 | tf_op jit(solution)/shard_map/all_to_all | solution.py:357
  87.2 10.9 %attend.1 = (bf16[8,64,256]{2,1,0:T(8,128)(2,1)}, f32[8,64,256]{2,1,0:T(8,128)}, f32[8,1,256]{2,1,0:T(1,128)}) custom-call(s32[8]{0:T(128)S(1)} %get-tuple-element.132.refs_0_, bf16[8,192,256]{2,1,0:T(8,128)(2,1)} %copy-done.10), custom_call_target="tpu_custom_call" | custom-call | flops 10000000000 | bytes 8388608 | tf_op jit(solution)/shard_map/attend/pallas_call | solution.py:414
  101.5 12.5 %all_to_all.25 = bf16[8,64,256]{2,1,0:T(8,128)(2,1)} all-to-all(bf16[8,64,256]{2,1,0:T(8,128)(2,1)S(1)} %copy-done.13), channel_id=1, replica_groups=mesh['fsdp'=8,'tp'=4] {'fsdp'}, dimensions={0} | all-to-all | bytes 524288 | tf_op jit(solution)/shard_map/all_to_all | solution.py:357
  114.1 3.4 %mix_out.1 = (bf16[256,1024]{1,0:T(8,128)(2,1)S(1)}, f32[256,1024]{1,0:T(8,128)S(1)}, bf16[256,1024]{1,0:T(8,128)(2,1)}) custom-call(s32[1]{0:T(128)} %bitcast.26.refs_0_, s32[8]{0:T(128)S(1)} %get-tuple-element.133.refs_0_.refs_1_, bf16[2,256,256]{2,1,0:T(8,128)(2,1)} %bitcast.188, bf16[8,912,128]{2,1,0:T(8,128)(2,1)} %bitcast.200), custom_call_target="tpu_custom_call" | custom-call | flops 3000000000 | bytes 8388608 | tf_op jit(solution)/shard_map/mix_out/pallas_call | solution.py:414
  125.8 9.1 %collective-permute-done.17.refs_4_ = bf16[256,1024]{1,0:T(8,128)(2,1)S(1)} collective-permute-done((bf16[256,1024]{1,0:T(8,128)(2,1)S(1)}, bf16[256,1024]{1,0:T(8,128)(2,1)S(1)}, u32[]{:S(2)}, u32[]{:S(2)}) %collective-permute-start.17) | collective-permute-done | bytes 524320 | tf_op jit(solution)/shard_map/ppermute | solution.py:353
  139.9 8.3 %feed.1 = (bf16[256,1024]{1,0:T(8,128)(2,1)S(1)}, f32[256,1024]{1,0:T(8,128)S(1)}, bf16[512,656]{1,0:T(8,128)(2,1)S(1)}, bf16[512,656]{1,0:T(8,128)(2,1)S(1)}, b...) custom-call(s32[8]{0:T(128)S(1)} %get-tuple-element.133.refs_0_.refs_1_, ...), custom_call_target="tpu_custom_call" | custom-call | flops 8000000000 | bytes 8388608 | tf_op jit(solution)/shard_map/feed/pallas_call | solution.py:414
  151.9 4.5 %feed_grad.1 = bf16[8,1968,128]{2,1,0:T(8,128)(2,1)} custom-call(s32[8]{0:T(128)S(1)} %get-tuple-element.133.refs_0_.refs_1_, bf16[512,656]{1,0:T(8,128)(2,1)S(1)} %get-tuple-element.190.refs_1_, bf16[512,656]{1,0:T(8,128)(2,1)S(1)} %get-tuple-element.191.refs_2_, bf16[512,656]{1,0:T(8,128)(2,1)S(1)} %get-tuple-element.192.refs_3_, ...), custom_call_target="tpu_custom_call" | custom-call | flops 5000000000 | bytes 8388608 | tf_op jit(solution)/shard_map/feed_grad/pallas_call | solution.py:414
  156.4 8.0 %collective-permute-done.20.refs_1_ = bf16[256,1024]{1,0:T(8,128)(2,1)S(1)} collective-permute-done((bf16[256,1024]{1,0:T(8,128)(2,1)S(1)}, bf16[256,1024]{1,0:T(8,128)(2,1)S(1)}, u32[]{:S(2)}, u32[]{:S(2)}) %collective-permute-start.20) | collective-permute-done | bytes 524320 | tf_op jit(solution)/shard_map/ppermute | solution.py:353
  171.1 3.7 %all-to-all-start.2 = ((bf16[8,64,256]{2,1,0:T(8,128)(2,1)}), bf16[8,64,256]{2,1,0:T(8,128)(2,1)S(1)}, u32[]{:S(2)}, u32[]{:S(2)}) async-start(bf16[8,64,256]{2,1,0:T(8,128)(2,1)} %mix_back.1), calls=%async_computation.2 | async-start | bytes 524288 | tf_op jit(solution)/shard_map/all_to_all | solution.py:357
  182.4 10.3 %collective-permute-done.22.refs_1_ = bf16[4,256,128]{2,1,0:T(8,128)(2,1)S(1)} collective-permute-done((bf16[4,256,128]{2,1,0:T(8,128)(2,1)S(1)}, bf16[4,256,128]{2,1,0:T(8,128)(2,1)S(1)}, u32[]{:S(2)}, u32[]{:S(2)}) %collective-permute-start.22) | collective-permute-done | bytes 262176 | tf_op jit(solution)/shard_map/ppermute | solution.py:345
  193.4 15.1 %attend_back.1 = bf16[8,192,256]{2,1,0:T(8,128)(2,1)} custom-call(s32[8]{0:T(128)S(1)} %get-tuple-element.132.refs_0_, bf16[8,192,256]{2,1,0:T(8,128)(2,1)} %copy-done.10, f32[8,64,256]{2,1,0:T(8,128)} %get-tuple-element.153.refs_2_, f32[8,1,256]{2,1,0:T(1,128)} %get-tuple-element.154.refs_3_, bf16[8,64,256]{2,1,0:T(8,128)(2,1)} %copy-done.14, ...), custom_call_target="tpu_custom_call" | custom-call | flops 28000000000 | bytes 8388608 | tf_op jit(solution)/shard_map/attend_back/pallas_call | solution.py:414
  208.6 3.6 %all-to-all-start.3 = ((bf16[8,192,256]{2,1,0:T(8,128)(2,1)}), bf16[8,192,256]{2,1,0:T(8,128)(2,1)S(1)}, u32[]{:S(2)}, u32[]{:S(2)}) async-start(bf16[8,192,256]{2,1,0:T(8,128)(2,1)} %attend_back.1), calls=%async_computation.3 | async-start | bytes 1572864 | tf_op jit(solution)/shard_map/all_to_all | solution.py:357
  212.1 3.5 %result.1 = bf16[128,1024]{1,0:T(8,128)(2,1)} custom-call(s32[8]{0:T(128)S(1)} %get-tuple-element.133.refs_0_.refs_1_, s32[1,128]{1,0:T(1,128)S(1)} %reshape.266.refs_1_, f32[256,1024]{1,0:T(8,128)} %get-tuple-element.194.refs_2_, bf16[256,1024]{1,0:T(8,128)(2,1)} %copy-done.12, bf16[256,1024]{1,0:T(8,128)(2,1)} %copy-done.25), custom_call_target="tpu_custom_call" | custom-call | flops 3000000000 | bytes 8388608 | tf_op jit(solution)/shard_map/result/pallas_call | solution.py:414
  216.8 15.9 %all-to-all-done.3 = bf16[8,192,256]{2,1,0:T(8,128)(2,1)S(1)} async-done(((bf16[8,192,256]{2,1,0:T(8,128)(2,1)}), bf16[8,192,256]{2,1,0:T(8,128)(2,1)S(1)}, u32[]{:S(2)}, u32[]{:S(2)}) %all-to-all-start.3) | async-done | bytes 786464 | tf_op jit(solution)/shard_map/all_to_all | solution.py:357
  233.5 4.4 %project_back.1 = (bf16[4,768,128]{2,1,0:T(8,128)(2,1)}, f32[4,768,128]{2,1,0:T(8,128)}, bf16[256,1024]{1,0:T(8,128)(2,1)S(1)}, f32[256,1024]{1,0:T(8,128)S(1)}) custom-call(s32[1]{0:T(128)} %bitcast.26.refs_0_, bf16[2,768,256]{2,1,0:T(8,128)(2,1)} %bitcast.185, bf16[512,1024]{1,0:T(8,128)(2,1)} %get-tuple-element.218.refs_2_, ...), custom_call_target="tpu_custom_call" | custom-call | flops 3000000000 | bytes 8388608 | tf_op jit(solution)/shard_map/project_back/pallas_call | solution.py:414
  241.6 3.8 %all-to-all-start.4 = ((bf16[8,16,1024]{2,1,0:T(8,128)(2,1)}), bf16[8,16,1024]{2,1,0:T(8,128)(2,1)S(1)}, u32[]{:S(2)}, u32[]{:S(2)}) async-start(bf16[8,16,1024]{2,1,0:T(8,128)(2,1)} %bitcast.50), calls=%async_computation.4 | async-start | bytes 524288 | tf_op jit(solution)/shard_map/all_to_all | solution.py:357
  249.8 4.3 %collective-permute-done.27.refs_4_ = bf16[256,1024]{1,0:T(8,128)(2,1)S(1)} collective-permute-done((bf16[256,1024]{1,0:T(8,128)(2,1)S(1)}, bf16[256,1024]{1,0:T(8,128)(2,1)S(1)}, u32[]{:S(2)}, u32[]{:S(2)}) %collective-permute-start.27) | collective-permute-done | bytes 524320 | tf_op jit(solution)/shard_map/ppermute | solution.py:353
  257.2 3.8 %collective-permute-done.29 = bf16[256,128]{1,0:T(8,128)(2,1)S(1)} collective-permute-done((bf16[256,128]{1,0:T(8,128)(2,1)S(1)}, bf16[256,128]{1,0:T(8,128)(2,1)S(1)}, u32[]{:S(2)}, u32[]{:S(2)}) %collective-permute-start.29) | collective-permute-done | bytes 65568 | tf_op jit(solution)/shard_map/ppermute | solution.py:345
  267.4 5.1 %collective-permute-done.31 = bf16[768,128]{1,0:T(8,128)(2,1)S(1)} collective-permute-done((bf16[768,128]{1,0:T(8,128)(2,1)S(1)}, bf16[768,128]{1,0:T(8,128)(2,1)S(1)}, u32[]{:S(2)}, u32[]{:S(2)}) %collective-permute-start.31) | collective-permute-done | bytes 196640 | tf_op jit(solution)/shard_map/ppermute | solution.py:345
  (222 shorter events, 100.4 us)
Async XLA Ops:
  7.2 106.9 %all-gather.5.cloned.1.call-start = ((), (), s32[]{:S(2)}) async-start(), calls=%async_computation.7 | async-start | bytes 2101248 | tf_op jit(solution)/shard_map/all_gather | solution.py:982
  9.4 28.2 %collective-permute-start.3 = (bf16[784,128]{1,0:T(8,128)(2,1)S(1)}, bf16[784,128]{1,0:T(8,128)(2,1)S(1)}, u32[]{:S(2)}, u32[]{:S(2)}) collective-permute-start(bf16[784,128]{1,0:T(8,128)(2,1)S(1)} %maximum_maximum_fusion.refs_3_), channel_id=1, source_target_pairs={{0,4},{4,0},{8,12},{12,8},{16,20},{20,16},{24,28},{28,24},{1,5},{5... | collective-permute-start | bytes 602120 | tf_op jit(solution)/shard_map/ppermute | solution.py:345
  16.0 19.5 %collective-permute-start.1 = (bf16[784,128]{1,0:T(8,128)(2,1)S(1)}, bf16[784,128]{1,0:T(8,128)(2,1)S(1)}, u32[]{:S(2)}, u32[]{:S(2)}) collective-permute-start(bf16[784,128]{1,0:T(8,128)(2,1)S(1)} %maximum_maximum_fusion.refs_3_), channel_id=1, source_target_pairs={{0,16},{4,20},{8,24},{12,28},{16,0},{20,4},{24,8},{28,12},{1,17},{... | collective-permute-start | bytes 602120 | tf_op jit(solution)/shard_map/ppermute | solution.py:345
  16.0 19.5 %collective-permute-start = (bf16[784,128]{1,0:T(8,128)(2,1)S(1)}, bf16[784,128]{1,0:T(8,128)(2,1)S(1)}, u32[]{:S(2)}, u32[]{:S(2)}) collective-permute-start(bf16[784,128]{1,0:T(8,128)(2,1)S(1)} %maximum_maximum_fusion.refs_3_), channel_id=1, source_target_pairs={{0,8},{4,12},{8,0},{12,4},{16,24},{20,28},{24,16},{28,20},{1,9},{5... | collective-permute-start | bytes 602120 | tf_op jit(solution)/shard_map/ppermute | solution.py:345
  48.7 35.8 %all-to-all-start = ((bf16[8,192,256]{2,1,0:T(8,128)(2,1)}), bf16[8,192,256]{2,1,0:T(8,128)(2,1)S(1)}, u32[]{:S(2)}, u32[]{:S(2)}) async-start(bf16[8,192,256]{2,1,0:T(8,128)(2,1)} %get-tuple-element.152), calls=%async_computation | async-start | bytes 1572864 | tf_op jit(solution)/shard_map/all_to_all | solution.py:357
  53.8 85.4 %all-gather.7.cloned.1.call-start = ((), (), s32[]{:S(2)}) async-start(), calls=%async_computation.8 | async-start | bytes 3022848 | tf_op jit(solution)/shard_map/all_gather | solution.py:983
  53.8 30.7 %collective-permute-start.7 = (bf16[2,8,1024]{2,1,0:T(8,128)(2,1)S(1)}, bf16[2,8,1024]{2,1,0:T(8,128)(2,1)S(1)}, u32[]{:S(2)}, u32[]{:S(2)}) collective-permute-start(bf16[2,8,1024]{2,1,0:T(8,128)(2,1)S(1)} %get-tuple-element.157), channel_id=1, source_target_pairs={{0,8},{4,12},{8,0},{12,4},{16,24},{20,28},{24,16},{28,20},{1,9},{5... | collective-permute-start | bytes 98312 | tf_op jit(solution)/shard_map/ppermute | solution.py:345
  55.9 29.0 %collective-permute-start.8 = (bf16[2,8,1024]{2,1,0:T(8,128)(2,1)S(1)}, bf16[2,8,1024]{2,1,0:T(8,128)(2,1)S(1)}, u32[]{:S(2)}, u32[]{:S(2)}) collective-permute-start(bf16[2,8,1024]{2,1,0:T(8,128)(2,1)S(1)} %get-tuple-element.158), channel_id=1, source_target_pairs={{0,16},{4,20},{8,24},{12,28},{16,0},{20,4},{24,8},{28,12},{1,17},{... | collective-permute-start | bytes 98312 | tf_op jit(solution)/shard_map/ppermute | solution.py:345
  59.0 213.5 %reduce-scatter.2.cloned.1.call-start = ((), (), s32[]{:S(2)}) async-start(), calls=%async_computation.6 | async-start | bytes 4534272 | tf_op jit(solution)/shard_map/reduce_scatter | solution.py:1052
  59.1 39.1 %collective-permute-start.9 = (bf16[2,8,1024]{2,1,0:T(8,128)(2,1)S(1)}, bf16[2,8,1024]{2,1,0:T(8,128)(2,1)S(1)}, u32[]{:S(2)}, u32[]{:S(2)}) collective-permute-start(bf16[2,8,1024]{2,1,0:T(8,128)(2,1)S(1)} %get-tuple-element.159), channel_id=1, source_target_pairs={{0,24},{4,28},{8,16},{12,20},{16,8},{20,12},{24,0},{28,4},{1,25},{... | collective-permute-start | bytes 98312 | tf_op jit(solution)/shard_map/ppermute | solution.py:345
  59.2 38.9 %collective-permute-start.10 = (bf16[2,8,1024]{2,1,0:T(8,128)(2,1)S(1)}, bf16[2,8,1024]{2,1,0:T(8,128)(2,1)S(1)}, u32[]{:S(2)}, u32[]{:S(2)}) collective-permute-start(bf16[2,8,1024]{2,1,0:T(8,128)(2,1)S(1)} %get-tuple-element.160), channel_id=1, source_target_pairs={{0,4},{4,0},{8,12},{12,8},{16,20},{20,16},{24,28},{28,24},{1,5},{5... | collective-permute-start | bytes 98312 | tf_op jit(solution)/shard_map/ppermute | solution.py:345
  61.2 37.0 %collective-permute-start.11 = (bf16[2,8,1024]{2,1,0:T(8,128)(2,1)S(1)}, bf16[2,8,1024]{2,1,0:T(8,128)(2,1)S(1)}, u32[]{:S(2)}, u32[]{:S(2)}) collective-permute-start(bf16[2,8,1024]{2,1,0:T(8,128)(2,1)S(1)} %get-tuple-element.161), channel_id=1, source_target_pairs={{0,12},{4,8},{8,4},{12,0},{16,28},{20,24},{24,20},{28,16},{1,13},{... | collective-permute-start | bytes 98312 | tf_op jit(solution)/shard_map/ppermute | solution.py:345
  84.5 13.7 %collective-permute-start.12 = (bf16[2,8,1024]{2,1,0:T(8,128)(2,1)S(1)}, bf16[2,8,1024]{2,1,0:T(8,128)(2,1)S(1)}, u32[]{:S(2)}, u32[]{:S(2)}) collective-permute-start(bf16[2,8,1024]{2,1,0:T(8,128)(2,1)S(1)} %get-tuple-element.162), channel_id=1, source_target_pairs={{0,20},{4,16},{8,28},{12,24},{16,4},{20,0},{24,12},{28,8},{1,21},{... | collective-permute-start | bytes 98312 | tf_op jit(solution)/shard_map/ppermute | solution.py:345
  100.0 14.1 %collective-permute-start.15 = (bf16[2,8,2,8,1024]{4,3,0,1,2:T(8,128)(2,1)S(1)}, bf16[2,8,2,8,1024]{4,3,0,1,2:T(8,128)(2,1)}, u32[]{:S(2)}, u32[]{:S(2)}) collective-permute-start(bf16[2,8,2,8,1024]{4,3,0,1,2:T(8,128)(2,1)S(1)} %pad_maximum_fusion.2), channel_id=1, source_target_pairs={{0,2},{1,3},{2,0},{3,1},{4,6},{5,7},{6,4},{7,5},{8,10},{9,11},{10,... | collective-permute-start | bytes 1572872 | tf_op jit(solution)/shard_map/ppermute | solution.py:353
  120.9 14.0 %collective-permute-start.17 = (bf16[256,1024]{1,0:T(8,128)(2,1)S(1)}, bf16[256,1024]{1,0:T(8,128)(2,1)S(1)}, u32[]{:S(2)}, u32[]{:S(2)}) collective-permute-start(bf16[256,1024]{1,0:T(8,128)(2,1)S(1)} %add_convert_fusion.3.refs_3_), channel_id=1, source_target_pairs={{0,2},{1,3},{2,0},{3,1},{4,6},{5,7},{6,4},{7,5},{8,10},{9,11},{10,... | collective-permute-start | bytes 1572872 | tf_op jit(solution)/shard_map/ppermute | solution.py:353
  150.3 14.0 %collective-permute-start.20 = (bf16[256,1024]{1,0:T(8,128)(2,1)S(1)}, bf16[256,1024]{1,0:T(8,128)(2,1)S(1)}, u32[]{:S(2)}, u32[]{:S(2)}) collective-permute-start(bf16[256,1024]{1,0:T(8,128)(2,1)S(1)} %add_convert_fusion.2.refs_0_), channel_id=1, source_target_pairs={{0,2},{1,3},{2,0},{3,1},{4,6},{5,7},{6,4},{7,5},{8,10},{9,11},{10,... | collective-permute-start | bytes 1572872 | tf_op jit(solution)/shard_map/ppermute | solution.py:353
  171.1 21.5 %all-to-all-start.2 = ((bf16[8,64,256]{2,1,0:T(8,128)(2,1)}), bf16[8,64,256]{2,1,0:T(8,128)(2,1)S(1)}, u32[]{:S(2)}, u32[]{:S(2)}) async-start(bf16[8,64,256]{2,1,0:T(8,128)(2,1)} %mix_back.1), calls=%async_computation.2 | async-start | bytes 524288 | tf_op jit(solution)/shard_map/all_to_all | solution.py:357
  176.2 16.4 %collective-permute-start.24 = (bf16[256,1024]{1,0:T(8,128)(2,1)S(1)}, bf16[256,1024]{1,0:T(8,128)(2,1)S(1)}, u32[]{:S(2)}, u32[]{:S(2)}) collective-permute-start(bf16[256,1024]{1,0:T(8,128)(2,1)S(1)} %add_convert_fusion.1.refs_3_), channel_id=1, source_target_pairs={{0,2},{1,3},{2,0},{3,1},{4,6},{5,7},{6,4},{7,5},{8,10},{9,11},{10,... | collective-permute-start | bytes 1572872 | tf_op jit(solution)/shard_map/ppermute | solution.py:353
  208.6 24.1 %all-to-all-start.3 = ((bf16[8,192,256]{2,1,0:T(8,128)(2,1)}), bf16[8,192,256]{2,1,0:T(8,128)(2,1)S(1)}, u32[]{:S(2)}, u32[]{:S(2)}) async-start(bf16[8,192,256]{2,1,0:T(8,128)(2,1)} %attend_back.1), calls=%async_computation.3 | async-start | bytes 1572864 | tf_op jit(solution)/shard_map/all_to_all | solution.py:357
  238.0 23.0 %collective-permute-start.25 = (bf16[4,768,128]{2,1,0:T(8,128)(2,1)}, bf16[4,768,128]{2,1,0:T(8,128)(2,1)}, u32[]{:S(2)}, u32[]{:S(2)}) collective-permute-start(bf16[4,768,128]{2,1,0:T(8,128)(2,1)} %get-tuple-element.221), channel_id=1, source_target_pairs={{0,4},{4,0},{8,12},{12,8},{16,20},{20,16},{24,28},{28,24},{1,5},{5... | collective-permute-start | bytes 2359304 | tf_op jit(solution)/shard_map/ppermute | solution.py:345
  240.1 14.0 %collective-permute-start.27 = (bf16[256,1024]{1,0:T(8,128)(2,1)S(1)}, bf16[256,1024]{1,0:T(8,128)(2,1)S(1)}, u32[]{:S(2)}, u32[]{:S(2)}) collective-permute-start(bf16[256,1024]{1,0:T(8,128)(2,1)S(1)} %add_convert_fusion.refs_3_), channel_id=1, source_target_pairs={{0,2},{1,3},{2,0},{3,1},{4,6},{5,7},{6,4},{7,5},{8,10},{9,11},{10,... | collective-permute-start | bytes 1572872 | tf_op jit(solution)/shard_map/ppermute | solution.py:353
  241.6 25.7 %all-to-all-start.4 = ((bf16[8,16,1024]{2,1,0:T(8,128)(2,1)}), bf16[8,16,1024]{2,1,0:T(8,128)(2,1)S(1)}, u32[]{:S(2)}, u32[]{:S(2)}) async-start(bf16[8,16,1024]{2,1,0:T(8,128)(2,1)} %bitcast.50), calls=%async_computation.4 | async-start | bytes 524288 | tf_op jit(solution)/shard_map/all_to_all | solution.py:357
  264.7 18.5 %collective-permute-start.32 = (bf16[768,128]{1,0:T(8,128)(2,1)S(1)}, bf16[768,128]{1,0:T(8,128)(2,1)S(1)}, u32[]{:S(2)}, u32[]{:S(2)}) collective-permute-start(bf16[768,128]{1,0:T(8,128)(2,1)S(1)} %get-tuple-element.233), channel_id=1, source_target_pairs={{0,16},{4,20},{8,24},{12,28},{16,0},{20,4},{24,8},{28,12},{1,17},{... | collective-permute-start | bytes 589832 | tf_op jit(solution)/shard_map/ppermute | solution.py:345
  264.7 18.4 %collective-permute-start.33 = (bf16[768,128]{1,0:T(8,128)(2,1)S(1)}, bf16[768,128]{1,0:T(8,128)(2,1)S(1)}, u32[]{:S(2)}, u32[]{:S(2)}) collective-permute-start(bf16[768,128]{1,0:T(8,128)(2,1)S(1)} %get-tuple-element.234), channel_id=1, source_target_pairs={{0,24},{4,28},{8,16},{12,20},{16,8},{20,12},{24,0},{28,4},{1,25},{... | collective-permute-start | bytes 589832 | tf_op jit(solution)/shard_map/ppermute | solution.py:345
  (50 other events, 335.9 us)
Sparse Core Ops, SparseCore 0:
  19.6 63.5 all-gather.4
  85.9 53.1 all-gather.6
  156.5 96.6 reduce-scatter.1
